TPU v7x, 128 devices: a whole 4x4x4 slice. The times are simulated.
128 devices in a mesh: wide: 32 (over x, z, core), narrow: 4 (over y).
Axes of the slice: x: 4, y: 4, z: 4, core: 2. Of those that a mesh axis runs over, the one named last changes fastest.
Arguments:
- member: bfloat16 [2048, 8192], P('narrow', 'wide'), may hold values from 0.01 to 300, as said below
Outputs:
- transition: float32 [8192, 8192], P('wide', 'narrow')
- stationary: float32 [8192], P('wide')
Inputs may be any that keep to these rules, and one draw needn't show every extreme that they name: `member`: strictly positive weights.
All inputs are finite; a program needn't handle non-finite values.
Results may differ from a plain program's by a relative error of at most 0.0003.
Values may be sent and summed in bfloat16 or wider, within the bound.
No kernel may reach another device: no remote copies, remote signals or barrier semaphores. Data moves between devices by JAX's collectives and lax.ppermute only.
A program may use at most 128 MiB of HBM per device.

v0:
```python
import jax
import jax.numpy as jnp
from jax import lax
from jax.experimental import pallas as pl
from jax.experimental.pallas import tpu as pltpu
from jax.sharding import Mesh, PartitionSpec as P


STATES = 8192
TAU = 64
FRAMES = 2048
WIDE = ("x", "z", "c")
ALL = ("x", "z", "c", "y")
BLOCK = 512
WIDTH = 256
COLS = 2048
GROUPS = COLS // WIDTH
FIRST = 256
STACK = 2 * WIDTH + 16
LANES = 128


def place(x, y, z, c):
    return ((x * 4 + z) * 2 + c) * 4 + y


def across():
    return [
        (place(x, y, z, c), place(y, x, z, c))
        for x in range(4) for y in range(4) for z in range(4) for c in range(2)
    ]


def along(k):
    return [(i, (i + k) % 4) for i in range(4)]


def ring(v, axis):
    return [v] + [lax.ppermute(v, axis, along(k)) for k in (1, 2, 3)]


def to_all(values):
    sent = jnp.broadcast_to(values[None], (128,) + values.shape)
    return lax.all_to_all(sent, ALL, 0, 0).reshape((32, 4) + values.shape)


VMEM = pl.BlockSpec(memory_space=pltpu.VMEM)
SMEM = pl.BlockSpec(memory_space=pltpu.SMEM)


def f32(*shape):
    return jax.ShapeDtypeStruct(shape, jnp.float32)


def row_parts(sym_ref, ratio_rows, ratio_cols):
    parts = []
    for top in range(0, WIDTH, 64):
        acc = jnp.zeros((64, LANES), jnp.float32)
        for k in range(COLS // LANES):
            g, lo = divmod(k * LANES, WIDTH)
            acc += sym_ref[top:top + 64, k * LANES:(k + 1) * LANES] / (
                ratio_rows[top:top + 64] + ratio_cols[g:g + 1, lo:lo + LANES])
        parts.append(acc)
    return jnp.sum(jnp.concatenate(parts, axis=0).T, axis=0, keepdims=True)


def products(where, left, by_x, by_z, before):
    def kernel(where_ref, left_ref, *refs):
        x_refs, z_refs = refs[:4], refs[4:8]
        x, z, c = where_ref[0], where_ref[2], where_ref[3]
        if before is None:
            sym_ref, visit_ref, total_ref, visit_row_ref, total_row_ref = refs[8:]
            core = c
            sums = lax.dot_general(
                left_ref[:2 * WIDTH], left_ref[2 * WIDTH:], (((1,), (1,)), ((), ())),
                preferred_element_type=jnp.float32)
            sums = jnp.sum(sums[:, 6:9], axis=1, keepdims=True)
            visit = jnp.broadcast_to(sums[:WIDTH], (WIDTH, LANES))
            visit_row_ref[...] = visit
            total_row_ref[...] = visit + sums[WIDTH:]
        else:
            visit_row_ref, total_row_ref = refs[11:13]
            sym_ref, visit_ref, total_ref, send_ref = refs[13:]
            core = 1 - c
            sym_ref[...], visit_ref[...], total_ref[...] = (ref[...] for ref in refs[8:11])
        for dz in range(4):
            acc = jnp.zeros((STACK, WIDTH), jnp.float32)
            for dx in range(4):
                lo = pl.multiple_of(lax.rem(x + 4 - dx, 4) * BLOCK, BLOCK)
                block = jnp.concatenate([x_refs[dx][dz], z_refs[dz][dx]], axis=0)
                acc += jnp.dot(left_ref[:, pl.ds(lo, BLOCK)], block,
                               preferred_element_type=jnp.float32)
            g = lax.rem(z + 4 - dz, 4) * 2 + core
            sym_ref[:, pl.ds(pl.multiple_of(g * WIDTH, WIDTH), WIDTH)] = (
                acc[:WIDTH] + acc[WIDTH:2 * WIDTH])
            frame = acc[2 * WIDTH:]
            visit_ref[pl.ds(g, 1), :] = jnp.sum(frame[:3], axis=0, keepdims=True)
            total_ref[pl.ds(g, 1), :] = jnp.sum(frame[:6], axis=0, keepdims=True)
        if before is not None:
            send_ref[...] = row_parts(sym_ref, visit_row_ref[...] / total_row_ref[...],
                                      visit_ref[...] / total_ref[...])

    operands = [where, left] + by_x + by_z
    out = [f32(WIDTH, COLS), f32(GROUPS, WIDTH), f32(GROUPS, WIDTH)]
    if before is None:
        out += [f32(WIDTH, LANES)] * 2
    else:
        operands += list(before)
        out += [f32(1, WIDTH)]
    return pl.pallas_call(
        kernel,
        in_specs=[SMEM] + [VMEM] * (len(operands) - 1),
        out_specs=[VMEM] * len(out),
        out_shape=out,
        compiler_params=pltpu.CompilerParams(vmem_limit_bytes=16 << 20),
    )(*[operands[0]] + [pltpu.with_memory_space_constraint(v, pltpu.VMEM) for v in operands[1:]])


def three_parts(v):
    hi = v.astype(jnp.bfloat16)
    rest = v - hi.astype(jnp.float32)
    mid = rest.astype(jnp.bfloat16)
    lo = (rest - mid.astype(jnp.float32)).astype(jnp.bfloat16)
    return [hi, mid, lo]


def own_rows(member):
    y = lax.axis_index("y")
    later = [lax.ppermute(member, "y", along(-k)) for k in (1, 2, 3)]
    turned = jnp.concatenate([member] + later, axis=0).T
    rows = jnp.roll(turned, y * BLOCK, axis=1)
    return jnp.pad(rows, ((0, 0), (TAU, TAU)))


def frame_weights(member, after):
    part = jnp.sum(member, axis=1, dtype=jnp.float32)
    got = to_all(part)
    got, _ = lax.optimization_barrier((got, after))
    frame = jnp.sum(got, axis=0).reshape(FRAMES)
    up = jnp.pad(frame[TAU:], (0, TAU))
    down = jnp.pad(frame[:FRAMES - TAU], (TAU, 0))
    weights = jnp.stack(three_parts(up) + three_parts(down) + three_parts(frame))
    return jnp.pad(weights, ((0, 7), (0, 0)))


def shards(member):
    where = jnp.stack([lax.axis_index(a) for a in ("x", "y", "z", "c")])
    moved = lax.ppermute(member, ALL, across())
    once_x = jnp.stack(ring(moved[:FIRST], "z"))
    once_z = jnp.stack(ring(moved[FIRST:], "x"))
    by_x = ring(once_x, "x")
    by_z = ring(once_z, "z")
    other_x = [lax.ppermute(v, "c", [(0, 1), (1, 0)]) for v in by_x]
    other_z = [lax.ppermute(v, "c", [(0, 1), (1, 0)]) for v in by_z]
    rows = own_rows(member)
    left = jnp.concatenate([rows[:, :FRAMES], rows[:, 2 * TAU:], frame_weights(member, (once_x, once_z))], axis=0)
    own = products(where, left, by_x, by_z, None)
    sym, visit_cols, _, part = products(where, left, other_x, other_z, own)
    visit_cols = visit_cols.reshape(COLS)
    visit_rows = own[3][:, 0]
    part = part.reshape(WIDTH)
    w = (where[0] * 4 + where[2]) * 2 + where[3]
    for step in range(3):
        totals = jnp.sum(to_all(part), axis=1).reshape(STATES)
        total_rows = lax.dynamic_slice_in_dim(totals, w * WIDTH, WIDTH)
        total_cols = lax.dynamic_slice_in_dim(totals, where[1] * COLS, COLS)
        if step == 2:
            break
        estimate = sym / ((visit_rows / total_rows)[:, None] + (visit_cols / total_cols)[None, :])
        part = jnp.sum(estimate, axis=1)
    transition = STATES * estimate / total_rows[:, None]
    stationary = STATES * total_rows / jnp.sum(totals)
    return (transition, stationary)


def solution(mesh):
    mesh = Mesh(mesh.devices.reshape(4, 4, 2, 4), ALL)
    return jax.shard_map(
        shards,
        mesh=mesh,
        in_specs=(P("y", WIDE),),
        out_specs=(P(WIDE, "y"), P(WIDE)),
        check_vma=False,
    )
```

profile of v0, /device:TPU:1, one launch (start us, length us, event | category | flops | bytes accessed | tf_op | source)
XLA Modules:
  0.0 150.3 jit_solution(9011001651635280979)
XLA Ops:
  0.6 1.6 %collective-permute-start.3 = (bf16[512,256]{1,0:T(8,128)(2,1)}, bf16[512,256]{1,0:T(8,128)(2,1)S(1)}, u32[]{:S(2)}, u32[]{:S(2)}) collective-permute-start(bf16[512,256]{1,0:T(8,128)(2,1)} %param.1), channel_id=1, source_target_pairs={{0,0},{4,4},{8,8},{12,12},{16,16},{20,20},{24,24},{28,28},{1,32},{... | collective-permute-start | bytes 786440 | tf_op jit(solution)/shard_map/ppermute | solution.py:148
  2.3 11.5 %collective-permute-start.7 = (bf16[256,256]{1,0:T(8,128)(2,1)S(1)}, bf16[256,256]{1,0:T(8,128)(2,1)S(1)}, u32[]{:S(2)}, u32[]{:S(2)}) collective-permute-start(bf16[256,256]{1,0:T(8,128)(2,1)S(1)} %get-tuple-element.28), channel_id=1, source_target_pairs={{0,32},{32,64},{64,96},{96,0},{1,33},{33,65},{65,97},{97,1},{2,34}... | collective-permute-start | bytes 393224 | tf_op jit(solution)/shard_map/ppermute | solution.py:39
  13.8 9.7 %collective-permute-start.8 = (bf16[256,256]{1,0:T(8,128)(2,1)S(1)}, bf16[256,256]{1,0:T(8,128)(2,1)S(1)}, u32[]{:S(2)}, u32[]{:S(2)}) collective-permute-start(bf16[256,256]{1,0:T(8,128)(2,1)S(1)} %get-tuple-element.28), channel_id=1, source_target_pairs={{0,64},{32,96},{64,0},{96,32},{1,65},{33,97},{65,1},{97,33},{2,66}... | collective-permute-start | bytes 393224 | tf_op jit(solution)/shard_map/ppermute | solution.py:39
  23.5 1.6 %collective-permute-start.4 = (bf16[256,256]{1,0:T(8,128)(2,1)S(1)}, bf16[256,256]{1,0:T(8,128)(2,1)S(1)}, u32[]{:S(2)}, u32[]{:S(2)}) collective-permute-start(bf16[256,256]{1,0:T(8,128)(2,1)S(1)} %get-tuple-element.29), channel_id=1, source_target_pairs={{0,8},{8,16},{16,24},{24,0},{1,9},{9,17},{17,25},{25,1},{2,10},{10... | collective-permute-start | bytes 393224 | tf_op jit(solution)/shard_map/ppermute | solution.py:39
  25.1 1.8 %copy.26 = bf16[512,256]{0,1:T(8,128)(2,1)} copy(bf16[512,256]{1,0:T(8,128)(2,1)} %param.1) | data formatting | bytes 524288 | tf_op args[0]
  26.9 2.3 %collective-permute-start = (bf16[512,256]{0,1:T(8,128)(2,1)}, bf16[512,256]{0,1:T(8,128)(2,1)}, u32[]{:S(2)}, u32[]{:S(2)}) collective-permute-start(bf16[512,256]{0,1:T(8,128)(2,1)} %copy.26), channel_id=1, source_target_pairs={{0,3},{1,0},{2,1},{3,2},{4,7},{5,4},{6,5},{7,6},{8,11},{9,8},{10,9... | collective-permute-start | bytes 786440 | tf_op jit(solution)/shard_map/ppermute | solution.py:129
  29.2 3.4 %collective-permute-start.5 = (bf16[256,256]{1,0:T(8,128)(2,1)S(1)}, bf16[256,256]{1,0:T(8,128)(2,1)S(1)}, u32[]{:S(2)}, u32[]{:S(2)}) collective-permute-start(bf16[256,256]{1,0:T(8,128)(2,1)S(1)} %get-tuple-element.29), channel_id=1, source_target_pairs={{0,16},{8,24},{16,0},{24,8},{1,17},{9,25},{17,1},{25,9},{2,18},{10... | collective-permute-start | bytes 393224 | tf_op jit(solution)/shard_map/ppermute | solution.py:39
  33.3 1.1 convert_reduce_fusion
  35.3 9.8 %all-to-all-start = ((f32[128,1,512]{2,1,0:T(1,128)}), f32[128,1,512]{2,1,0:T(1,128)S(1)}, u32[]{:S(2)}, u32[]{:S(2)}) async-start(f32[128,1,512]{2,1,0:T(1,128)} %broadcast_in_dim.8), calls=%async_computation | async-start | bytes 524288 | tf_op jit(solution)/shard_map/all_to_all | solution.py:44
  45.1 1.4 collective-permute-start.2
  46.6 1.4 collective-permute-start.18
  48.0 2.9 %collective-permute-start.20 = (bf16[4,256,256]{2,1,0:T(8,128)(2,1)S(1)}, bf16[4,256,256]{2,1,0:T(8,128)(2,1)S(1)}, u32[]{:S(2)}, u32[]{:S(2)}) collective-permute-start(bf16[4,256,256]{2,1,0:T(8,128)(2,1)S(1)} %pad_maximum_fusion.1.refs_4_), channel_id=1, source_target_pairs={{0,16},{8,24},{16,0},{24,8},{1,17},{9,25},{17,1},{25,9},{2,18},{10... | collective-permute-start | bytes 1572872 | tf_op jit(solution)/shard_map/ppermute | solution.py:39
  52.0 1.2 collective-permute-start.11
  53.3 3.1 %all-to-all-done = f32[128,1,512]{2,1,0:T(1,128)S(1)} async-done(((f32[128,1,512]{2,1,0:T(1,128)}), f32[128,1,512]{2,1,0:T(1,128)S(1)}, u32[]{:S(2)}, u32[]{:S(2)}) %all-to-all-start) | async-done | bytes 262176 | tf_op jit(solution)/shard_map/all_to_all | solution.py:44
  56.3 1.4 reduce.3
  58.7 1.3 maximum_bitcast_fusion
  61.5 2.7 %collective-permute-done.18.refs_5_ = bf16[4,256,256]{2,1,0:T(8,128)(2,1)S(1)} collective-permute-done((bf16[4,256,256]{2,1,0:T(8,128)(2,1)S(1)}, bf16[4,256,256]{2,1,0:T(8,128)(2,1)S(1)}, u32[]{:S(2)}, u32[]{:S(2)}) %collective-permute-start.18) | collective-permute-done | bytes 524320 | tf_op jit(solution)/shard_map/ppermute | solution.py:39
  64.2 2.2 %collective-permute-start.15 = (bf16[4,256,256]{2,1,0:T(8,128)(2,1)S(1)}, bf16[4,256,256]{2,1,0:T(8,128)(2,1)}, u32[]{:S(2)}, u32[]{:S(2)}) collective-permute-start(bf16[4,256,256]{2,1,0:T(8,128)(2,1)S(1)} %pad_maximum_fusion.refs_0_), channel_id=1, source_target_pairs={{0,96},{32,0},{64,32},{96,64},{1,97},{33,1},{65,33},{97,65},{2,98}... | collective-permute-start | bytes 1572872 | tf_op jit(solution)/shard_map/ppermute | solution.py:39
  66.4 9.6 %collective-permute-done.20.refs_6_ = bf16[4,256,256]{2,1,0:T(8,128)(2,1)S(1)} collective-permute-done((bf16[4,256,256]{2,1,0:T(8,128)(2,1)S(1)}, bf16[4,256,256]{2,1,0:T(8,128)(2,1)S(1)}, u32[]{:S(2)}, u32[]{:S(2)}) %collective-permute-start.20) | collective-permute-done | bytes 524320 | tf_op jit(solution)/shard_map/ppermute | solution.py:39
  77.4 2.6 %pad_slice_fusion.1 = (bf16[256,2048]{1,0:T(8,128)(2,1)}, bf16[256,2048]{1,0:T(8,128)(2,1)}) fusion(bf16[256,2048]{1,0:T(8,128)(2,1)S(1)} %fusion.3), kind=kLoop, calls=%fused_computation.12 | loop fusion | bytes 3145728 | tf_op jit(solution)/shard_map/slice | solution.py:156
  80.6 4.7 %collective-permute-done.15.refs_3_ = bf16[4,256,256]{2,1,0:T(8,128)(2,1)} collective-permute-done((bf16[4,256,256]{2,1,0:T(8,128)(2,1)S(1)}, bf16[4,256,256]{2,1,0:T(8,128)(2,1)}, u32[]{:S(2)}, u32[]{:S(2)}) %collective-permute-start.15) | collective-permute-done | bytes 524320 | tf_op jit(solution)/shard_map/ppermute | solution.py:39
  85.3 1.1 collective-permute-start.23
  87.3 1.7 %fusion.1.left_ref = bf16[528,2048]{1,0:T(8,128)(2,1)S(1)} fusion(bf16[9,2048]{1,0:T(8,128)(2,1)S(1)} %stack.90, bf16[256,2048]{1,0:T(8,128)(2,1)} %get-tuple-element.25, bf16[256,2048]{1,0:T(8,128)(2,1)} %get-tuple-element.24), kind=kLoop, calls=%fused_computation.2 | loop fusion | flops 8650752 | bytes 4296704 | tf_op jit(solution)/shard_map/concatenate | solution.py:156
  89.0 4.2 %shard_map.30 = (f32[256,2048]{1,0:T(8,128)S(1)}, f32[8,256]{1,0:T(8,128)S(1)}, f32[8,256]{1,0:T(8,128)S(1)}, f32[256,128]{1,0:T(8,128)S(1)}, f32[256,128]{1,0:T(8,128)S(1)}) custom-call(s32[4]{0:T(128)S(1)} %pad_add_fusion.where_ref, bf16[528,2048]{1,0:T(8,128)(2,1)S(1)} %fusion.1.left_ref, bf16[4,256,256]{2,1,0:T(8,128)(2,1)S(1)} %pad_maximum_fusion.refs_0_, ...), custom_call_target="tpu_custom_call" | custom-call | tf_op jit(solution)/shard_map/pallas_call | solution.py:110
  93.3 5.5 %shard_map.31 = (f32[256,2048]{1,0:T(8,128)S(1)}, f32[8,256]{1,0:T(8,128)S(1)}, f32[8,256]{1,0:T(8,128)}, f32[1,256]{1,0:T(1,128)S(1)}) custom-call(s32[4]{0:T(128)S(1)} %pad_add_fusion.where_ref, bf16[528,2048]{1,0:T(8,128)(2,1)S(1)} %fusion.1.left_ref, bf16[4,256,256]{2,1,0:T(8,128)(2,1)} %collective-permute-done.10.refs_0_, ...), custom_call_target="tpu_custom_call" | custom-call | tf_op jit(solution)/shard_map/pallas_call | solution.py:110
  99.5 6.3 %all-to-all-start.1 = ((f32[128,1,256]{2,1,0:T(1,128)}), f32[128,1,256]{2,1,0:T(1,128)S(1)}, u32[]{:S(2)}, u32[]{:S(2)}) async-start(f32[128,1,256]{2,1,0:T(1,128)} %broadcast_in_dim.9), calls=%async_computation.1 | async-start | bytes 262144 | tf_op jit(solution)/shard_map/all_to_all | solution.py:44
  106.0 9.9 %all-to-all-done.1 = f32[128,1,256]{2,1,0:T(1,128)S(1)} async-done(((f32[128,1,256]{2,1,0:T(1,128)}), f32[128,1,256]{2,1,0:T(1,128)S(1)}, u32[]{:S(2)}, u32[]{:S(2)}) %all-to-all-start.1) | async-done | bytes 131104 | tf_op jit(solution)/shard_map/all_to_all | solution.py:44
  117.0 14.0 %all_to_all.24 = f32[128,1,256]{2,1,0:T(1,128)S(1)} all-to-all(f32[128,1,256]{2,1,0:T(1,128)S(1)} %broadcast_in_dim.10), channel_id=1, replica_groups=mesh['x'=4,'z'=4,'c'=2,'y'=4] {'x','z','c','y'}, dimensions={0} | all-to-all | bytes 262144 | tf_op jit(solution)/shard_map/all_to_all | solution.py:44
  132.1 13.9 %all_to_all.25 = f32[128,1,256]{2,1,0:T(1,128)S(1)} all-to-all(f32[128,1,256]{2,1,0:T(1,128)S(1)} %broadcast_in_dim.11), channel_id=1, replica_groups=mesh['x'=4,'z'=4,'c'=2,'y'=4] {'x','z','c','y'}, dimensions={0} | all-to-all | bytes 262144 | tf_op jit(solution)/shard_map/all_to_all | solution.py:44
  146.0 1.1 fusion.8
  147.2 1.3 multiply_divide_fusion.1
  148.5 1.8 %multiply_divide_fusion = f32[256,2048]{1,0:T(8,128)} fusion(f32[256]{0:T(256)S(1)} %get-tuple-element.23, f32[256,2048]{1,0:T(8,128)S(1)} %get-tuple-element.17, f32[2048]{0:T(1024)S(1)} %dynamic-slice_divide_fusion, f32[256]{0:T(256)S(1)} %dynamic-slice_divide_fusion.2), kind=kLoop, calls=%fused_computation.5 | loop fusion | flops 2097152 | bytes 4204544 | tf_op jit(solution)/shard_map/div | solution.py:171
  (77 shorter events, 11.2 us)
Async XLA Ops:
  0.6 1.6 %collective-permute-start.3 = (bf16[512,256]{1,0:T(8,128)(2,1)}, bf16[512,256]{1,0:T(8,128)(2,1)S(1)}, u32[]{:S(2)}, u32[]{:S(2)}) collective-permute-start(bf16[512,256]{1,0:T(8,128)(2,1)} %param.1), channel_id=1, source_target_pairs={{0,0},{4,4},{8,8},{12,12},{16,16},{20,20},{24,24},{28,28},{1,32},{... | collective-permute-start | bytes 786440 | tf_op jit(solution)/shard_map/ppermute | solution.py:148
  2.3 26.9 %collective-permute-start.7 = (bf16[256,256]{1,0:T(8,128)(2,1)S(1)}, bf16[256,256]{1,0:T(8,128)(2,1)S(1)}, u32[]{:S(2)}, u32[]{:S(2)}) collective-permute-start(bf16[256,256]{1,0:T(8,128)(2,1)S(1)} %get-tuple-element.28), channel_id=1, source_target_pairs={{0,32},{32,64},{64,96},{96,0},{1,33},{33,65},{65,97},{97,1},{2,34}... | collective-permute-start | bytes 393224 | tf_op jit(solution)/shard_map/ppermute | solution.py:39
  13.8 15.4 %collective-permute-start.8 = (bf16[256,256]{1,0:T(8,128)(2,1)S(1)}, bf16[256,256]{1,0:T(8,128)(2,1)S(1)}, u32[]{:S(2)}, u32[]{:S(2)}) collective-permute-start(bf16[256,256]{1,0:T(8,128)(2,1)S(1)} %get-tuple-element.28), channel_id=1, source_target_pairs={{0,64},{32,96},{64,0},{96,32},{1,65},{33,97},{65,1},{97,33},{2,66}... | collective-permute-start | bytes 393224 | tf_op jit(solution)/shard_map/ppermute | solution.py:39
  23.5 9.1 %collective-permute-start.9 = (bf16[256,256]{1,0:T(8,128)(2,1)S(1)}, bf16[256,256]{1,0:T(8,128)(2,1)S(1)}, u32[]{:S(2)}, u32[]{:S(2)}) collective-permute-start(bf16[256,256]{1,0:T(8,128)(2,1)S(1)} %get-tuple-element.28), channel_id=1, source_target_pairs={{0,96},{32,0},{64,32},{96,64},{1,97},{33,1},{65,33},{97,65},{2,98}... | collective-permute-start | bytes 393224 | tf_op jit(solution)/shard_map/ppermute | solution.py:39
  23.5 21.6 %collective-permute-start.4 = (bf16[256,256]{1,0:T(8,128)(2,1)S(1)}, bf16[256,256]{1,0:T(8,128)(2,1)S(1)}, u32[]{:S(2)}, u32[]{:S(2)}) collective-permute-start(bf16[256,256]{1,0:T(8,128)(2,1)S(1)} %get-tuple-element.29), channel_id=1, source_target_pairs={{0,8},{8,16},{16,24},{24,0},{1,9},{9,17},{17,25},{25,1},{2,10},{10... | collective-permute-start | bytes 393224 | tf_op jit(solution)/shard_map/ppermute | solution.py:39
  26.9 24.1 %collective-permute-start = (bf16[512,256]{0,1:T(8,128)(2,1)}, bf16[512,256]{0,1:T(8,128)(2,1)}, u32[]{:S(2)}, u32[]{:S(2)}) collective-permute-start(bf16[512,256]{0,1:T(8,128)(2,1)} %copy.26), channel_id=1, source_target_pairs={{0,3},{1,0},{2,1},{3,2},{4,7},{5,4},{6,5},{7,6},{8,11},{9,8},{10,9... | collective-permute-start | bytes 786440 | tf_op jit(solution)/shard_map/ppermute | solution.py:129
  29.2 22.8 %collective-permute-start.1 = (bf16[512,256]{0,1:T(8,128)(2,1)}, bf16[512,256]{0,1:T(8,128)(2,1)}, u32[]{:S(2)}, u32[]{:S(2)}) collective-permute-start(bf16[512,256]{0,1:T(8,128)(2,1)} %copy.26), channel_id=1, source_target_pairs={{0,2},{1,3},{2,0},{3,1},{4,6},{5,7},{6,4},{7,5},{8,10},{9,11},{10,... | collective-permute-start | bytes 786440 | tf_op jit(solution)/shard_map/ppermute | solution.py:129
  29.2 17.4 %collective-permute-start.5 = (bf16[256,256]{1,0:T(8,128)(2,1)S(1)}, bf16[256,256]{1,0:T(8,128)(2,1)S(1)}, u32[]{:S(2)}, u32[]{:S(2)}) collective-permute-start(bf16[256,256]{1,0:T(8,128)(2,1)S(1)} %get-tuple-element.29), channel_id=1, source_target_pairs={{0,16},{8,24},{16,0},{24,8},{1,17},{9,25},{17,1},{25,9},{2,18},{10... | collective-permute-start | bytes 393224 | tf_op jit(solution)/shard_map/ppermute | solution.py:39
  32.6 15.4 %collective-permute-start.6 = (bf16[256,256]{1,0:T(8,128)(2,1)S(1)}, bf16[256,256]{1,0:T(8,128)(2,1)S(1)}, u32[]{:S(2)}, u32[]{:S(2)}) collective-permute-start(bf16[256,256]{1,0:T(8,128)(2,1)S(1)} %get-tuple-element.29), channel_id=1, source_target_pairs={{0,24},{8,0},{16,8},{24,16},{1,25},{9,1},{17,9},{25,17},{2,26},{10... | collective-permute-start | bytes 393224 | tf_op jit(solution)/shard_map/ppermute | solution.py:39
  35.3 21.1 %all-to-all-start = ((f32[128,1,512]{2,1,0:T(1,128)}), f32[128,1,512]{2,1,0:T(1,128)S(1)}, u32[]{:S(2)}, u32[]{:S(2)}) async-start(f32[128,1,512]{2,1,0:T(1,128)} %broadcast_in_dim.8), calls=%async_computation | async-start | bytes 524288 | tf_op jit(solution)/shard_map/all_to_all | solution.py:44
  45.1 13.7 %collective-permute-start.2 = (bf16[512,256]{0,1:T(8,128)(2,1)}, bf16[512,256]{0,1:T(8,128)(2,1)}, u32[]{:S(2)}, u32[]{:S(2)}) collective-permute-start(bf16[512,256]{0,1:T(8,128)(2,1)} %copy.26), channel_id=1, source_target_pairs={{0,1},{1,2},{2,3},{3,0},{4,5},{5,6},{6,7},{7,4},{8,9},{9,10},{10,1... | collective-permute-start | bytes 786440 | tf_op jit(solution)/shard_map/ppermute | solution.py:129
  46.6 17.6 %collective-permute-start.18 = (bf16[4,256,256]{2,1,0:T(8,128)(2,1)S(1)}, bf16[4,256,256]{2,1,0:T(8,128)(2,1)S(1)}, u32[]{:S(2)}, u32[]{:S(2)}) collective-permute-start(bf16[4,256,256]{2,1,0:T(8,128)(2,1)S(1)} %pad_maximum_fusion.1.refs_4_), channel_id=1, source_target_pairs={{0,8},{8,16},{16,24},{24,0},{1,9},{9,17},{17,25},{25,1},{2,10},{10... | collective-permute-start | bytes 1572872 | tf_op jit(solution)/shard_map/ppermute | solution.py:39
  48.0 28.1 %collective-permute-start.20 = (bf16[4,256,256]{2,1,0:T(8,128)(2,1)S(1)}, bf16[4,256,256]{2,1,0:T(8,128)(2,1)S(1)}, u32[]{:S(2)}, u32[]{:S(2)}) collective-permute-start(bf16[4,256,256]{2,1,0:T(8,128)(2,1)S(1)} %pad_maximum_fusion.1.refs_4_), channel_id=1, source_target_pairs={{0,16},{8,24},{16,0},{24,8},{1,17},{9,25},{17,1},{25,9},{2,18},{10... | collective-permute-start | bytes 1572872 | tf_op jit(solution)/shard_map/ppermute | solution.py:39
  51.0 25.8 %collective-permute-start.22 = (bf16[4,256,256]{2,1,0:T(8,128)(2,1)S(1)}, bf16[4,256,256]{2,1,0:T(8,128)(2,1)S(1)}, u32[]{:S(2)}, u32[]{:S(2)}) collective-permute-start(bf16[4,256,256]{2,1,0:T(8,128)(2,1)S(1)} %pad_maximum_fusion.1.refs_4_), channel_id=1, source_target_pairs={{0,24},{8,0},{16,8},{24,16},{1,25},{9,1},{17,9},{25,17},{2,26},{10... | collective-permute-start | bytes 1572872 | tf_op jit(solution)/shard_map/ppermute | solution.py:39
  52.0 24.9 %collective-permute-start.11 = (bf16[4,256,256]{2,1,0:T(8,128)(2,1)S(1)}, bf16[4,256,256]{2,1,0:T(8,128)(2,1)S(1)}, u32[]{:S(2)}, u32[]{:S(2)}) collective-permute-start(bf16[4,256,256]{2,1,0:T(8,128)(2,1)S(1)} %pad_maximum_fusion.refs_0_), channel_id=1, source_target_pairs={{0,32},{32,64},{64,96},{96,0},{1,33},{33,65},{65,97},{97,1},{2,34}... | collective-permute-start | bytes 1572872 | tf_op jit(solution)/shard_map/ppermute | solution.py:39
  60.6 19.8 %collective-permute-start.13 = (bf16[4,256,256]{2,1,0:T(8,128)(2,1)S(1)}, bf16[4,256,256]{2,1,0:T(8,128)(2,1)}, u32[]{:S(2)}, u32[]{:S(2)}) collective-permute-start(bf16[4,256,256]{2,1,0:T(8,128)(2,1)S(1)} %pad_maximum_fusion.refs_0_), channel_id=1, source_target_pairs={{0,64},{32,96},{64,0},{96,32},{1,65},{33,97},{65,1},{97,33},{2,66}... | collective-permute-start | bytes 1572872 | tf_op jit(solution)/shard_map/ppermute | solution.py:39
  64.2 21.1 %collective-permute-start.15 = (bf16[4,256,256]{2,1,0:T(8,128)(2,1)S(1)}, bf16[4,256,256]{2,1,0:T(8,128)(2,1)}, u32[]{:S(2)}, u32[]{:S(2)}) collective-permute-start(bf16[4,256,256]{2,1,0:T(8,128)(2,1)S(1)} %pad_maximum_fusion.refs_0_), channel_id=1, source_target_pairs={{0,96},{32,0},{64,32},{96,64},{1,97},{33,1},{65,33},{97,65},{2,98}... | collective-permute-start | bytes 1572872 | tf_op jit(solution)/shard_map/ppermute | solution.py:39
  76.1 10.3 %collective-permute-start.17 = (bf16[4,256,256]{2,1,0:T(8,128)(2,1)S(1)}, bf16[4,256,256]{2,1,0:T(8,128)(2,1)}, u32[]{:S(2)}, u32[]{:S(2)}) collective-permute-start(bf16[4,256,256]{2,1,0:T(8,128)(2,1)S(1)} %pad_maximum_fusion.1.refs_4_), channel_id=1, source_target_pairs={{0,4},{4,0},{1,5},{5,1},{2,6},{6,2},{3,7},{7,3},{8,12},{12,8},{9,1... | collective-permute-start | bytes 1572872 | tf_op jit(solution)/shard_map/ppermute | solution.py:154
  76.9 9.5 %collective-permute-start.10 = (bf16[4,256,256]{2,1,0:T(8,128)(2,1)S(1)}, bf16[4,256,256]{2,1,0:T(8,128)(2,1)}, u32[]{:S(2)}, u32[]{:S(2)}) collective-permute-start(bf16[4,256,256]{2,1,0:T(8,128)(2,1)S(1)} %pad_maximum_fusion.refs_0_), channel_id=1, source_target_pairs={{0,4},{4,0},{1,5},{5,1},{2,6},{6,2},{3,7},{7,3},{8,12},{12,8},{9,1... | collective-permute-start | bytes 1572872 | tf_op jit(solution)/shard_map/ppermute | solution.py:153
  76.9 10.0 %collective-permute-start.19 = (bf16[4,256,256]{2,1,0:T(8,128)(2,1)S(1)}, bf16[4,256,256]{2,1,0:T(8,128)(2,1)}, u32[]{:S(2)}, u32[]{:S(2)}) collective-permute-start(bf16[4,256,256]{2,1,0:T(8,128)(2,1)S(1)} %collective-permute-done.18.refs_5_), channel_id=1, source_target_pairs={{0,4},{4,0},{1,5},{5,1},{2,6},{6,2},{3,7},{7,3},{8,12},{12,8},{9,1... | collective-permute-start | bytes 1572872 | tf_op jit(solution)/shard_map/ppermute | solution.py:154
  80.4 12.8 %collective-permute-start.21 = (bf16[4,256,256]{2,1,0:T(8,128)(2,1)S(1)}, bf16[4,256,256]{2,1,0:T(8,128)(2,1)}, u32[]{:S(2)}, u32[]{:S(2)}) collective-permute-start(bf16[4,256,256]{2,1,0:T(8,128)(2,1)S(1)} %collective-permute-done.20.refs_6_), channel_id=1, source_target_pairs={{0,4},{4,0},{1,5},{5,1},{2,6},{6,2},{3,7},{7,3},{8,12},{12,8},{9,1... | collective-permute-start | bytes 1572872 | tf_op jit(solution)/shard_map/ppermute | solution.py:154
  85.3 7.9 %collective-permute-start.23 = (bf16[4,256,256]{2,1,0:T(8,128)(2,1)S(1)}, bf16[4,256,256]{2,1,0:T(8,128)(2,1)}, u32[]{:S(2)}, u32[]{:S(2)}) collective-permute-start(bf16[4,256,256]{2,1,0:T(8,128)(2,1)S(1)} %collective-permute-done.22.refs_7_), channel_id=1, source_target_pairs={{0,4},{4,0},{1,5},{5,1},{2,6},{6,2},{3,7},{7,3},{8,12},{12,8},{9,1... | collective-permute-start | bytes 1572872 | tf_op jit(solution)/shard_map/ppermute | solution.py:154
  86.4 6.8 %collective-permute-start.12 = (bf16[4,256,256]{2,1,0:T(8,128)(2,1)S(1)}, bf16[4,256,256]{2,1,0:T(8,128)(2,1)}, u32[]{:S(2)}, u32[]{:S(2)}) collective-permute-start(bf16[4,256,256]{2,1,0:T(8,128)(2,1)S(1)} %collective-permute-done.11.refs_1_), channel_id=1, source_target_pairs={{0,4},{4,0},{1,5},{5,1},{2,6},{6,2},{3,7},{7,3},{8,12},{12,8},{9,1... | collective-permute-start | bytes 1572872 | tf_op jit(solution)/shard_map/ppermute | solution.py:153
  86.4 6.8 %collective-permute-start.14 = (bf16[4,256,256]{2,1,0:T(8,128)(2,1)}, bf16[4,256,256]{2,1,0:T(8,128)(2,1)}, u32[]{:S(2)}, u32[]{:S(2)}) collective-permute-start(bf16[4,256,256]{2,1,0:T(8,128)(2,1)} %collective-permute-done.13.refs_2_), channel_id=1, source_target_pairs={{0,4},{4,0},{1,5},{5,1},{2,6},{6,2},{3,7},{7,3},{8,12},{12,8},{9,1... | collective-permute-start | bytes 1572872 | tf_op jit(solution)/shard_map/ppermute | solution.py:153
  86.9 6.3 %collective-permute-start.16 = (bf16[4,256,256]{2,1,0:T(8,128)(2,1)}, bf16[4,256,256]{2,1,0:T(8,128)(2,1)}, u32[]{:S(2)}, u32[]{:S(2)}) collective-permute-start(bf16[4,256,256]{2,1,0:T(8,128)(2,1)} %collective-permute-done.15.refs_3_), channel_id=1, source_target_pairs={{0,4},{4,0},{1,5},{5,1},{2,6},{6,2},{3,7},{7,3},{8,12},{12,8},{9,1... | collective-permute-start | bytes 1572872 | tf_op jit(solution)/shard_map/ppermute | solution.py:153
  99.5 16.4 %all-to-all-start.1 = ((f32[128,1,256]{2,1,0:T(1,128)}), f32[128,1,256]{2,1,0:T(1,128)S(1)}, u32[]{:S(2)}, u32[]{:S(2)}) async-start(f32[128,1,256]{2,1,0:T(1,128)} %broadcast_in_dim.9), calls=%async_computation.1 | async-start | bytes 262144 | tf_op jit(solution)/shard_map/all_to_all | solution.py:44
where the time goes:
time: 151 us; the launch traced here: 150 us
  starting transfers between devices  61.4 us (41%)
  waiting for transfers between devices  30.1 us (20%)
  blocking collectives  27.9 us (18%)
  other arithmetic  12.5 us (8%)
  Pallas kernels  9.71 us (6%)
  local copies, waits for them, and re-layouts  7.76 us (5%)
    ppermute x12, starting transfers between devices, ring(): return [v] + [lax.ppermute(v, axis, along(k)) for k in (1, 2, 3)]  36.6 us
    all_to_all x2, blocking collectives, to_all(): return lax.all_to_all(sent, ALL, 0, 0).reshape((32, 4) + values.shape)  27.9 us
    ppermute x12, waiting for transfers between devices, ring(): return [v] + [lax.ppermute(v, axis, along(k)) for k in (1, 2, 3)]  17.1 us
    all_to_all x2, starting transfers between devices, to_all(): return lax.all_to_all(sent, ALL, 0, 0).reshape((32, 4) + values.shape)  16.1 us
    all_to_all x2, waiting for transfers between devices, to_all(): return lax.all_to_all(sent, ALL, 0, 0).reshape((32, 4) + values.shape)  13 us
    pallas_call x2, Pallas kernels, products(): pl.pallas_call(kernel, in_specs=[SMEM] + [VMEM] * (len(operands) - 1), ou...  9.71 us
    ppermute x3, starting transfers between devices, own_rows(): later = [lax.ppermute(member, 'y', along(-k)) for k in (1, 2, 3)]  3.74 us
  transfers between devices with their start and end apart: 26, of which 5 were waited for; matrix products, arithmetic and copies ran while one was open for 9% of the time, Pallas kernels for 3%

commit v1 on v0

--- a/solution.py
+++ b/solution.py
@@ -15,7 +15,7 @@
 WIDTH = 256
 COLS = 2048
 GROUPS = COLS // WIDTH
-FIRST = 256
+FIRST = 224
 STACK = 2 * WIDTH + 16
 LANES = 128
 
@@ -67,7 +67,7 @@
 def products(where, left, by_x, by_z, before):
     def kernel(where_ref, left_ref, *refs):
         x_refs, z_refs = refs[:4], refs[4:8]
-        x, z, c = where_ref[0], where_ref[2], where_ref[3]
+        x, y, z, c = (where_ref[i] for i in range(4))
         if before is None:
             sym_ref, visit_ref, total_ref, visit_row_ref, total_row_ref = refs[8:]
             core = c
@@ -87,7 +87,8 @@
             acc = jnp.zeros((STACK, WIDTH), jnp.float32)
             for dx in range(4):
                 lo = pl.multiple_of(lax.rem(x + 4 - dx, 4) * BLOCK, BLOCK)
-                block = jnp.concatenate([x_refs[dx][dz], z_refs[dz][dx]], axis=0)
+                rest = z_refs[dz][lax.rem(y + 4 - x + dx, 4)]
+                block = jnp.concatenate([x_refs[dx][dz], rest], axis=0)
                 acc += jnp.dot(left_ref[:, pl.ds(lo, BLOCK)], block,
                                preferred_element_type=jnp.float32)
             g = lax.rem(z + 4 - dz, 4) * 2 + core
@@ -145,9 +146,12 @@
 
 def shards(member):
     where = jnp.stack([lax.axis_index(a) for a in ("x", "y", "z", "c")])
-    moved = lax.ppermute(member, ALL, across())
-    once_x = jnp.stack(ring(moved[:FIRST], "z"))
-    once_z = jnp.stack(ring(moved[FIRST:], "x"))
+    x, y = where[0], where[1]
+    moved = lax.ppermute(member[:FIRST], ALL, across())
+    planes = jnp.stack(ring(member[FIRST:], "x"))
+    once_x = jnp.stack(ring(moved, "z"))
+    leave = [lax.dynamic_index_in_dim(planes, lax.rem(x + 8 - y - k, 4), 0, False) for k in range(4)]
+    once_z = jnp.stack([leave[0]] + [lax.ppermute(leave[k], "y", along(k)) for k in (1, 2, 3)])
     by_x = ring(once_x, "x")
     by_z = ring(once_z, "z")
     other_x = [lax.ppermute(v, "c", [(0, 1), (1, 0)]) for v in by_x]
@@ -166,9 +170,9 @@
         total_cols = lax.dynamic_slice_in_dim(totals, where[1] * COLS, COLS)
         if step == 2:
             break
-        estimate = sym / ((visit_rows / total_rows)[:, None] + (visit_cols / total_cols)[None, :])
-        part = jnp.sum(estimate, axis=1)
-    transition = STATES * estimate / total_rows[:, None]
+        ratio = (visit_rows / total_rows)[:, None] + (visit_cols / total_cols)[None, :]
+        part = jnp.sum(sym / ratio, axis=1)
+    transition = sym * (STATES / total_rows)[:, None] / ratio
     stationary = STATES * total_rows / jnp.sum(totals)
     return (transition, stationary)
 

time: 151 us -> 150 us (level)
  waiting for transfers between devices: 30.1 us -> 35.9 us
  starting transfers between devices: 61.4 us -> 55.7 us
  local copies, waits for them, and re-layouts: 7.76 us -> 9.47 us
  other arithmetic: 12.5 us -> 10.8 us
    ppermute x12, starting transfers between devices: 36.6 us -> 15.7 us  [ring(): return [v] + [lax.ppermute(v, axis, along(k)) for k in (1, 2, 3)]]
    ppermute x12, waiting for transfers between devices: 17.1 us -> 25.9 us  [ring(): return [v] + [lax.ppermute(v, axis, along(k)) for k in (1, 2, 3)]]
    ppermute x4, starting transfers between devices: 2.58 us -> 11.2 us  [shards(): other_z = [lax.ppermute(v, 'c', [(0, 1), (1, 0)]) for v in by_z]]
    ppermute x4, starting transfers between devices: 0.78 us -> 4.07 us  [shards(): other_x = [lax.ppermute(v, 'c', [(0, 1), (1, 0)]) for v in by_x]]
    all_to_all x2, waiting for transfers between devices: 13 us -> 9.95 us  [to_all(): return lax.all_to_all(sent, ALL, 0, 0).reshape((32, 4) + values.shape)]
    ppermute x1 -> x4, starting transfers between devices: 1.61 us -> 4.04 us  [the longest x3 3.38 us: shards(): lax.ppermute(leave[k], 'y', along(k))]
    ppermute x3, starting transfers between devices: 3.74 us -> 6.03 us  [own_rows(): later = [lax.ppermute(member, 'y', along(-k)) for k in (1, 2, 3)]]
  transfers between devices with their start and end apart: 26 -> 29, of which waited for: 5 -> 7; matrix products, arithmetic and copies ran while one was open for 9% -> 7% of each run, Pallas kernels for 3% -> 3%
where the time goes in v1:
time: 150 us
  starting transfers between devices  55.7 us (37%)
  waiting for transfers between devices  35.9 us (24%)
  blocking collectives  27.9 us (19%)
  other arithmetic  10.8 us (7%)
  local copies, waits for them, and re-layouts  9.47 us (6%)
  Pallas kernels  9.12 us (6%)
    all_to_all x2, blocking collectives, to_all(): return lax.all_to_all(sent, ALL, 0, 0).reshape((32, 4) + values.shape)  27.9 us
    ppermute x12, waiting for transfers between devices, ring(): return [v] + [lax.ppermute(v, axis, along(k)) for k in (1, 2, 3)]  25.9 us
    ppermute x12, starting transfers between devices, ring(): return [v] + [lax.ppermute(v, axis, along(k)) for k in (1, 2, 3)]  15.7 us
    all_to_all x2, starting transfers between devices, to_all(): return lax.all_to_all(sent, ALL, 0, 0).reshape((32, 4) + values.shape)  14.7 us
    ppermute x4, starting transfers between devices, shards(): other_z = [lax.ppermute(v, 'c', [(0, 1), (1, 0)]) for v in by_z]  11.2 us
    all_to_all x2, waiting for transfers between devices, to_all(): return lax.all_to_all(sent, ALL, 0, 0).reshape((32, 4) + values.shape)  9.95 us
    pallas_call x2, Pallas kernels, products(): pl.pallas_call(kernel, in_specs=[SMEM] + [VMEM] * (len(operands) - 1), ou...  9.12 us
    ppermute x3, starting transfers between devices, own_rows(): later = [lax.ppermute(member, 'y', along(-k)) for k in (1, 2, 3)]  6.03 us
  transfers between devices with their start and end apart: 29, of which 7 were waited for; matrix products, arithmetic and copies ran while one was open for 7% of the time, Pallas kernels for 3%

profile of v1, /device:TPU:1, one launch (start us, length us, event | category | flops | bytes accessed | tf_op | source)
XLA Modules:
  0.0 150.0 jit_solution(3212408082945656893)
XLA Ops:
  1.6 2.1 %collective-permute-start.7 = (bf16[288,256]{1,0:T(8,128)(2,1)S(1)}, bf16[288,256]{1,0:T(8,128)(2,1)S(1)}, u32[]{:S(2)}, u32[]{:S(2)}) collective-permute-start(bf16[288,256]{1,0:T(8,128)(2,1)S(1)} %get-tuple-element.29), channel_id=1, source_target_pairs={{0,32},{32,64},{64,96},{96,0},{1,33},{33,65},{65,97},{97,1},{2,34}... | collective-permute-start | bytes 442376 | tf_op jit(solution)/shard_map/ppermute | solution.py:39
  3.7 2.5 %collective-permute-start.8 = (bf16[288,256]{1,0:T(8,128)(2,1)S(1)}, bf16[288,256]{1,0:T(8,128)(2,1)S(1)}, u32[]{:S(2)}, u32[]{:S(2)}) collective-permute-start(bf16[288,256]{1,0:T(8,128)(2,1)S(1)} %get-tuple-element.29), channel_id=1, source_target_pairs={{0,64},{32,96},{64,0},{96,32},{1,65},{33,97},{65,1},{97,33},{2,66}... | collective-permute-start | bytes 442376 | tf_op jit(solution)/shard_map/ppermute | solution.py:39
  6.1 1.2 collective-permute-start.9
  7.3 1.1 copy.26
  8.4 2.8 %collective-permute-start = (bf16[512,256]{0,1:T(8,128)(2,1)S(1)}, bf16[512,256]{0,1:T(8,128)(2,1)S(1)}, u32[]{:S(2)}, u32[]{:S(2)}) collective-permute-start(bf16[512,256]{0,1:T(8,128)(2,1)S(1)} %copy.26), channel_id=1, source_target_pairs={{0,3},{1,0},{2,1},{3,2},{4,7},{5,4},{6,5},{7,6},{8,11},{9,8},{10,9... | collective-permute-start | bytes 786440 | tf_op jit(solution)/shard_map/ppermute | solution.py:130
  12.7 1.1 convert_reduce_fusion
  14.7 11.1 %all-to-all-start = ((f32[128,1,512]{2,1,0:T(1,128)}), f32[128,1,512]{2,1,0:T(1,128)S(1)}, u32[]{:S(2)}, u32[]{:S(2)}) async-start(f32[128,1,512]{2,1,0:T(1,128)} %broadcast_in_dim.8), calls=%async_computation | async-start | bytes 524288 | tf_op jit(solution)/shard_map/all_to_all | solution.py:44
  25.9 2.9 %collective-permute-start.1 = (bf16[512,256]{0,1:T(8,128)(2,1)S(1)}, bf16[512,256]{0,1:T(8,128)(2,1)S(1)}, u32[]{:S(2)}, u32[]{:S(2)}) collective-permute-start(bf16[512,256]{0,1:T(8,128)(2,1)S(1)} %copy.26), channel_id=1, source_target_pairs={{0,2},{1,3},{2,0},{3,1},{4,6},{5,7},{6,4},{7,5},{8,10},{9,11},{10,... | collective-permute-start | bytes 786440 | tf_op jit(solution)/shard_map/ppermute | solution.py:130
  29.2 1.5 collective-permute-start.4
  30.6 2.9 %collective-permute-start.5 = (bf16[224,256]{1,0:T(8,128)(2,1)S(1)}, bf16[224,256]{1,0:T(8,128)(2,1)S(1)}, u32[]{:S(2)}, u32[]{:S(2)}) collective-permute-start(bf16[224,256]{1,0:T(8,128)(2,1)S(1)} %collective-permute-done.3), channel_id=1, source_target_pairs={{0,16},{8,24},{16,0},{24,8},{1,17},{9,25},{17,1},{25,9},{2,18},{10... | collective-permute-start | bytes 344072 | tf_op jit(solution)/shard_map/ppermute | solution.py:39
  33.6 3.4 %collective-permute-done.4 = bf16[224,256]{1,0:T(8,128)(2,1)S(1)} collective-permute-done((bf16[224,256]{1,0:T(8,128)(2,1)S(1)}, bf16[224,256]{1,0:T(8,128)(2,1)S(1)}, u32[]{:S(2)}, u32[]{:S(2)}) %collective-permute-start.4) | collective-permute-done | bytes 114720 | tf_op jit(solution)/shard_map/ppermute | solution.py:39
  37.6 2.1 %collective-permute-done.5 = bf16[224,256]{1,0:T(8,128)(2,1)S(1)} collective-permute-done((bf16[224,256]{1,0:T(8,128)(2,1)S(1)}, bf16[224,256]{1,0:T(8,128)(2,1)S(1)}, u32[]{:S(2)}, u32[]{:S(2)}) %collective-permute-start.5) | collective-permute-done | bytes 114720 | tf_op jit(solution)/shard_map/ppermute | solution.py:39
  41.0 1.8 %collective-permute-start.11 = (bf16[288,256]{1,0:T(8,128)(2,1)S(1)}, bf16[288,256]{1,0:T(8,128)(2,1)S(1)}, u32[]{:S(2)}, u32[]{:S(2)}) collective-permute-start(bf16[288,256]{1,0:T(8,128)(2,1)S(1)} %get-tuple-element.26), channel_id=1, source_target_pairs={{0,2},{1,3},{2,0},{3,1},{4,6},{5,7},{6,4},{7,5},{8,10},{9,11},{10,... | collective-permute-start | bytes 442376 | tf_op jit(solution)/shard_map/ppermute | solution.py:154
  45.3 2.1 %collective-permute-start.16 = (bf16[4,224,256]{2,1,0:T(8,128)(2,1)S(1)}, bf16[4,224,256]{2,1,0:T(8,128)(2,1)S(1)}, u32[]{:S(2)}, u32[]{:S(2)}) collective-permute-start(bf16[4,224,256]{2,1,0:T(8,128)(2,1)S(1)} %pad_maximum_fusion.2.refs_0_), channel_id=1, source_target_pairs={{0,64},{32,96},{64,0},{96,32},{1,65},{33,97},{65,1},{97,33},{2,66}... | collective-permute-start | bytes 1376264 | tf_op jit(solution)/shard_map/ppermute | solution.py:39
  47.5 1.2 collective-permute-start.18
  48.8 3.4 %collective-permute-start.13 = (bf16[4,224,256]{2,1,0:T(8,128)(2,1)S(1)}, bf16[4,224,256]{2,1,0:T(8,128)(2,1)}, u32[]{:S(2)}, u32[]{:S(2)}) collective-permute-start(bf16[4,224,256]{2,1,0:T(8,128)(2,1)S(1)} %pad_maximum_fusion.2.refs_0_), channel_id=1, source_target_pairs={{0,4},{4,0},{1,5},{5,1},{2,6},{6,2},{3,7},{7,3},{8,12},{12,8},{9,1... | collective-permute-start | bytes 1376264 | tf_op jit(solution)/shard_map/ppermute | solution.py:157
  52.9 2.8 %collective-permute-done.14.refs_1_ = bf16[4,224,256]{2,1,0:T(8,128)(2,1)} collective-permute-done((bf16[4,224,256]{2,1,0:T(8,128)(2,1)S(1)}, bf16[4,224,256]{2,1,0:T(8,128)(2,1)}, u32[]{:S(2)}, u32[]{:S(2)}) %collective-permute-start.14) | collective-permute-done | bytes 458784 | tf_op jit(solution)/shard_map/ppermute | solution.py:39
  56.7 8.7 %collective-permute-done.16.refs_2_ = bf16[4,224,256]{2,1,0:T(8,128)(2,1)S(1)} collective-permute-done((bf16[4,224,256]{2,1,0:T(8,128)(2,1)S(1)}, bf16[4,224,256]{2,1,0:T(8,128)(2,1)S(1)}, u32[]{:S(2)}, u32[]{:S(2)}) %collective-permute-start.16) | collective-permute-done | bytes 458784 | tf_op jit(solution)/shard_map/ppermute | solution.py:39
  66.2 2.6 %pad_slice_fusion.1 = (bf16[256,2048]{1,0:T(8,128)(2,1)}, bf16[256,2048]{1,0:T(8,128)(2,1)}) fusion(bf16[256,2048]{1,0:T(8,128)(2,1)S(1)} %fusion.4), kind=kLoop, calls=%fused_computation.13 | loop fusion | bytes 3145728 | tf_op jit(solution)/shard_map/slice | solution.py:160
  68.8 5.2 %collective-permute-start.20 = (bf16[4,288,256]{2,1,0:T(8,128)(2,1)S(1)}, bf16[4,288,256]{2,1,0:T(8,128)(2,1)S(1)}, u32[]{:S(2)}, u32[]{:S(2)}) collective-permute-start(bf16[4,288,256]{2,1,0:T(8,128)(2,1)S(1)} %pad_maximum_fusion.1.refs_4_), channel_id=1, source_target_pairs={{0,4},{4,0},{1,5},{5,1},{2,6},{6,2},{3,7},{7,3},{8,12},{12,8},{9,1... | collective-permute-start | bytes 1769480 | tf_op jit(solution)/shard_map/ppermute | solution.py:158
  74.7 8.1 %collective-permute-done.23.refs_6_ = bf16[4,288,256]{2,1,0:T(8,128)(2,1)S(1)} collective-permute-done((bf16[4,288,256]{2,1,0:T(8,128)(2,1)S(1)}, bf16[4,288,256]{2,1,0:T(8,128)(2,1)S(1)}, u32[]{:S(2)}, u32[]{:S(2)}) %collective-permute-start.23) | collective-permute-done | bytes 589856 | tf_op jit(solution)/shard_map/ppermute | solution.py:39
  83.6 4.7 %collective-permute-start.26 = (bf16[4,288,256]{2,1,0:T(8,128)(2,1)S(1)}, bf16[4,288,256]{2,1,0:T(8,128)(2,1)}, u32[]{:S(2)}, u32[]{:S(2)}) collective-permute-start(bf16[4,288,256]{2,1,0:T(8,128)(2,1)S(1)} %collective-permute-done.25.refs_7_), channel_id=1, source_target_pairs={{0,4},{4,0},{1,5},{5,1},{2,6},{6,2},{3,7},{7,3},{8,12},{12,8},{9,1... | collective-permute-start | bytes 1769480 | tf_op jit(solution)/shard_map/ppermute | solution.py:158
  90.1 1.7 %fusion.1.left_ref = bf16[528,2048]{1,0:T(8,128)(2,1)S(1)} fusion(bf16[9,2048]{1,0:T(8,128)(2,1)S(1)} %stack.107, bf16[256,2048]{1,0:T(8,128)(2,1)} %get-tuple-element.23, bf16[256,2048]{1,0:T(8,128)(2,1)} %get-tuple-element.22), kind=kLoop, calls=%fused_computation.4 | loop fusion | flops 8650752 | bytes 4296704 | tf_op jit(solution)/shard_map/concatenate | solution.py:160
  91.9 4.2 %shard_map.30 = (f32[256,2048]{1,0:T(8,128)S(1)}, f32[8,256]{1,0:T(8,128)S(1)}, f32[8,256]{1,0:T(8,128)S(1)}, f32[256,128]{1,0:T(8,128)S(1)}, f32[256,128]{1,0:T(8,128)S(1)}) custom-call(s32[4]{0:T(128)S(1)} %pad_add_fusion.where_ref, bf16[528,2048]{1,0:T(8,128)(2,1)S(1)} %fusion.1.left_ref, bf16[4,224,256]{2,1,0:T(8,128)(2,1)S(1)} %pad_maximum_fusion.2.refs_0_, ...), custom_call_target="tpu_custom_call" | custom-call | tf_op jit(solution)/shard_map/pallas_call | solution.py:111
  96.1 4.9 %shard_map.31 = (f32[256,2048]{1,0:T(8,128)S(1)}, f32[8,256]{1,0:T(8,128)S(1)}, f32[8,256]{1,0:T(8,128)}, f32[1,256]{1,0:T(1,128)S(1)}) custom-call(s32[4]{0:T(128)S(1)} %pad_add_fusion.where_ref, bf16[528,2048]{1,0:T(8,128)(2,1)S(1)} %fusion.1.left_ref, bf16[4,224,256]{2,1,0:T(8,128)(2,1)} %collective-permute-done.13.refs_0_, ...), custom_call_target="tpu_custom_call" | custom-call | tf_op jit(solution)/shard_map/pallas_call | solution.py:111
  101.8 3.5 %all-to-all-start.1 = ((f32[128,1,256]{2,1,0:T(1,128)}), f32[128,1,256]{2,1,0:T(1,128)S(1)}, u32[]{:S(2)}, u32[]{:S(2)}) async-start(f32[128,1,256]{2,1,0:T(1,128)} %broadcast_in_dim.9), calls=%async_computation.1 | async-start | bytes 262144 | tf_op jit(solution)/shard_map/all_to_all | solution.py:44
  105.5 9.9 %all-to-all-done.1 = f32[128,1,256]{2,1,0:T(1,128)S(1)} async-done(((f32[128,1,256]{2,1,0:T(1,128)}), f32[128,1,256]{2,1,0:T(1,128)S(1)}, u32[]{:S(2)}, u32[]{:S(2)}) %all-to-all-start.1) | async-done | bytes 131104 | tf_op jit(solution)/shard_map/all_to_all | solution.py:44
  116.5 14.0 %all_to_all.24 = f32[128,1,256]{2,1,0:T(1,128)S(1)} all-to-all(f32[128,1,256]{2,1,0:T(1,128)S(1)} %broadcast_in_dim.10), channel_id=1, replica_groups=mesh['x'=4,'z'=4,'c'=2,'y'=4] {'x','z','c','y'}, dimensions={0} | all-to-all | bytes 262144 | tf_op jit(solution)/shard_map/all_to_all | solution.py:44
  131.6 13.9 %all_to_all.25 = f32[128,1,256]{2,1,0:T(1,128)S(1)} all-to-all(f32[128,1,256]{2,1,0:T(1,128)S(1)} %broadcast_in_dim.11), channel_id=1, replica_groups=mesh['x'=4,'z'=4,'c'=2,'y'=4] {'x','z','c','y'}, dimensions={0} | all-to-all | bytes 262144 | tf_op jit(solution)/shard_map/all_to_all | solution.py:44
  145.5 1.1 fusion.8
  146.8 1.3 multiply_divide_fusion
  148.1 1.9 %add_divide_fusion = f32[256,2048]{1,0:T(8,128)} fusion(f32[256,2048]{1,0:T(8,128)S(1)} %get-tuple-element.17, f32[256]{0:T(256)S(1)} %get-tuple-element.31, f32[2048]{0:T(1024)S(1)} %dynamic-slice_divide_fusion, f32[256]{0:T(256)S(1)} %dynamic-slice_divide_fusion.2), kind=kLoop, calls=%fused_computation.2 | loop fusion | flops 1572864 | bytes 4204544 | tf_op jit(solution)/shard_map/div | solution.py:175
  (94 shorter events, 17.1 us)
Async XLA Ops:
  1.6 27.3 %collective-permute-start.7 = (bf16[288,256]{1,0:T(8,128)(2,1)S(1)}, bf16[288,256]{1,0:T(8,128)(2,1)S(1)}, u32[]{:S(2)}, u32[]{:S(2)}) collective-permute-start(bf16[288,256]{1,0:T(8,128)(2,1)S(1)} %get-tuple-element.29), channel_id=1, source_target_pairs={{0,32},{32,64},{64,96},{96,0},{1,33},{33,65},{65,97},{97,1},{2,34}... | collective-permute-start | bytes 442376 | tf_op jit(solution)/shard_map/ppermute | solution.py:39
  3.7 25.5 %collective-permute-start.8 = (bf16[288,256]{1,0:T(8,128)(2,1)S(1)}, bf16[288,256]{1,0:T(8,128)(2,1)S(1)}, u32[]{:S(2)}, u32[]{:S(2)}) collective-permute-start(bf16[288,256]{1,0:T(8,128)(2,1)S(1)} %get-tuple-element.29), channel_id=1, source_target_pairs={{0,64},{32,96},{64,0},{96,32},{1,65},{33,97},{65,1},{97,33},{2,66}... | collective-permute-start | bytes 442376 | tf_op jit(solution)/shard_map/ppermute | solution.py:39
  6.1 24.5 %collective-permute-start.9 = (bf16[288,256]{1,0:T(8,128)(2,1)S(1)}, bf16[288,256]{1,0:T(8,128)(2,1)S(1)}, u32[]{:S(2)}, u32[]{:S(2)}) collective-permute-start(bf16[288,256]{1,0:T(8,128)(2,1)S(1)} %get-tuple-element.29), channel_id=1, source_target_pairs={{0,96},{32,0},{64,32},{96,64},{1,97},{33,1},{65,33},{97,65},{2,98}... | collective-permute-start | bytes 442376 | tf_op jit(solution)/shard_map/ppermute | solution.py:39
  8.4 35.2 %collective-permute-start = (bf16[512,256]{0,1:T(8,128)(2,1)S(1)}, bf16[512,256]{0,1:T(8,128)(2,1)S(1)}, u32[]{:S(2)}, u32[]{:S(2)}) collective-permute-start(bf16[512,256]{0,1:T(8,128)(2,1)S(1)} %copy.26), channel_id=1, source_target_pairs={{0,3},{1,0},{2,1},{3,2},{4,7},{5,4},{6,5},{7,6},{8,11},{9,8},{10,9... | collective-permute-start | bytes 786440 | tf_op jit(solution)/shard_map/ppermute | solution.py:130
  12.1 13.9 %collective-permute-start.3 = (bf16[224,256]{1,0:T(8,128)(2,1)S(1)}, bf16[224,256]{1,0:T(8,128)(2,1)S(1)}, u32[]{:S(2)}, u32[]{:S(2)}) collective-permute-start(bf16[224,256]{1,0:T(8,128)(2,1)S(1)} %slice.23), channel_id=1, source_target_pairs={{0,0},{4,4},{8,8},{12,12},{16,16},{20,20},{24,24},{28,28},{1,32},{... | collective-permute-start | bytes 344072 | tf_op jit(solution)/shard_map/ppermute | solution.py:150
  14.7 28.2 %all-to-all-start = ((f32[128,1,512]{2,1,0:T(1,128)}), f32[128,1,512]{2,1,0:T(1,128)S(1)}, u32[]{:S(2)}, u32[]{:S(2)}) async-start(f32[128,1,512]{2,1,0:T(1,128)} %broadcast_in_dim.8), calls=%async_computation | async-start | bytes 524288 | tf_op jit(solution)/shard_map/all_to_all | solution.py:44
  25.9 18.7 %collective-permute-start.1 = (bf16[512,256]{0,1:T(8,128)(2,1)S(1)}, bf16[512,256]{0,1:T(8,128)(2,1)S(1)}, u32[]{:S(2)}, u32[]{:S(2)}) collective-permute-start(bf16[512,256]{0,1:T(8,128)(2,1)S(1)} %copy.26), channel_id=1, source_target_pairs={{0,2},{1,3},{2,0},{3,1},{4,6},{5,7},{6,4},{7,5},{8,10},{9,11},{10,... | collective-permute-start | bytes 786440 | tf_op jit(solution)/shard_map/ppermute | solution.py:130
  28.8 16.5 %collective-permute-start.2 = (bf16[512,256]{0,1:T(8,128)(2,1)S(1)}, bf16[512,256]{0,1:T(8,128)(2,1)S(1)}, u32[]{:S(2)}, u32[]{:S(2)}) collective-permute-start(bf16[512,256]{0,1:T(8,128)(2,1)S(1)} %copy.26), channel_id=1, source_target_pairs={{0,1},{1,2},{2,3},{3,0},{4,5},{5,6},{6,7},{7,4},{8,9},{9,10},{10,1... | collective-permute-start | bytes 786440 | tf_op jit(solution)/shard_map/ppermute | solution.py:130
  29.2 7.9 %collective-permute-start.4 = (bf16[224,256]{1,0:T(8,128)(2,1)S(1)}, bf16[224,256]{1,0:T(8,128)(2,1)S(1)}, u32[]{:S(2)}, u32[]{:S(2)}) collective-permute-start(bf16[224,256]{1,0:T(8,128)(2,1)S(1)} %collective-permute-done.3), channel_id=1, source_target_pairs={{0,8},{8,16},{16,24},{24,0},{1,9},{9,17},{17,25},{25,1},{2,10},{10... | collective-permute-start | bytes 344072 | tf_op jit(solution)/shard_map/ppermute | solution.py:39
  30.6 9.1 %collective-permute-start.5 = (bf16[224,256]{1,0:T(8,128)(2,1)S(1)}, bf16[224,256]{1,0:T(8,128)(2,1)S(1)}, u32[]{:S(2)}, u32[]{:S(2)}) collective-permute-start(bf16[224,256]{1,0:T(8,128)(2,1)S(1)} %collective-permute-done.3), channel_id=1, source_target_pairs={{0,16},{8,24},{16,0},{24,8},{1,17},{9,25},{17,1},{25,9},{2,18},{10... | collective-permute-start | bytes 344072 | tf_op jit(solution)/shard_map/ppermute | solution.py:39
  37.0 3.9 %collective-permute-start.6 = (bf16[224,256]{1,0:T(8,128)(2,1)S(1)}, bf16[224,256]{1,0:T(8,128)(2,1)S(1)}, u32[]{:S(2)}, u32[]{:S(2)}) collective-permute-start(bf16[224,256]{1,0:T(8,128)(2,1)S(1)} %collective-permute-done.3), channel_id=1, source_target_pairs={{0,24},{8,0},{16,8},{24,16},{1,25},{9,1},{17,9},{25,17},{2,26},{10... | collective-permute-start | bytes 344072 | tf_op jit(solution)/shard_map/ppermute | solution.py:39
  39.7 7.8 %collective-permute-start.10 = (bf16[288,256]{1,0:T(8,128)(2,1)S(1)}, bf16[288,256]{1,0:T(8,128)(2,1)S(1)}, u32[]{:S(2)}, u32[]{:S(2)}) collective-permute-start(bf16[288,256]{1,0:T(8,128)(2,1)S(1)} %get-tuple-element.27), channel_id=1, source_target_pairs={{0,1},{1,2},{2,3},{3,0},{4,5},{5,6},{6,7},{7,4},{8,9},{9,10},{10,1... | collective-permute-start | bytes 442376 | tf_op jit(solution)/shard_map/ppermute | solution.py:154
  41.0 7.8 %collective-permute-start.11 = (bf16[288,256]{1,0:T(8,128)(2,1)S(1)}, bf16[288,256]{1,0:T(8,128)(2,1)S(1)}, u32[]{:S(2)}, u32[]{:S(2)}) collective-permute-start(bf16[288,256]{1,0:T(8,128)(2,1)S(1)} %get-tuple-element.26), channel_id=1, source_target_pairs={{0,2},{1,3},{2,0},{3,1},{4,6},{5,7},{6,4},{7,5},{8,10},{9,11},{10,... | collective-permute-start | bytes 442376 | tf_op jit(solution)/shard_map/ppermute | solution.py:154
  43.6 9.2 %collective-permute-start.12 = (bf16[288,256]{1,0:T(8,128)(2,1)S(1)}, bf16[288,256]{1,0:T(8,128)(2,1)S(1)}, u32[]{:S(2)}, u32[]{:S(2)}) collective-permute-start(bf16[288,256]{1,0:T(8,128)(2,1)S(1)} %get-tuple-element.25), channel_id=1, source_target_pairs={{0,3},{1,0},{2,1},{3,2},{4,7},{5,4},{6,5},{7,6},{8,11},{9,8},{10,9... | collective-permute-start | bytes 442376 | tf_op jit(solution)/shard_map/ppermute | solution.py:154
  44.6 11.2 %collective-permute-start.14 = (bf16[4,224,256]{2,1,0:T(8,128)(2,1)S(1)}, bf16[4,224,256]{2,1,0:T(8,128)(2,1)}, u32[]{:S(2)}, u32[]{:S(2)}) collective-permute-start(bf16[4,224,256]{2,1,0:T(8,128)(2,1)S(1)} %pad_maximum_fusion.2.refs_0_), channel_id=1, source_target_pairs={{0,32},{32,64},{64,96},{96,0},{1,33},{33,65},{65,97},{97,1},{2,34}... | collective-permute-start | bytes 1376264 | tf_op jit(solution)/shard_map/ppermute | solution.py:39
  45.3 20.1 %collective-permute-start.16 = (bf16[4,224,256]{2,1,0:T(8,128)(2,1)S(1)}, bf16[4,224,256]{2,1,0:T(8,128)(2,1)S(1)}, u32[]{:S(2)}, u32[]{:S(2)}) collective-permute-start(bf16[4,224,256]{2,1,0:T(8,128)(2,1)S(1)} %pad_maximum_fusion.2.refs_0_), channel_id=1, source_target_pairs={{0,64},{32,96},{64,0},{96,32},{1,65},{33,97},{65,1},{97,33},{2,66}... | collective-permute-start | bytes 1376264 | tf_op jit(solution)/shard_map/ppermute | solution.py:39
  47.5 21.3 %collective-permute-start.18 = (bf16[4,224,256]{2,1,0:T(8,128)(2,1)S(1)}, bf16[4,224,256]{2,1,0:T(8,128)(2,1)}, u32[]{:S(2)}, u32[]{:S(2)}) collective-permute-start(bf16[4,224,256]{2,1,0:T(8,128)(2,1)S(1)} %pad_maximum_fusion.2.refs_0_), channel_id=1, source_target_pairs={{0,96},{32,0},{64,32},{96,64},{1,97},{33,1},{65,33},{97,65},{2,98}... | collective-permute-start | bytes 1376264 | tf_op jit(solution)/shard_map/ppermute | solution.py:39
  48.8 25.3 %collective-permute-start.13 = (bf16[4,224,256]{2,1,0:T(8,128)(2,1)S(1)}, bf16[4,224,256]{2,1,0:T(8,128)(2,1)}, u32[]{:S(2)}, u32[]{:S(2)}) collective-permute-start(bf16[4,224,256]{2,1,0:T(8,128)(2,1)S(1)} %pad_maximum_fusion.2.refs_0_), channel_id=1, source_target_pairs={{0,4},{4,0},{1,5},{5,1},{2,6},{6,2},{3,7},{7,3},{8,12},{12,8},{9,1... | collective-permute-start | bytes 1376264 | tf_op jit(solution)/shard_map/ppermute | solution.py:157
  52.9 21.3 %collective-permute-start.21 = (bf16[4,288,256]{2,1,0:T(8,128)(2,1)S(1)}, bf16[4,288,256]{2,1,0:T(8,128)(2,1)S(1)}, u32[]{:S(2)}, u32[]{:S(2)}) collective-permute-start(bf16[4,288,256]{2,1,0:T(8,128)(2,1)S(1)} %pad_maximum_fusion.1.refs_4_), channel_id=1, source_target_pairs={{0,8},{8,16},{16,24},{24,0},{1,9},{9,17},{17,25},{25,1},{2,10},{10... | collective-permute-start | bytes 1769480 | tf_op jit(solution)/shard_map/ppermute | solution.py:39
  55.8 27.0 %collective-permute-start.23 = (bf16[4,288,256]{2,1,0:T(8,128)(2,1)S(1)}, bf16[4,288,256]{2,1,0:T(8,128)(2,1)S(1)}, u32[]{:S(2)}, u32[]{:S(2)}) collective-permute-start(bf16[4,288,256]{2,1,0:T(8,128)(2,1)S(1)} %pad_maximum_fusion.1.refs_4_), channel_id=1, source_target_pairs={{0,16},{8,24},{16,0},{24,8},{1,17},{9,25},{17,1},{25,9},{2,18},{10... | collective-permute-start | bytes 1769480 | tf_op jit(solution)/shard_map/ppermute | solution.py:39
  65.4 0.8 copy-start
  66.2 17.5 %collective-permute-start.25 = (bf16[4,288,256]{2,1,0:T(8,128)(2,1)S(1)}, bf16[4,288,256]{2,1,0:T(8,128)(2,1)S(1)}, u32[]{:S(2)}, u32[]{:S(2)}) collective-permute-start(bf16[4,288,256]{2,1,0:T(8,128)(2,1)S(1)} %pad_maximum_fusion.1.refs_4_), channel_id=1, source_target_pairs={{0,24},{8,0},{16,8},{24,16},{1,25},{9,1},{17,9},{25,17},{2,26},{10... | collective-permute-start | bytes 1769480 | tf_op jit(solution)/shard_map/ppermute | solution.py:39
  68.8 19.5 %collective-permute-start.20 = (bf16[4,288,256]{2,1,0:T(8,128)(2,1)S(1)}, bf16[4,288,256]{2,1,0:T(8,128)(2,1)S(1)}, u32[]{:S(2)}, u32[]{:S(2)}) collective-permute-start(bf16[4,288,256]{2,1,0:T(8,128)(2,1)S(1)} %pad_maximum_fusion.1.refs_4_), channel_id=1, source_target_pairs={{0,4},{4,0},{1,5},{5,1},{2,6},{6,2},{3,7},{7,3},{8,12},{12,8},{9,1... | collective-permute-start | bytes 1769480 | tf_op jit(solution)/shard_map/ppermute | solution.py:158
  74.1 14.4 %collective-permute-start.15 = (bf16[4,224,256]{2,1,0:T(8,128)(2,1)}, bf16[4,224,256]{2,1,0:T(8,128)(2,1)S(1)}, u32[]{:S(2)}, u32[]{:S(2)}) collective-permute-start(bf16[4,224,256]{2,1,0:T(8,128)(2,1)} %collective-permute-done.14.refs_1_), channel_id=1, source_target_pairs={{0,4},{4,0},{1,5},{5,1},{2,6},{6,2},{3,7},{7,3},{8,12},{12,8},{9,1... | collective-permute-start | bytes 1376264 | tf_op jit(solution)/shard_map/ppermute | solution.py:157
  74.2 21.9 %collective-permute-start.22 = (bf16[4,288,256]{2,1,0:T(8,128)(2,1)S(1)}, bf16[4,288,256]{2,1,0:T(8,128)(2,1)}, u32[]{:S(2)}, u32[]{:S(2)}) collective-permute-start(bf16[4,288,256]{2,1,0:T(8,128)(2,1)S(1)} %collective-permute-done.21.refs_5_), channel_id=1, source_target_pairs={{0,4},{4,0},{1,5},{5,1},{2,6},{6,2},{3,7},{7,3},{8,12},{12,8},{9,1... | collective-permute-start | bytes 1769480 | tf_op jit(solution)/shard_map/ppermute | solution.py:158
  82.8 13.3 %collective-permute-start.24 = (bf16[4,288,256]{2,1,0:T(8,128)(2,1)S(1)}, bf16[4,288,256]{2,1,0:T(8,128)(2,1)}, u32[]{:S(2)}, u32[]{:S(2)}) collective-permute-start(bf16[4,288,256]{2,1,0:T(8,128)(2,1)S(1)} %collective-permute-done.23.refs_6_), channel_id=1, source_target_pairs={{0,4},{4,0},{1,5},{5,1},{2,6},{6,2},{3,7},{7,3},{8,12},{12,8},{9,1... | collective-permute-start | bytes 1769480 | tf_op jit(solution)/shard_map/ppermute | solution.py:158
  83.6 12.5 %collective-permute-start.26 = (bf16[4,288,256]{2,1,0:T(8,128)(2,1)S(1)}, bf16[4,288,256]{2,1,0:T(8,128)(2,1)}, u32[]{:S(2)}, u32[]{:S(2)}) collective-permute-start(bf16[4,288,256]{2,1,0:T(8,128)(2,1)S(1)} %collective-permute-done.25.refs_7_), channel_id=1, source_target_pairs={{0,4},{4,0},{1,5},{5,1},{2,6},{6,2},{3,7},{7,3},{8,12},{12,8},{9,1... | collective-permute-start | bytes 1769480 | tf_op jit(solution)/shard_map/ppermute | solution.py:158
  88.4 7.7 %collective-permute-start.17 = (bf16[4,224,256]{2,1,0:T(8,128)(2,1)}, bf16[4,224,256]{2,1,0:T(8,128)(2,1)}, u32[]{:S(2)}, u32[]{:S(2)}) collective-permute-start(bf16[4,224,256]{2,1,0:T(8,128)(2,1)} %copy-done), channel_id=1, source_target_pairs={{0,4},{4,0},{1,5},{5,1},{2,6},{6,2},{3,7},{7,3},{8,12},{12,8},{9,1... | collective-permute-start | bytes 1376264 | tf_op jit(solution)/shard_map/ppermute | solution.py:157
  89.3 6.8 %collective-permute-start.19 = (bf16[4,224,256]{2,1,0:T(8,128)(2,1)}, bf16[4,224,256]{2,1,0:T(8,128)(2,1)}, u32[]{:S(2)}, u32[]{:S(2)}) collective-permute-start(bf16[4,224,256]{2,1,0:T(8,128)(2,1)} %collective-permute-done.18.refs_3_), channel_id=1, source_target_pairs={{0,4},{4,0},{1,5},{5,1},{2,6},{6,2},{3,7},{7,3},{8,12},{12,8},{9,1... | collective-permute-start | bytes 1376264 | tf_op jit(solution)/shard_map/ppermute | solution.py:157
  90.1 1.8 %copy-start.1 = (bf16[4,224,256]{2,1,0:T(8,128)(2,1)S(1)}, bf16[4,224,256]{2,1,0:T(8,128)(2,1)}, u32[]{:S(2)}) copy-start(bf16[4,224,256]{2,1,0:T(8,128)(2,1)} %copy-done) | copy-start | bytes 1376260
  91.9 4.3 %copy-start.3 = (bf16[4,224,256]{2,1,0:T(8,128)(2,1)S(1)}, bf16[4,224,256]{2,1,0:T(8,128)(2,1)}, u32[]{:S(2)}) copy-start(bf16[4,224,256]{2,1,0:T(8,128)(2,1)} %copy-done.2) | copy-start | bytes 1376260
  101.8 13.6 %all-to-all-start.1 = ((f32[128,1,256]{2,1,0:T(1,128)}), f32[128,1,256]{2,1,0:T(1,128)S(1)}, u32[]{:S(2)}, u32[]{:S(2)}) async-start(f32[128,1,256]{2,1,0:T(1,128)} %broadcast_in_dim.9), calls=%async_computation.1 | async-start | bytes 262144 | tf_op jit(solution)/shard_map/all_to_all | solution.py:44
  (1 other events, 0.8 us)

commit v2 on v1

--- a/solution.py
+++ b/solution.py
@@ -15,7 +15,7 @@
 WIDTH = 256
 COLS = 2048
 GROUPS = COLS // WIDTH
-FIRST = 224
+FIRST = 288
 STACK = 2 * WIDTH + 16
 LANES = 128
 
@@ -69,18 +69,17 @@
         x_refs, z_refs = refs[:4], refs[4:8]
         x, y, z, c = (where_ref[i] for i in range(4))
         if before is None:
-            sym_ref, visit_ref, total_ref, visit_row_ref, total_row_ref = refs[8:]
+            sym_ref, visit_ref, total_ref, ratio_ref, visit_row_ref = refs[8:]
             core = c
             sums = lax.dot_general(
                 left_ref[:2 * WIDTH], left_ref[2 * WIDTH:], (((1,), (1,)), ((), ())),
                 preferred_element_type=jnp.float32)
             sums = jnp.sum(sums[:, 6:9], axis=1, keepdims=True)
             visit = jnp.broadcast_to(sums[:WIDTH], (WIDTH, LANES))
-            visit_row_ref[...] = visit
-            total_row_ref[...] = visit + sums[WIDTH:]
+            ratio_ref[...] = visit / (visit + sums[WIDTH:])
+            visit_row_ref[...] = visit.T[:1]
         else:
-            visit_row_ref, total_row_ref = refs[11:13]
-            sym_ref, visit_ref, total_ref, send_ref = refs[13:]
+            sym_ref, visit_ref, total_ref, send_ref = refs[12:]
             core = 1 - c
             sym_ref[...], visit_ref[...], total_ref[...] = (ref[...] for ref in refs[8:11])
         for dz in range(4):
@@ -98,15 +97,14 @@
             visit_ref[pl.ds(g, 1), :] = jnp.sum(frame[:3], axis=0, keepdims=True)
             total_ref[pl.ds(g, 1), :] = jnp.sum(frame[:6], axis=0, keepdims=True)
         if before is not None:
-            send_ref[...] = row_parts(sym_ref, visit_row_ref[...] / total_row_ref[...],
-                                      visit_ref[...] / total_ref[...])
+            send_ref[...] = row_parts(sym_ref, refs[11][...], visit_ref[...] / total_ref[...])
 
     operands = [where, left] + by_x + by_z
     out = [f32(WIDTH, COLS), f32(GROUPS, WIDTH), f32(GROUPS, WIDTH)]
     if before is None:
-        out += [f32(WIDTH, LANES)] * 2
+        out += [f32(WIDTH, LANES), f32(1, WIDTH)]
     else:
-        operands += list(before)
+        operands += list(before[:4])
         out += [f32(1, WIDTH)]
     return pl.pallas_call(
         kernel,
@@ -133,10 +131,9 @@
     return jnp.pad(rows, ((0, 0), (TAU, TAU)))
 
 
-def frame_weights(member, after):
+def frame_weights(member):
     part = jnp.sum(member, axis=1, dtype=jnp.float32)
     got = to_all(part)
-    got, _ = lax.optimization_barrier((got, after))
     frame = jnp.sum(got, axis=0).reshape(FRAMES)
     up = jnp.pad(frame[TAU:], (0, TAU))
     down = jnp.pad(frame[:FRAMES - TAU], (TAU, 0))
@@ -157,20 +154,18 @@
     other_x = [lax.ppermute(v, "c", [(0, 1), (1, 0)]) for v in by_x]
     other_z = [lax.ppermute(v, "c", [(0, 1), (1, 0)]) for v in by_z]
     rows = own_rows(member)
-    left = jnp.concatenate([rows[:, :FRAMES], rows[:, 2 * TAU:], frame_weights(member, (once_x, once_z))], axis=0)
+    left = jnp.concatenate([rows[:, :FRAMES], rows[:, 2 * TAU:], frame_weights(member)], axis=0)
     own = products(where, left, by_x, by_z, None)
     sym, visit_cols, _, part = products(where, left, other_x, other_z, own)
-    visit_cols = visit_cols.reshape(COLS)
-    visit_rows = own[3][:, 0]
-    part = part.reshape(WIDTH)
-    w = (where[0] * 4 + where[2]) * 2 + where[3]
+    w = (x * 4 + where[2]) * 2 + where[3]
     for step in range(3):
-        totals = jnp.sum(to_all(part), axis=1).reshape(STATES)
-        total_rows = lax.dynamic_slice_in_dim(totals, w * WIDTH, WIDTH)
-        total_cols = lax.dynamic_slice_in_dim(totals, where[1] * COLS, COLS)
+        totals = jnp.sum(to_all(part.reshape(WIDTH)), axis=1)
+        total_rows = lax.dynamic_slice_in_dim(totals, w, 1).reshape(WIDTH)
+        total_cols = lax.dynamic_slice_in_dim(totals, y * GROUPS, GROUPS)
         if step == 2:
             break
-        ratio = (visit_rows / total_rows)[:, None] + (visit_cols / total_cols)[None, :]
+        ratio_rows = own[4].reshape(WIDTH) / total_rows
+        ratio = ratio_rows[:, None] + (visit_cols / total_cols).reshape(COLS)[None, :]
         part = jnp.sum(sym / ratio, axis=1)
     transition = sym * (STATES / total_rows)[:, None] / ratio
     stationary = STATES * total_rows / jnp.sum(totals)

time: 150 us -> 152 us (1.013)
  starting transfers between devices: 55.7 us -> 70.4 us
  waiting for transfers between devices: 35.9 us -> 27.9 us
  local copies, waits for them, and re-layouts: 9.47 us -> 6.61 us
  other arithmetic: 10.8 us -> 9.25 us
    ppermute x12, waiting for transfers between devices: 25.9 us -> 17.3 us  [ring(): return [v] + [lax.ppermute(v, axis, along(k)) for k in (1, 2, 3)]]
    ppermute x12, starting transfers between devices: 15.7 us -> 21.2 us  [ring(): return [v] + [lax.ppermute(v, axis, along(k)) for k in (1, 2, 3)]]
    ppermute x4, starting transfers between devices: 4.07 us -> 8.06 us  [shards(): other_x = [lax.ppermute(v, 'c', [(0, 1), (1, 0)]) for v in by_x]]
    ppermute x3, starting transfers between devices: 3.38 us -> 6.63 us  [shards(): lax.ppermute(leave[k], 'y', along(k))]
    unnamed x15 -> x23, local copies, waits for them, and re-layouts: 2.7 us -> 1.16 us
  transfers between devices with their start and end apart: 29 -> 29, of which waited for: 7 -> 8; matrix products, arithmetic and copies ran while one was open for 7% -> 5% of each run, Pallas kernels for 3% -> 3%
where the time goes in v2:
time: 152 us; the launch traced here: 151 us
  starting transfers between devices  70.4 us (46%)
  waiting for transfers between devices  27.9 us (18%)
  blocking collectives  27.9 us (18%)
  other arithmetic  9.25 us (6%)
  Pallas kernels  8.11 us (5%)
  local copies, waits for them, and re-layouts  6.61 us (4%)
    all_to_all x2, blocking collectives, to_all(): return lax.all_to_all(sent, ALL, 0, 0).reshape((32, 4) + values.shape)  27.9 us
    ppermute x12, starting transfers between devices, ring(): return [v] + [lax.ppermute(v, axis, along(k)) for k in (1, 2, 3)]  21.2 us
    ppermute x12, waiting for transfers between devices, ring(): return [v] + [lax.ppermute(v, axis, along(k)) for k in (1, 2, 3)]  17.3 us
    all_to_all x2, starting transfers between devices, to_all(): return lax.all_to_all(sent, ALL, 0, 0).reshape((32, 4) + values.shape)  15.8 us
    ppermute x4, starting transfers between devices, shards(): other_z = [lax.ppermute(v, 'c', [(0, 1), (1, 0)]) for v in by_z]  11.8 us
    all_to_all x2, waiting for transfers between devices, to_all(): return lax.all_to_all(sent, ALL, 0, 0).reshape((32, 4) + values.shape)  10.1 us
    pallas_call x2, Pallas kernels, products(): pl.pallas_call(kernel, in_specs=[SMEM] + [VMEM] * (len(operands) - 1), ou...  8.11 us
    ppermute x4, starting transfers between devices, shards(): other_x = [lax.ppermute(v, 'c', [(0, 1), (1, 0)]) for v in by_x]  8.06 us
  transfers between devices with their start and end apart: 29, of which 8 were waited for; matrix products, arithmetic and copies ran while one was open for 5% of the time, Pallas kernels for 3%

profile of v2, /device:TPU:1, one launch (start us, length us, event | category | flops | bytes accessed | tf_op | source)
XLA Modules:
  0.0 151.4 jit_solution(3689292225163618779)
XLA Ops:
  1.6 2.1 %collective-permute-start.14 = (bf16[224,256]{1,0:T(8,128)(2,1)S(1)}, bf16[224,256]{1,0:T(8,128)(2,1)S(1)}, u32[]{:S(2)}, u32[]{:S(2)}) collective-permute-start(bf16[224,256]{1,0:T(8,128)(2,1)S(1)} %get-tuple-element.27), channel_id=1, source_target_pairs={{0,32},{32,64},{64,96},{96,0},{1,33},{33,65},{65,97},{97,1},{2,34}... | collective-permute-start | bytes 344072 | tf_op jit(solution)/shard_map/ppermute | solution.py:39
  3.7 2.5 %collective-permute-start.15 = (bf16[224,256]{1,0:T(8,128)(2,1)S(1)}, bf16[224,256]{1,0:T(8,128)(2,1)S(1)}, u32[]{:S(2)}, u32[]{:S(2)}) collective-permute-start(bf16[224,256]{1,0:T(8,128)(2,1)S(1)} %get-tuple-element.27), channel_id=1, source_target_pairs={{0,64},{32,96},{64,0},{96,32},{1,65},{33,97},{65,1},{97,33},{2,66}... | collective-permute-start | bytes 344072 | tf_op jit(solution)/shard_map/ppermute | solution.py:39
  8.4 2.8 %collective-permute-start = (bf16[512,256]{0,1:T(8,128)(2,1)S(1)}, bf16[512,256]{0,1:T(8,128)(2,1)S(1)}, u32[]{:S(2)}, u32[]{:S(2)}) collective-permute-start(bf16[512,256]{0,1:T(8,128)(2,1)S(1)} %copy.23), channel_id=1, source_target_pairs={{0,3},{1,0},{2,1},{3,2},{4,7},{5,4},{6,5},{7,6},{8,11},{9,8},{10,9... | collective-permute-start | bytes 786440 | tf_op jit(solution)/shard_map/ppermute | solution.py:128
  13.0 2.8 %collective-permute-start.17 = (bf16[224,256]{1,0:T(8,128)(2,1)S(1)}, bf16[224,256]{1,0:T(8,128)(2,1)S(1)}, u32[]{:S(2)}, u32[]{:S(2)}) collective-permute-start(bf16[224,256]{1,0:T(8,128)(2,1)S(1)} %get-tuple-element.25), channel_id=1, source_target_pairs={{0,1},{1,2},{2,3},{3,0},{4,5},{5,6},{6,7},{7,4},{8,9},{9,10},{10,1... | collective-permute-start | bytes 344072 | tf_op jit(solution)/shard_map/ppermute | solution.py:151
  16.8 10.9 %all-to-all-start = ((f32[128,1,512]{2,1,0:T(1,128)}), f32[128,1,512]{2,1,0:T(1,128)S(1)}, u32[]{:S(2)}, u32[]{:S(2)}) async-start(f32[128,1,512]{2,1,0:T(1,128)} %broadcast_in_dim.8), calls=%async_computation | async-start | bytes 524288 | tf_op jit(solution)/shard_map/all_to_all | solution.py:44
  27.7 2.9 %collective-permute-start.18 = (bf16[224,256]{1,0:T(8,128)(2,1)S(1)}, bf16[224,256]{1,0:T(8,128)(2,1)S(1)}, u32[]{:S(2)}, u32[]{:S(2)}) collective-permute-start(bf16[224,256]{1,0:T(8,128)(2,1)S(1)} %get-tuple-element.24), channel_id=1, source_target_pairs={{0,2},{1,3},{2,0},{3,1},{4,6},{5,7},{6,4},{7,5},{8,10},{9,11},{10,... | collective-permute-start | bytes 344072 | tf_op jit(solution)/shard_map/ppermute | solution.py:151
  31.6 1.4 collective-permute-start.4
  32.9 2.9 %collective-permute-start.5 = (bf16[288,256]{1,0:T(8,128)(2,1)S(1)}, bf16[288,256]{1,0:T(8,128)(2,1)S(1)}, u32[]{:S(2)}, u32[]{:S(2)}) collective-permute-start(bf16[288,256]{1,0:T(8,128)(2,1)S(1)} %collective-permute-done.3), channel_id=1, source_target_pairs={{0,16},{8,24},{16,0},{24,8},{1,17},{9,25},{17,1},{25,9},{2,18},{10... | collective-permute-start | bytes 442376 | tf_op jit(solution)/shard_map/ppermute | solution.py:39
  36.0 1.9 %collective-permute-start.1 = (bf16[512,256]{0,1:T(8,128)(2,1)S(1)}, bf16[512,256]{0,1:T(8,128)(2,1)S(1)}, u32[]{:S(2)}, u32[]{:S(2)}) collective-permute-start(bf16[512,256]{0,1:T(8,128)(2,1)S(1)} %copy.23), channel_id=1, source_target_pairs={{0,2},{1,3},{2,0},{3,1},{4,6},{5,7},{6,4},{7,5},{8,10},{9,11},{10,... | collective-permute-start | bytes 786440 | tf_op jit(solution)/shard_map/ppermute | solution.py:128
  38.4 1.6 %collective-permute-start.2 = (bf16[512,256]{0,1:T(8,128)(2,1)S(1)}, bf16[512,256]{0,1:T(8,128)(2,1)S(1)}, u32[]{:S(2)}, u32[]{:S(2)}) collective-permute-start(bf16[512,256]{0,1:T(8,128)(2,1)S(1)} %copy.23), channel_id=1, source_target_pairs={{0,1},{1,2},{2,3},{3,0},{4,5},{5,6},{6,7},{7,4},{8,9},{9,10},{10,1... | collective-permute-start | bytes 786440 | tf_op jit(solution)/shard_map/ppermute | solution.py:128
  40.8 3.3 %collective-permute-start.6 = (bf16[288,256]{1,0:T(8,128)(2,1)S(1)}, bf16[288,256]{1,0:T(8,128)(2,1)S(1)}, u32[]{:S(2)}, u32[]{:S(2)}) collective-permute-start(bf16[288,256]{1,0:T(8,128)(2,1)S(1)} %collective-permute-done.3), channel_id=1, source_target_pairs={{0,24},{8,0},{16,8},{24,16},{1,25},{9,1},{17,9},{25,17},{2,26},{10... | collective-permute-start | bytes 442376 | tf_op jit(solution)/shard_map/ppermute | solution.py:39
  44.1 1.5 collective-permute-start.23
  46.6 3.4 %collective-permute-start.25 = (bf16[4,224,256]{2,1,0:T(8,128)(2,1)S(1)}, bf16[4,224,256]{2,1,0:T(8,128)(2,1)S(1)}, u32[]{:S(2)}, u32[]{:S(2)}) collective-permute-start(bf16[4,224,256]{2,1,0:T(8,128)(2,1)S(1)} %pad_maximum_fusion.2.refs_4_), channel_id=1, source_target_pairs={{0,24},{8,0},{16,8},{24,16},{1,25},{9,1},{17,9},{25,17},{2,26},{10... | collective-permute-start | bytes 1376264 | tf_op jit(solution)/shard_map/ppermute | solution.py:39
  50.1 10.4 %collective-permute-start.20 = (bf16[4,224,256]{2,1,0:T(8,128)(2,1)S(1)}, bf16[4,224,256]{2,1,0:T(8,128)(2,1)}, u32[]{:S(2)}, u32[]{:S(2)}) collective-permute-start(bf16[4,224,256]{2,1,0:T(8,128)(2,1)S(1)} %pad_maximum_fusion.2.refs_4_), channel_id=1, source_target_pairs={{0,4},{4,0},{1,5},{5,1},{2,6},{6,2},{3,7},{7,3},{8,12},{12,8},{9,1... | collective-permute-start | bytes 1376264 | tf_op jit(solution)/shard_map/ppermute | solution.py:155
  60.5 1.3 collective-permute-start.10
  61.9 1.3 collective-permute-start.12
  63.2 2.0 %collective-permute-done.23.refs_6_ = bf16[4,224,256]{2,1,0:T(8,128)(2,1)S(1)} collective-permute-done((bf16[4,224,256]{2,1,0:T(8,128)(2,1)S(1)}, bf16[4,224,256]{2,1,0:T(8,128)(2,1)S(1)}, u32[]{:S(2)}, u32[]{:S(2)}) %collective-permute-start.23) | collective-permute-done | bytes 458784 | tf_op jit(solution)/shard_map/ppermute | solution.py:39
  65.5 1.3 collective-permute-done.25.refs_7_
  66.8 3.8 %collective-permute-start.7 = (bf16[4,288,256]{2,1,0:T(8,128)(2,1)S(1)}, bf16[4,288,256]{2,1,0:T(8,128)(2,1)S(1)}, u32[]{:S(2)}, u32[]{:S(2)}) collective-permute-start(bf16[4,288,256]{2,1,0:T(8,128)(2,1)S(1)} %pad_maximum_fusion.refs_0_), channel_id=1, source_target_pairs={{0,4},{4,0},{1,5},{5,1},{2,6},{6,2},{3,7},{7,3},{8,12},{12,8},{9,1... | collective-permute-start | bytes 1769480 | tf_op jit(solution)/shard_map/ppermute | solution.py:154
  71.7 1.3 maximum_bitcast_fusion
  73.0 3.5 %collective-permute-done.10.refs_2_ = bf16[4,288,256]{2,1,0:T(8,128)(2,1)S(1)} collective-permute-done((bf16[4,288,256]{2,1,0:T(8,128)(2,1)S(1)}, bf16[4,288,256]{2,1,0:T(8,128)(2,1)S(1)}, u32[]{:S(2)}, u32[]{:S(2)}) %collective-permute-start.10) | collective-permute-done | bytes 589856 | tf_op jit(solution)/shard_map/ppermute | solution.py:39
  76.5 2.4 %collective-permute-start.11 = (bf16[4,288,256]{2,1,0:T(8,128)(2,1)S(1)}, bf16[4,288,256]{2,1,0:T(8,128)(2,1)S(1)}, u32[]{:S(2)}, u32[]{:S(2)}) collective-permute-start(bf16[4,288,256]{2,1,0:T(8,128)(2,1)S(1)} %collective-permute-done.10.refs_2_), channel_id=1, source_target_pairs={{0,4},{4,0},{1,5},{5,1},{2,6},{6,2},{3,7},{7,3},{8,12},{12,8},{9,1... | collective-permute-start | bytes 1769480 | tf_op jit(solution)/shard_map/ppermute | solution.py:154
  78.9 9.0 %collective-permute-done.12.refs_3_ = bf16[4,288,256]{2,1,0:T(8,128)(2,1)S(1)} collective-permute-done((bf16[4,288,256]{2,1,0:T(8,128)(2,1)S(1)}, bf16[4,288,256]{2,1,0:T(8,128)(2,1)S(1)}, u32[]{:S(2)}, u32[]{:S(2)}) %collective-permute-start.12) | collective-permute-done | bytes 589856 | tf_op jit(solution)/shard_map/ppermute | solution.py:39
  87.9 1.4 collective-permute-start.13
  91.7 1.3 pad_slice_fusion.1
  93.2 4.0 %shard_map.30 = (f32[256,2048]{1,0:T(8,128)S(1)}, f32[8,256]{1,0:T(8,128)S(1)}, f32[8,256]{1,0:T(8,128)S(1)}, f32[256,128]{1,0:T(8,128)S(1)}, f32[1,256]{1,0:T(1,128)S(1)}) custom-call(s32[4]{0:T(128)S(1)} %pad_add_fusion.where_ref, bf16[528,2048]{1,0:T(8,128)(2,1)S(1)} %fusion.1.left_ref, bf16[4,288,256]{2,1,0:T(8,128)(2,1)S(1)} %pad_maximum_fusion.refs_0_, ...), custom_call_target="tpu_custom_call" | custom-call | tf_op jit(solution)/shard_map/pallas_call | solution.py:109
  97.3 4.1 %shard_map.31 = (f32[256,2048]{1,0:T(8,128)S(1)}, f32[8,256]{1,0:T(8,128)S(1)}, f32[8,256]{1,0:T(8,128)}, f32[1,256]{1,0:T(1,128)S(1)}) custom-call(s32[4]{0:T(128)S(1)} %pad_add_fusion.where_ref, bf16[528,2048]{1,0:T(8,128)(2,1)S(1)} %fusion.1.left_ref, bf16[4,288,256]{2,1,0:T(8,128)(2,1)S(1)} %collective-permute-done.7.refs_0_, ...), custom_call_target="tpu_custom_call" | custom-call | tf_op jit(solution)/shard_map/pallas_call | solution.py:109
  102.1 4.9 %all-to-all-start.1 = ((f32[128,1,256]{2,1,0:T(1,128)}), f32[128,1,256]{2,1,0:T(1,128)S(1)}, u32[]{:S(2)}, u32[]{:S(2)}) async-start(f32[128,1,256]{2,1,0:T(1,128)} %broadcast_in_dim.9), calls=%async_computation.1 | async-start | bytes 262144 | tf_op jit(solution)/shard_map/all_to_all | solution.py:44
  107.1 10.1 %all-to-all-done.1 = f32[128,1,256]{2,1,0:T(1,128)S(1)} async-done(((f32[128,1,256]{2,1,0:T(1,128)}), f32[128,1,256]{2,1,0:T(1,128)S(1)}, u32[]{:S(2)}, u32[]{:S(2)}) %all-to-all-start.1) | async-done | bytes 131104 | tf_op jit(solution)/shard_map/all_to_all | solution.py:44
  118.1 14.0 %all_to_all.24 = f32[128,1,256]{2,1,0:T(1,128)S(1)} all-to-all(f32[128,1,256]{2,1,0:T(1,128)S(1)} %broadcast_in_dim.10), channel_id=1, replica_groups=mesh['x'=4,'z'=4,'c'=2,'y'=4] {'x','z','c','y'}, dimensions={0} | all-to-all | bytes 262144 | tf_op jit(solution)/shard_map/all_to_all | solution.py:44
  133.2 13.9 %all_to_all.25 = f32[128,1,256]{2,1,0:T(1,128)S(1)} all-to-all(f32[128,1,256]{2,1,0:T(1,128)S(1)} %broadcast_in_dim.11), channel_id=1, replica_groups=mesh['x'=4,'z'=4,'c'=2,'y'=4] {'x','z','c','y'}, dimensions={0} | all-to-all | bytes 262144 | tf_op jit(solution)/shard_map/all_to_all | solution.py:44
  149.5 1.9 %add_divide_fusion = f32[256,2048]{1,0:T(8,128)} fusion(f32[256,2048]{1,0:T(8,128)S(1)} %get-tuple-element.14, f32[256]{0:T(256)S(1)} %bitcast.62, f32[2048]{0:T(1024)S(1)} %bitcast.52, f32[256]{0:T(256)S(1)} %bitcast.60), kind=kLoop, calls=%fused_computation.2 | loop fusion | flops 1572864 | bytes 4204544 | tf_op jit(solution)/shard_map/div | solution.py:170
  (101 shorter events, 18.4 us)
Async XLA Ops:
  1.6 11.2 %collective-permute-start.14 = (bf16[224,256]{1,0:T(8,128)(2,1)S(1)}, bf16[224,256]{1,0:T(8,128)(2,1)S(1)}, u32[]{:S(2)}, u32[]{:S(2)}) collective-permute-start(bf16[224,256]{1,0:T(8,128)(2,1)S(1)} %get-tuple-element.27), channel_id=1, source_target_pairs={{0,32},{32,64},{64,96},{96,0},{1,33},{33,65},{65,97},{97,1},{2,34}... | collective-permute-start | bytes 344072 | tf_op jit(solution)/shard_map/ppermute | solution.py:39
  3.7 9.2 %collective-permute-start.15 = (bf16[224,256]{1,0:T(8,128)(2,1)S(1)}, bf16[224,256]{1,0:T(8,128)(2,1)S(1)}, u32[]{:S(2)}, u32[]{:S(2)}) collective-permute-start(bf16[224,256]{1,0:T(8,128)(2,1)S(1)} %get-tuple-element.27), channel_id=1, source_target_pairs={{0,64},{32,96},{64,0},{96,32},{1,65},{33,97},{65,1},{97,33},{2,66}... | collective-permute-start | bytes 344072 | tf_op jit(solution)/shard_map/ppermute | solution.py:39
  6.2 6.7 %collective-permute-start.16 = (bf16[224,256]{1,0:T(8,128)(2,1)S(1)}, bf16[224,256]{1,0:T(8,128)(2,1)S(1)}, u32[]{:S(2)}, u32[]{:S(2)}) collective-permute-start(bf16[224,256]{1,0:T(8,128)(2,1)S(1)} %get-tuple-element.27), channel_id=1, source_target_pairs={{0,96},{32,0},{64,32},{96,64},{1,97},{33,1},{65,33},{97,65},{2,98}... | collective-permute-start | bytes 344072 | tf_op jit(solution)/shard_map/ppermute | solution.py:39
  8.4 52.1 %copy-start.5 = (bf16[512,256]{0,1:T(8,128)(2,1)}, bf16[512,256]{0,1:T(8,128)(2,1)S(1)}, u32[]{:S(2)}) copy-start(bf16[512,256]{0,1:T(8,128)(2,1)S(1)} %copy.23) | copy-start | bytes 786436
  8.4 32.4 %collective-permute-start = (bf16[512,256]{0,1:T(8,128)(2,1)S(1)}, bf16[512,256]{0,1:T(8,128)(2,1)S(1)}, u32[]{:S(2)}, u32[]{:S(2)}) collective-permute-start(bf16[512,256]{0,1:T(8,128)(2,1)S(1)} %copy.23), channel_id=1, source_target_pairs={{0,3},{1,0},{2,1},{3,2},{4,7},{5,4},{6,5},{7,6},{8,11},{9,8},{10,9... | collective-permute-start | bytes 786440 | tf_op jit(solution)/shard_map/ppermute | solution.py:128
  12.2 19.4 %collective-permute-start.3 = (bf16[288,256]{1,0:T(8,128)(2,1)S(1)}, bf16[288,256]{1,0:T(8,128)(2,1)S(1)}, u32[]{:S(2)}, u32[]{:S(2)}) collective-permute-start(bf16[288,256]{1,0:T(8,128)(2,1)S(1)} %slice.22), channel_id=1, source_target_pairs={{0,0},{4,4},{8,8},{12,12},{16,16},{20,20},{24,24},{28,28},{1,32},{... | collective-permute-start | bytes 442376 | tf_op jit(solution)/shard_map/ppermute | solution.py:147
  13.0 19.9 %collective-permute-start.17 = (bf16[224,256]{1,0:T(8,128)(2,1)S(1)}, bf16[224,256]{1,0:T(8,128)(2,1)S(1)}, u32[]{:S(2)}, u32[]{:S(2)}) collective-permute-start(bf16[224,256]{1,0:T(8,128)(2,1)S(1)} %get-tuple-element.25), channel_id=1, source_target_pairs={{0,1},{1,2},{2,3},{3,0},{4,5},{5,6},{6,7},{7,4},{8,9},{9,10},{10,1... | collective-permute-start | bytes 344072 | tf_op jit(solution)/shard_map/ppermute | solution.py:151
  16.8 23.2 %all-to-all-start = ((f32[128,1,512]{2,1,0:T(1,128)}), f32[128,1,512]{2,1,0:T(1,128)S(1)}, u32[]{:S(2)}, u32[]{:S(2)}) async-start(f32[128,1,512]{2,1,0:T(1,128)} %broadcast_in_dim.8), calls=%async_computation | async-start | bytes 524288 | tf_op jit(solution)/shard_map/all_to_all | solution.py:44
  27.7 8.2 %collective-permute-start.18 = (bf16[224,256]{1,0:T(8,128)(2,1)S(1)}, bf16[224,256]{1,0:T(8,128)(2,1)S(1)}, u32[]{:S(2)}, u32[]{:S(2)}) collective-permute-start(bf16[224,256]{1,0:T(8,128)(2,1)S(1)} %get-tuple-element.24), channel_id=1, source_target_pairs={{0,2},{1,3},{2,0},{3,1},{4,6},{5,7},{6,4},{7,5},{8,10},{9,11},{10,... | collective-permute-start | bytes 344072 | tf_op jit(solution)/shard_map/ppermute | solution.py:151
  30.7 7.7 %collective-permute-start.19 = (bf16[224,256]{1,0:T(8,128)(2,1)S(1)}, bf16[224,256]{1,0:T(8,128)(2,1)S(1)}, u32[]{:S(2)}, u32[]{:S(2)}) collective-permute-start(bf16[224,256]{1,0:T(8,128)(2,1)S(1)} %get-tuple-element.23), channel_id=1, source_target_pairs={{0,3},{1,0},{2,1},{3,2},{4,7},{5,4},{6,5},{7,6},{8,11},{9,8},{10,9... | collective-permute-start | bytes 344072 | tf_op jit(solution)/shard_map/ppermute | solution.py:151
  31.6 12.5 %collective-permute-start.4 = (bf16[288,256]{1,0:T(8,128)(2,1)S(1)}, bf16[288,256]{1,0:T(8,128)(2,1)S(1)}, u32[]{:S(2)}, u32[]{:S(2)}) collective-permute-start(bf16[288,256]{1,0:T(8,128)(2,1)S(1)} %collective-permute-done.3), channel_id=1, source_target_pairs={{0,8},{8,16},{16,24},{24,0},{1,9},{9,17},{17,25},{25,1},{2,10},{10... | collective-permute-start | bytes 442376 | tf_op jit(solution)/shard_map/ppermute | solution.py:39
  32.9 11.2 %collective-permute-start.5 = (bf16[288,256]{1,0:T(8,128)(2,1)S(1)}, bf16[288,256]{1,0:T(8,128)(2,1)S(1)}, u32[]{:S(2)}, u32[]{:S(2)}) collective-permute-start(bf16[288,256]{1,0:T(8,128)(2,1)S(1)} %collective-permute-done.3), channel_id=1, source_target_pairs={{0,16},{8,24},{16,0},{24,8},{1,17},{9,25},{17,1},{25,9},{2,18},{10... | collective-permute-start | bytes 442376 | tf_op jit(solution)/shard_map/ppermute | solution.py:39
  36.0 14.2 %collective-permute-start.1 = (bf16[512,256]{0,1:T(8,128)(2,1)S(1)}, bf16[512,256]{0,1:T(8,128)(2,1)S(1)}, u32[]{:S(2)}, u32[]{:S(2)}) collective-permute-start(bf16[512,256]{0,1:T(8,128)(2,1)S(1)} %copy.23), channel_id=1, source_target_pairs={{0,2},{1,3},{2,0},{3,1},{4,6},{5,7},{6,4},{7,5},{8,10},{9,11},{10,... | collective-permute-start | bytes 786440 | tf_op jit(solution)/shard_map/ppermute | solution.py:128
  38.4 22.1 %collective-permute-start.2 = (bf16[512,256]{0,1:T(8,128)(2,1)S(1)}, bf16[512,256]{0,1:T(8,128)(2,1)S(1)}, u32[]{:S(2)}, u32[]{:S(2)}) collective-permute-start(bf16[512,256]{0,1:T(8,128)(2,1)S(1)} %copy.23), channel_id=1, source_target_pairs={{0,1},{1,2},{2,3},{3,0},{4,5},{5,6},{6,7},{7,4},{8,9},{9,10},{10,1... | collective-permute-start | bytes 786440 | tf_op jit(solution)/shard_map/ppermute | solution.py:128
  40.8 5.8 %collective-permute-start.6 = (bf16[288,256]{1,0:T(8,128)(2,1)S(1)}, bf16[288,256]{1,0:T(8,128)(2,1)S(1)}, u32[]{:S(2)}, u32[]{:S(2)}) collective-permute-start(bf16[288,256]{1,0:T(8,128)(2,1)S(1)} %collective-permute-done.3), channel_id=1, source_target_pairs={{0,24},{8,0},{16,8},{24,16},{1,25},{9,1},{17,9},{25,17},{2,26},{10... | collective-permute-start | bytes 442376 | tf_op jit(solution)/shard_map/ppermute | solution.py:39
  44.1 17.8 %collective-permute-start.21 = (bf16[4,224,256]{2,1,0:T(8,128)(2,1)S(1)}, bf16[4,224,256]{2,1,0:T(8,128)(2,1)}, u32[]{:S(2)}, u32[]{:S(2)}) collective-permute-start(bf16[4,224,256]{2,1,0:T(8,128)(2,1)S(1)} %pad_maximum_fusion.2.refs_4_), channel_id=1, source_target_pairs={{0,8},{8,16},{16,24},{24,0},{1,9},{9,17},{17,25},{25,1},{2,10},{10... | collective-permute-start | bytes 1376264 | tf_op jit(solution)/shard_map/ppermute | solution.py:39
  44.1 21.0 %collective-permute-start.23 = (bf16[4,224,256]{2,1,0:T(8,128)(2,1)S(1)}, bf16[4,224,256]{2,1,0:T(8,128)(2,1)S(1)}, u32[]{:S(2)}, u32[]{:S(2)}) collective-permute-start(bf16[4,224,256]{2,1,0:T(8,128)(2,1)S(1)} %pad_maximum_fusion.2.refs_4_), channel_id=1, source_target_pairs={{0,16},{8,24},{16,0},{24,8},{1,17},{9,25},{17,1},{25,9},{2,18},{10... | collective-permute-start | bytes 1376264 | tf_op jit(solution)/shard_map/ppermute | solution.py:39
  46.6 20.1 %collective-permute-start.25 = (bf16[4,224,256]{2,1,0:T(8,128)(2,1)S(1)}, bf16[4,224,256]{2,1,0:T(8,128)(2,1)S(1)}, u32[]{:S(2)}, u32[]{:S(2)}) collective-permute-start(bf16[4,224,256]{2,1,0:T(8,128)(2,1)S(1)} %pad_maximum_fusion.2.refs_4_), channel_id=1, source_target_pairs={{0,24},{8,0},{16,8},{24,16},{1,25},{9,1},{17,9},{25,17},{2,26},{10... | collective-permute-start | bytes 1376264 | tf_op jit(solution)/shard_map/ppermute | solution.py:39
  50.1 20.7 %collective-permute-start.20 = (bf16[4,224,256]{2,1,0:T(8,128)(2,1)S(1)}, bf16[4,224,256]{2,1,0:T(8,128)(2,1)}, u32[]{:S(2)}, u32[]{:S(2)}) collective-permute-start(bf16[4,224,256]{2,1,0:T(8,128)(2,1)S(1)} %pad_maximum_fusion.2.refs_4_), channel_id=1, source_target_pairs={{0,4},{4,0},{1,5},{5,1},{2,6},{6,2},{3,7},{7,3},{8,12},{12,8},{9,1... | collective-permute-start | bytes 1376264 | tf_op jit(solution)/shard_map/ppermute | solution.py:155
  60.5 16.0 %collective-permute-start.10 = (bf16[4,288,256]{2,1,0:T(8,128)(2,1)S(1)}, bf16[4,288,256]{2,1,0:T(8,128)(2,1)S(1)}, u32[]{:S(2)}, u32[]{:S(2)}) collective-permute-start(bf16[4,288,256]{2,1,0:T(8,128)(2,1)S(1)} %pad_maximum_fusion.refs_0_), channel_id=1, source_target_pairs={{0,64},{32,96},{64,0},{96,32},{1,65},{33,97},{65,1},{97,33},{2,66}... | collective-permute-start | bytes 1769480 | tf_op jit(solution)/shard_map/ppermute | solution.py:39
  61.9 26.0 %collective-permute-start.12 = (bf16[4,288,256]{2,1,0:T(8,128)(2,1)S(1)}, bf16[4,288,256]{2,1,0:T(8,128)(2,1)S(1)}, u32[]{:S(2)}, u32[]{:S(2)}) collective-permute-start(bf16[4,288,256]{2,1,0:T(8,128)(2,1)S(1)} %pad_maximum_fusion.refs_0_), channel_id=1, source_target_pairs={{0,96},{32,0},{64,32},{96,64},{1,97},{33,1},{65,33},{97,65},{2,98}... | collective-permute-start | bytes 1769480 | tf_op jit(solution)/shard_map/ppermute | solution.py:39
  65.2 24.8 %collective-permute-start.8 = (bf16[4,288,256]{2,1,0:T(8,128)(2,1)S(1)}, bf16[4,288,256]{2,1,0:T(8,128)(2,1)S(1)}, u32[]{:S(2)}, u32[]{:S(2)}) collective-permute-start(bf16[4,288,256]{2,1,0:T(8,128)(2,1)S(1)} %pad_maximum_fusion.refs_0_), channel_id=1, source_target_pairs={{0,32},{32,64},{64,96},{96,0},{1,33},{33,65},{65,97},{97,1},{2,34}... | collective-permute-start | bytes 1769480 | tf_op jit(solution)/shard_map/ppermute | solution.py:39
  66.8 24.3 %collective-permute-start.7 = (bf16[4,288,256]{2,1,0:T(8,128)(2,1)S(1)}, bf16[4,288,256]{2,1,0:T(8,128)(2,1)S(1)}, u32[]{:S(2)}, u32[]{:S(2)}) collective-permute-start(bf16[4,288,256]{2,1,0:T(8,128)(2,1)S(1)} %pad_maximum_fusion.refs_0_), channel_id=1, source_target_pairs={{0,4},{4,0},{1,5},{5,1},{2,6},{6,2},{3,7},{7,3},{8,12},{12,8},{9,1... | collective-permute-start | bytes 1769480 | tf_op jit(solution)/shard_map/ppermute | solution.py:154
  70.8 20.3 %copy-start.1 = (bf16[4,224,256]{2,1,0:T(8,128)(2,1)S(1)}, bf16[4,224,256]{2,1,0:T(8,128)(2,1)}, u32[]{:S(2)}) copy-start(bf16[4,224,256]{2,1,0:T(8,128)(2,1)} %copy-done) | copy-start | bytes 1376260
  70.8 20.4 %copy-start.3 = (bf16[4,224,256]{2,1,0:T(8,128)(2,1)S(1)}, bf16[4,224,256]{2,1,0:T(8,128)(2,1)}, u32[]{:S(2)}) copy-start(bf16[4,224,256]{2,1,0:T(8,128)(2,1)} %copy-done.2) | copy-start | bytes 1376260
  70.8 20.4 %collective-permute-start.22 = (bf16[4,224,256]{2,1,0:T(8,128)(2,1)}, bf16[4,224,256]{2,1,0:T(8,128)(2,1)S(1)}, u32[]{:S(2)}, u32[]{:S(2)}) collective-permute-start(bf16[4,224,256]{2,1,0:T(8,128)(2,1)} %collective-permute-done.21.refs_5_), channel_id=1, source_target_pairs={{0,4},{4,0},{1,5},{5,1},{2,6},{6,2},{3,7},{7,3},{8,12},{12,8},{9,1... | collective-permute-start | bytes 1376264 | tf_op jit(solution)/shard_map/ppermute | solution.py:155
  76.5 20.8 %collective-permute-start.11 = (bf16[4,288,256]{2,1,0:T(8,128)(2,1)S(1)}, bf16[4,288,256]{2,1,0:T(8,128)(2,1)S(1)}, u32[]{:S(2)}, u32[]{:S(2)}) collective-permute-start(bf16[4,288,256]{2,1,0:T(8,128)(2,1)S(1)} %collective-permute-done.10.refs_2_), channel_id=1, source_target_pairs={{0,4},{4,0},{1,5},{5,1},{2,6},{6,2},{3,7},{7,3},{8,12},{12,8},{9,1... | collective-permute-start | bytes 1769480 | tf_op jit(solution)/shard_map/ppermute | solution.py:154
  87.9 9.4 %collective-permute-start.13 = (bf16[4,288,256]{2,1,0:T(8,128)(2,1)S(1)}, bf16[4,288,256]{2,1,0:T(8,128)(2,1)S(1)}, u32[]{:S(2)}, u32[]{:S(2)}) collective-permute-start(bf16[4,288,256]{2,1,0:T(8,128)(2,1)S(1)} %collective-permute-done.12.refs_3_), channel_id=1, source_target_pairs={{0,4},{4,0},{1,5},{5,1},{2,6},{6,2},{3,7},{7,3},{8,12},{12,8},{9,1... | collective-permute-start | bytes 1769480 | tf_op jit(solution)/shard_map/ppermute | solution.py:154
  90.0 7.3 %collective-permute-start.9 = (bf16[4,288,256]{2,1,0:T(8,128)(2,1)S(1)}, bf16[4,288,256]{2,1,0:T(8,128)(2,1)S(1)}, u32[]{:S(2)}, u32[]{:S(2)}) collective-permute-start(bf16[4,288,256]{2,1,0:T(8,128)(2,1)S(1)} %collective-permute-done.8.refs_1_), channel_id=1, source_target_pairs={{0,4},{4,0},{1,5},{5,1},{2,6},{6,2},{3,7},{7,3},{8,12},{12,8},{9,1... | collective-permute-start | bytes 1769480 | tf_op jit(solution)/shard_map/ppermute | solution.py:154
  91.1 6.2 %collective-permute-start.24 = (bf16[4,224,256]{2,1,0:T(8,128)(2,1)S(1)}, bf16[4,224,256]{2,1,0:T(8,128)(2,1)S(1)}, u32[]{:S(2)}, u32[]{:S(2)}) collective-permute-start(bf16[4,224,256]{2,1,0:T(8,128)(2,1)S(1)} %copy-done.1), channel_id=1, source_target_pairs={{0,4},{4,0},{1,5},{5,1},{2,6},{6,2},{3,7},{7,3},{8,12},{12,8},{9,1... | collective-permute-start | bytes 1376264 | tf_op jit(solution)/shard_map/ppermute | solution.py:155
  91.2 6.1 %collective-permute-start.26 = (bf16[4,224,256]{2,1,0:T(8,128)(2,1)S(1)}, bf16[4,224,256]{2,1,0:T(8,128)(2,1)S(1)}, u32[]{:S(2)}, u32[]{:S(2)}) collective-permute-start(bf16[4,224,256]{2,1,0:T(8,128)(2,1)S(1)} %copy-done.3), channel_id=1, source_target_pairs={{0,4},{4,0},{1,5},{5,1},{2,6},{6,2},{3,7},{7,3},{8,12},{12,8},{9,1... | collective-permute-start | bytes 1376264 | tf_op jit(solution)/shard_map/ppermute | solution.py:155
  102.1 15.0 %all-to-all-start.1 = ((f32[128,1,256]{2,1,0:T(1,128)}), f32[128,1,256]{2,1,0:T(1,128)S(1)}, u32[]{:S(2)}, u32[]{:S(2)}) async-start(f32[128,1,256]{2,1,0:T(1,128)} %broadcast_in_dim.9), calls=%async_computation.1 | async-start | bytes 262144 | tf_op jit(solution)/shard_map/all_to_all | solution.py:44
  (6 other events, 52.0 us)

commit v3 on v2

v3 whole, which is shorter than its diff:
```python
import jax
import jax.numpy as jnp
from jax import lax
from jax.experimental import pallas as pl
from jax.experimental.pallas import tpu as pltpu
from jax.sharding import Mesh, PartitionSpec as P


STATES = 8192
TAU = 64
FRAMES = 2048
WIDE = ("x", "z", "c")
ALL = ("x", "z", "c", "y")
BLOCK = 512
WIDTH = 256
COLS = 2048
GROUPS = COLS // WIDTH
FIRST = 256
STACK = WIDTH + 16
LANES = 128


def place(x, y, z, c):
    return ((x * 4 + z) * 2 + c) * 4 + y


def across():
    return [
        (place(x, y, z, c), place(y, x, z, c))
        for x in range(4) for y in range(4) for z in range(4) for c in range(2)
    ]


def along(k):
    return [(i, (i + k) % 4) for i in range(4)]


def ring(v, axis):
    return [v] + [lax.ppermute(v, axis, along(k)) for k in (1, 2, 3)]


def to_all(values):
    sent = jnp.broadcast_to(values[None], (128,) + values.shape)
    return lax.all_to_all(sent, ALL, 0, 0).reshape((32, 4) + values.shape)


VMEM = pl.BlockSpec(memory_space=pltpu.VMEM)
SMEM = pl.BlockSpec(memory_space=pltpu.SMEM)


def f32(*shape):
    return jax.ShapeDtypeStruct(shape, jnp.float32)


def row_parts(sym_ref, ratio_rows, ratio_cols):
    parts = []
    for top in range(0, WIDTH, 64):
        acc = jnp.zeros((64, LANES), jnp.float32)
        for k in range(COLS // LANES):
            g, lo = divmod(k * LANES, WIDTH)
            acc += sym_ref[top:top + 64, k * LANES:(k + 1) * LANES] / (
                ratio_rows[top:top + 64] + ratio_cols[g:g + 1, lo:lo + LANES])
        parts.append(acc)
    return jnp.sum(jnp.concatenate(parts, axis=0).T, axis=0, keepdims=True)


def products(where, left, by_x, by_z, before):
    def kernel(where_ref, left_ref, *refs):
        x_refs, z_refs = refs[:4], refs[4:8]
        x, _, z, c = (where_ref[i] for i in range(4))
        if before is None:
            sym_ref, visit_ref, total_ref = refs[8:]
            core = c
        else:
            sym_ref, visit_ref, total_ref, send_ref = refs[12:]
            core = 1 - c
            sym_ref[...], visit_ref[...], total_ref[...] = (ref[...] for ref in refs[8:11])
        for dz in range(4):
            acc = jnp.zeros((STACK, WIDTH), jnp.float32)
            for dx in range(4):
                lo = pl.multiple_of(lax.rem(x + 4 - dx, 4) * BLOCK, BLOCK)
                block = jnp.concatenate([x_refs[dx][dz], z_refs[dz][dx]], axis=0)
                acc += jnp.dot(left_ref[:, pl.ds(lo, BLOCK)], block,
                               preferred_element_type=jnp.float32)
            g = lax.rem(z + 4 - dz, 4) * 2 + core
            sym_ref[:, pl.ds(pl.multiple_of(g * WIDTH, WIDTH), WIDTH)] = acc[:WIDTH]
            frame = acc[WIDTH:]
            visit_ref[pl.ds(g, 1), :] = jnp.sum(frame[:3], axis=0, keepdims=True)
            total_ref[pl.ds(g, 1), :] = jnp.sum(frame[:6], axis=0, keepdims=True)
        if before is not None:
            send_ref[...] = row_parts(sym_ref, refs[11][...], visit_ref[...] / total_ref[...])

    operands = [where, left] + by_x + by_z
    out = [f32(WIDTH, COLS), f32(GROUPS, WIDTH), f32(GROUPS, WIDTH)]
    if before is not None:
        operands += list(before)
        out += [f32(1, WIDTH)]
    return pl.pallas_call(
        kernel,
        in_specs=[SMEM] + [VMEM] * (len(operands) - 1),
        out_specs=[VMEM] * len(out),
        out_shape=out,
        compiler_params=pltpu.CompilerParams(vmem_limit_bytes=16 << 20),
    )(*[operands[0]] + [pltpu.with_memory_space_constraint(v, pltpu.VMEM) for v in operands[1:]])


def three_parts(v):
    hi = v.astype(jnp.bfloat16).astype(jnp.float32)
    mid = (v - hi).astype(jnp.bfloat16).astype(jnp.float32)
    return [hi, mid, v - hi - mid]


def prepare(where, blocks, frame):
    def kernel(where_ref, *refs):
        frame_ref, left_ref, visit_ref, ratio_ref, rows_ref = refs[4:]
        edge = jnp.zeros((TAU, WIDTH), jnp.bfloat16)
        rows_ref[:TAU, :] = edge
        rows_ref[TAU + FRAMES:, :] = edge
        for k in range(4):
            lo = lax.rem(where_ref[1] + k, 4) * BLOCK + TAU
            rows_ref[pl.ds(pl.multiple_of(lo, TAU), BLOCK), :] = refs[k][...]
        for lo in range(0, FRAMES, 256):
            both = (rows_ref[lo:lo + 256, :].astype(jnp.float32)
                    + rows_ref[lo + 2 * TAU:lo + 2 * TAU + 256, :].astype(jnp.float32))
            left_ref[:WIDTH, lo:lo + 256] = both.T.astype(jnp.bfloat16)
        total = jnp.concatenate([frame_ref[q:q + 1, :] for q in range(4)], axis=1)
        total = jnp.broadcast_to(total, (16, FRAMES))
        at = lax.broadcasted_iota(jnp.int32, (16, FRAMES), 1)
        line = lax.broadcasted_iota(jnp.int32, (16, FRAMES), 0)
        up = jnp.where(at < FRAMES - TAU, pltpu.roll(total, FRAMES - TAU, 1), 0.0)
        down = jnp.where(at >= TAU, pltpu.roll(total, TAU, 1), 0.0)
        weight = jnp.zeros((16, FRAMES), jnp.float32)
        for i, v in enumerate(three_parts(up) + three_parts(down)):
            weight = jnp.where(line == i, v, weight)
        left_ref[WIDTH:, :] = weight.astype(jnp.bfloat16)
        weight = jnp.zeros((16, FRAMES), jnp.float32)
        for i, v in enumerate(three_parts(total)):
            weight = jnp.where(line == i, v, weight)
        weight = weight.astype(jnp.bfloat16)
        visit = jnp.sum(jnp.dot(weight, rows_ref[:FRAMES, :], preferred_element_type=jnp.float32),
                        axis=0, keepdims=True)
        back = jnp.sum(jnp.dot(weight, rows_ref[2 * TAU:, :], preferred_element_type=jnp.float32),
                       axis=0, keepdims=True)
        visit_ref[...] = visit
        ratio_ref[...] = jnp.broadcast_to(visit / (visit + back), (LANES, WIDTH)).T

    return pl.pallas_call(
        kernel,
        in_specs=[SMEM] + [VMEM] * 5,
        out_specs=[VMEM] * 3,
        out_shape=[jax.ShapeDtypeStruct((STACK, FRAMES), jnp.bfloat16), f32(1, WIDTH), f32(WIDTH, LANES)],
        scratch_shapes=[pltpu.VMEM((FRAMES + 2 * TAU, WIDTH), jnp.bfloat16)],
        compiler_params=pltpu.CompilerParams(vmem_limit_bytes=16 << 20),
    )(where, *[pltpu.with_memory_space_constraint(v, pltpu.VMEM) for v in blocks + [frame]])


def shards(member):
    where = jnp.stack([lax.axis_index(a) for a in ("x", "y", "z", "c")])
    x, y, z, c = (where[i] for i in range(4))
    moved = lax.ppermute(member, ALL, across())
    got = to_all(jnp.sum(member, axis=1, dtype=jnp.float32))
    once_x = jnp.stack(ring(moved[:FIRST], "z"))
    once_z = jnp.stack(ring(moved[FIRST:], "x"))
    got, _ = lax.optimization_barrier((got, (once_x, once_z)))
    by_x = ring(once_x, "x")
    by_z = ring(once_z, "z")
    blocks = [member] + [lax.ppermute(member, "y", along(-k)) for k in (1, 2, 3)]
    other_x = [lax.ppermute(v, "c", [(0, 1), (1, 0)]) for v in by_x]
    other_z = [lax.ppermute(v, "c", [(0, 1), (1, 0)]) for v in by_z]
    left, visit_rows, ratio_rows = prepare(where, blocks, jnp.sum(got, axis=0))
    own = products(where, left, by_x, by_z, None)
    sym, visit_cols, _, part = products(where, left, other_x, other_z, list(own) + [ratio_rows])
    w = (x * 4 + z) * 2 + c
    for step in range(3):
        totals = jnp.sum(to_all(part.reshape(WIDTH)), axis=1)
        total_rows = lax.dynamic_slice_in_dim(totals, w, 1).reshape(WIDTH)
        total_cols = lax.dynamic_slice_in_dim(totals, y * GROUPS, GROUPS)
        if step == 2:
            break
        ratio_rows = visit_rows.reshape(WIDTH) / total_rows
        ratio = ratio_rows[:, None] + (visit_cols / total_cols).reshape(COLS)[None, :]
        part = jnp.sum(sym / ratio, axis=1)
    transition = sym * (STATES / total_rows)[:, None] / ratio
    stationary = STATES * total_rows / jnp.sum(totals)
    return (transition, stationary)


def solution(mesh):
    mesh = Mesh(mesh.devices.reshape(4, 4, 2, 4), ALL)
    return jax.shard_map(
        shards,
        mesh=mesh,
        in_specs=(P("y", WIDE),),
        out_specs=(P(WIDE, "y"), P(WIDE)),
        check_vma=False,
    )
```

time: 152 us -> 166 us (1.092)
  waiting for transfers between devices: 27.9 us -> 42.5 us
  starting transfers between devices: 70.4 us -> 68.4 us
    ppermute x12, starting transfers between devices: 21.2 us -> 45.7 us  [ring(): return [v] + [lax.ppermute(v, axis, along(k)) for k in (1, 2, 3)]]
    all_to_all x2, waiting for transfers between devices: 10.1 us -> 21 us  [to_all(): return lax.all_to_all(sent, ALL, 0, 0).reshape((32, 4) + values.shape)]
    ppermute x7 -> x4, starting transfers between devices: 13.6 us -> 3.53 us  [the longest x3 1.79 us: shards(): lax.ppermute(member, 'y', along(-k))]
    ppermute x4, starting transfers between devices: 8.06 us -> 0.7 us  [shards(): other_x = [lax.ppermute(v, 'c', [(0, 1), (1, 0)]) for v in by_x]]
    all_to_all x2, starting transfers between devices: 15.8 us -> 8.74 us  [to_all(): return lax.all_to_all(sent, ALL, 0, 0).reshape((32, 4) + values.shape)]
    ppermute x7 -> x4, waiting for transfers between devices: 0.54 us -> 6.73 us  [the longest x3 6.73 us: shards(): lax.ppermute(member, 'y', along(-k))]
    unnamed x23 -> x16, local copies, waits for them, and re-layouts: 1.16 us -> 4.55 us
    ppermute x12, waiting for transfers between devices: 17.3 us -> 14.8 us  [ring(): return [v] + [lax.ppermute(v, axis, along(k)) for k in (1, 2, 3)]]
  transfers between devices with their start and end apart: 29 -> 26, of which waited for: 8 -> 6; matrix products, arithmetic and copies ran while one was open for 5% -> 4% of each run, Pallas kernels for 3% -> 3%
where the time goes in v3:
time: 166 us; the launch traced here: 165 us
  starting transfers between devices  68.4 us (41%)
  waiting for transfers between devices  42.5 us (26%)
  blocking collectives  27.9 us (17%)
  other arithmetic  9.57 us (6%)
  local copies, waits for them, and re-layouts  8.11 us (5%)
  Pallas kernels  7.9 us (5%)
    ppermute x12, starting transfers between devices, ring(): return [v] + [lax.ppermute(v, axis, along(k)) for k in (1, 2, 3)]  45.7 us
    all_to_all x2, blocking collectives, to_all(): return lax.all_to_all(sent, ALL, 0, 0).reshape((32, 4) + values.shape)  27.9 us
    all_to_all x2, waiting for transfers between devices, to_all(): return lax.all_to_all(sent, ALL, 0, 0).reshape((32, 4) + values.shape)  21 us
    ppermute x12, waiting for transfers between devices, ring(): return [v] + [lax.ppermute(v, axis, along(k)) for k in (1, 2, 3)]  14.8 us
    ppermute x4, starting transfers between devices, shards(): other_z = [lax.ppermute(v, 'c', [(0, 1), (1, 0)]) for v in by_z]  9.72 us
    all_to_all x2, starting transfers between devices, to_all(): return lax.all_to_all(sent, ALL, 0, 0).reshape((32, 4) + values.shape)  8.74 us
    pallas_call x2, Pallas kernels, products(): pl.pallas_call(kernel, in_specs=[SMEM] + [VMEM] * (len(operands) - 1), ou...  6.76 us
    ppermute x3, waiting for transfers between devices, shards(): lax.ppermute(member, 'y', along(-k))  6.73 us
  transfers between devices with their start and end apart: 26, of which 6 were waited for; matrix products, arithmetic and copies ran while one was open for 4% of the time, Pallas kernels for 3%

profile of v3, /device:TPU:1, one launch (start us, length us, event | category | flops | bytes accessed | tf_op | source)
XLA Modules:
  0.0 165.5 jit_solution(5247738786146619543)
XLA Ops:
  0.6 1.7 %collective-permute-start.3 = (bf16[512,256]{1,0:T(8,128)(2,1)}, bf16[512,256]{1,0:T(8,128)(2,1)S(1)}, u32[]{:S(2)}, u32[]{:S(2)}) collective-permute-start(bf16[512,256]{1,0:T(8,128)(2,1)} %refs_0_.1), channel_id=1, source_target_pairs={{0,0},{4,4},{8,8},{12,12},{16,16},{20,20},{24,24},{28,28},{1,32},{... | collective-permute-start | bytes 786440 | tf_op jit(solution)/shard_map/ppermute | solution.py:160
  2.4 18.8 %collective-permute-start.8 = (bf16[256,256]{1,0:T(8,128)(2,1)S(1)}, bf16[256,256]{1,0:T(8,128)(2,1)S(1)}, u32[]{:S(2)}, u32[]{:S(2)}) collective-permute-start(bf16[256,256]{1,0:T(8,128)(2,1)S(1)} %get-tuple-element.26), channel_id=1, source_target_pairs={{0,64},{32,96},{64,0},{96,32},{1,65},{33,97},{65,1},{97,33},{2,66}... | collective-permute-start | bytes 393224 | tf_op jit(solution)/shard_map/ppermute | solution.py:39
  21.3 1.2 collective-permute-start.9
  23.0 1.8 %collective-permute-start = (bf16[512,256]{1,0:T(8,128)(2,1)}, bf16[512,256]{1,0:T(8,128)(2,1)S(1)}, u32[]{:S(2)}, u32[]{:S(2)}) collective-permute-start(bf16[512,256]{1,0:T(8,128)(2,1)} %refs_0_.1), channel_id=1, source_target_pairs={{0,3},{1,0},{2,1},{3,2},{4,7},{5,4},{6,5},{7,6},{8,11},{9,8},{10,9... | collective-permute-start | bytes 786440 | tf_op jit(solution)/shard_map/ppermute | solution.py:167
  24.8 1.6 collective-permute-start.4
  26.4 3.3 %collective-permute-start.5 = (bf16[256,256]{1,0:T(8,128)(2,1)S(1)}, bf16[256,256]{1,0:T(8,128)(2,1)S(1)}, u32[]{:S(2)}, u32[]{:S(2)}) collective-permute-start(bf16[256,256]{1,0:T(8,128)(2,1)S(1)} %get-tuple-element.27), channel_id=1, source_target_pairs={{0,16},{8,24},{16,0},{24,8},{1,17},{9,25},{17,1},{25,9},{2,18},{10... | collective-permute-start | bytes 393224 | tf_op jit(solution)/shard_map/ppermute | solution.py:39
  29.7 1.9 %collective-permute-start.6 = (bf16[256,256]{1,0:T(8,128)(2,1)S(1)}, bf16[256,256]{1,0:T(8,128)(2,1)S(1)}, u32[]{:S(2)}, u32[]{:S(2)}) collective-permute-start(bf16[256,256]{1,0:T(8,128)(2,1)S(1)} %get-tuple-element.27), channel_id=1, source_target_pairs={{0,24},{8,0},{16,8},{24,16},{1,25},{9,1},{17,9},{25,17},{2,26},{10... | collective-permute-start | bytes 393224 | tf_op jit(solution)/shard_map/ppermute | solution.py:39
  31.8 1.8 %collective-permute-done.5 = bf16[256,256]{1,0:T(8,128)(2,1)S(1)} collective-permute-done((bf16[256,256]{1,0:T(8,128)(2,1)S(1)}, bf16[256,256]{1,0:T(8,128)(2,1)S(1)}, u32[]{:S(2)}, u32[]{:S(2)}) %collective-permute-start.5) | collective-permute-done | bytes 131104 | tf_op jit(solution)/shard_map/ppermute | solution.py:39
  33.6 2.5 %collective-permute-start.20 = (bf16[4,256,256]{2,1,0:T(8,128)(2,1)S(1)}, bf16[4,256,256]{2,1,0:T(8,128)(2,1)}, u32[]{:S(2)}, u32[]{:S(2)}) collective-permute-start(bf16[4,256,256]{2,1,0:T(8,128)(2,1)S(1)} %pad_maximum_fusion.1.refs_4_), channel_id=1, source_target_pairs={{0,16},{8,24},{16,0},{24,8},{1,17},{9,25},{17,1},{25,9},{2,18},{10... | collective-permute-start | bytes 1572872 | tf_op jit(solution)/shard_map/ppermute | solution.py:39
  36.1 2.0 %collective-permute-start.22 = (bf16[4,256,256]{2,1,0:T(8,128)(2,1)S(1)}, bf16[4,256,256]{2,1,0:T(8,128)(2,1)}, u32[]{:S(2)}, u32[]{:S(2)}) collective-permute-start(bf16[4,256,256]{2,1,0:T(8,128)(2,1)S(1)} %pad_maximum_fusion.1.refs_4_), channel_id=1, source_target_pairs={{0,24},{8,0},{16,8},{24,16},{1,25},{9,1},{17,9},{25,17},{2,26},{10... | collective-permute-start | bytes 1572872 | tf_op jit(solution)/shard_map/ppermute | solution.py:39
  38.2 1.4 collective-permute-start.11
  39.6 6.7 %collective-permute-done.2.refs_3_ = bf16[512,256]{1,0:T(8,128)(2,1)S(1)} collective-permute-done((bf16[512,256]{1,0:T(8,128)(2,1)S(1)}, bf16[512,256]{1,0:T(8,128)(2,1)S(1)}, u32[]{:S(2)}, u32[]{:S(2)}) %collective-permute-start.2) | collective-permute-done | bytes 262176 | tf_op jit(solution)/shard_map/ppermute | solution.py:167
  47.0 12.4 %collective-permute-start.13 = (bf16[4,256,256]{2,1,0:T(8,128)(2,1)S(1)}, bf16[4,256,256]{2,1,0:T(8,128)(2,1)}, u32[]{:S(2)}, u32[]{:S(2)}) collective-permute-start(bf16[4,256,256]{2,1,0:T(8,128)(2,1)S(1)} %pad_maximum_fusion.refs_0_), channel_id=1, source_target_pairs={{0,64},{32,96},{64,0},{96,32},{1,65},{33,97},{65,1},{97,33},{2,66}... | collective-permute-start | bytes 1572872 | tf_op jit(solution)/shard_map/ppermute | solution.py:39
  59.4 3.3 %collective-permute-start.17 = (bf16[4,256,256]{2,1,0:T(8,128)(2,1)S(1)}, bf16[4,256,256]{2,1,0:T(8,128)(2,1)S(1)}, u32[]{:S(2)}, u32[]{:S(2)}) collective-permute-start(bf16[4,256,256]{2,1,0:T(8,128)(2,1)S(1)} %pad_maximum_fusion.1.refs_4_), channel_id=1, source_target_pairs={{0,4},{4,0},{1,5},{5,1},{2,6},{6,2},{3,7},{7,3},{8,12},{12,8},{9,1... | collective-permute-start | bytes 1572872 | tf_op jit(solution)/shard_map/ppermute | solution.py:169
  62.8 1.9 %collective-permute-start.19 = (bf16[4,256,256]{2,1,0:T(8,128)(2,1)S(1)}, bf16[4,256,256]{2,1,0:T(8,128)(2,1)S(1)}, u32[]{:S(2)}, u32[]{:S(2)}) collective-permute-start(bf16[4,256,256]{2,1,0:T(8,128)(2,1)S(1)} %collective-permute-done.18.refs_5_), channel_id=1, source_target_pairs={{0,4},{4,0},{1,5},{5,1},{2,6},{6,2},{3,7},{7,3},{8,12},{12,8},{9,1... | collective-permute-start | bytes 1572872 | tf_op jit(solution)/shard_map/ppermute | solution.py:169
  65.5 7.6 %collective-permute-done.13.refs_2_ = bf16[4,256,256]{2,1,0:T(8,128)(2,1)} collective-permute-done((bf16[4,256,256]{2,1,0:T(8,128)(2,1)S(1)}, bf16[4,256,256]{2,1,0:T(8,128)(2,1)}, u32[]{:S(2)}, u32[]{:S(2)}) %collective-permute-start.13) | collective-permute-done | bytes 524320 | tf_op jit(solution)/shard_map/ppermute | solution.py:39
  73.1 2.8 %collective-permute-start.21 = (bf16[4,256,256]{2,1,0:T(8,128)(2,1)}, bf16[4,256,256]{2,1,0:T(8,128)(2,1)}, u32[]{:S(2)}, u32[]{:S(2)}) collective-permute-start(bf16[4,256,256]{2,1,0:T(8,128)(2,1)} %collective-permute-done.20.refs_6_), channel_id=1, source_target_pairs={{0,4},{4,0},{1,5},{5,1},{2,6},{6,2},{3,7},{7,3},{8,12},{12,8},{9,1... | collective-permute-start | bytes 1572872 | tf_op jit(solution)/shard_map/ppermute | solution.py:169
  75.9 5.4 %collective-permute-done.15.refs_3_ = bf16[4,256,256]{2,1,0:T(8,128)(2,1)} collective-permute-done((bf16[4,256,256]{2,1,0:T(8,128)(2,1)S(1)}, bf16[4,256,256]{2,1,0:T(8,128)(2,1)}, u32[]{:S(2)}, u32[]{:S(2)}) %collective-permute-start.15) | collective-permute-done | bytes 524320 | tf_op jit(solution)/shard_map/ppermute | solution.py:39
  81.3 1.7 %collective-permute-start.23 = (bf16[4,256,256]{2,1,0:T(8,128)(2,1)}, bf16[4,256,256]{2,1,0:T(8,128)(2,1)}, u32[]{:S(2)}, u32[]{:S(2)}) collective-permute-start(bf16[4,256,256]{2,1,0:T(8,128)(2,1)} %collective-permute-done.22.refs_7_), channel_id=1, source_target_pairs={{0,4},{4,0},{1,5},{5,1},{2,6},{6,2},{3,7},{7,3},{8,12},{12,8},{9,1... | collective-permute-start | bytes 1572872 | tf_op jit(solution)/shard_map/ppermute | solution.py:169
  84.6 4.9 %all-to-all-start = ((f32[128,1,512]{2,1,0:T(1,128)}), f32[128,1,512]{2,1,0:T(1,128)}, u32[]{:S(2)}, u32[]{:S(2)}) async-start(f32[128,1,512]{2,1,0:T(1,128)} %broadcast_in_dim.8), calls=%async_computation | async-start | bytes 524288 | tf_op jit(solution)/shard_map/all_to_all | solution.py:44
  89.5 11.0 %all-to-all-done = f32[128,1,512]{2,1,0:T(1,128)} async-done(((f32[128,1,512]{2,1,0:T(1,128)}), f32[128,1,512]{2,1,0:T(1,128)}, u32[]{:S(2)}, u32[]{:S(2)}) %all-to-all-start) | async-done | bytes 262176 | tf_op jit(solution)/shard_map/all_to_all | solution.py:44
  100.5 2.3 %reduce.3 = f32[128,512]{1,0:T(8,128)} reduce(f32[128,1,512]{2,1,0:T(1,128)} %all-to-all-done, f32[]{:T(128)} %constant.30), dimensions={1}, to_apply=%all_to_all.16.reduce_sub_computation | reduce | bytes 524292 | tf_op jit(solution)/shard_map/all_to_all | solution.py:44
  102.8 1.7 %reshape.82 = f32[32,4,512]{2,1,0:T(4,128)} reshape(f32[128,512]{1,0:T(8,128)} %reduce.3) | data formatting | bytes 524288 | tf_op jit(solution)/shard_map/reshape | solution.py:44
  106.5 1.1 shard_map.30
  108.7 3.0 %shard_map.31 = (f32[256,2048]{1,0:T(8,128)S(1)}, f32[8,256]{1,0:T(8,128)S(1)}, f32[8,256]{1,0:T(8,128)S(1)}) custom-call(s32[4]{0:T(128)S(1)} %pad_add_fusion.where_ref, bf16[272,2048]{1,0:T(8,128)(2,1)S(1)} %get-tuple-element.13.left_ref, bf16[4,256,256]{2,1,0:T(8,128)(2,1)S(1)} %pad_maximum_fusion.refs_0_, ...), custom_call_target="tpu_custom_call" | custom-call | tf_op jit(solution)/shard_map/pallas_call | solution.py:98
  112.8 3.7 %shard_map.32 = (f32[256,2048]{1,0:T(8,128)S(1)}, f32[8,256]{1,0:T(8,128)S(1)}, f32[8,256]{1,0:T(8,128)}, f32[1,256]{1,0:T(1,128)S(1)}) custom-call(s32[4]{0:T(128)S(1)} %pad_add_fusion.where_ref, bf16[272,2048]{1,0:T(8,128)(2,1)S(1)} %get-tuple-element.13.left_ref, bf16[4,256,256]{2,1,0:T(8,128)(2,1)S(1)} %collective-permute-done.10.refs_0_, ...), custom_call_target="tpu_custom_call" | custom-call | tf_op jit(solution)/shard_map/pallas_call | solution.py:98
  117.2 3.9 %all-to-all-start.1 = ((f32[128,1,256]{2,1,0:T(1,128)}), f32[128,1,256]{2,1,0:T(1,128)S(1)}, u32[]{:S(2)}, u32[]{:S(2)}) async-start(f32[128,1,256]{2,1,0:T(1,128)} %broadcast_in_dim.9), calls=%async_computation.1 | async-start | bytes 262144 | tf_op jit(solution)/shard_map/all_to_all | solution.py:44
  121.1 10.1 %all-to-all-done.1 = f32[128,1,256]{2,1,0:T(1,128)S(1)} async-done(((f32[128,1,256]{2,1,0:T(1,128)}), f32[128,1,256]{2,1,0:T(1,128)S(1)}, u32[]{:S(2)}, u32[]{:S(2)}) %all-to-all-start.1) | async-done | bytes 131104 | tf_op jit(solution)/shard_map/all_to_all | solution.py:44
  132.2 14.0 %all_to_all.24 = f32[128,1,256]{2,1,0:T(1,128)S(1)} all-to-all(f32[128,1,256]{2,1,0:T(1,128)S(1)} %broadcast_in_dim.10), channel_id=1, replica_groups=mesh['x'=4,'z'=4,'c'=2,'y'=4] {'x','z','c','y'}, dimensions={0} | all-to-all | bytes 262144 | tf_op jit(solution)/shard_map/all_to_all | solution.py:44
  147.2 13.9 %all_to_all.25 = f32[128,1,256]{2,1,0:T(1,128)S(1)} all-to-all(f32[128,1,256]{2,1,0:T(1,128)S(1)} %broadcast_in_dim.11), channel_id=1, replica_groups=mesh['x'=4,'z'=4,'c'=2,'y'=4] {'x','z','c','y'}, dimensions={0} | all-to-all | bytes 262144 | tf_op jit(solution)/shard_map/all_to_all | solution.py:44
  162.4 1.2 multiply_divide_fusion
  163.6 1.9 %add_divide_fusion = f32[256,2048]{1,0:T(8,128)} fusion(f32[256,2048]{1,0:T(8,128)S(1)} %get-tuple-element.18, f32[256]{0:T(256)S(1)} %bitcast.38, f32[2048]{0:T(1024)S(1)} %bitcast.33, f32[256]{0:T(256)S(1)} %bitcast.36), kind=kLoop, calls=%fused_computation | loop fusion | flops 1572864 | bytes 4204544 | tf_op jit(solution)/shard_map/div | solution.py:183
  (70 shorter events, 12.0 us)
Async XLA Ops:
  0.6 38.9 %copy-start = (bf16[512,256]{1,0:T(8,128)(2,1)S(1)}, bf16[512,256]{1,0:T(8,128)(2,1)}, u32[]{:S(2)}) copy-start(bf16[512,256]{1,0:T(8,128)(2,1)} %refs_0_.1) | copy-start | bytes 786436
  0.6 1.7 %collective-permute-start.3 = (bf16[512,256]{1,0:T(8,128)(2,1)}, bf16[512,256]{1,0:T(8,128)(2,1)S(1)}, u32[]{:S(2)}, u32[]{:S(2)}) collective-permute-start(bf16[512,256]{1,0:T(8,128)(2,1)} %refs_0_.1), channel_id=1, source_target_pairs={{0,0},{4,4},{8,8},{12,12},{16,16},{20,20},{24,24},{28,28},{1,32},{... | collective-permute-start | bytes 786440 | tf_op jit(solution)/shard_map/ppermute | solution.py:160
  2.4 24.0 %collective-permute-start.8 = (bf16[256,256]{1,0:T(8,128)(2,1)S(1)}, bf16[256,256]{1,0:T(8,128)(2,1)S(1)}, u32[]{:S(2)}, u32[]{:S(2)}) collective-permute-start(bf16[256,256]{1,0:T(8,128)(2,1)S(1)} %get-tuple-element.26), channel_id=1, source_target_pairs={{0,64},{32,96},{64,0},{96,32},{1,65},{33,97},{65,1},{97,33},{2,66}... | collective-permute-start | bytes 393224 | tf_op jit(solution)/shard_map/ppermute | solution.py:39
  21.3 8.5 %collective-permute-start.9 = (bf16[256,256]{1,0:T(8,128)(2,1)S(1)}, bf16[256,256]{1,0:T(8,128)(2,1)S(1)}, u32[]{:S(2)}, u32[]{:S(2)}) collective-permute-start(bf16[256,256]{1,0:T(8,128)(2,1)S(1)} %get-tuple-element.26), channel_id=1, source_target_pairs={{0,96},{32,0},{64,32},{96,64},{1,97},{33,1},{65,33},{97,65},{2,98}... | collective-permute-start | bytes 393224 | tf_op jit(solution)/shard_map/ppermute | solution.py:39
  22.5 9.2 %collective-permute-start.7 = (bf16[256,256]{1,0:T(8,128)(2,1)S(1)}, bf16[256,256]{1,0:T(8,128)(2,1)S(1)}, u32[]{:S(2)}, u32[]{:S(2)}) collective-permute-start(bf16[256,256]{1,0:T(8,128)(2,1)S(1)} %get-tuple-element.26), channel_id=1, source_target_pairs={{0,32},{32,64},{64,96},{96,0},{1,33},{33,65},{65,97},{97,1},{2,34}... | collective-permute-start | bytes 393224 | tf_op jit(solution)/shard_map/ppermute | solution.py:39
  23.0 15.2 %collective-permute-start = (bf16[512,256]{1,0:T(8,128)(2,1)}, bf16[512,256]{1,0:T(8,128)(2,1)S(1)}, u32[]{:S(2)}, u32[]{:S(2)}) collective-permute-start(bf16[512,256]{1,0:T(8,128)(2,1)} %refs_0_.1), channel_id=1, source_target_pairs={{0,3},{1,0},{2,1},{3,2},{4,7},{5,4},{6,5},{7,6},{8,11},{9,8},{10,9... | collective-permute-start | bytes 786440 | tf_op jit(solution)/shard_map/ppermute | solution.py:167
  24.8 7.0 %collective-permute-start.4 = (bf16[256,256]{1,0:T(8,128)(2,1)S(1)}, bf16[256,256]{1,0:T(8,128)(2,1)S(1)}, u32[]{:S(2)}, u32[]{:S(2)}) collective-permute-start(bf16[256,256]{1,0:T(8,128)(2,1)S(1)} %get-tuple-element.27), channel_id=1, source_target_pairs={{0,8},{8,16},{16,24},{24,0},{1,9},{9,17},{17,25},{25,1},{2,10},{10... | collective-permute-start | bytes 393224 | tf_op jit(solution)/shard_map/ppermute | solution.py:39
  26.4 7.2 %collective-permute-start.5 = (bf16[256,256]{1,0:T(8,128)(2,1)S(1)}, bf16[256,256]{1,0:T(8,128)(2,1)S(1)}, u32[]{:S(2)}, u32[]{:S(2)}) collective-permute-start(bf16[256,256]{1,0:T(8,128)(2,1)S(1)} %get-tuple-element.27), channel_id=1, source_target_pairs={{0,16},{8,24},{16,0},{24,8},{1,17},{9,25},{17,1},{25,9},{2,18},{10... | collective-permute-start | bytes 393224 | tf_op jit(solution)/shard_map/ppermute | solution.py:39
  29.7 6.3 %collective-permute-start.6 = (bf16[256,256]{1,0:T(8,128)(2,1)S(1)}, bf16[256,256]{1,0:T(8,128)(2,1)S(1)}, u32[]{:S(2)}, u32[]{:S(2)}) collective-permute-start(bf16[256,256]{1,0:T(8,128)(2,1)S(1)} %get-tuple-element.27), channel_id=1, source_target_pairs={{0,24},{8,0},{16,8},{24,16},{1,25},{9,1},{17,9},{25,17},{2,26},{10... | collective-permute-start | bytes 393224 | tf_op jit(solution)/shard_map/ppermute | solution.py:39
  31.7 7.9 %collective-permute-start.1 = (bf16[512,256]{1,0:T(8,128)(2,1)}, bf16[512,256]{1,0:T(8,128)(2,1)S(1)}, u32[]{:S(2)}, u32[]{:S(2)}) collective-permute-start(bf16[512,256]{1,0:T(8,128)(2,1)} %refs_0_.1), channel_id=1, source_target_pairs={{0,2},{1,3},{2,0},{3,1},{4,6},{5,7},{6,4},{7,5},{8,10},{9,11},{10,... | collective-permute-start | bytes 786440 | tf_op jit(solution)/shard_map/ppermute | solution.py:167
  31.7 27.6 %collective-permute-start.18 = (bf16[4,256,256]{2,1,0:T(8,128)(2,1)S(1)}, bf16[4,256,256]{2,1,0:T(8,128)(2,1)S(1)}, u32[]{:S(2)}, u32[]{:S(2)}) collective-permute-start(bf16[4,256,256]{2,1,0:T(8,128)(2,1)S(1)} %pad_maximum_fusion.1.refs_4_), channel_id=1, source_target_pairs={{0,8},{8,16},{16,24},{24,0},{1,9},{9,17},{17,25},{25,1},{2,10},{10... | collective-permute-start | bytes 1572872 | tf_op jit(solution)/shard_map/ppermute | solution.py:39
  33.6 25.8 %collective-permute-start.20 = (bf16[4,256,256]{2,1,0:T(8,128)(2,1)S(1)}, bf16[4,256,256]{2,1,0:T(8,128)(2,1)}, u32[]{:S(2)}, u32[]{:S(2)}) collective-permute-start(bf16[4,256,256]{2,1,0:T(8,128)(2,1)S(1)} %pad_maximum_fusion.1.refs_4_), channel_id=1, source_target_pairs={{0,16},{8,24},{16,0},{24,8},{1,17},{9,25},{17,1},{25,9},{2,18},{10... | collective-permute-start | bytes 1572872 | tf_op jit(solution)/shard_map/ppermute | solution.py:39
  36.1 26.6 %collective-permute-start.22 = (bf16[4,256,256]{2,1,0:T(8,128)(2,1)S(1)}, bf16[4,256,256]{2,1,0:T(8,128)(2,1)}, u32[]{:S(2)}, u32[]{:S(2)}) collective-permute-start(bf16[4,256,256]{2,1,0:T(8,128)(2,1)S(1)} %pad_maximum_fusion.1.refs_4_), channel_id=1, source_target_pairs={{0,24},{8,0},{16,8},{24,16},{1,25},{9,1},{17,9},{25,17},{2,26},{10... | collective-permute-start | bytes 1572872 | tf_op jit(solution)/shard_map/ppermute | solution.py:39
  38.2 24.6 %collective-permute-start.11 = (bf16[4,256,256]{2,1,0:T(8,128)(2,1)S(1)}, bf16[4,256,256]{2,1,0:T(8,128)(2,1)}, u32[]{:S(2)}, u32[]{:S(2)}) collective-permute-start(bf16[4,256,256]{2,1,0:T(8,128)(2,1)S(1)} %pad_maximum_fusion.refs_0_), channel_id=1, source_target_pairs={{0,32},{32,64},{64,96},{96,0},{1,33},{33,65},{65,97},{97,1},{2,34}... | collective-permute-start | bytes 1572872 | tf_op jit(solution)/shard_map/ppermute | solution.py:39
  39.6 6.7 %collective-permute-start.2 = (bf16[512,256]{1,0:T(8,128)(2,1)S(1)}, bf16[512,256]{1,0:T(8,128)(2,1)S(1)}, u32[]{:S(2)}, u32[]{:S(2)}) collective-permute-start(bf16[512,256]{1,0:T(8,128)(2,1)S(1)} %copy-done), channel_id=1, source_target_pairs={{0,1},{1,2},{2,3},{3,0},{4,5},{5,6},{6,7},{7,4},{8,9},{9,10},{10,1... | collective-permute-start | bytes 786440 | tf_op jit(solution)/shard_map/ppermute | solution.py:167
  47.0 26.1 %collective-permute-start.13 = (bf16[4,256,256]{2,1,0:T(8,128)(2,1)S(1)}, bf16[4,256,256]{2,1,0:T(8,128)(2,1)}, u32[]{:S(2)}, u32[]{:S(2)}) collective-permute-start(bf16[4,256,256]{2,1,0:T(8,128)(2,1)S(1)} %pad_maximum_fusion.refs_0_), channel_id=1, source_target_pairs={{0,64},{32,96},{64,0},{96,32},{1,65},{33,97},{65,1},{97,33},{2,66}... | collective-permute-start | bytes 1572872 | tf_op jit(solution)/shard_map/ppermute | solution.py:39
  59.3 22.0 %collective-permute-start.15 = (bf16[4,256,256]{2,1,0:T(8,128)(2,1)S(1)}, bf16[4,256,256]{2,1,0:T(8,128)(2,1)}, u32[]{:S(2)}, u32[]{:S(2)}) collective-permute-start(bf16[4,256,256]{2,1,0:T(8,128)(2,1)S(1)} %pad_maximum_fusion.refs_0_), channel_id=1, source_target_pairs={{0,96},{32,0},{64,32},{96,64},{1,97},{33,1},{65,33},{97,65},{2,98}... | collective-permute-start | bytes 1572872 | tf_op jit(solution)/shard_map/ppermute | solution.py:39
  59.4 23.6 %collective-permute-start.17 = (bf16[4,256,256]{2,1,0:T(8,128)(2,1)S(1)}, bf16[4,256,256]{2,1,0:T(8,128)(2,1)S(1)}, u32[]{:S(2)}, u32[]{:S(2)}) collective-permute-start(bf16[4,256,256]{2,1,0:T(8,128)(2,1)S(1)} %pad_maximum_fusion.1.refs_4_), channel_id=1, source_target_pairs={{0,4},{4,0},{1,5},{5,1},{2,6},{6,2},{3,7},{7,3},{8,12},{12,8},{9,1... | collective-permute-start | bytes 1572872 | tf_op jit(solution)/shard_map/ppermute | solution.py:169
  62.7 20.3 %collective-permute-start.10 = (bf16[4,256,256]{2,1,0:T(8,128)(2,1)S(1)}, bf16[4,256,256]{2,1,0:T(8,128)(2,1)S(1)}, u32[]{:S(2)}, u32[]{:S(2)}) collective-permute-start(bf16[4,256,256]{2,1,0:T(8,128)(2,1)S(1)} %pad_maximum_fusion.refs_0_), channel_id=1, source_target_pairs={{0,4},{4,0},{1,5},{5,1},{2,6},{6,2},{3,7},{7,3},{8,12},{12,8},{9,1... | collective-permute-start | bytes 1572872 | tf_op jit(solution)/shard_map/ppermute | solution.py:168
  62.8 20.7 %collective-permute-start.19 = (bf16[4,256,256]{2,1,0:T(8,128)(2,1)S(1)}, bf16[4,256,256]{2,1,0:T(8,128)(2,1)S(1)}, u32[]{:S(2)}, u32[]{:S(2)}) collective-permute-start(bf16[4,256,256]{2,1,0:T(8,128)(2,1)S(1)} %collective-permute-done.18.refs_5_), channel_id=1, source_target_pairs={{0,4},{4,0},{1,5},{5,1},{2,6},{6,2},{3,7},{7,3},{8,12},{12,8},{9,1... | collective-permute-start | bytes 1572872 | tf_op jit(solution)/shard_map/ppermute | solution.py:169
  64.7 0.8 copy-start.3
  73.1 38.6 %collective-permute-start.21 = (bf16[4,256,256]{2,1,0:T(8,128)(2,1)}, bf16[4,256,256]{2,1,0:T(8,128)(2,1)}, u32[]{:S(2)}, u32[]{:S(2)}) collective-permute-start(bf16[4,256,256]{2,1,0:T(8,128)(2,1)} %collective-permute-done.20.refs_6_), channel_id=1, source_target_pairs={{0,4},{4,0},{1,5},{5,1},{2,6},{6,2},{3,7},{7,3},{8,12},{12,8},{9,1... | collective-permute-start | bytes 1572872 | tf_op jit(solution)/shard_map/ppermute | solution.py:169
  81.3 30.4 %collective-permute-start.23 = (bf16[4,256,256]{2,1,0:T(8,128)(2,1)}, bf16[4,256,256]{2,1,0:T(8,128)(2,1)}, u32[]{:S(2)}, u32[]{:S(2)}) collective-permute-start(bf16[4,256,256]{2,1,0:T(8,128)(2,1)} %collective-permute-done.22.refs_7_), channel_id=1, source_target_pairs={{0,4},{4,0},{1,5},{5,1},{2,6},{6,2},{3,7},{7,3},{8,12},{12,8},{9,1... | collective-permute-start | bytes 1572872 | tf_op jit(solution)/shard_map/ppermute | solution.py:169
  83.0 28.8 %collective-permute-start.12 = (bf16[4,256,256]{2,1,0:T(8,128)(2,1)}, bf16[4,256,256]{2,1,0:T(8,128)(2,1)}, u32[]{:S(2)}, u32[]{:S(2)}) collective-permute-start(bf16[4,256,256]{2,1,0:T(8,128)(2,1)} %collective-permute-done.11.refs_1_), channel_id=1, source_target_pairs={{0,4},{4,0},{1,5},{5,1},{2,6},{6,2},{3,7},{7,3},{8,12},{12,8},{9,1... | collective-permute-start | bytes 1572872 | tf_op jit(solution)/shard_map/ppermute | solution.py:168
  83.0 28.8 %collective-permute-start.14 = (bf16[4,256,256]{2,1,0:T(8,128)(2,1)}, bf16[4,256,256]{2,1,0:T(8,128)(2,1)}, u32[]{:S(2)}, u32[]{:S(2)}) collective-permute-start(bf16[4,256,256]{2,1,0:T(8,128)(2,1)} %collective-permute-done.13.refs_2_), channel_id=1, source_target_pairs={{0,4},{4,0},{1,5},{5,1},{2,6},{6,2},{3,7},{7,3},{8,12},{12,8},{9,1... | collective-permute-start | bytes 1572872 | tf_op jit(solution)/shard_map/ppermute | solution.py:168
  83.5 28.2 %copy-start.1 = (bf16[4,256,256]{2,1,0:T(8,128)(2,1)}, bf16[4,256,256]{2,1,0:T(8,128)(2,1)S(1)}, u32[]{:S(2)}) copy-start(bf16[4,256,256]{2,1,0:T(8,128)(2,1)S(1)} %collective-permute-done.19.refs_5_) | copy-start | bytes 1572868
  83.5 28.3 %collective-permute-start.16 = (bf16[4,256,256]{2,1,0:T(8,128)(2,1)}, bf16[4,256,256]{2,1,0:T(8,128)(2,1)}, u32[]{:S(2)}, u32[]{:S(2)}) collective-permute-start(bf16[4,256,256]{2,1,0:T(8,128)(2,1)} %collective-permute-done.15.refs_3_), channel_id=1, source_target_pairs={{0,4},{4,0},{1,5},{5,1},{2,6},{6,2},{3,7},{7,3},{8,12},{12,8},{9,1... | collective-permute-start | bytes 1572872 | tf_op jit(solution)/shard_map/ppermute | solution.py:168
  84.6 15.9 %all-to-all-start = ((f32[128,1,512]{2,1,0:T(1,128)}), f32[128,1,512]{2,1,0:T(1,128)}, u32[]{:S(2)}, u32[]{:S(2)}) async-start(f32[128,1,512]{2,1,0:T(1,128)} %broadcast_in_dim.8), calls=%async_computation | async-start | bytes 524288 | tf_op jit(solution)/shard_map/all_to_all | solution.py:44
  105.5 0.9 copy-start.6
  107.6 1.0 copy-start.4
  111.8 1.0 copy-start.2
  117.2 13.9 %all-to-all-start.1 = ((f32[128,1,256]{2,1,0:T(1,128)}), f32[128,1,256]{2,1,0:T(1,128)S(1)}, u32[]{:S(2)}, u32[]{:S(2)}) async-start(f32[128,1,256]{2,1,0:T(1,128)} %broadcast_in_dim.9), calls=%async_computation.1 | async-start | bytes 262144 | tf_op jit(solution)/shard_map/all_to_all | solution.py:44
  (1 other events, 0.7 us)

commit v4 on v3

v4 whole, which is shorter than its diff:
```python
import jax
import jax.numpy as jnp
from jax import lax
from jax.experimental import pallas as pl
from jax.experimental.pallas import tpu as pltpu
from jax.sharding import Mesh, PartitionSpec as P


STATES = 8192
TAU = 64
FRAMES = 2048
WIDE = ("x", "z", "c")
ALL = ("x", "z", "c", "y")
BLOCK = 512
WIDTH = 256
COLS = 2048
GROUPS = COLS // WIDTH
FIRST = 256
STACK = 2 * WIDTH + 16
PART = WIDTH + 16
LANES = 128


def place(x, y, z, c):
    return ((x * 4 + z) * 2 + c) * 4 + y


def across():
    return [
        (place(x, y, z, c), place(y, x, z, c))
        for x in range(4) for y in range(4) for z in range(4) for c in range(2)
    ]


def along(k):
    return [(i, (i + k) % 4) for i in range(4)]


def ring(v, axis):
    return [v] + [lax.ppermute(v, axis, along(k)) for k in (1, 2, 3)]


def to_all(values):
    sent = jnp.broadcast_to(values[None], (128,) + values.shape)
    return lax.all_to_all(sent, ALL, 0, 0).reshape((32, 4) + values.shape)


VMEM = pl.BlockSpec(memory_space=pltpu.VMEM)
SMEM = pl.BlockSpec(memory_space=pltpu.SMEM)


def f32(*shape):
    return jax.ShapeDtypeStruct(shape, jnp.float32)


def row_parts(sym_ref, ratio_rows, ratio_cols):
    parts = []
    for top in range(0, WIDTH, 64):
        acc = jnp.zeros((64, LANES), jnp.float32)
        for k in range(COLS // LANES):
            g, lo = divmod(k * LANES, WIDTH)
            acc += sym_ref[top:top + 64, k * LANES:(k + 1) * LANES] / (
                ratio_rows[top:top + 64] + ratio_cols[g:g + 1, lo:lo + LANES])
        parts.append(acc)
    return jnp.sum(jnp.concatenate(parts, axis=0).T, axis=0, keepdims=True)


def grouped(acc):
    return jnp.concatenate([acc[:WIDTH] + acc[WIDTH:2 * WIDTH], acc[2 * WIDTH:]], axis=0)


def call(kernel, out, *operands):
    return pl.pallas_call(
        kernel,
        in_specs=[SMEM] + [VMEM] * (len(operands) - 1),
        out_specs=[VMEM] * len(out),
        out_shape=out,
        compiler_params=pltpu.CompilerParams(vmem_limit_bytes=16 << 20),
    )(operands[0], *[pltpu.with_memory_space_constraint(v, pltpu.VMEM) for v in operands[1:]])


def left_of(where_ref, left_ref, dx, late):
    lo = lax.rem(where_ref[0] + 4 - dx, 4) * BLOCK + late * FIRST
    return left_ref[:, pl.ds(pl.multiple_of(lo, FIRST), FIRST)]


NEAR = (0, 1, 3)


def near(where, left, by_x, by_z):
    def kernel(where_ref, left_ref, *refs):
        x_refs, z_refs, out_ref = refs[:3], refs[3:6], refs[6]
        for dz in range(4):
            acc = jnp.zeros((STACK, WIDTH), jnp.float32)
            for i, dx in enumerate(NEAR):
                acc += jnp.dot(left_of(where_ref, left_ref, dx, 0), x_refs[i][dz],
                               preferred_element_type=jnp.float32)
            if dz in NEAR:
                for dx in range(4):
                    acc += jnp.dot(left_of(where_ref, left_ref, dx, 1), z_refs[NEAR.index(dz)][dx],
                                   preferred_element_type=jnp.float32)
            out_ref[dz] = grouped(acc)

    return call(kernel, [f32(4, PART, WIDTH)], where, left, *by_x, *by_z)[0]


def far_sums(where_ref, left_ref, x_refs, z_refs, dz):
    acc = jnp.dot(left_of(where_ref, left_ref, 2, 0), x_refs[dz // 2][dz % 2],
                  preferred_element_type=jnp.float32)
    if dz == 2:
        for dx in range(4):
            acc += jnp.dot(left_of(where_ref, left_ref, dx, 1), z_refs[dx // 2][dx % 2],
                           preferred_element_type=jnp.float32)
    return grouped(acc)


def far(where, left, by_x, by_z, so_far):
    def kernel(where_ref, left_ref, xa, xb, za, zb, near_ref, out_ref):
        for dz in range(4):
            out_ref[dz] = near_ref[dz] + far_sums(where_ref, left_ref, (xa, xb), (za, zb), dz)

    return call(kernel, [f32(4, PART, WIDTH)], where, left, *by_x, *by_z, so_far)[0]


def far_and_first(where, left, by_x, by_z, so_far, own, ratio_rows):
    def kernel(where_ref, left_ref, xa, xb, za, zb, near_ref, own_ref, ratio_ref,
               sym_ref, visit_ref, send_ref, total_ref):
        z, c = where_ref[2], where_ref[3]
        for dz in range(4):
            mine = own_ref[dz]
            theirs = near_ref[dz] + far_sums(where_ref, left_ref, (xa, xb), (za, zb), dz)
            for core, part in ((c, mine), (1 - c, theirs)):
                g = lax.rem(z + 4 - dz, 4) * 2 + core
                sym_ref[:, pl.ds(pl.multiple_of(g * WIDTH, WIDTH), WIDTH)] = part[:WIDTH]
                frame = part[WIDTH:]
                visit_ref[pl.ds(g, 1), :] = jnp.sum(frame[:3], axis=0, keepdims=True)
                total_ref[pl.ds(g, 1), :] = jnp.sum(frame[:6], axis=0, keepdims=True)
        send_ref[...] = row_parts(sym_ref, ratio_ref[...], visit_ref[...] / total_ref[...])

    out = [f32(WIDTH, COLS), f32(GROUPS, WIDTH), f32(1, WIDTH), f32(GROUPS, WIDTH)]
    return call(kernel, out, where, left, *by_x, *by_z, so_far, own, ratio_rows)[:3]


def three_parts(v):
    hi = v.astype(jnp.bfloat16).astype(jnp.float32)
    mid = (v - hi).astype(jnp.bfloat16).astype(jnp.float32)
    return [hi, mid, v - hi - mid]


def prepare(where, blocks, frames):
    def kernel(where_ref, *refs):
        frame_ref, left_ref, visit_ref, ratio_ref, rows_ref = refs[4:]
        edge = jnp.zeros((TAU, WIDTH), jnp.bfloat16)
        rows_ref[:TAU, :] = edge
        rows_ref[TAU + FRAMES:, :] = edge
        for k in range(4):
            lo = lax.rem(where_ref[1] + k, 4) * BLOCK + TAU
            rows_ref[pl.ds(pl.multiple_of(lo, TAU), BLOCK), :] = refs[k][...]
        for lo in range(0, FRAMES + 2 * TAU, LANES):
            turned = rows_ref[lo:lo + LANES, :].astype(jnp.float32).T.astype(jnp.bfloat16)
            if lo < FRAMES:
                left_ref[:WIDTH, lo:lo + LANES] = turned
            if lo >= 2 * TAU:
                left_ref[WIDTH:2 * WIDTH, lo - 2 * TAU:lo - 2 * TAU + LANES] = turned
        total = jnp.concatenate(
            [jnp.sum(frame_ref[32 * q:32 * q + 32, :], axis=0, keepdims=True) for q in range(4)], axis=1)
        total = jnp.broadcast_to(total, (16, FRAMES))
        at = lax.broadcasted_iota(jnp.int32, (16, FRAMES), 1)
        line = lax.broadcasted_iota(jnp.int32, (16, FRAMES), 0)
        up = jnp.where(at < FRAMES - TAU, pltpu.roll(total, FRAMES - TAU, 1), 0.0)
        down = jnp.where(at >= TAU, pltpu.roll(total, TAU, 1), 0.0)
        weight = jnp.zeros((16, FRAMES), jnp.float32)
        for i, v in enumerate(three_parts(up) + three_parts(down)):
            weight = jnp.where(line == i, v, weight)
        left_ref[2 * WIDTH:, :] = weight.astype(jnp.bfloat16)
        weight = jnp.zeros((16, FRAMES), jnp.float32)
        for i, v in enumerate(three_parts(total)):
            weight = jnp.where(line == i, v, weight)
        weight = weight.astype(jnp.bfloat16)
        visit = jnp.sum(jnp.dot(weight, rows_ref[:FRAMES, :], preferred_element_type=jnp.float32),
                        axis=0, keepdims=True)
        back = jnp.sum(jnp.dot(weight, rows_ref[2 * TAU:, :], preferred_element_type=jnp.float32),
                       axis=0, keepdims=True)
        visit_ref[...] = visit
        ratio_ref[...] = jnp.broadcast_to(visit / (visit + back), (LANES, WIDTH)).T

    return pl.pallas_call(
        kernel,
        in_specs=[SMEM] + [VMEM] * 5,
        out_specs=[VMEM] * 3,
        out_shape=[jax.ShapeDtypeStruct((STACK, FRAMES), jnp.bfloat16), f32(1, WIDTH), f32(WIDTH, LANES)],
        scratch_shapes=[pltpu.VMEM((FRAMES + 2 * TAU, WIDTH), jnp.bfloat16)],
        compiler_params=pltpu.CompilerParams(vmem_limit_bytes=16 << 20),
    )(where, *[pltpu.with_memory_space_constraint(v, pltpu.VMEM) for v in blocks + [frames]])


def from_sides(v, axis):
    return [lax.ppermute(v, axis, along(k)) for k in (1, 3)]


def from_afar(sides, axis):
    return [lax.ppermute(sides[0][:2], axis, along(1)), lax.ppermute(sides[1][2:], axis, along(3))]


def swapped(vs):
    return [lax.ppermute(v, "c", [(0, 1), (1, 0)]) for v in vs]


def shards(member):
    where = jnp.stack([lax.axis_index(a) for a in ("x", "y", "z", "c")])
    x, y, z, c = (where[i] for i in range(4))
    moved = lax.ppermute(member, ALL, across())
    part = jnp.sum(member, axis=1, dtype=jnp.float32)
    frames = lax.all_to_all(jnp.broadcast_to(part[None], (128, BLOCK)), ("y",) + WIDE, 0, 0)
    once_x = jnp.stack(ring(moved[:FIRST], "z"))
    once_z = jnp.stack(ring(moved[FIRST:], "x"))
    near_x = from_sides(once_x, "x")
    near_z = from_sides(once_z, "z")
    far_x = from_afar(near_x, "x")
    far_z = from_afar(near_z, "z")
    kept, frames = lax.optimization_barrier((member, frames))
    blocks = [member] + [lax.ppermute(kept, "y", along(-k)) for k in (1, 2, 3)]
    left, visit_rows, ratio_rows = prepare(where, blocks, frames)
    own = near(where, left, [once_x] + near_x, [once_z] + near_z)
    once_x, once_z = swapped([once_x, once_z])
    near_x, near_z = swapped(near_x), swapped(near_z)
    sibling = near(where, left, [once_x] + near_x, [once_z] + near_z)
    own = far(where, left, far_x, far_z, own)
    far_x, far_z = swapped(far_x), swapped(far_z)
    sym, visit_cols, part = far_and_first(where, left, far_x, far_z, sibling, own, ratio_rows)
    w = (x * 4 + z) * 2 + c
    for step in range(3):
        totals = jnp.sum(to_all(part.reshape(WIDTH)), axis=1)
        total_rows = lax.dynamic_slice_in_dim(totals, w, 1).reshape(WIDTH)
        total_cols = lax.dynamic_slice_in_dim(totals, y * GROUPS, GROUPS)
        if step == 2:
            break
        ratio_rows = visit_rows.reshape(WIDTH) / total_rows
        ratio = ratio_rows[:, None] + (visit_cols / total_cols).reshape(COLS)[None, :]
        part = jnp.sum(sym / ratio, axis=1)
    transition = sym * (STATES / total_rows)[:, None] / ratio
    stationary = STATES * total_rows / jnp.sum(totals)
    return (transition, stationary)


def solution(mesh):
    mesh = Mesh(mesh.devices.reshape(4, 4, 2, 4), ALL)
    return jax.shard_map(
        shards,
        mesh=mesh,
        in_specs=(P("y", WIDE),),
        out_specs=(P(WIDE, "y"), P(WIDE)),
        check_vma=False,
    )
```

time: 166 us -> 172 us (1.036)
  local copies, waits for them, and re-layouts: 8.11 us -> 11.8 us
  Pallas kernels: 7.9 us -> 11.2 us
  other arithmetic: 9.57 us -> 7.25 us
    ppermute x12 -> x6, starting transfers between devices: 45.7 us -> 8.6 us  [ring(): return [v] + [lax.ppermute(v, axis, along(k)) for k in (1, 2, 3)]]
    all_to_all x0 -> x1, starting transfers between devices: none -> 23.4 us  [shards(): lax.all_to_all(jnp.broadcast_to(part[None], (128, BLOCK)), ('y',) + WIDE,...]
    ppermute x11 -> x21, starting transfers between devices: 12.2 us -> 29.7 us  [the longest x10 14.1 us: swapped(): return [lax.ppermute(v, 'c', [(0, 1), (1, 0)]) for v in vs]]
    ppermute x11 -> x21, waiting for transfers between devices: 6.75 us -> 18.3 us  [the longest x3 11.3 us: shards(): blocks = [member] + [lax.ppermute(kept, 'y', along(-k)) for k in (1, 2, 3)]]
    all_to_all x2 -> x1, waiting for transfers between devices: 21 us -> 10.1 us  [to_all(): return lax.all_to_all(sent, ALL, 0, 0).reshape((32, 4) + values.shape)]
    all_to_all x0 -> x1, waiting for transfers between devices: none -> 6.1 us  [shards(): lax.all_to_all(jnp.broadcast_to(part[None], (128, BLOCK)), ('y',) + WIDE,...]
    unnamed x16 -> x39, local copies, waits for them, and re-layouts: 4.55 us -> 9.87 us
    ppermute x12 -> x6, waiting for transfers between devices: 14.8 us -> 9.45 us  [ring(): return [v] + [lax.ppermute(v, axis, along(k)) for k in (1, 2, 3)]]
  transfers between devices with their start and end apart: 26 -> 30, of which waited for: 6 -> 8; matrix products, arithmetic and copies ran while one was open for 4% -> 2% of each run, Pallas kernels for 3% -> 5%
where the time goes in v4:
time: 172 us; the launch traced here: 171 us
  starting transfers between devices  67.9 us (39%)
  waiting for transfers between devices  43.9 us (26%)
  blocking collectives  27.9 us (16%)
  local copies, waits for them, and re-layouts  11.8 us (7%)
  Pallas kernels  11.2 us (7%)
  other arithmetic  7.25 us (4%)
    all_to_all x2, blocking collectives, to_all(): return lax.all_to_all(sent, ALL, 0, 0).reshape((32, 4) + values.shape)  27.9 us
    all_to_all x1, starting transfers between devices, shards(): lax.all_to_all(jnp.broadcast_to(part[None], (128, BLOCK)), ('y',) + WIDE,...  23.4 us
    ppermute x10, starting transfers between devices, swapped(): return [lax.ppermute(v, 'c', [(0, 1), (1, 0)]) for v in vs]  14.1 us
    ppermute x3, waiting for transfers between devices, shards(): blocks = [member] + [lax.ppermute(kept, 'y', along(-k)) for k in (1, 2, 3)]  11.3 us
    all_to_all x1, waiting for transfers between devices, to_all(): return lax.all_to_all(sent, ALL, 0, 0).reshape((32, 4) + values.shape)  10.1 us
    pallas_call x4, Pallas kernels, call(): pl.pallas_call(kernel, in_specs=[SMEM] + [VMEM] * (len(operands) - 1), ou...  10 us
    unnamed x39, local copies, waits for them, and re-layouts  9.87 us
    ppermute x6, waiting for transfers between devices, ring(): return [v] + [lax.ppermute(v, axis, along(k)) for k in (1, 2, 3)]  9.45 us
  transfers between devices with their start and end apart: 30, of which 8 were waited for; matrix products, arithmetic and copies ran while one was open for 2% of the time, Pallas kernels for 5%

profile of v4, /device:TPU:1, one launch (start us, length us, event | category | flops | bytes accessed | tf_op | source)
XLA Modules:
  0.0 171.1 jit_solution(11891930619359012641)
XLA Ops:
  0.6 1.7 %collective-permute-start.3 = (bf16[512,256]{1,0:T(8,128)(2,1)}, bf16[512,256]{1,0:T(8,128)(2,1)S(1)}, u32[]{:S(2)}, u32[]{:S(2)}) collective-permute-start(bf16[512,256]{1,0:T(8,128)(2,1)} %refs_0_.1), channel_id=1, source_target_pairs={{0,0},{4,4},{8,8},{12,12},{16,16},{20,20},{24,24},{28,28},{1,32},{... | collective-permute-start | bytes 786440 | tf_op jit(solution)/shard_map/ppermute | solution.py:212
  2.4 2.5 %collective-permute-start.4 = (bf16[256,256]{1,0:T(8,128)(2,1)S(1)}, bf16[256,256]{1,0:T(8,128)(2,1)S(1)}, u32[]{:S(2)}, u32[]{:S(2)}) collective-permute-start(bf16[256,256]{1,0:T(8,128)(2,1)S(1)} %get-tuple-element.23), channel_id=1, source_target_pairs={{0,8},{8,16},{16,24},{24,0},{1,9},{9,17},{17,25},{25,1},{2,10},{10... | collective-permute-start | bytes 393224 | tf_op jit(solution)/shard_map/ppermute | solution.py:40
  4.9 3.3 %collective-permute-start.5 = (bf16[256,256]{1,0:T(8,128)(2,1)S(1)}, bf16[256,256]{1,0:T(8,128)(2,1)S(1)}, u32[]{:S(2)}, u32[]{:S(2)}) collective-permute-start(bf16[256,256]{1,0:T(8,128)(2,1)S(1)} %get-tuple-element.23), channel_id=1, source_target_pairs={{0,16},{8,24},{16,0},{24,8},{1,17},{9,25},{17,1},{25,9},{2,18},{10... | collective-permute-start | bytes 393224 | tf_op jit(solution)/shard_map/ppermute | solution.py:40
  10.9 23.4 %all-to-all-start = ((f32[128,1,512]{2,1,0:T(1,128)}), f32[128,1,512]{2,1,0:T(1,128)S(1)}, u32[]{:S(2)}, u32[]{:S(2)}) async-start(f32[128,1,512]{2,1,0:T(1,128)} %broadcast_in_dim.8), calls=%async_computation | async-start | bytes 524288 | tf_op jit(solution)/shard_map/all_to_all | solution.py:214
  34.4 2.6 %collective-permute-start.10 = (bf16[4,256,256]{2,1,0:T(8,128)(2,1)S(1)}, bf16[4,256,256]{2,1,0:T(8,128)(2,1)S(1)}, u32[]{:S(2)}, u32[]{:S(2)}) collective-permute-start(bf16[4,256,256]{2,1,0:T(8,128)(2,1)S(1)} %pad_maximum_fusion.refs_0_), channel_id=1, source_target_pairs={{0,96},{32,0},{64,32},{96,64},{1,97},{33,1},{65,33},{97,65},{2,98}... | collective-permute-start | bytes 1572872 | tf_op jit(solution)/shard_map/ppermute | solution.py:198
  39.1 6.1 %all-to-all-done = f32[128,1,512]{2,1,0:T(1,128)S(1)} async-done(((f32[128,1,512]{2,1,0:T(1,128)}), f32[128,1,512]{2,1,0:T(1,128)S(1)}, u32[]{:S(2)}, u32[]{:S(2)}) %all-to-all-start) | async-done | bytes 262176 | tf_op jit(solution)/shard_map/all_to_all | solution.py:214
  45.9 9.4 %collective-permute-done.15 = bf16[256,256]{1,0:T(8,128)(2,1)S(1)} collective-permute-done((bf16[256,256]{1,0:T(8,128)(2,1)S(1)}, bf16[256,256]{1,0:T(8,128)(2,1)S(1)}, u32[]{:S(2)}, u32[]{:S(2)}) %collective-permute-start.15) | collective-permute-done | bytes 131104 | tf_op jit(solution)/shard_map/ppermute | solution.py:40
  55.4 1.4 collective-permute-start.16
  56.8 2.6 %collective-permute-start = (bf16[512,256]{1,0:T(8,128)(2,1)S(1)}, bf16[512,256]{1,0:T(8,128)(2,1)S(1)}, u32[]{:S(2)}, u32[]{:S(2)}) collective-permute-start(bf16[512,256]{1,0:T(8,128)(2,1)S(1)} %copy-done), channel_id=1, source_target_pairs={{0,3},{1,0},{2,1},{3,2},{4,7},{5,4},{6,5},{7,6},{8,11},{9,8},{10,9... | collective-permute-start | bytes 786440 | tf_op jit(solution)/shard_map/ppermute | solution.py:222
  59.9 1.8 %collective-permute-start.19 = (bf16[4,256,256]{2,1,0:T(8,128)(2,1)S(1)}, bf16[4,256,256]{2,1,0:T(8,128)(2,1)S(1)}, u32[]{:S(2)}, u32[]{:S(2)}) collective-permute-start(bf16[4,256,256]{2,1,0:T(8,128)(2,1)S(1)} %pad_maximum_fusion.1.refs_3_), channel_id=1, source_target_pairs={{0,24},{8,0},{16,8},{24,16},{1,25},{9,1},{17,9},{25,17},{2,26},{10... | collective-permute-start | bytes 1572872 | tf_op jit(solution)/shard_map/ppermute | solution.py:198
  61.7 3.0 %collective-permute-done.refs_1_ = bf16[512,256]{1,0:T(8,128)(2,1)S(1)} collective-permute-done((bf16[512,256]{1,0:T(8,128)(2,1)S(1)}, bf16[512,256]{1,0:T(8,128)(2,1)S(1)}, u32[]{:S(2)}, u32[]{:S(2)}) %collective-permute-start) | collective-permute-done | bytes 262176 | tf_op jit(solution)/shard_map/ppermute | solution.py:222
  65.5 1.5 collective-permute-start.7
  68.0 6.6 %collective-permute-start.22 = (bf16[4,256,256]{2,1,0:T(8,128)(2,1)S(1)}, bf16[4,256,256]{2,1,0:T(8,128)(2,1)S(1)}, u32[]{:S(2)}, u32[]{:S(2)}) collective-permute-start(bf16[4,256,256]{2,1,0:T(8,128)(2,1)S(1)} %pad_maximum_fusion.refs_0_), channel_id=1, source_target_pairs={{0,4},{4,0},{1,5},{5,1},{2,6},{6,2},{3,7},{7,3},{8,12},{12,8},{9,1... | collective-permute-start | bytes 1572872 | tf_op jit(solution)/shard_map/ppermute | solution.py:206
  74.7 1.7 collective-permute-start.11
  76.5 7.9 %collective-permute-done.2.refs_3_ = bf16[512,256]{1,0:T(8,128)(2,1)S(1)} collective-permute-done((bf16[512,256]{1,0:T(8,128)(2,1)S(1)}, bf16[512,256]{1,0:T(8,128)(2,1)S(1)}, u32[]{:S(2)}, u32[]{:S(2)}) %collective-permute-start.2) | collective-permute-done | bytes 262176 | tf_op jit(solution)/shard_map/ppermute | solution.py:222
  85.1 1.4 collective-permute-start.17
  86.5 1.2 collective-permute-start.20
  87.7 1.6 collective-permute-start.23
  90.7 2.6 %collective-permute-done.17.za = bf16[2,256,256]{2,1,0:T(8,128)(2,1)} collective-permute-done((bf16[2,256,256]{2,1,0:T(8,128)(2,1)S(1)}, bf16[2,256,256]{2,1,0:T(8,128)(2,1)}, u32[]{:S(2)}, u32[]{:S(2)}) %collective-permute-start.17) | collective-permute-done | bytes 262176 | tf_op jit(solution)/shard_map/ppermute | solution.py:202
  94.0 2.1 %collective-permute-start.27 = (bf16[4,256,256]{2,1,0:T(8,128)(2,1)S(1)}, bf16[4,256,256]{2,1,0:T(8,128)(2,1)}, u32[]{:S(2)}, u32[]{:S(2)}) collective-permute-start(bf16[4,256,256]{2,1,0:T(8,128)(2,1)S(1)} %collective-permute-done.19.refs_5_), channel_id=1, source_target_pairs={{0,4},{4,0},{1,5},{5,1},{2,6},{6,2},{3,7},{7,3},{8,12},{12,8},{9,1... | collective-permute-start | bytes 1572872 | tf_op jit(solution)/shard_map/ppermute | solution.py:206
  96.1 4.4 %collective-permute-done.8.xa = bf16[2,256,256]{2,1,0:T(8,128)(2,1)} collective-permute-done((bf16[2,256,256]{2,1,0:T(8,128)(2,1)S(1)}, bf16[2,256,256]{2,1,0:T(8,128)(2,1)}, u32[]{:S(2)}, u32[]{:S(2)}) %collective-permute-start.8) | collective-permute-done | bytes 262176 | tf_op jit(solution)/shard_map/ppermute | solution.py:202
  100.5 2.7 %collective-permute-start.12 = (bf16[2,256,256]{2,1,0:T(8,128)(2,1)}, bf16[2,256,256]{2,1,0:T(8,128)(2,1)}, u32[]{:S(2)}, u32[]{:S(2)}) collective-permute-start(bf16[2,256,256]{2,1,0:T(8,128)(2,1)} %collective-permute-done.11.xb), channel_id=1, source_target_pairs={{0,4},{4,0},{1,5},{5,1},{2,6},{6,2},{3,7},{7,3},{8,12},{12,8},{9,1... | collective-permute-start | bytes 786440 | tf_op jit(solution)/shard_map/ppermute | solution.py:206
  111.2 2.4 %shard_map.32.near_ref = f32[4,272,256]{2,1,0:T(8,128)S(1)} custom-call(s32[4]{0:T(128)S(1)} %pad_add_fusion.where_ref, bf16[528,2048]{1,0:T(8,128)(2,1)S(1)} %get-tuple-element.12.left_ref, bf16[4,256,256]{2,1,0:T(8,128)(2,1)S(1)} %pad_maximum_fusion.refs_0_, bf16[4,256,256]{2,1,0:T(8,128)(2,1)S(1)} %collective-permute-done.7.refs_1_, ...), custom_call_target="tpu_custom_call" | custom-call | tf_op jit(solution)/shard_map/pallas_call | solution.py:73
  113.7 2.1 %shard_map.33.own_ref = f32[4,272,256]{2,1,0:T(8,128)S(1)} custom-call(s32[4]{0:T(128)S(1)} %pad_add_fusion.where_ref, bf16[528,2048]{1,0:T(8,128)(2,1)S(1)} %get-tuple-element.12.left_ref, bf16[2,256,256]{2,1,0:T(8,128)(2,1)} %collective-permute-done.8.xa, bf16[2,256,256]{2,1,0:T(8,128)(2,1)} %collective-permute-done.11.xb, ...), custom_call_target="tpu_custom_call" | custom-call | tf_op jit(solution)/shard_map/pallas_call | solution.py:73
  115.8 2.9 %shard_map.31.near_ref = f32[4,272,256]{2,1,0:T(8,128)S(1)} custom-call(s32[4]{0:T(128)S(1)} %pad_add_fusion.where_ref, bf16[528,2048]{1,0:T(8,128)(2,1)S(1)} %get-tuple-element.12.left_ref, bf16[4,256,256]{2,1,0:T(8,128)(2,1)S(1)} %copy-done.3, bf16[4,256,256]{2,1,0:T(8,128)(2,1)S(1)} %copy-done.7, bf16[4,256,256]{2,1,0:T(8,128)(2,1)S(1)} %copy-done.9, ...), custom_call_target="tpu_custom_call" | custom-call | tf_op jit(solution)/shard_map/pallas_call | solution.py:73
  118.8 2.6 %shard_map.34 = (f32[256,2048]{1,0:T(8,128)S(1)}, f32[8,256]{1,0:T(8,128)S(1)}, f32[1,256]{1,0:T(1,128)S(1)}, f32[8,256]{1,0:T(8,128)}) custom-call(s32[4]{0:T(128)S(1)} %pad_add_fusion.where_ref, bf16[528,2048]{1,0:T(8,128)(2,1)S(1)} %get-tuple-element.12.left_ref, bf16[2,256,256]{2,1,0:T(8,128)(2,1)} %collective-permute-done.9.xa, ...), custom_call_target="tpu_custom_call" | custom-call | tf_op jit(solution)/shard_map/pallas_call | solution.py:73
  122.2 4.6 %all-to-all-start.1 = ((f32[128,1,256]{2,1,0:T(1,128)}), f32[128,1,256]{2,1,0:T(1,128)S(1)}, u32[]{:S(2)}, u32[]{:S(2)}) async-start(f32[128,1,256]{2,1,0:T(1,128)} %broadcast_in_dim.9), calls=%async_computation.1 | async-start | bytes 262144 | tf_op jit(solution)/shard_map/all_to_all | solution.py:45
  126.7 10.1 %all-to-all-done.1 = f32[128,1,256]{2,1,0:T(1,128)S(1)} async-done(((f32[128,1,256]{2,1,0:T(1,128)}), f32[128,1,256]{2,1,0:T(1,128)S(1)}, u32[]{:S(2)}, u32[]{:S(2)}) %all-to-all-start.1) | async-done | bytes 131104 | tf_op jit(solution)/shard_map/all_to_all | solution.py:45
  137.8 14.0 %all_to_all.27 = f32[128,1,256]{2,1,0:T(1,128)S(1)} all-to-all(f32[128,1,256]{2,1,0:T(1,128)S(1)} %broadcast_in_dim.10), channel_id=1, replica_groups=mesh['x'=4,'z'=4,'c'=2,'y'=4] {'x','z','c','y'}, dimensions={0} | all-to-all | bytes 262144 | tf_op jit(solution)/shard_map/all_to_all | solution.py:45
  152.8 13.9 %all_to_all.28 = f32[128,1,256]{2,1,0:T(1,128)S(1)} all-to-all(f32[128,1,256]{2,1,0:T(1,128)S(1)} %broadcast_in_dim.11), channel_id=1, replica_groups=mesh['x'=4,'z'=4,'c'=2,'y'=4] {'x','z','c','y'}, dimensions={0} | all-to-all | bytes 262144 | tf_op jit(solution)/shard_map/all_to_all | solution.py:45
  168.0 1.2 multiply_divide_fusion
  169.2 1.9 %add_divide_fusion = f32[256,2048]{1,0:T(8,128)} fusion(f32[256,2048]{1,0:T(8,128)S(1)} %get-tuple-element.14, f32[256]{0:T(256)S(1)} %bitcast.42, f32[2048]{0:T(1024)S(1)} %bitcast.37, f32[256]{0:T(256)S(1)} %bitcast.40), kind=kLoop, calls=%fused_computation | loop fusion | flops 1572864 | bytes 4204544 | tf_op jit(solution)/shard_map/div | solution.py:241
  (104 shorter events, 22.6 us)
Async XLA Ops:
  0.6 56.2 %copy-start = (bf16[512,256]{1,0:T(8,128)(2,1)S(1)}, bf16[512,256]{1,0:T(8,128)(2,1)}, u32[]{:S(2)}) copy-start(bf16[512,256]{1,0:T(8,128)(2,1)} %refs_0_.1) | copy-start | bytes 786436
  0.6 1.7 %collective-permute-start.3 = (bf16[512,256]{1,0:T(8,128)(2,1)}, bf16[512,256]{1,0:T(8,128)(2,1)S(1)}, u32[]{:S(2)}, u32[]{:S(2)}) collective-permute-start(bf16[512,256]{1,0:T(8,128)(2,1)} %refs_0_.1), channel_id=1, source_target_pairs={{0,0},{4,4},{8,8},{12,12},{16,16},{20,20},{24,24},{28,28},{1,32},{... | collective-permute-start | bytes 786440 | tf_op jit(solution)/shard_map/ppermute | solution.py:212
  2.4 31.9 %collective-permute-start.4 = (bf16[256,256]{1,0:T(8,128)(2,1)S(1)}, bf16[256,256]{1,0:T(8,128)(2,1)S(1)}, u32[]{:S(2)}, u32[]{:S(2)}) collective-permute-start(bf16[256,256]{1,0:T(8,128)(2,1)S(1)} %get-tuple-element.23), channel_id=1, source_target_pairs={{0,8},{8,16},{16,24},{24,0},{1,9},{9,17},{17,25},{25,1},{2,10},{10... | collective-permute-start | bytes 393224 | tf_op jit(solution)/shard_map/ppermute | solution.py:40
  4.9 29.4 %collective-permute-start.5 = (bf16[256,256]{1,0:T(8,128)(2,1)S(1)}, bf16[256,256]{1,0:T(8,128)(2,1)S(1)}, u32[]{:S(2)}, u32[]{:S(2)}) collective-permute-start(bf16[256,256]{1,0:T(8,128)(2,1)S(1)} %get-tuple-element.23), channel_id=1, source_target_pairs={{0,16},{8,24},{16,0},{24,8},{1,17},{9,25},{17,1},{25,9},{2,18},{10... | collective-permute-start | bytes 393224 | tf_op jit(solution)/shard_map/ppermute | solution.py:40
  8.3 26.1 %collective-permute-start.6 = (bf16[256,256]{1,0:T(8,128)(2,1)S(1)}, bf16[256,256]{1,0:T(8,128)(2,1)S(1)}, u32[]{:S(2)}, u32[]{:S(2)}) collective-permute-start(bf16[256,256]{1,0:T(8,128)(2,1)S(1)} %get-tuple-element.23), channel_id=1, source_target_pairs={{0,24},{8,0},{16,8},{24,16},{1,25},{9,1},{17,9},{25,17},{2,26},{10... | collective-permute-start | bytes 393224 | tf_op jit(solution)/shard_map/ppermute | solution.py:40
  10.9 34.3 %all-to-all-start = ((f32[128,1,512]{2,1,0:T(1,128)}), f32[128,1,512]{2,1,0:T(1,128)S(1)}, u32[]{:S(2)}, u32[]{:S(2)}) async-start(f32[128,1,512]{2,1,0:T(1,128)} %broadcast_in_dim.8), calls=%async_computation | async-start | bytes 524288 | tf_op jit(solution)/shard_map/all_to_all | solution.py:214
  34.4 40.2 %collective-permute-start.10 = (bf16[4,256,256]{2,1,0:T(8,128)(2,1)S(1)}, bf16[4,256,256]{2,1,0:T(8,128)(2,1)S(1)}, u32[]{:S(2)}, u32[]{:S(2)}) collective-permute-start(bf16[4,256,256]{2,1,0:T(8,128)(2,1)S(1)} %pad_maximum_fusion.refs_0_), channel_id=1, source_target_pairs={{0,96},{32,0},{64,32},{96,64},{1,97},{33,1},{65,33},{97,65},{2,98}... | collective-permute-start | bytes 1572872 | tf_op jit(solution)/shard_map/ppermute | solution.py:198
  37.0 8.9 %collective-permute-start.14 = (bf16[256,256]{1,0:T(8,128)(2,1)S(1)}, bf16[256,256]{1,0:T(8,128)(2,1)S(1)}, u32[]{:S(2)}, u32[]{:S(2)}) collective-permute-start(bf16[256,256]{1,0:T(8,128)(2,1)S(1)} %get-tuple-element.22), channel_id=1, source_target_pairs={{0,64},{32,96},{64,0},{96,32},{1,65},{33,97},{65,1},{97,33},{2,66}... | collective-permute-start | bytes 393224 | tf_op jit(solution)/shard_map/ppermute | solution.py:40
  37.6 17.7 %collective-permute-start.15 = (bf16[256,256]{1,0:T(8,128)(2,1)S(1)}, bf16[256,256]{1,0:T(8,128)(2,1)S(1)}, u32[]{:S(2)}, u32[]{:S(2)}) collective-permute-start(bf16[256,256]{1,0:T(8,128)(2,1)S(1)} %get-tuple-element.22), channel_id=1, source_target_pairs={{0,96},{32,0},{64,32},{96,64},{1,97},{33,1},{65,33},{97,65},{2,98}... | collective-permute-start | bytes 393224 | tf_op jit(solution)/shard_map/ppermute | solution.py:40
  38.3 17.0 %collective-permute-start.13 = (bf16[256,256]{1,0:T(8,128)(2,1)S(1)}, bf16[256,256]{1,0:T(8,128)(2,1)S(1)}, u32[]{:S(2)}, u32[]{:S(2)}) collective-permute-start(bf16[256,256]{1,0:T(8,128)(2,1)S(1)} %get-tuple-element.22), channel_id=1, source_target_pairs={{0,32},{32,64},{64,96},{96,0},{1,33},{33,65},{65,97},{97,1},{2,34}... | collective-permute-start | bytes 393224 | tf_op jit(solution)/shard_map/ppermute | solution.py:40
  55.4 19.2 %collective-permute-start.16 = (bf16[4,256,256]{2,1,0:T(8,128)(2,1)S(1)}, bf16[4,256,256]{2,1,0:T(8,128)(2,1)S(1)}, u32[]{:S(2)}, u32[]{:S(2)}) collective-permute-start(bf16[4,256,256]{2,1,0:T(8,128)(2,1)S(1)} %pad_maximum_fusion.1.refs_3_), channel_id=1, source_target_pairs={{0,8},{8,16},{16,24},{24,0},{1,9},{9,17},{17,25},{25,1},{2,10},{10... | collective-permute-start | bytes 1572872 | tf_op jit(solution)/shard_map/ppermute | solution.py:198
  56.8 7.9 %collective-permute-start = (bf16[512,256]{1,0:T(8,128)(2,1)S(1)}, bf16[512,256]{1,0:T(8,128)(2,1)S(1)}, u32[]{:S(2)}, u32[]{:S(2)}) collective-permute-start(bf16[512,256]{1,0:T(8,128)(2,1)S(1)} %copy-done), channel_id=1, source_target_pairs={{0,3},{1,0},{2,1},{3,2},{4,7},{5,4},{6,5},{7,6},{8,11},{9,8},{10,9... | collective-permute-start | bytes 786440 | tf_op jit(solution)/shard_map/ppermute | solution.py:222
  59.4 7.8 %collective-permute-start.1 = (bf16[512,256]{1,0:T(8,128)(2,1)S(1)}, bf16[512,256]{1,0:T(8,128)(2,1)S(1)}, u32[]{:S(2)}, u32[]{:S(2)}) collective-permute-start(bf16[512,256]{1,0:T(8,128)(2,1)S(1)} %copy-done), channel_id=1, source_target_pairs={{0,2},{1,3},{2,0},{3,1},{4,6},{5,7},{6,4},{7,5},{8,10},{9,11},{10,... | collective-permute-start | bytes 786440 | tf_op jit(solution)/shard_map/ppermute | solution.py:222
  59.9 14.9 %collective-permute-start.19 = (bf16[4,256,256]{2,1,0:T(8,128)(2,1)S(1)}, bf16[4,256,256]{2,1,0:T(8,128)(2,1)S(1)}, u32[]{:S(2)}, u32[]{:S(2)}) collective-permute-start(bf16[4,256,256]{2,1,0:T(8,128)(2,1)S(1)} %pad_maximum_fusion.1.refs_3_), channel_id=1, source_target_pairs={{0,24},{8,0},{16,8},{24,16},{1,25},{9,1},{17,9},{25,17},{2,26},{10... | collective-permute-start | bytes 1572872 | tf_op jit(solution)/shard_map/ppermute | solution.py:198
  65.5 21.0 %collective-permute-start.7 = (bf16[4,256,256]{2,1,0:T(8,128)(2,1)S(1)}, bf16[4,256,256]{2,1,0:T(8,128)(2,1)S(1)}, u32[]{:S(2)}, u32[]{:S(2)}) collective-permute-start(bf16[4,256,256]{2,1,0:T(8,128)(2,1)S(1)} %pad_maximum_fusion.refs_0_), channel_id=1, source_target_pairs={{0,32},{32,64},{64,96},{96,0},{1,33},{33,65},{65,97},{97,1},{2,34}... | collective-permute-start | bytes 1572872 | tf_op jit(solution)/shard_map/ppermute | solution.py:198
  68.0 19.8 %collective-permute-start.22 = (bf16[4,256,256]{2,1,0:T(8,128)(2,1)S(1)}, bf16[4,256,256]{2,1,0:T(8,128)(2,1)S(1)}, u32[]{:S(2)}, u32[]{:S(2)}) collective-permute-start(bf16[4,256,256]{2,1,0:T(8,128)(2,1)S(1)} %pad_maximum_fusion.refs_0_), channel_id=1, source_target_pairs={{0,4},{4,0},{1,5},{5,1},{2,6},{6,2},{3,7},{7,3},{8,12},{12,8},{9,1... | collective-permute-start | bytes 1572872 | tf_op jit(solution)/shard_map/ppermute | solution.py:206
  74.6 14.7 %collective-permute-start.25 = (bf16[4,256,256]{2,1,0:T(8,128)(2,1)S(1)}, bf16[4,256,256]{2,1,0:T(8,128)(2,1)S(1)}, u32[]{:S(2)}, u32[]{:S(2)}) collective-permute-start(bf16[4,256,256]{2,1,0:T(8,128)(2,1)S(1)} %pad_maximum_fusion.1.refs_3_), channel_id=1, source_target_pairs={{0,4},{4,0},{1,5},{5,1},{2,6},{6,2},{3,7},{7,3},{8,12},{12,8},{9,1... | collective-permute-start | bytes 1572872 | tf_op jit(solution)/shard_map/ppermute | solution.py:206
  74.6 9.7 %collective-permute-start.2 = (bf16[512,256]{1,0:T(8,128)(2,1)S(1)}, bf16[512,256]{1,0:T(8,128)(2,1)S(1)}, u32[]{:S(2)}, u32[]{:S(2)}) collective-permute-start(bf16[512,256]{1,0:T(8,128)(2,1)S(1)} %copy-done), channel_id=1, source_target_pairs={{0,1},{1,2},{2,3},{3,0},{4,5},{5,6},{6,7},{7,4},{8,9},{9,10},{10,1... | collective-permute-start | bytes 786440 | tf_op jit(solution)/shard_map/ppermute | solution.py:222
  74.7 15.4 %collective-permute-start.11 = (bf16[2,256,256]{2,1,0:T(8,128)(2,1)S(1)}, bf16[2,256,256]{2,1,0:T(8,128)(2,1)}, u32[]{:S(2)}, u32[]{:S(2)}) collective-permute-start(bf16[2,256,256]{2,1,0:T(8,128)(2,1)S(1)} %slice.26), channel_id=1, source_target_pairs={{0,96},{32,0},{64,32},{96,64},{1,97},{33,1},{65,33},{97,65},{2,98}... | collective-permute-start | bytes 786440 | tf_op jit(solution)/shard_map/ppermute | solution.py:202
  85.1 8.2 %collective-permute-start.17 = (bf16[2,256,256]{2,1,0:T(8,128)(2,1)S(1)}, bf16[2,256,256]{2,1,0:T(8,128)(2,1)}, u32[]{:S(2)}, u32[]{:S(2)}) collective-permute-start(bf16[2,256,256]{2,1,0:T(8,128)(2,1)S(1)} %slice.28), channel_id=1, source_target_pairs={{0,8},{8,16},{16,24},{24,0},{1,9},{9,17},{17,25},{25,1},{2,10},{10... | collective-permute-start | bytes 786440 | tf_op jit(solution)/shard_map/ppermute | solution.py:202
  86.5 7.5 %collective-permute-start.20 = (bf16[2,256,256]{2,1,0:T(8,128)(2,1)S(1)}, bf16[2,256,256]{2,1,0:T(8,128)(2,1)}, u32[]{:S(2)}, u32[]{:S(2)}) collective-permute-start(bf16[2,256,256]{2,1,0:T(8,128)(2,1)S(1)} %slice.29), channel_id=1, source_target_pairs={{0,24},{8,0},{16,8},{24,16},{1,25},{9,1},{17,9},{25,17},{2,26},{10... | collective-permute-start | bytes 786440 | tf_op jit(solution)/shard_map/ppermute | solution.py:202
  87.7 17.7 %copy-start.2 = (bf16[4,256,256]{2,1,0:T(8,128)(2,1)}, bf16[4,256,256]{2,1,0:T(8,128)(2,1)S(1)}, u32[]{:S(2)}) copy-start(bf16[4,256,256]{2,1,0:T(8,128)(2,1)S(1)} %collective-permute-done.22.refs_0_) | copy-start | bytes 1572868
  87.7 15.5 %collective-permute-start.23 = (bf16[4,256,256]{2,1,0:T(8,128)(2,1)S(1)}, bf16[4,256,256]{2,1,0:T(8,128)(2,1)S(1)}, u32[]{:S(2)}, u32[]{:S(2)}) collective-permute-start(bf16[4,256,256]{2,1,0:T(8,128)(2,1)S(1)} %collective-permute-done.7.refs_1_), channel_id=1, source_target_pairs={{0,4},{4,0},{1,5},{5,1},{2,6},{6,2},{3,7},{7,3},{8,12},{12,8},{9,1... | collective-permute-start | bytes 1572872 | tf_op jit(solution)/shard_map/ppermute | solution.py:206
  90.1 14.0 %collective-permute-start.24 = (bf16[4,256,256]{2,1,0:T(8,128)(2,1)S(1)}, bf16[4,256,256]{2,1,0:T(8,128)(2,1)S(1)}, u32[]{:S(2)}, u32[]{:S(2)}) collective-permute-start(bf16[4,256,256]{2,1,0:T(8,128)(2,1)S(1)} %collective-permute-done.10.refs_2_), channel_id=1, source_target_pairs={{0,4},{4,0},{1,5},{5,1},{2,6},{6,2},{3,7},{7,3},{8,12},{12,8},{9,1... | collective-permute-start | bytes 1572872 | tf_op jit(solution)/shard_map/ppermute | solution.py:206
  90.2 15.2 %collective-permute-start.26 = (bf16[4,256,256]{2,1,0:T(8,128)(2,1)S(1)}, bf16[4,256,256]{2,1,0:T(8,128)(2,1)S(1)}, u32[]{:S(2)}, u32[]{:S(2)}) collective-permute-start(bf16[4,256,256]{2,1,0:T(8,128)(2,1)S(1)} %collective-permute-done.16.refs_4_), channel_id=1, source_target_pairs={{0,4},{4,0},{1,5},{5,1},{2,6},{6,2},{3,7},{7,3},{8,12},{12,8},{9,1... | collective-permute-start | bytes 1572872 | tf_op jit(solution)/shard_map/ppermute | solution.py:206
  93.2 7.3 %collective-permute-start.8 = (bf16[2,256,256]{2,1,0:T(8,128)(2,1)S(1)}, bf16[2,256,256]{2,1,0:T(8,128)(2,1)}, u32[]{:S(2)}, u32[]{:S(2)}) collective-permute-start(bf16[2,256,256]{2,1,0:T(8,128)(2,1)S(1)} %slice.25), channel_id=1, source_target_pairs={{0,32},{32,64},{64,96},{96,0},{1,33},{33,65},{65,97},{97,1},{2,34}... | collective-permute-start | bytes 786440 | tf_op jit(solution)/shard_map/ppermute | solution.py:202
  94.0 21.8 %collective-permute-start.27 = (bf16[4,256,256]{2,1,0:T(8,128)(2,1)S(1)}, bf16[4,256,256]{2,1,0:T(8,128)(2,1)}, u32[]{:S(2)}, u32[]{:S(2)}) collective-permute-start(bf16[4,256,256]{2,1,0:T(8,128)(2,1)S(1)} %collective-permute-done.19.refs_5_), channel_id=1, source_target_pairs={{0,4},{4,0},{1,5},{5,1},{2,6},{6,2},{3,7},{7,3},{8,12},{12,8},{9,1... | collective-permute-start | bytes 1572872 | tf_op jit(solution)/shard_map/ppermute | solution.py:206
  100.5 18.2 %collective-permute-start.12 = (bf16[2,256,256]{2,1,0:T(8,128)(2,1)}, bf16[2,256,256]{2,1,0:T(8,128)(2,1)}, u32[]{:S(2)}, u32[]{:S(2)}) collective-permute-start(bf16[2,256,256]{2,1,0:T(8,128)(2,1)} %collective-permute-done.11.xb), channel_id=1, source_target_pairs={{0,4},{4,0},{1,5},{5,1},{2,6},{6,2},{3,7},{7,3},{8,12},{12,8},{9,1... | collective-permute-start | bytes 786440 | tf_op jit(solution)/shard_map/ppermute | solution.py:206
  104.1 14.7 %collective-permute-start.18 = (bf16[2,256,256]{2,1,0:T(8,128)(2,1)}, bf16[2,256,256]{2,1,0:T(8,128)(2,1)}, u32[]{:S(2)}, u32[]{:S(2)}) collective-permute-start(bf16[2,256,256]{2,1,0:T(8,128)(2,1)} %collective-permute-done.17.za), channel_id=1, source_target_pairs={{0,4},{4,0},{1,5},{5,1},{2,6},{6,2},{3,7},{7,3},{8,12},{12,8},{9,1... | collective-permute-start | bytes 786440 | tf_op jit(solution)/shard_map/ppermute | solution.py:206
  104.9 13.9 %collective-permute-start.21 = (bf16[2,256,256]{2,1,0:T(8,128)(2,1)}, bf16[2,256,256]{2,1,0:T(8,128)(2,1)}, u32[]{:S(2)}, u32[]{:S(2)}) collective-permute-start(bf16[2,256,256]{2,1,0:T(8,128)(2,1)} %collective-permute-done.20.zb), channel_id=1, source_target_pairs={{0,4},{4,0},{1,5},{5,1},{2,6},{6,2},{3,7},{7,3},{8,12},{12,8},{9,1... | collective-permute-start | bytes 786440 | tf_op jit(solution)/shard_map/ppermute | solution.py:206
  106.2 12.6 %collective-permute-start.9 = (bf16[2,256,256]{2,1,0:T(8,128)(2,1)}, bf16[2,256,256]{2,1,0:T(8,128)(2,1)}, u32[]{:S(2)}, u32[]{:S(2)}) collective-permute-start(bf16[2,256,256]{2,1,0:T(8,128)(2,1)} %collective-permute-done.8.xa), channel_id=1, source_target_pairs={{0,4},{4,0},{1,5},{5,1},{2,6},{6,2},{3,7},{7,3},{8,12},{12,8},{9,1... | collective-permute-start | bytes 786440 | tf_op jit(solution)/shard_map/ppermute | solution.py:206
  122.2 14.6 %all-to-all-start.1 = ((f32[128,1,256]{2,1,0:T(1,128)}), f32[128,1,256]{2,1,0:T(1,128)S(1)}, u32[]{:S(2)}, u32[]{:S(2)}) async-start(f32[128,1,256]{2,1,0:T(1,128)} %broadcast_in_dim.9), calls=%async_computation.1 | async-start | bytes 262144 | tf_op jit(solution)/shard_map/all_to_all | solution.py:45
  (16 other events, 19.9 us)

commit v5 on v4

--- a/solution.py
+++ b/solution.py
@@ -40,9 +40,8 @@
     return [v] + [lax.ppermute(v, axis, along(k)) for k in (1, 2, 3)]
 
 
-def to_all(values):
-    sent = jnp.broadcast_to(values[None], (128,) + values.shape)
-    return lax.all_to_all(sent, ALL, 0, 0).reshape((32, 4) + values.shape)
+def to_all(sent):
+    return lax.all_to_all(sent, ALL, 0, 0).reshape(32, 4, sent.shape[-1])
 
 
 VMEM = pl.BlockSpec(memory_space=pltpu.VMEM)
@@ -135,9 +134,10 @@
                 frame = part[WIDTH:]
                 visit_ref[pl.ds(g, 1), :] = jnp.sum(frame[:3], axis=0, keepdims=True)
                 total_ref[pl.ds(g, 1), :] = jnp.sum(frame[:6], axis=0, keepdims=True)
-        send_ref[...] = row_parts(sym_ref, ratio_ref[...], visit_ref[...] / total_ref[...])
-
-    out = [f32(WIDTH, COLS), f32(GROUPS, WIDTH), f32(1, WIDTH), f32(GROUPS, WIDTH)]
+        sums = row_parts(sym_ref, ratio_ref[...], visit_ref[...] / total_ref[...])
+        send_ref[...] = jnp.broadcast_to(sums[None], send_ref.shape)
+
+    out = [f32(WIDTH, COLS), f32(GROUPS, WIDTH), f32(128, 1, WIDTH), f32(GROUPS, WIDTH)]
     return call(kernel, out, where, left, *by_x, *by_z, so_far, own, ratio_rows)[:3]
 
 
@@ -163,7 +163,7 @@
             if lo >= 2 * TAU:
                 left_ref[WIDTH:2 * WIDTH, lo - 2 * TAU:lo - 2 * TAU + LANES] = turned
         total = jnp.concatenate(
-            [jnp.sum(frame_ref[32 * q:32 * q + 32, :], axis=0, keepdims=True) for q in range(4)], axis=1)
+            [jnp.sum(frame_ref[32 * q:32 * q + 32], axis=0) for q in range(4)], axis=1)
         total = jnp.broadcast_to(total, (16, FRAMES))
         at = lax.broadcasted_iota(jnp.int32, (16, FRAMES), 1)
         line = lax.broadcasted_iota(jnp.int32, (16, FRAMES), 0)
@@ -198,8 +198,14 @@
     return [lax.ppermute(v, axis, along(k)) for k in (1, 3)]
 
 
-def from_afar(sides, axis):
-    return [lax.ppermute(sides[0][:2], axis, along(1)), lax.ppermute(sides[1][2:], axis, along(3))]
+def from_afar(where, sides, axis):
+    def cut(_, back_ref, on_ref, first_ref, second_ref):
+        first_ref[...] = back_ref[:2]
+        second_ref[...] = on_ref[2:]
+
+    half = jax.ShapeDtypeStruct((2,) + sides[0].shape[1:], sides[0].dtype)
+    halves = call(cut, [half, half], where, *sides)
+    return [lax.ppermute(halves[0], axis, along(1)), lax.ppermute(halves[1], axis, along(3))]
 
 
 def swapped(vs):
@@ -211,13 +217,14 @@
     x, y, z, c = (where[i] for i in range(4))
     moved = lax.ppermute(member, ALL, across())
     part = jnp.sum(member, axis=1, dtype=jnp.float32)
-    frames = lax.all_to_all(jnp.broadcast_to(part[None], (128, BLOCK)), ("y",) + WIDE, 0, 0)
+    part, where = lax.optimization_barrier((part, where))
+    frames = lax.all_to_all(jnp.broadcast_to(part, (128, 1, BLOCK)), ("y",) + WIDE, 0, 0)
     once_x = jnp.stack(ring(moved[:FIRST], "z"))
     once_z = jnp.stack(ring(moved[FIRST:], "x"))
     near_x = from_sides(once_x, "x")
     near_z = from_sides(once_z, "z")
-    far_x = from_afar(near_x, "x")
-    far_z = from_afar(near_z, "z")
+    far_x = from_afar(where, near_x, "x")
+    far_z = from_afar(where, near_z, "z")
     kept, frames = lax.optimization_barrier((member, frames))
     blocks = [member] + [lax.ppermute(kept, "y", along(-k)) for k in (1, 2, 3)]
     left, visit_rows, ratio_rows = prepare(where, blocks, frames)
@@ -227,17 +234,17 @@
     sibling = near(where, left, [once_x] + near_x, [once_z] + near_z)
     own = far(where, left, far_x, far_z, own)
     far_x, far_z = swapped(far_x), swapped(far_z)
-    sym, visit_cols, part = far_and_first(where, left, far_x, far_z, sibling, own, ratio_rows)
+    sym, visit_cols, send = far_and_first(where, left, far_x, far_z, sibling, own, ratio_rows)
     w = (x * 4 + z) * 2 + c
     for step in range(3):
-        totals = jnp.sum(to_all(part.reshape(WIDTH)), axis=1)
+        totals = jnp.sum(to_all(send), axis=1)
         total_rows = lax.dynamic_slice_in_dim(totals, w, 1).reshape(WIDTH)
         total_cols = lax.dynamic_slice_in_dim(totals, y * GROUPS, GROUPS)
         if step == 2:
             break
         ratio_rows = visit_rows.reshape(WIDTH) / total_rows
         ratio = ratio_rows[:, None] + (visit_cols / total_cols).reshape(COLS)[None, :]
-        part = jnp.sum(sym / ratio, axis=1)
+        send = jnp.broadcast_to(jnp.sum(sym / ratio, axis=1), (128, 1, WIDTH))
     transition = sym * (STATES / total_rows)[:, None] / ratio
     stationary = STATES * total_rows / jnp.sum(totals)
     return (transition, stationary)

time: 172 us -> 158 us (0.919)
  local copies, waits for them, and re-layouts: 11.8 us -> 1.16 us
  starting transfers between devices: 67.9 us -> 62.4 us
  waiting for transfers between devices: 43.9 us -> 47 us
    ppermute x6, starting transfers between devices: 8.6 us -> 25.6 us  [ring(): return [v] + [lax.ppermute(v, axis, along(k)) for k in (1, 2, 3)]]
    all_to_all x2, starting transfers between devices: 27.9 us -> 14.6 us  [the longest x1 10.8 us: shards(): lax.all_to_all(jnp.broadcast_to(part, (128, 1, BLOCK)), ('y',) + WIDE, 0, 0)]
    unnamed x39 -> x4, local copies, waits for them, and re-layouts: 9.87 us -> 0.02 us
    ppermute x10, starting transfers between devices: 14.1 us -> 6.35 us  [swapped(): return [lax.ppermute(v, 'c', [(0, 1), (1, 0)]) for v in vs]]
    ppermute x6, waiting for transfers between devices: 9.45 us -> 12.7 us  [ring(): return [v] + [lax.ppermute(v, axis, along(k)) for k in (1, 2, 3)]]
    ppermute x3, starting transfers between devices: 3.11 us -> 5.75 us  [shards(): blocks = [member] + [lax.ppermute(kept, 'y', along(-k)) for k in (1, 2, 3)]]
    ppermute x4, starting transfers between devices: 5.11 us -> 2.79 us  [the longest x2 2.71 us: from_afar(): lax.ppermute(halves[1], axis, along(3))]
    all_to_all x2, waiting for transfers between devices: 16.2 us -> 14.3 us  [the longest x1 10.1 us: to_all(): return lax.all_to_all(sent, ALL, 0, 0).reshape(32, 4, sent.shape[-1])]
  transfers between devices with their start and end apart: 30 -> 30, of which waited for: 8 -> 10; matrix products, arithmetic and copies ran while one was open for 2% -> 1% of each run, Pallas kernels for 5% -> 5%
where the time goes in v5:
time: 158 us
  starting transfers between devices  62.4 us (39%)
  waiting for transfers between devices  47 us (30%)
  blocking collectives  27.9 us (18%)
  Pallas kernels  11 us (7%)
  other arithmetic  7.24 us (5%)
    all_to_all x2, blocking collectives, to_all(): return lax.all_to_all(sent, ALL, 0, 0).reshape(32, 4, sent.shape[-1])  27.9 us
    ppermute x6, starting transfers between devices, ring(): return [v] + [lax.ppermute(v, axis, along(k)) for k in (1, 2, 3)]  25.6 us
    ppermute x6, waiting for transfers between devices, ring(): return [v] + [lax.ppermute(v, axis, along(k)) for k in (1, 2, 3)]  12.7 us
    all_to_all x1, starting transfers between devices, shards(): lax.all_to_all(jnp.broadcast_to(part, (128, 1, BLOCK)), ('y',) + WIDE, 0, 0)  10.8 us
    ppermute x3, waiting for transfers between devices, shards(): blocks = [member] + [lax.ppermute(kept, 'y', along(-k)) for k in (1, 2, 3)]  10.7 us
    all_to_all x1, waiting for transfers between devices, to_all(): return lax.all_to_all(sent, ALL, 0, 0).reshape(32, 4, sent.shape[-1])  10.1 us
    pallas_call x6, Pallas kernels, call(): pl.pallas_call(kernel, in_specs=[SMEM] + [VMEM] * (len(operands) - 1), ou...  9.7 us
    ppermute x10, starting transfers between devices, swapped(): return [lax.ppermute(v, 'c', [(0, 1), (1, 0)]) for v in vs]  6.35 us
  transfers between devices with their start and end apart: 30, of which 10 were waited for; matrix products, arithmetic and copies ran while one was open for 1% of the time, Pallas kernels for 5%

profile of v5, /device:TPU:1, one launch (start us, length us, event | category | flops | bytes accessed | tf_op | source)
XLA Modules:
  0.0 157.7 jit_solution(11487311941220202101)
XLA Ops:
  0.6 1.7 %collective-permute-start.3 = (bf16[512,256]{1,0:T(8,128)(2,1)}, bf16[512,256]{1,0:T(8,128)(2,1)S(1)}, u32[]{:S(2)}, u32[]{:S(2)}) collective-permute-start(bf16[512,256]{1,0:T(8,128)(2,1)} %refs_0_.1), channel_id=1, source_target_pairs={{0,0},{4,4},{8,8},{12,12},{16,16},{20,20},{24,24},{28,28},{1,32},{... | collective-permute-start | bytes 786440 | tf_op jit(solution)/shard_map/ppermute | solution.py:218
  2.4 18.8 %collective-permute-start.14 = (bf16[256,256]{1,0:T(8,128)(2,1)S(1)}, bf16[256,256]{1,0:T(8,128)(2,1)S(1)}, u32[]{:S(2)}, u32[]{:S(2)}) collective-permute-start(bf16[256,256]{1,0:T(8,128)(2,1)S(1)} %get-tuple-element.34), channel_id=1, source_target_pairs={{0,64},{32,96},{64,0},{96,32},{1,65},{33,97},{65,1},{97,33},{2,66}... | collective-permute-start | bytes 393224 | tf_op jit(solution)/shard_map/ppermute | solution.py:40
  25.0 10.8 %all-to-all-start = ((f32[128,1,512]{2,1,0:T(1,128)}), f32[128,1,512]{2,1,0:T(1,128)S(1)}, u32[]{:S(2)}, u32[]{:S(2)}) async-start(f32[128,1,512]{2,1,0:T(1,128)} %broadcast_in_dim.12), calls=%async_computation | async-start | bytes 524288 | tf_op jit(solution)/shard_map/all_to_all | solution.py:221
  36.0 1.6 collective-permute-start.16
  37.5 1.5 collective-permute-start.4
  39.0 1.6 collective-permute-start.5
  40.5 2.0 %collective-permute-start.6 = (bf16[256,256]{1,0:T(8,128)(2,1)S(1)}, bf16[256,256]{1,0:T(8,128)(2,1)S(1)}, u32[]{:S(2)}, u32[]{:S(2)}) collective-permute-start(bf16[256,256]{1,0:T(8,128)(2,1)S(1)} %get-tuple-element.35), channel_id=1, source_target_pairs={{0,24},{8,0},{16,8},{24,16},{1,25},{9,1},{17,9},{25,17},{2,26},{10... | collective-permute-start | bytes 393224 | tf_op jit(solution)/shard_map/ppermute | solution.py:40
  42.5 4.2 %all-to-all-done.refs_4_ = f32[128,1,512]{2,1,0:T(1,128)S(1)} async-done(((f32[128,1,512]{2,1,0:T(1,128)}), f32[128,1,512]{2,1,0:T(1,128)S(1)}, u32[]{:S(2)}, u32[]{:S(2)}) %all-to-all-start) | async-done | bytes 262176 | tf_op jit(solution)/shard_map/all_to_all | solution.py:221
  47.8 8.7 %collective-permute-done.4 = bf16[256,256]{1,0:T(8,128)(2,1)S(1)} collective-permute-done((bf16[256,256]{1,0:T(8,128)(2,1)S(1)}, bf16[256,256]{1,0:T(8,128)(2,1)S(1)}, u32[]{:S(2)}, u32[]{:S(2)}) %collective-permute-start.4) | collective-permute-done | bytes 131104 | tf_op jit(solution)/shard_map/ppermute | solution.py:40
  56.4 4.1 %collective-permute-done.5 = bf16[256,256]{1,0:T(8,128)(2,1)S(1)} collective-permute-done((bf16[256,256]{1,0:T(8,128)(2,1)S(1)}, bf16[256,256]{1,0:T(8,128)(2,1)S(1)}, u32[]{:S(2)}, u32[]{:S(2)}) %collective-permute-start.5) | collective-permute-done | bytes 131104 | tf_op jit(solution)/shard_map/ppermute | solution.py:40
  61.6 2.1 %collective-permute-start = (bf16[512,256]{1,0:T(8,128)(2,1)S(1)}, bf16[512,256]{1,0:T(8,128)(2,1)S(1)}, u32[]{:S(2)}, u32[]{:S(2)}) collective-permute-start(bf16[512,256]{1,0:T(8,128)(2,1)S(1)} %copy-done), channel_id=1, source_target_pairs={{0,3},{1,0},{2,1},{3,2},{4,7},{5,4},{6,5},{7,6},{8,11},{9,8},{10,9... | collective-permute-start | bytes 786440 | tf_op jit(solution)/shard_map/ppermute | solution.py:229
  63.7 2.0 %collective-permute-start.8 = (bf16[4,256,256]{2,1,0:T(8,128)(2,1)S(1)}, bf16[4,256,256]{2,1,0:T(8,128)(2,1)S(1)}, u32[]{:S(2)}, u32[]{:S(2)}) collective-permute-start(bf16[4,256,256]{2,1,0:T(8,128)(2,1)S(1)} %pad_maximum_fusion.refs_0_), channel_id=1, source_target_pairs={{0,96},{32,0},{64,32},{96,64},{1,97},{33,1},{65,33},{97,65},{2,98}... | collective-permute-start | bytes 1572872 | tf_op jit(solution)/shard_map/ppermute | solution.py:198
  65.7 2.9 %collective-permute-done.refs_1_ = bf16[512,256]{1,0:T(8,128)(2,1)S(1)} collective-permute-done((bf16[512,256]{1,0:T(8,128)(2,1)S(1)}, bf16[512,256]{1,0:T(8,128)(2,1)S(1)}, u32[]{:S(2)}, u32[]{:S(2)}) %collective-permute-start) | collective-permute-done | bytes 262176 | tf_op jit(solution)/shard_map/ppermute | solution.py:229
  68.6 1.7 %collective-permute-start.22 = (bf16[4,256,256]{2,1,0:T(8,128)(2,1)S(1)}, bf16[4,256,256]{2,1,0:T(8,128)(2,1)S(1)}, u32[]{:S(2)}, u32[]{:S(2)}) collective-permute-start(bf16[4,256,256]{2,1,0:T(8,128)(2,1)S(1)} %pad_maximum_fusion.refs_0_), channel_id=1, source_target_pairs={{0,4},{4,0},{1,5},{5,1},{2,6},{6,2},{3,7},{7,3},{8,12},{12,8},{9,1... | collective-permute-start | bytes 1572872 | tf_op jit(solution)/shard_map/ppermute | solution.py:212
  70.3 2.3 %collective-permute-start.1 = (bf16[512,256]{1,0:T(8,128)(2,1)S(1)}, bf16[512,256]{1,0:T(8,128)(2,1)S(1)}, u32[]{:S(2)}, u32[]{:S(2)}) collective-permute-start(bf16[512,256]{1,0:T(8,128)(2,1)S(1)} %copy-done), channel_id=1, source_target_pairs={{0,2},{1,3},{2,0},{3,1},{4,6},{5,7},{6,4},{7,5},{8,10},{9,11},{10,... | collective-permute-start | bytes 786440 | tf_op jit(solution)/shard_map/ppermute | solution.py:229
  72.6 1.8 %collective-permute-done.7.back_ref.refs_1_ = bf16[4,256,256]{2,1,0:T(8,128)(2,1)S(1)} collective-permute-done((bf16[4,256,256]{2,1,0:T(8,128)(2,1)S(1)}, bf16[4,256,256]{2,1,0:T(8,128)(2,1)S(1)}, u32[]{:S(2)}, u32[]{:S(2)}) %collective-permute-start.7) | collective-permute-done | bytes 524320 | tf_op jit(solution)/shard_map/ppermute | solution.py:198
  74.4 1.4 collective-permute-start.2
  77.1 2.3 %collective-permute-done.1.refs_2_ = bf16[512,256]{1,0:T(8,128)(2,1)S(1)} collective-permute-done((bf16[512,256]{1,0:T(8,128)(2,1)S(1)}, bf16[512,256]{1,0:T(8,128)(2,1)S(1)}, u32[]{:S(2)}, u32[]{:S(2)}) %collective-permute-start.1) | collective-permute-done | bytes 262176 | tf_op jit(solution)/shard_map/ppermute | solution.py:229
  79.8 5.5 %collective-permute-done.2.refs_3_ = bf16[512,256]{1,0:T(8,128)(2,1)S(1)} collective-permute-done((bf16[512,256]{1,0:T(8,128)(2,1)S(1)}, bf16[512,256]{1,0:T(8,128)(2,1)S(1)}, u32[]{:S(2)}, u32[]{:S(2)}) %collective-permute-start.2) | collective-permute-done | bytes 262176 | tf_op jit(solution)/shard_map/ppermute | solution.py:229
  85.3 2.2 %collective-permute-start.11 = (bf16[2,256,256]{2,1,0:T(8,128)(2,1)S(1)}, bf16[2,256,256]{2,1,0:T(8,128)(2,1)S(1)}, u32[]{:S(2)}, u32[]{:S(2)}) collective-permute-start(bf16[2,256,256]{2,1,0:T(8,128)(2,1)S(1)} %get-tuple-element.22), channel_id=1, source_target_pairs={{0,96},{32,0},{64,32},{96,64},{1,97},{33,1},{65,33},{97,65},{2,98}... | collective-permute-start | bytes 786440 | tf_op jit(solution)/shard_map/ppermute | solution.py:208
  89.0 3.7 %collective-permute-done.11.xb = bf16[2,256,256]{2,1,0:T(8,128)(2,1)S(1)} collective-permute-done((bf16[2,256,256]{2,1,0:T(8,128)(2,1)S(1)}, bf16[2,256,256]{2,1,0:T(8,128)(2,1)S(1)}, u32[]{:S(2)}, u32[]{:S(2)}) %collective-permute-start.11) | collective-permute-done | bytes 262176 | tf_op jit(solution)/shard_map/ppermute | solution.py:208
  92.7 1.5 collective-permute-start.27
  94.3 3.7 %collective-permute-done.9.xa = bf16[2,256,256]{2,1,0:T(8,128)(2,1)S(1)} collective-permute-done((bf16[2,256,256]{2,1,0:T(8,128)(2,1)S(1)}, bf16[2,256,256]{2,1,0:T(8,128)(2,1)S(1)}, u32[]{:S(2)}, u32[]{:S(2)}) %collective-permute-start.9) | collective-permute-done | bytes 262176 | tf_op jit(solution)/shard_map/ppermute | solution.py:208
  100.9 2.4 %shard_map.34.near_ref = f32[4,272,256]{2,1,0:T(8,128)S(1)} custom-call(s32[4]{0:T(128)S(1)} %pad_add_fusion.where_ref._, bf16[528,2048]{1,0:T(8,128)(2,1)S(1)} %get-tuple-element.20.left_ref, bf16[4,256,256]{2,1,0:T(8,128)(2,1)S(1)} %pad_maximum_fusion.refs_0_, bf16[4,256,256]{2,1,0:T(8,128)(2,1)S(1)} %collective-permute-done.7.back_ref.refs_1_, ...), custom_call_target="tpu_custom_call" | custom-call | tf_op jit(solution)/shard_map/pallas_call | solution.py:72
  103.4 1.3 shard_map.35.own_ref
  104.7 2.4 %shard_map.33.near_ref = f32[4,272,256]{2,1,0:T(8,128)S(1)} custom-call(s32[4]{0:T(128)S(1)} %pad_add_fusion.where_ref._, bf16[528,2048]{1,0:T(8,128)(2,1)S(1)} %get-tuple-element.20.left_ref, bf16[4,256,256]{2,1,0:T(8,128)(2,1)S(1)} %collective-permute-done.22.refs_0_, bf16[4,256,256]{2,1,0:T(8,128)(2,1)S(1)} %collective-permute-done.23.refs_1_, ...), custom_call_target="tpu_custom_call" | custom-call | tf_op jit(solution)/shard_map/pallas_call | solution.py:72
  107.1 2.4 %shard_map.36 = (f32[256,2048]{1,0:T(8,128)S(1)}, f32[8,256]{1,0:T(8,128)S(1)}, f32[128,1,256]{2,1,0:T(1,128)}, f32[8,256]{1,0:T(8,128)}) custom-call(s32[4]{0:T(128)S(1)} %pad_add_fusion.where_ref._, bf16[528,2048]{1,0:T(8,128)(2,1)S(1)} %get-tuple-element.20.left_ref, bf16[2,256,256]{2,1,0:T(8,128)(2,1)S(1)} %collective-permute-done.10.xa, ...), custom_call_target="tpu_custom_call" | custom-call | tf_op jit(solution)/shard_map/pallas_call | solution.py:72
  109.6 3.8 %all-to-all-start.1 = ((f32[128,1,256]{2,1,0:T(1,128)}), f32[128,1,256]{2,1,0:T(1,128)S(1)}, u32[]{:S(2)}, u32[]{:S(2)}) async-start(f32[128,1,256]{2,1,0:T(1,128)} %get-tuple-element.28), calls=%async_computation.1 | async-start | bytes 262144 | tf_op jit(solution)/shard_map/all_to_all | solution.py:44
  113.4 10.1 %all-to-all-done.1 = f32[128,1,256]{2,1,0:T(1,128)S(1)} async-done(((f32[128,1,256]{2,1,0:T(1,128)}), f32[128,1,256]{2,1,0:T(1,128)S(1)}, u32[]{:S(2)}, u32[]{:S(2)}) %all-to-all-start.1) | async-done | bytes 131104 | tf_op jit(solution)/shard_map/all_to_all | solution.py:44
  124.5 14.0 %all_to_all.20 = f32[128,1,256]{2,1,0:T(1,128)S(1)} all-to-all(f32[128,1,256]{2,1,0:T(1,128)S(1)} %broadcast_in_dim.13), channel_id=1, replica_groups=mesh['x'=4,'z'=4,'c'=2,'y'=4] {'x','z','c','y'}, dimensions={0} | all-to-all | bytes 262144 | tf_op jit(solution)/shard_map/all_to_all | solution.py:44
  139.5 13.9 %all_to_all.21 = f32[128,1,256]{2,1,0:T(1,128)S(1)} all-to-all(f32[128,1,256]{2,1,0:T(1,128)S(1)} %broadcast_in_dim.14), channel_id=1, replica_groups=mesh['x'=4,'z'=4,'c'=2,'y'=4] {'x','z','c','y'}, dimensions={0} | all-to-all | bytes 262144 | tf_op jit(solution)/shard_map/all_to_all | solution.py:44
  155.9 1.9 %add_divide_fusion = f32[256,2048]{1,0:T(8,128)} fusion(f32[256,2048]{1,0:T(8,128)S(1)} %get-tuple-element.26, f32[256]{0:T(256)S(1)} %bitcast.36, f32[2048]{0:T(1024)S(1)} %bitcast.31, f32[256]{0:T(256)S(1)} %bitcast.34), kind=kLoop, calls=%fused_computation | loop fusion | flops 1572864 | bytes 4204544 | tf_op jit(solution)/shard_map/div | solution.py:248
  (66 shorter events, 16.4 us)
Async XLA Ops:
  0.6 61.0 %copy-start = (bf16[512,256]{1,0:T(8,128)(2,1)S(1)}, bf16[512,256]{1,0:T(8,128)(2,1)}, u32[]{:S(2)}) copy-start(bf16[512,256]{1,0:T(8,128)(2,1)} %refs_0_.1) | copy-start | bytes 786436
  0.6 1.7 %collective-permute-start.3 = (bf16[512,256]{1,0:T(8,128)(2,1)}, bf16[512,256]{1,0:T(8,128)(2,1)S(1)}, u32[]{:S(2)}, u32[]{:S(2)}) collective-permute-start(bf16[512,256]{1,0:T(8,128)(2,1)} %refs_0_.1), channel_id=1, source_target_pairs={{0,0},{4,4},{8,8},{12,12},{16,16},{20,20},{24,24},{28,28},{1,32},{... | collective-permute-start | bytes 786440 | tf_op jit(solution)/shard_map/ppermute | solution.py:218
  2.4 33.4 %collective-permute-start.14 = (bf16[256,256]{1,0:T(8,128)(2,1)S(1)}, bf16[256,256]{1,0:T(8,128)(2,1)S(1)}, u32[]{:S(2)}, u32[]{:S(2)}) collective-permute-start(bf16[256,256]{1,0:T(8,128)(2,1)S(1)} %get-tuple-element.34), channel_id=1, source_target_pairs={{0,64},{32,96},{64,0},{96,32},{1,65},{33,97},{65,1},{97,33},{2,66}... | collective-permute-start | bytes 393224 | tf_op jit(solution)/shard_map/ppermute | solution.py:40
  21.3 14.6 %collective-permute-start.15 = (bf16[256,256]{1,0:T(8,128)(2,1)S(1)}, bf16[256,256]{1,0:T(8,128)(2,1)S(1)}, u32[]{:S(2)}, u32[]{:S(2)}) collective-permute-start(bf16[256,256]{1,0:T(8,128)(2,1)S(1)} %get-tuple-element.34), channel_id=1, source_target_pairs={{0,96},{32,0},{64,32},{96,64},{1,97},{33,1},{65,33},{97,65},{2,98}... | collective-permute-start | bytes 393224 | tf_op jit(solution)/shard_map/ppermute | solution.py:40
  22.5 13.4 %collective-permute-start.13 = (bf16[256,256]{1,0:T(8,128)(2,1)S(1)}, bf16[256,256]{1,0:T(8,128)(2,1)S(1)}, u32[]{:S(2)}, u32[]{:S(2)}) collective-permute-start(bf16[256,256]{1,0:T(8,128)(2,1)S(1)} %get-tuple-element.34), channel_id=1, source_target_pairs={{0,32},{32,64},{64,96},{96,0},{1,33},{33,65},{65,97},{97,1},{2,34}... | collective-permute-start | bytes 393224 | tf_op jit(solution)/shard_map/ppermute | solution.py:40
  25.0 21.7 %all-to-all-start = ((f32[128,1,512]{2,1,0:T(1,128)}), f32[128,1,512]{2,1,0:T(1,128)S(1)}, u32[]{:S(2)}, u32[]{:S(2)}) async-start(f32[128,1,512]{2,1,0:T(1,128)} %broadcast_in_dim.12), calls=%async_computation | async-start | bytes 524288 | tf_op jit(solution)/shard_map/all_to_all | solution.py:221
  36.0 34.4 %collective-permute-start.16 = (bf16[4,256,256]{2,1,0:T(8,128)(2,1)S(1)}, bf16[4,256,256]{2,1,0:T(8,128)(2,1)S(1)}, u32[]{:S(2)}, u32[]{:S(2)}) collective-permute-start(bf16[4,256,256]{2,1,0:T(8,128)(2,1)S(1)} %pad_maximum_fusion.1.refs_3_), channel_id=1, source_target_pairs={{0,8},{8,16},{16,24},{24,0},{1,9},{9,17},{17,25},{25,1},{2,10},{10... | collective-permute-start | bytes 1572872 | tf_op jit(solution)/shard_map/ppermute | solution.py:198
  37.5 18.9 %collective-permute-start.4 = (bf16[256,256]{1,0:T(8,128)(2,1)S(1)}, bf16[256,256]{1,0:T(8,128)(2,1)S(1)}, u32[]{:S(2)}, u32[]{:S(2)}) collective-permute-start(bf16[256,256]{1,0:T(8,128)(2,1)S(1)} %get-tuple-element.35), channel_id=1, source_target_pairs={{0,8},{8,16},{16,24},{24,0},{1,9},{9,17},{17,25},{25,1},{2,10},{10... | collective-permute-start | bytes 393224 | tf_op jit(solution)/shard_map/ppermute | solution.py:40
  39.0 21.5 %collective-permute-start.5 = (bf16[256,256]{1,0:T(8,128)(2,1)S(1)}, bf16[256,256]{1,0:T(8,128)(2,1)S(1)}, u32[]{:S(2)}, u32[]{:S(2)}) collective-permute-start(bf16[256,256]{1,0:T(8,128)(2,1)S(1)} %get-tuple-element.35), channel_id=1, source_target_pairs={{0,16},{8,24},{16,0},{24,8},{1,17},{9,25},{17,1},{25,9},{2,18},{10... | collective-permute-start | bytes 393224 | tf_op jit(solution)/shard_map/ppermute | solution.py:40
  40.5 20.0 %collective-permute-start.6 = (bf16[256,256]{1,0:T(8,128)(2,1)S(1)}, bf16[256,256]{1,0:T(8,128)(2,1)S(1)}, u32[]{:S(2)}, u32[]{:S(2)}) collective-permute-start(bf16[256,256]{1,0:T(8,128)(2,1)S(1)} %get-tuple-element.35), channel_id=1, source_target_pairs={{0,24},{8,0},{16,8},{24,16},{1,25},{9,1},{17,9},{25,17},{2,26},{10... | collective-permute-start | bytes 393224 | tf_op jit(solution)/shard_map/ppermute | solution.py:40
  46.7 23.6 %collective-permute-start.17 = (bf16[4,256,256]{2,1,0:T(8,128)(2,1)S(1)}, bf16[4,256,256]{2,1,0:T(8,128)(2,1)S(1)}, u32[]{:S(2)}, u32[]{:S(2)}) collective-permute-start(bf16[4,256,256]{2,1,0:T(8,128)(2,1)S(1)} %pad_maximum_fusion.1.refs_3_), channel_id=1, source_target_pairs={{0,24},{8,0},{16,8},{24,16},{1,25},{9,1},{17,9},{25,17},{2,26},{10... | collective-permute-start | bytes 1572872 | tf_op jit(solution)/shard_map/ppermute | solution.py:198
  60.6 13.9 %collective-permute-start.7 = (bf16[4,256,256]{2,1,0:T(8,128)(2,1)S(1)}, bf16[4,256,256]{2,1,0:T(8,128)(2,1)S(1)}, u32[]{:S(2)}, u32[]{:S(2)}) collective-permute-start(bf16[4,256,256]{2,1,0:T(8,128)(2,1)S(1)} %pad_maximum_fusion.refs_0_), channel_id=1, source_target_pairs={{0,32},{32,64},{64,96},{96,0},{1,33},{33,65},{65,97},{97,1},{2,34}... | collective-permute-start | bytes 1572872 | tf_op jit(solution)/shard_map/ppermute | solution.py:198
  61.6 7.0 %collective-permute-start = (bf16[512,256]{1,0:T(8,128)(2,1)S(1)}, bf16[512,256]{1,0:T(8,128)(2,1)S(1)}, u32[]{:S(2)}, u32[]{:S(2)}) collective-permute-start(bf16[512,256]{1,0:T(8,128)(2,1)S(1)} %copy-done), channel_id=1, source_target_pairs={{0,3},{1,0},{2,1},{3,2},{4,7},{5,4},{6,5},{7,6},{8,11},{9,8},{10,9... | collective-permute-start | bytes 786440 | tf_op jit(solution)/shard_map/ppermute | solution.py:229
  63.7 12.7 %collective-permute-start.8 = (bf16[4,256,256]{2,1,0:T(8,128)(2,1)S(1)}, bf16[4,256,256]{2,1,0:T(8,128)(2,1)S(1)}, u32[]{:S(2)}, u32[]{:S(2)}) collective-permute-start(bf16[4,256,256]{2,1,0:T(8,128)(2,1)S(1)} %pad_maximum_fusion.refs_0_), channel_id=1, source_target_pairs={{0,96},{32,0},{64,32},{96,64},{1,97},{33,1},{65,33},{97,65},{2,98}... | collective-permute-start | bytes 1572872 | tf_op jit(solution)/shard_map/ppermute | solution.py:198
  68.6 19.0 %collective-permute-start.22 = (bf16[4,256,256]{2,1,0:T(8,128)(2,1)S(1)}, bf16[4,256,256]{2,1,0:T(8,128)(2,1)S(1)}, u32[]{:S(2)}, u32[]{:S(2)}) collective-permute-start(bf16[4,256,256]{2,1,0:T(8,128)(2,1)S(1)} %pad_maximum_fusion.refs_0_), channel_id=1, source_target_pairs={{0,4},{4,0},{1,5},{5,1},{2,6},{6,2},{3,7},{7,3},{8,12},{12,8},{9,1... | collective-permute-start | bytes 1572872 | tf_op jit(solution)/shard_map/ppermute | solution.py:212
  70.3 18.1 %collective-permute-start.25 = (bf16[4,256,256]{2,1,0:T(8,128)(2,1)S(1)}, bf16[4,256,256]{2,1,0:T(8,128)(2,1)S(1)}, u32[]{:S(2)}, u32[]{:S(2)}) collective-permute-start(bf16[4,256,256]{2,1,0:T(8,128)(2,1)S(1)} %pad_maximum_fusion.1.refs_3_), channel_id=1, source_target_pairs={{0,4},{4,0},{1,5},{5,1},{2,6},{6,2},{3,7},{7,3},{8,12},{12,8},{9,1... | collective-permute-start | bytes 1572872 | tf_op jit(solution)/shard_map/ppermute | solution.py:212
  70.3 9.0 %collective-permute-start.1 = (bf16[512,256]{1,0:T(8,128)(2,1)S(1)}, bf16[512,256]{1,0:T(8,128)(2,1)S(1)}, u32[]{:S(2)}, u32[]{:S(2)}) collective-permute-start(bf16[512,256]{1,0:T(8,128)(2,1)S(1)} %copy-done), channel_id=1, source_target_pairs={{0,2},{1,3},{2,0},{3,1},{4,6},{5,7},{6,4},{7,5},{8,10},{9,11},{10,... | collective-permute-start | bytes 786440 | tf_op jit(solution)/shard_map/ppermute | solution.py:229
  74.4 10.9 %collective-permute-start.2 = (bf16[512,256]{1,0:T(8,128)(2,1)S(1)}, bf16[512,256]{1,0:T(8,128)(2,1)S(1)}, u32[]{:S(2)}, u32[]{:S(2)}) collective-permute-start(bf16[512,256]{1,0:T(8,128)(2,1)S(1)} %copy-done), channel_id=1, source_target_pairs={{0,1},{1,2},{2,3},{3,0},{4,5},{5,6},{6,7},{7,4},{8,9},{9,10},{10,1... | collective-permute-start | bytes 786440 | tf_op jit(solution)/shard_map/ppermute | solution.py:229
  76.4 12.1 %collective-permute-start.18 = (bf16[2,256,256]{2,1,0:T(8,128)(2,1)S(1)}, bf16[2,256,256]{2,1,0:T(8,128)(2,1)S(1)}, u32[]{:S(2)}, u32[]{:S(2)}) collective-permute-start(bf16[2,256,256]{2,1,0:T(8,128)(2,1)S(1)} %get-tuple-element.23), channel_id=1, source_target_pairs={{0,8},{8,16},{16,24},{24,0},{1,9},{9,17},{17,25},{25,1},{2,10},{10... | collective-permute-start | bytes 786440 | tf_op jit(solution)/shard_map/ppermute | solution.py:208
  79.4 9.6 %collective-permute-start.20 = (bf16[2,256,256]{2,1,0:T(8,128)(2,1)S(1)}, bf16[2,256,256]{2,1,0:T(8,128)(2,1)S(1)}, u32[]{:S(2)}, u32[]{:S(2)}) collective-permute-start(bf16[2,256,256]{2,1,0:T(8,128)(2,1)S(1)} %get-tuple-element.24), channel_id=1, source_target_pairs={{0,24},{8,0},{16,8},{24,16},{1,25},{9,1},{17,9},{25,17},{2,26},{10... | collective-permute-start | bytes 786440 | tf_op jit(solution)/shard_map/ppermute | solution.py:208
  85.3 7.4 %collective-permute-start.11 = (bf16[2,256,256]{2,1,0:T(8,128)(2,1)S(1)}, bf16[2,256,256]{2,1,0:T(8,128)(2,1)S(1)}, u32[]{:S(2)}, u32[]{:S(2)}) collective-permute-start(bf16[2,256,256]{2,1,0:T(8,128)(2,1)S(1)} %get-tuple-element.22), channel_id=1, source_target_pairs={{0,96},{32,0},{64,32},{96,64},{1,97},{33,1},{65,33},{97,65},{2,98}... | collective-permute-start | bytes 786440 | tf_op jit(solution)/shard_map/ppermute | solution.py:208
  87.6 11.3 %collective-permute-start.23 = (bf16[4,256,256]{2,1,0:T(8,128)(2,1)S(1)}, bf16[4,256,256]{2,1,0:T(8,128)(2,1)S(1)}, u32[]{:S(2)}, u32[]{:S(2)}) collective-permute-start(bf16[4,256,256]{2,1,0:T(8,128)(2,1)S(1)} %collective-permute-done.7.back_ref.refs_1_), channel_id=1, source_target_pairs={{0,4},{4,0},{1,5},{5,1},{2,6},{6,2},{3,7},{7,3},{8,12},{12,8},{9,1... | collective-permute-start | bytes 1572872 | tf_op jit(solution)/shard_map/ppermute | solution.py:212
  88.4 10.5 %collective-permute-start.24 = (bf16[4,256,256]{2,1,0:T(8,128)(2,1)S(1)}, bf16[4,256,256]{2,1,0:T(8,128)(2,1)S(1)}, u32[]{:S(2)}, u32[]{:S(2)}) collective-permute-start(bf16[4,256,256]{2,1,0:T(8,128)(2,1)S(1)} %collective-permute-done.8.on_ref.refs_2_), channel_id=1, source_target_pairs={{0,4},{4,0},{1,5},{5,1},{2,6},{6,2},{3,7},{7,3},{8,12},{12,8},{9,1... | collective-permute-start | bytes 1572872 | tf_op jit(solution)/shard_map/ppermute | solution.py:212
  88.5 10.9 %collective-permute-start.26 = (bf16[4,256,256]{2,1,0:T(8,128)(2,1)S(1)}, bf16[4,256,256]{2,1,0:T(8,128)(2,1)S(1)}, u32[]{:S(2)}, u32[]{:S(2)}) collective-permute-start(bf16[4,256,256]{2,1,0:T(8,128)(2,1)S(1)} %collective-permute-done.16.back_ref.refs_4_), channel_id=1, source_target_pairs={{0,4},{4,0},{1,5},{5,1},{2,6},{6,2},{3,7},{7,3},{8,12},{12,8},{9,1... | collective-permute-start | bytes 1572872 | tf_op jit(solution)/shard_map/ppermute | solution.py:212
  89.0 9.0 %collective-permute-start.9 = (bf16[2,256,256]{2,1,0:T(8,128)(2,1)S(1)}, bf16[2,256,256]{2,1,0:T(8,128)(2,1)S(1)}, u32[]{:S(2)}, u32[]{:S(2)}) collective-permute-start(bf16[2,256,256]{2,1,0:T(8,128)(2,1)S(1)} %get-tuple-element.21), channel_id=1, source_target_pairs={{0,32},{32,64},{64,96},{96,0},{1,33},{33,65},{65,97},{97,1},{2,34}... | collective-permute-start | bytes 786440 | tf_op jit(solution)/shard_map/ppermute | solution.py:208
  92.7 12.0 %collective-permute-start.27 = (bf16[4,256,256]{2,1,0:T(8,128)(2,1)S(1)}, bf16[4,256,256]{2,1,0:T(8,128)(2,1)S(1)}, u32[]{:S(2)}, u32[]{:S(2)}) collective-permute-start(bf16[4,256,256]{2,1,0:T(8,128)(2,1)S(1)} %collective-permute-done.17.on_ref.refs_5_), channel_id=1, source_target_pairs={{0,4},{4,0},{1,5},{5,1},{2,6},{6,2},{3,7},{7,3},{8,12},{12,8},{9,1... | collective-permute-start | bytes 1572872 | tf_op jit(solution)/shard_map/ppermute | solution.py:212
  97.9 9.1 %collective-permute-start.19 = (bf16[2,256,256]{2,1,0:T(8,128)(2,1)S(1)}, bf16[2,256,256]{2,1,0:T(8,128)(2,1)S(1)}, u32[]{:S(2)}, u32[]{:S(2)}) collective-permute-start(bf16[2,256,256]{2,1,0:T(8,128)(2,1)S(1)} %collective-permute-done.18.za), channel_id=1, source_target_pairs={{0,4},{4,0},{1,5},{5,1},{2,6},{6,2},{3,7},{7,3},{8,12},{12,8},{9,1... | collective-permute-start | bytes 786440 | tf_op jit(solution)/shard_map/ppermute | solution.py:212
  98.9 8.2 %collective-permute-start.21 = (bf16[2,256,256]{2,1,0:T(8,128)(2,1)S(1)}, bf16[2,256,256]{2,1,0:T(8,128)(2,1)S(1)}, u32[]{:S(2)}, u32[]{:S(2)}) collective-permute-start(bf16[2,256,256]{2,1,0:T(8,128)(2,1)S(1)} %collective-permute-done.20.zb), channel_id=1, source_target_pairs={{0,4},{4,0},{1,5},{5,1},{2,6},{6,2},{3,7},{7,3},{8,12},{12,8},{9,1... | collective-permute-start | bytes 786440 | tf_op jit(solution)/shard_map/ppermute | solution.py:212
  98.9 8.2 %collective-permute-start.10 = (bf16[2,256,256]{2,1,0:T(8,128)(2,1)S(1)}, bf16[2,256,256]{2,1,0:T(8,128)(2,1)S(1)}, u32[]{:S(2)}, u32[]{:S(2)}) collective-permute-start(bf16[2,256,256]{2,1,0:T(8,128)(2,1)S(1)} %collective-permute-done.9.xa), channel_id=1, source_target_pairs={{0,4},{4,0},{1,5},{5,1},{2,6},{6,2},{3,7},{7,3},{8,12},{12,8},{9,1... | collective-permute-start | bytes 786440 | tf_op jit(solution)/shard_map/ppermute | solution.py:212
  99.4 7.7 %collective-permute-start.12 = (bf16[2,256,256]{2,1,0:T(8,128)(2,1)S(1)}, bf16[2,256,256]{2,1,0:T(8,128)(2,1)S(1)}, u32[]{:S(2)}, u32[]{:S(2)}) collective-permute-start(bf16[2,256,256]{2,1,0:T(8,128)(2,1)S(1)} %collective-permute-done.11.xb), channel_id=1, source_target_pairs={{0,4},{4,0},{1,5},{5,1},{2,6},{6,2},{3,7},{7,3},{8,12},{12,8},{9,1... | collective-permute-start | bytes 786440 | tf_op jit(solution)/shard_map/ppermute | solution.py:212
  109.6 13.9 %all-to-all-start.1 = ((f32[128,1,256]{2,1,0:T(1,128)}), f32[128,1,256]{2,1,0:T(1,128)S(1)}, u32[]{:S(2)}, u32[]{:S(2)}) async-start(f32[128,1,256]{2,1,0:T(1,128)} %get-tuple-element.28), calls=%async_computation.1 | async-start | bytes 262144 | tf_op jit(solution)/shard_map/all_to_all | solution.py:44

commit v6 on v5

--- a/solution.py
+++ b/solution.py
@@ -41,7 +41,7 @@
 
 
 def to_all(sent):
-    return lax.all_to_all(sent, ALL, 0, 0).reshape(32, 4, sent.shape[-1])
+    return lax.all_to_all(sent, ("y",) + WIDE, 0, 0)
 
 
 VMEM = pl.BlockSpec(memory_space=pltpu.VMEM)
@@ -212,13 +212,47 @@
     return [lax.ppermute(v, "c", [(0, 1), (1, 0)]) for v in vs]
 
 
+def finish(where, got, last, sym, visit_cols, visit_rows):
+    def kernel(where_ref, got_ref, last_ref, sym_ref, visit_col_ref, visit_row_ref,
+               out_ref, share_ref, total_ref, row_ref, scale_ref):
+        g = pl.program_id(0)
+        x, y, z, c = (where_ref[i] for i in range(4))
+
+        @pl.when(g == 0)
+        def _():
+            w = (x * 4 + z) * 2 + c
+            total_ref[...] = sum(last_ref[32 * k:32 * k + 32] for k in range(4))
+            own = total_ref[w]
+            scale_ref[...] = jnp.broadcast_to(STATES / own, (LANES, WIDTH)).T
+            grand = jnp.sum(jnp.sum(total_ref[...], axis=0), axis=1, keepdims=True)
+            share_ref[...] = STATES * own / grand
+            total_ref[...] = sum(got_ref[32 * k:32 * k + 32] for k in range(4))
+            row_ref[...] = jnp.broadcast_to(visit_row_ref[...] / total_ref[w], (LANES, WIDTH)).T
+
+        col = visit_col_ref[pl.ds(g, 1), :] / total_ref[y * GROUPS + g]
+        for lo in range(0, WIDTH, LANES):
+            out_ref[:, lo:lo + LANES] = scale_ref[...] * sym_ref[:, lo:lo + LANES] / (
+                row_ref[...] + col[:, lo:lo + LANES])
+
+    return pl.pallas_call(
+        kernel,
+        grid=(GROUPS,),
+        in_specs=[SMEM, VMEM, VMEM, pl.BlockSpec((WIDTH, WIDTH), lambda g: (0, g)), VMEM, VMEM],
+        out_specs=[pl.BlockSpec((WIDTH, WIDTH), lambda g: (0, g)),
+                   pl.BlockSpec((1, WIDTH), lambda g: (0, 0))],
+        out_shape=[f32(WIDTH, COLS), f32(1, WIDTH)],
+        scratch_shapes=[pltpu.VMEM((32, 1, WIDTH), jnp.float32)] + [pltpu.VMEM((WIDTH, LANES), jnp.float32)] * 2,
+        compiler_params=pltpu.CompilerParams(vmem_limit_bytes=16 << 20),
+    )(where, got, last, sym, visit_cols, visit_rows)
+
+
 def shards(member):
     where = jnp.stack([lax.axis_index(a) for a in ("x", "y", "z", "c")])
     x, y, z, c = (where[i] for i in range(4))
     moved = lax.ppermute(member, ALL, across())
     part = jnp.sum(member, axis=1, dtype=jnp.float32)
     part, where = lax.optimization_barrier((part, where))
-    frames = lax.all_to_all(jnp.broadcast_to(part, (128, 1, BLOCK)), ("y",) + WIDE, 0, 0)
+    frames = to_all(jnp.broadcast_to(part, (128, 1, BLOCK)))
     once_x = jnp.stack(ring(moved[:FIRST], "z"))
     once_z = jnp.stack(ring(moved[FIRST:], "x"))
     near_x = from_sides(once_x, "x")
@@ -235,19 +269,17 @@
     own = far(where, left, far_x, far_z, own)
     far_x, far_z = swapped(far_x), swapped(far_z)
     sym, visit_cols, send = far_and_first(where, left, far_x, far_z, sibling, own, ratio_rows)
-    w = (x * 4 + z) * 2 + c
-    for step in range(3):
-        totals = jnp.sum(to_all(send), axis=1)
+    w, first = (x * 4 + z) * 2 + c, y * GROUPS
+    for _ in range(2):
+        got = to_all(send)
+        totals = jnp.sum(got.reshape(4, 32, WIDTH), axis=0)
         total_rows = lax.dynamic_slice_in_dim(totals, w, 1).reshape(WIDTH)
-        total_cols = lax.dynamic_slice_in_dim(totals, y * GROUPS, GROUPS)
-        if step == 2:
-            break
+        total_cols = lax.dynamic_slice_in_dim(totals, first, GROUPS)
         ratio_rows = visit_rows.reshape(WIDTH) / total_rows
         ratio = ratio_rows[:, None] + (visit_cols / total_cols).reshape(COLS)[None, :]
         send = jnp.broadcast_to(jnp.sum(sym / ratio, axis=1), (128, 1, WIDTH))
-    transition = sym * (STATES / total_rows)[:, None] / ratio
-    stationary = STATES * total_rows / jnp.sum(totals)
-    return (transition, stationary)
+    transition, stationary = finish(where, got, to_all(send), sym, visit_cols, visit_rows)
+    return (transition, stationary.reshape(WIDTH))
 
 
 def solution(mesh):

time: 158 us -> 157 us (level)
  other arithmetic: 7.24 us -> 2.26 us
  Pallas kernels: 11 us -> 15 us
    pallas_call x0 -> x1, Pallas kernels: none -> 4.02 us  [finish(): pl.pallas_call(kernel, grid=(GROUPS,), in_specs=[SMEM, VMEM, VMEM, pl.Blo...]
    div x2 -> x0, other arithmetic: 3.08 us -> none  [the longest x1 1.86 us: shards(): transition = sym * (STATES / total_rows)[:, None] / ratio]
where the time goes in v6:
time: 157 us
  starting transfers between devices  62.5 us (40%)
  waiting for transfers between devices  46.8 us (30%)
  blocking collectives  28.2 us (18%)
  Pallas kernels  15 us (10%)
  other arithmetic  2.26 us (1%)
    all_to_all x2, blocking collectives, to_all(): return lax.all_to_all(sent, ('y',) + WIDE, 0, 0)  28.2 us
    ppermute x6, starting transfers between devices, ring(): return [v] + [lax.ppermute(v, axis, along(k)) for k in (1, 2, 3)]  25.6 us
    all_to_all x2, starting transfers between devices, to_all(): return lax.all_to_all(sent, ('y',) + WIDE, 0, 0)  14.6 us
    all_to_all x2, waiting for transfers between devices, to_all(): return lax.all_to_all(sent, ('y',) + WIDE, 0, 0)  14 us
    ppermute x6, waiting for transfers between devices, ring(): return [v] + [lax.ppermute(v, axis, along(k)) for k in (1, 2, 3)]  12.7 us
    ppermute x3, waiting for transfers between devices, shards(): blocks = [member] + [lax.ppermute(kept, 'y', along(-k)) for k in (1, 2, 3)]  10.7 us
    pallas_call x6, Pallas kernels, call(): pl.pallas_call(kernel, in_specs=[SMEM] + [VMEM] * (len(operands) - 1), ou...  9.7 us
    ppermute x10, starting transfers between devices, swapped(): return [lax.ppermute(v, 'c', [(0, 1), (1, 0)]) for v in vs]  6.35 us
  transfers between devices with their start and end apart: 30, of which 10 were waited for; matrix products, arithmetic and copies ran while one was open for 1% of the time, Pallas kernels for 5%

profile of v6, /device:TPU:1, one launch (start us, length us, event | category | flops | bytes accessed | tf_op | source)
XLA Modules:
  0.0 156.7 jit_solution(2352360148823572724)
XLA Ops:
  0.6 1.7 %collective-permute-start.3 = (bf16[512,256]{1,0:T(8,128)(2,1)}, bf16[512,256]{1,0:T(8,128)(2,1)S(1)}, u32[]{:S(2)}, u32[]{:S(2)}) collective-permute-start(bf16[512,256]{1,0:T(8,128)(2,1)} %refs_0_.1), channel_id=1, source_target_pairs={{0,0},{4,4},{8,8},{12,12},{16,16},{20,20},{24,24},{28,28},{1,32},{... | collective-permute-start | bytes 786440 | tf_op jit(solution)/shard_map/ppermute | solution.py:252
  2.4 18.8 %collective-permute-start.14 = (bf16[256,256]{1,0:T(8,128)(2,1)S(1)}, bf16[256,256]{1,0:T(8,128)(2,1)S(1)}, u32[]{:S(2)}, u32[]{:S(2)}) collective-permute-start(bf16[256,256]{1,0:T(8,128)(2,1)S(1)} %get-tuple-element.36), channel_id=1, source_target_pairs={{0,64},{32,96},{64,0},{96,32},{1,65},{33,97},{65,1},{97,33},{2,66}... | collective-permute-start | bytes 393224 | tf_op jit(solution)/shard_map/ppermute | solution.py:40
  25.0 10.8 %all-to-all-start = ((f32[128,1,512]{2,1,0:T(1,128)}), f32[128,1,512]{2,1,0:T(1,128)S(1)}, u32[]{:S(2)}, u32[]{:S(2)}) async-start(f32[128,1,512]{2,1,0:T(1,128)} %broadcast_in_dim.11), calls=%async_computation | async-start | bytes 524288 | tf_op jit(solution)/shard_map/all_to_all | solution.py:44
  36.0 1.6 collective-permute-start.16
  37.5 1.5 collective-permute-start.4
  39.0 1.6 collective-permute-start.5
  40.5 2.0 %collective-permute-start.6 = (bf16[256,256]{1,0:T(8,128)(2,1)S(1)}, bf16[256,256]{1,0:T(8,128)(2,1)S(1)}, u32[]{:S(2)}, u32[]{:S(2)}) collective-permute-start(bf16[256,256]{1,0:T(8,128)(2,1)S(1)} %get-tuple-element.37), channel_id=1, source_target_pairs={{0,24},{8,0},{16,8},{24,16},{1,25},{9,1},{17,9},{25,17},{2,26},{10... | collective-permute-start | bytes 393224 | tf_op jit(solution)/shard_map/ppermute | solution.py:40
  42.5 4.2 %all-to-all-done.refs_4_ = f32[128,1,512]{2,1,0:T(1,128)S(1)} async-done(((f32[128,1,512]{2,1,0:T(1,128)}), f32[128,1,512]{2,1,0:T(1,128)S(1)}, u32[]{:S(2)}, u32[]{:S(2)}) %all-to-all-start) | async-done | bytes 262176 | tf_op jit(solution)/shard_map/all_to_all | solution.py:44
  47.8 8.7 %collective-permute-done.4 = bf16[256,256]{1,0:T(8,128)(2,1)S(1)} collective-permute-done((bf16[256,256]{1,0:T(8,128)(2,1)S(1)}, bf16[256,256]{1,0:T(8,128)(2,1)S(1)}, u32[]{:S(2)}, u32[]{:S(2)}) %collective-permute-start.4) | collective-permute-done | bytes 131104 | tf_op jit(solution)/shard_map/ppermute | solution.py:40
  56.4 4.1 %collective-permute-done.5 = bf16[256,256]{1,0:T(8,128)(2,1)S(1)} collective-permute-done((bf16[256,256]{1,0:T(8,128)(2,1)S(1)}, bf16[256,256]{1,0:T(8,128)(2,1)S(1)}, u32[]{:S(2)}, u32[]{:S(2)}) %collective-permute-start.5) | collective-permute-done | bytes 131104 | tf_op jit(solution)/shard_map/ppermute | solution.py:40
  61.6 2.1 %collective-permute-start = (bf16[512,256]{1,0:T(8,128)(2,1)S(1)}, bf16[512,256]{1,0:T(8,128)(2,1)S(1)}, u32[]{:S(2)}, u32[]{:S(2)}) collective-permute-start(bf16[512,256]{1,0:T(8,128)(2,1)S(1)} %copy-done), channel_id=1, source_target_pairs={{0,3},{1,0},{2,1},{3,2},{4,7},{5,4},{6,5},{7,6},{8,11},{9,8},{10,9... | collective-permute-start | bytes 786440 | tf_op jit(solution)/shard_map/ppermute | solution.py:263
  63.7 2.0 %collective-permute-start.8 = (bf16[4,256,256]{2,1,0:T(8,128)(2,1)S(1)}, bf16[4,256,256]{2,1,0:T(8,128)(2,1)S(1)}, u32[]{:S(2)}, u32[]{:S(2)}) collective-permute-start(bf16[4,256,256]{2,1,0:T(8,128)(2,1)S(1)} %pad_maximum_fusion.refs_0_), channel_id=1, source_target_pairs={{0,96},{32,0},{64,32},{96,64},{1,97},{33,1},{65,33},{97,65},{2,98}... | collective-permute-start | bytes 1572872 | tf_op jit(solution)/shard_map/ppermute | solution.py:198
  65.7 2.9 %collective-permute-done.refs_1_ = bf16[512,256]{1,0:T(8,128)(2,1)S(1)} collective-permute-done((bf16[512,256]{1,0:T(8,128)(2,1)S(1)}, bf16[512,256]{1,0:T(8,128)(2,1)S(1)}, u32[]{:S(2)}, u32[]{:S(2)}) %collective-permute-start) | collective-permute-done | bytes 262176 | tf_op jit(solution)/shard_map/ppermute | solution.py:263
  68.6 1.7 %collective-permute-start.22 = (bf16[4,256,256]{2,1,0:T(8,128)(2,1)S(1)}, bf16[4,256,256]{2,1,0:T(8,128)(2,1)S(1)}, u32[]{:S(2)}, u32[]{:S(2)}) collective-permute-start(bf16[4,256,256]{2,1,0:T(8,128)(2,1)S(1)} %pad_maximum_fusion.refs_0_), channel_id=1, source_target_pairs={{0,4},{4,0},{1,5},{5,1},{2,6},{6,2},{3,7},{7,3},{8,12},{12,8},{9,1... | collective-permute-start | bytes 1572872 | tf_op jit(solution)/shard_map/ppermute | solution.py:212
  70.3 2.3 %collective-permute-start.1 = (bf16[512,256]{1,0:T(8,128)(2,1)S(1)}, bf16[512,256]{1,0:T(8,128)(2,1)S(1)}, u32[]{:S(2)}, u32[]{:S(2)}) collective-permute-start(bf16[512,256]{1,0:T(8,128)(2,1)S(1)} %copy-done), channel_id=1, source_target_pairs={{0,2},{1,3},{2,0},{3,1},{4,6},{5,7},{6,4},{7,5},{8,10},{9,11},{10,... | collective-permute-start | bytes 786440 | tf_op jit(solution)/shard_map/ppermute | solution.py:263
  72.6 1.8 %collective-permute-done.7.back_ref.refs_1_ = bf16[4,256,256]{2,1,0:T(8,128)(2,1)S(1)} collective-permute-done((bf16[4,256,256]{2,1,0:T(8,128)(2,1)S(1)}, bf16[4,256,256]{2,1,0:T(8,128)(2,1)S(1)}, u32[]{:S(2)}, u32[]{:S(2)}) %collective-permute-start.7) | collective-permute-done | bytes 524320 | tf_op jit(solution)/shard_map/ppermute | solution.py:198
  74.4 1.4 collective-permute-start.2
  77.1 2.3 %collective-permute-done.1.refs_2_ = bf16[512,256]{1,0:T(8,128)(2,1)S(1)} collective-permute-done((bf16[512,256]{1,0:T(8,128)(2,1)S(1)}, bf16[512,256]{1,0:T(8,128)(2,1)S(1)}, u32[]{:S(2)}, u32[]{:S(2)}) %collective-permute-start.1) | collective-permute-done | bytes 262176 | tf_op jit(solution)/shard_map/ppermute | solution.py:263
  79.8 5.5 %collective-permute-done.2.refs_3_ = bf16[512,256]{1,0:T(8,128)(2,1)S(1)} collective-permute-done((bf16[512,256]{1,0:T(8,128)(2,1)S(1)}, bf16[512,256]{1,0:T(8,128)(2,1)S(1)}, u32[]{:S(2)}, u32[]{:S(2)}) %collective-permute-start.2) | collective-permute-done | bytes 262176 | tf_op jit(solution)/shard_map/ppermute | solution.py:263
  85.3 2.2 %collective-permute-start.11 = (bf16[2,256,256]{2,1,0:T(8,128)(2,1)S(1)}, bf16[2,256,256]{2,1,0:T(8,128)(2,1)S(1)}, u32[]{:S(2)}, u32[]{:S(2)}) collective-permute-start(bf16[2,256,256]{2,1,0:T(8,128)(2,1)S(1)} %get-tuple-element.24), channel_id=1, source_target_pairs={{0,96},{32,0},{64,32},{96,64},{1,97},{33,1},{65,33},{97,65},{2,98}... | collective-permute-start | bytes 786440 | tf_op jit(solution)/shard_map/ppermute | solution.py:208
  89.0 3.7 %collective-permute-done.11.xb = bf16[2,256,256]{2,1,0:T(8,128)(2,1)S(1)} collective-permute-done((bf16[2,256,256]{2,1,0:T(8,128)(2,1)S(1)}, bf16[2,256,256]{2,1,0:T(8,128)(2,1)S(1)}, u32[]{:S(2)}, u32[]{:S(2)}) %collective-permute-start.11) | collective-permute-done | bytes 262176 | tf_op jit(solution)/shard_map/ppermute | solution.py:208
  92.7 1.5 collective-permute-start.27
  94.3 3.7 %collective-permute-done.9.xa = bf16[2,256,256]{2,1,0:T(8,128)(2,1)S(1)} collective-permute-done((bf16[2,256,256]{2,1,0:T(8,128)(2,1)S(1)}, bf16[2,256,256]{2,1,0:T(8,128)(2,1)S(1)}, u32[]{:S(2)}, u32[]{:S(2)}) %collective-permute-start.9) | collective-permute-done | bytes 262176 | tf_op jit(solution)/shard_map/ppermute | solution.py:208
  100.9 2.4 %shard_map.34.near_ref = f32[4,272,256]{2,1,0:T(8,128)S(1)} custom-call(s32[4]{0:T(128)S(1)} %pad_add_fusion.where_ref._, bf16[528,2048]{1,0:T(8,128)(2,1)S(1)} %get-tuple-element.22.left_ref, bf16[4,256,256]{2,1,0:T(8,128)(2,1)S(1)} %pad_maximum_fusion.refs_0_, bf16[4,256,256]{2,1,0:T(8,128)(2,1)S(1)} %collective-permute-done.7.back_ref.refs_1_, ...), custom_call_target="tpu_custom_call" | custom-call | tf_op jit(solution)/shard_map/pallas_call | solution.py:72
  103.4 1.3 shard_map.35.own_ref
  104.7 2.4 %shard_map.33.near_ref = f32[4,272,256]{2,1,0:T(8,128)S(1)} custom-call(s32[4]{0:T(128)S(1)} %pad_add_fusion.where_ref._, bf16[528,2048]{1,0:T(8,128)(2,1)S(1)} %get-tuple-element.22.left_ref, bf16[4,256,256]{2,1,0:T(8,128)(2,1)S(1)} %collective-permute-done.22.refs_0_, bf16[4,256,256]{2,1,0:T(8,128)(2,1)S(1)} %collective-permute-done.23.refs_1_, ...), custom_call_target="tpu_custom_call" | custom-call | tf_op jit(solution)/shard_map/pallas_call | solution.py:72
  107.1 2.4 %shard_map.36 = (f32[256,2048]{1,0:T(8,128)S(1)}, f32[8,256]{1,0:T(8,128)S(1)}, f32[128,1,256]{2,1,0:T(1,128)}, f32[8,256]{1,0:T(8,128)}) custom-call(s32[4]{0:T(128)S(1)} %pad_add_fusion.where_ref._, bf16[528,2048]{1,0:T(8,128)(2,1)S(1)} %get-tuple-element.22.left_ref, bf16[2,256,256]{2,1,0:T(8,128)(2,1)S(1)} %collective-permute-done.10.xa, ...), custom_call_target="tpu_custom_call" | custom-call | tf_op jit(solution)/shard_map/pallas_call | solution.py:72
  109.6 3.8 %all-to-all-start.1 = ((f32[128,1,256]{2,1,0:T(1,128)}), f32[128,1,256]{2,1,0:T(1,128)S(1)}, u32[]{:S(2)}, u32[]{:S(2)}) async-start(f32[128,1,256]{2,1,0:T(1,128)} %get-tuple-element.30), calls=%async_computation.1 | async-start | bytes 262144 | tf_op jit(solution)/shard_map/all_to_all | solution.py:44
  113.4 9.8 %all-to-all-done.1 = f32[128,1,256]{2,1,0:T(1,128)S(1)} async-done(((f32[128,1,256]{2,1,0:T(1,128)}), f32[128,1,256]{2,1,0:T(1,128)S(1)}, u32[]{:S(2)}, u32[]{:S(2)}) %all-to-all-start.1) | async-done | bytes 131104 | tf_op jit(solution)/shard_map/all_to_all | solution.py:44
  123.8 14.1 %all_to_all.20.got_ref = f32[128,1,256]{2,1,0:T(1,128)S(1)} all-to-all(f32[128,1,256]{2,1,0:T(1,128)S(1)} %broadcast_in_dim.12), channel_id=1, replica_groups=mesh['x'=4,'z'=4,'c'=2,'y'=4] {'y','x','z','c'}, dimensions={0} | all-to-all | bytes 262144 | tf_op jit(solution)/shard_map/all_to_all | solution.py:44
  138.5 14.2 %all_to_all.21.last_ref = f32[128,1,256]{2,1,0:T(1,128)S(1)} all-to-all(f32[128,1,256]{2,1,0:T(1,128)S(1)} %broadcast_in_dim.13), channel_id=1, replica_groups=mesh['x'=4,'z'=4,'c'=2,'y'=4] {'y','x','z','c'}, dimensions={0} | all-to-all | bytes 262144 | tf_op jit(solution)/shard_map/all_to_all | solution.py:44
  152.7 4.0 %shard_map.37 = (f32[256,2048]{1,0:T(8,128)}, f32[1,256]{1,0:T(1,128)}) custom-call(s32[4]{0:T(128)S(1)} %pad_add_fusion.where_ref._, f32[128,1,256]{2,1,0:T(1,128)S(1)} %all_to_all.20.got_ref, f32[128,1,256]{2,1,0:T(1,128)S(1)} %all_to_all.21.last_ref, f32[256,2048]{1,0:T(8,128)S(1)} %get-tuple-element.28.sym_ref, ...), custom_call_target="tpu_custom_call" | custom-call | tf_op jit(solution)/shard_map/pallas_call | solution.py:237
  (60 shorter events, 13.2 us)
Async XLA Ops:
  0.6 61.0 %copy-start = (bf16[512,256]{1,0:T(8,128)(2,1)S(1)}, bf16[512,256]{1,0:T(8,128)(2,1)}, u32[]{:S(2)}) copy-start(bf16[512,256]{1,0:T(8,128)(2,1)} %refs_0_.1) | copy-start | bytes 786436
  0.6 1.7 %collective-permute-start.3 = (bf16[512,256]{1,0:T(8,128)(2,1)}, bf16[512,256]{1,0:T(8,128)(2,1)S(1)}, u32[]{:S(2)}, u32[]{:S(2)}) collective-permute-start(bf16[512,256]{1,0:T(8,128)(2,1)} %refs_0_.1), channel_id=1, source_target_pairs={{0,0},{4,4},{8,8},{12,12},{16,16},{20,20},{24,24},{28,28},{1,32},{... | collective-permute-start | bytes 786440 | tf_op jit(solution)/shard_map/ppermute | solution.py:252
  2.4 33.4 %collective-permute-start.14 = (bf16[256,256]{1,0:T(8,128)(2,1)S(1)}, bf16[256,256]{1,0:T(8,128)(2,1)S(1)}, u32[]{:S(2)}, u32[]{:S(2)}) collective-permute-start(bf16[256,256]{1,0:T(8,128)(2,1)S(1)} %get-tuple-element.36), channel_id=1, source_target_pairs={{0,64},{32,96},{64,0},{96,32},{1,65},{33,97},{65,1},{97,33},{2,66}... | collective-permute-start | bytes 393224 | tf_op jit(solution)/shard_map/ppermute | solution.py:40
  21.3 14.6 %collective-permute-start.15 = (bf16[256,256]{1,0:T(8,128)(2,1)S(1)}, bf16[256,256]{1,0:T(8,128)(2,1)S(1)}, u32[]{:S(2)}, u32[]{:S(2)}) collective-permute-start(bf16[256,256]{1,0:T(8,128)(2,1)S(1)} %get-tuple-element.36), channel_id=1, source_target_pairs={{0,96},{32,0},{64,32},{96,64},{1,97},{33,1},{65,33},{97,65},{2,98}... | collective-permute-start | bytes 393224 | tf_op jit(solution)/shard_map/ppermute | solution.py:40
  22.5 13.4 %collective-permute-start.13 = (bf16[256,256]{1,0:T(8,128)(2,1)S(1)}, bf16[256,256]{1,0:T(8,128)(2,1)S(1)}, u32[]{:S(2)}, u32[]{:S(2)}) collective-permute-start(bf16[256,256]{1,0:T(8,128)(2,1)S(1)} %get-tuple-element.36), channel_id=1, source_target_pairs={{0,32},{32,64},{64,96},{96,0},{1,33},{33,65},{65,97},{97,1},{2,34}... | collective-permute-start | bytes 393224 | tf_op jit(solution)/shard_map/ppermute | solution.py:40
  25.0 21.7 %all-to-all-start = ((f32[128,1,512]{2,1,0:T(1,128)}), f32[128,1,512]{2,1,0:T(1,128)S(1)}, u32[]{:S(2)}, u32[]{:S(2)}) async-start(f32[128,1,512]{2,1,0:T(1,128)} %broadcast_in_dim.11), calls=%async_computation | async-start | bytes 524288 | tf_op jit(solution)/shard_map/all_to_all | solution.py:44
  36.0 34.4 %collective-permute-start.16 = (bf16[4,256,256]{2,1,0:T(8,128)(2,1)S(1)}, bf16[4,256,256]{2,1,0:T(8,128)(2,1)S(1)}, u32[]{:S(2)}, u32[]{:S(2)}) collective-permute-start(bf16[4,256,256]{2,1,0:T(8,128)(2,1)S(1)} %pad_maximum_fusion.1.refs_3_), channel_id=1, source_target_pairs={{0,8},{8,16},{16,24},{24,0},{1,9},{9,17},{17,25},{25,1},{2,10},{10... | collective-permute-start | bytes 1572872 | tf_op jit(solution)/shard_map/ppermute | solution.py:198
  37.5 18.9 %collective-permute-start.4 = (bf16[256,256]{1,0:T(8,128)(2,1)S(1)}, bf16[256,256]{1,0:T(8,128)(2,1)S(1)}, u32[]{:S(2)}, u32[]{:S(2)}) collective-permute-start(bf16[256,256]{1,0:T(8,128)(2,1)S(1)} %get-tuple-element.37), channel_id=1, source_target_pairs={{0,8},{8,16},{16,24},{24,0},{1,9},{9,17},{17,25},{25,1},{2,10},{10... | collective-permute-start | bytes 393224 | tf_op jit(solution)/shard_map/ppermute | solution.py:40
  39.0 21.5 %collective-permute-start.5 = (bf16[256,256]{1,0:T(8,128)(2,1)S(1)}, bf16[256,256]{1,0:T(8,128)(2,1)S(1)}, u32[]{:S(2)}, u32[]{:S(2)}) collective-permute-start(bf16[256,256]{1,0:T(8,128)(2,1)S(1)} %get-tuple-element.37), channel_id=1, source_target_pairs={{0,16},{8,24},{16,0},{24,8},{1,17},{9,25},{17,1},{25,9},{2,18},{10... | collective-permute-start | bytes 393224 | tf_op jit(solution)/shard_map/ppermute | solution.py:40
  40.5 20.0 %collective-permute-start.6 = (bf16[256,256]{1,0:T(8,128)(2,1)S(1)}, bf16[256,256]{1,0:T(8,128)(2,1)S(1)}, u32[]{:S(2)}, u32[]{:S(2)}) collective-permute-start(bf16[256,256]{1,0:T(8,128)(2,1)S(1)} %get-tuple-element.37), channel_id=1, source_target_pairs={{0,24},{8,0},{16,8},{24,16},{1,25},{9,1},{17,9},{25,17},{2,26},{10... | collective-permute-start | bytes 393224 | tf_op jit(solution)/shard_map/ppermute | solution.py:40
  46.7 23.6 %collective-permute-start.17 = (bf16[4,256,256]{2,1,0:T(8,128)(2,1)S(1)}, bf16[4,256,256]{2,1,0:T(8,128)(2,1)S(1)}, u32[]{:S(2)}, u32[]{:S(2)}) collective-permute-start(bf16[4,256,256]{2,1,0:T(8,128)(2,1)S(1)} %pad_maximum_fusion.1.refs_3_), channel_id=1, source_target_pairs={{0,24},{8,0},{16,8},{24,16},{1,25},{9,1},{17,9},{25,17},{2,26},{10... | collective-permute-start | bytes 1572872 | tf_op jit(solution)/shard_map/ppermute | solution.py:198
  60.6 13.9 %collective-permute-start.7 = (bf16[4,256,256]{2,1,0:T(8,128)(2,1)S(1)}, bf16[4,256,256]{2,1,0:T(8,128)(2,1)S(1)}, u32[]{:S(2)}, u32[]{:S(2)}) collective-permute-start(bf16[4,256,256]{2,1,0:T(8,128)(2,1)S(1)} %pad_maximum_fusion.refs_0_), channel_id=1, source_target_pairs={{0,32},{32,64},{64,96},{96,0},{1,33},{33,65},{65,97},{97,1},{2,34}... | collective-permute-start | bytes 1572872 | tf_op jit(solution)/shard_map/ppermute | solution.py:198
  61.6 7.0 %collective-permute-start = (bf16[512,256]{1,0:T(8,128)(2,1)S(1)}, bf16[512,256]{1,0:T(8,128)(2,1)S(1)}, u32[]{:S(2)}, u32[]{:S(2)}) collective-permute-start(bf16[512,256]{1,0:T(8,128)(2,1)S(1)} %copy-done), channel_id=1, source_target_pairs={{0,3},{1,0},{2,1},{3,2},{4,7},{5,4},{6,5},{7,6},{8,11},{9,8},{10,9... | collective-permute-start | bytes 786440 | tf_op jit(solution)/shard_map/ppermute | solution.py:263
  63.7 12.7 %collective-permute-start.8 = (bf16[4,256,256]{2,1,0:T(8,128)(2,1)S(1)}, bf16[4,256,256]{2,1,0:T(8,128)(2,1)S(1)}, u32[]{:S(2)}, u32[]{:S(2)}) collective-permute-start(bf16[4,256,256]{2,1,0:T(8,128)(2,1)S(1)} %pad_maximum_fusion.refs_0_), channel_id=1, source_target_pairs={{0,96},{32,0},{64,32},{96,64},{1,97},{33,1},{65,33},{97,65},{2,98}... | collective-permute-start | bytes 1572872 | tf_op jit(solution)/shard_map/ppermute | solution.py:198
  68.6 19.0 %collective-permute-start.22 = (bf16[4,256,256]{2,1,0:T(8,128)(2,1)S(1)}, bf16[4,256,256]{2,1,0:T(8,128)(2,1)S(1)}, u32[]{:S(2)}, u32[]{:S(2)}) collective-permute-start(bf16[4,256,256]{2,1,0:T(8,128)(2,1)S(1)} %pad_maximum_fusion.refs_0_), channel_id=1, source_target_pairs={{0,4},{4,0},{1,5},{5,1},{2,6},{6,2},{3,7},{7,3},{8,12},{12,8},{9,1... | collective-permute-start | bytes 1572872 | tf_op jit(solution)/shard_map/ppermute | solution.py:212
  70.3 18.1 %collective-permute-start.25 = (bf16[4,256,256]{2,1,0:T(8,128)(2,1)S(1)}, bf16[4,256,256]{2,1,0:T(8,128)(2,1)S(1)}, u32[]{:S(2)}, u32[]{:S(2)}) collective-permute-start(bf16[4,256,256]{2,1,0:T(8,128)(2,1)S(1)} %pad_maximum_fusion.1.refs_3_), channel_id=1, source_target_pairs={{0,4},{4,0},{1,5},{5,1},{2,6},{6,2},{3,7},{7,3},{8,12},{12,8},{9,1... | collective-permute-start | bytes 1572872 | tf_op jit(solution)/shard_map/ppermute | solution.py:212
  70.3 9.0 %collective-permute-start.1 = (bf16[512,256]{1,0:T(8,128)(2,1)S(1)}, bf16[512,256]{1,0:T(8,128)(2,1)S(1)}, u32[]{:S(2)}, u32[]{:S(2)}) collective-permute-start(bf16[512,256]{1,0:T(8,128)(2,1)S(1)} %copy-done), channel_id=1, source_target_pairs={{0,2},{1,3},{2,0},{3,1},{4,6},{5,7},{6,4},{7,5},{8,10},{9,11},{10,... | collective-permute-start | bytes 786440 | tf_op jit(solution)/shard_map/ppermute | solution.py:263
  74.4 10.9 %collective-permute-start.2 = (bf16[512,256]{1,0:T(8,128)(2,1)S(1)}, bf16[512,256]{1,0:T(8,128)(2,1)S(1)}, u32[]{:S(2)}, u32[]{:S(2)}) collective-permute-start(bf16[512,256]{1,0:T(8,128)(2,1)S(1)} %copy-done), channel_id=1, source_target_pairs={{0,1},{1,2},{2,3},{3,0},{4,5},{5,6},{6,7},{7,4},{8,9},{9,10},{10,1... | collective-permute-start | bytes 786440 | tf_op jit(solution)/shard_map/ppermute | solution.py:263
  76.4 12.1 %collective-permute-start.18 = (bf16[2,256,256]{2,1,0:T(8,128)(2,1)S(1)}, bf16[2,256,256]{2,1,0:T(8,128)(2,1)S(1)}, u32[]{:S(2)}, u32[]{:S(2)}) collective-permute-start(bf16[2,256,256]{2,1,0:T(8,128)(2,1)S(1)} %get-tuple-element.25), channel_id=1, source_target_pairs={{0,8},{8,16},{16,24},{24,0},{1,9},{9,17},{17,25},{25,1},{2,10},{10... | collective-permute-start | bytes 786440 | tf_op jit(solution)/shard_map/ppermute | solution.py:208
  79.4 9.6 %collective-permute-start.20 = (bf16[2,256,256]{2,1,0:T(8,128)(2,1)S(1)}, bf16[2,256,256]{2,1,0:T(8,128)(2,1)S(1)}, u32[]{:S(2)}, u32[]{:S(2)}) collective-permute-start(bf16[2,256,256]{2,1,0:T(8,128)(2,1)S(1)} %get-tuple-element.26), channel_id=1, source_target_pairs={{0,24},{8,0},{16,8},{24,16},{1,25},{9,1},{17,9},{25,17},{2,26},{10... | collective-permute-start | bytes 786440 | tf_op jit(solution)/shard_map/ppermute | solution.py:208
  85.3 7.4 %collective-permute-start.11 = (bf16[2,256,256]{2,1,0:T(8,128)(2,1)S(1)}, bf16[2,256,256]{2,1,0:T(8,128)(2,1)S(1)}, u32[]{:S(2)}, u32[]{:S(2)}) collective-permute-start(bf16[2,256,256]{2,1,0:T(8,128)(2,1)S(1)} %get-tuple-element.24), channel_id=1, source_target_pairs={{0,96},{32,0},{64,32},{96,64},{1,97},{33,1},{65,33},{97,65},{2,98}... | collective-permute-start | bytes 786440 | tf_op jit(solution)/shard_map/ppermute | solution.py:208
  87.6 11.3 %collective-permute-start.23 = (bf16[4,256,256]{2,1,0:T(8,128)(2,1)S(1)}, bf16[4,256,256]{2,1,0:T(8,128)(2,1)S(1)}, u32[]{:S(2)}, u32[]{:S(2)}) collective-permute-start(bf16[4,256,256]{2,1,0:T(8,128)(2,1)S(1)} %collective-permute-done.7.back_ref.refs_1_), channel_id=1, source_target_pairs={{0,4},{4,0},{1,5},{5,1},{2,6},{6,2},{3,7},{7,3},{8,12},{12,8},{9,1... | collective-permute-start | bytes 1572872 | tf_op jit(solution)/shard_map/ppermute | solution.py:212
  88.4 10.5 %collective-permute-start.24 = (bf16[4,256,256]{2,1,0:T(8,128)(2,1)S(1)}, bf16[4,256,256]{2,1,0:T(8,128)(2,1)S(1)}, u32[]{:S(2)}, u32[]{:S(2)}) collective-permute-start(bf16[4,256,256]{2,1,0:T(8,128)(2,1)S(1)} %collective-permute-done.8.on_ref.refs_2_), channel_id=1, source_target_pairs={{0,4},{4,0},{1,5},{5,1},{2,6},{6,2},{3,7},{7,3},{8,12},{12,8},{9,1... | collective-permute-start | bytes 1572872 | tf_op jit(solution)/shard_map/ppermute | solution.py:212
  88.5 10.9 %collective-permute-start.26 = (bf16[4,256,256]{2,1,0:T(8,128)(2,1)S(1)}, bf16[4,256,256]{2,1,0:T(8,128)(2,1)S(1)}, u32[]{:S(2)}, u32[]{:S(2)}) collective-permute-start(bf16[4,256,256]{2,1,0:T(8,128)(2,1)S(1)} %collective-permute-done.16.back_ref.refs_4_), channel_id=1, source_target_pairs={{0,4},{4,0},{1,5},{5,1},{2,6},{6,2},{3,7},{7,3},{8,12},{12,8},{9,1... | collective-permute-start | bytes 1572872 | tf_op jit(solution)/shard_map/ppermute | solution.py:212
  89.0 9.0 %collective-permute-start.9 = (bf16[2,256,256]{2,1,0:T(8,128)(2,1)S(1)}, bf16[2,256,256]{2,1,0:T(8,128)(2,1)S(1)}, u32[]{:S(2)}, u32[]{:S(2)}) collective-permute-start(bf16[2,256,256]{2,1,0:T(8,128)(2,1)S(1)} %get-tuple-element.23), channel_id=1, source_target_pairs={{0,32},{32,64},{64,96},{96,0},{1,33},{33,65},{65,97},{97,1},{2,34}... | collective-permute-start | bytes 786440 | tf_op jit(solution)/shard_map/ppermute | solution.py:208
  92.7 12.0 %collective-permute-start.27 = (bf16[4,256,256]{2,1,0:T(8,128)(2,1)S(1)}, bf16[4,256,256]{2,1,0:T(8,128)(2,1)S(1)}, u32[]{:S(2)}, u32[]{:S(2)}) collective-permute-start(bf16[4,256,256]{2,1,0:T(8,128)(2,1)S(1)} %collective-permute-done.17.on_ref.refs_5_), channel_id=1, source_target_pairs={{0,4},{4,0},{1,5},{5,1},{2,6},{6,2},{3,7},{7,3},{8,12},{12,8},{9,1... | collective-permute-start | bytes 1572872 | tf_op jit(solution)/shard_map/ppermute | solution.py:212
  97.9 9.1 %collective-permute-start.19 = (bf16[2,256,256]{2,1,0:T(8,128)(2,1)S(1)}, bf16[2,256,256]{2,1,0:T(8,128)(2,1)S(1)}, u32[]{:S(2)}, u32[]{:S(2)}) collective-permute-start(bf16[2,256,256]{2,1,0:T(8,128)(2,1)S(1)} %collective-permute-done.18.za), channel_id=1, source_target_pairs={{0,4},{4,0},{1,5},{5,1},{2,6},{6,2},{3,7},{7,3},{8,12},{12,8},{9,1... | collective-permute-start | bytes 786440 | tf_op jit(solution)/shard_map/ppermute | solution.py:212
  98.9 8.2 %collective-permute-start.21 = (bf16[2,256,256]{2,1,0:T(8,128)(2,1)S(1)}, bf16[2,256,256]{2,1,0:T(8,128)(2,1)S(1)}, u32[]{:S(2)}, u32[]{:S(2)}) collective-permute-start(bf16[2,256,256]{2,1,0:T(8,128)(2,1)S(1)} %collective-permute-done.20.zb), channel_id=1, source_target_pairs={{0,4},{4,0},{1,5},{5,1},{2,6},{6,2},{3,7},{7,3},{8,12},{12,8},{9,1... | collective-permute-start | bytes 786440 | tf_op jit(solution)/shard_map/ppermute | solution.py:212
  98.9 8.2 %collective-permute-start.10 = (bf16[2,256,256]{2,1,0:T(8,128)(2,1)S(1)}, bf16[2,256,256]{2,1,0:T(8,128)(2,1)S(1)}, u32[]{:S(2)}, u32[]{:S(2)}) collective-permute-start(bf16[2,256,256]{2,1,0:T(8,128)(2,1)S(1)} %collective-permute-done.9.xa), channel_id=1, source_target_pairs={{0,4},{4,0},{1,5},{5,1},{2,6},{6,2},{3,7},{7,3},{8,12},{12,8},{9,1... | collective-permute-start | bytes 786440 | tf_op jit(solution)/shard_map/ppermute | solution.py:212
  99.4 7.7 %collective-permute-start.12 = (bf16[2,256,256]{2,1,0:T(8,128)(2,1)S(1)}, bf16[2,256,256]{2,1,0:T(8,128)(2,1)S(1)}, u32[]{:S(2)}, u32[]{:S(2)}) collective-permute-start(bf16[2,256,256]{2,1,0:T(8,128)(2,1)S(1)} %collective-permute-done.11.xb), channel_id=1, source_target_pairs={{0,4},{4,0},{1,5},{5,1},{2,6},{6,2},{3,7},{7,3},{8,12},{12,8},{9,1... | collective-permute-start | bytes 786440 | tf_op jit(solution)/shard_map/ppermute | solution.py:212
  109.6 13.6 %all-to-all-start.1 = ((f32[128,1,256]{2,1,0:T(1,128)}), f32[128,1,256]{2,1,0:T(1,128)S(1)}, u32[]{:S(2)}, u32[]{:S(2)}) async-start(f32[128,1,256]{2,1,0:T(1,128)} %get-tuple-element.30), calls=%async_computation.1 | async-start | bytes 262144 | tf_op jit(solution)/shard_map/all_to_all | solution.py:44

commit v7 on v6

--- a/solution.py
+++ b/solution.py
@@ -19,6 +19,7 @@
 STACK = 2 * WIDTH + 16
 PART = WIDTH + 16
 LANES = 128
+ROWS = 64
 
 
 def place(x, y, z, c):
@@ -214,11 +215,11 @@
 
 def finish(where, got, last, sym, visit_cols, visit_rows):
     def kernel(where_ref, got_ref, last_ref, sym_ref, visit_col_ref, visit_row_ref,
-               out_ref, share_ref, total_ref, row_ref, scale_ref):
-        g = pl.program_id(0)
+               out_ref, share_ref, total_ref, row_ref, scale_ref, col_ref):
+        step = pl.program_id(0)
         x, y, z, c = (where_ref[i] for i in range(4))
 
-        @pl.when(g == 0)
+        @pl.when(step == 0)
         def _():
             w = (x * 4 + z) * 2 + c
             total_ref[...] = sum(last_ref[32 * k:32 * k + 32] for k in range(4))
@@ -228,30 +229,36 @@
             share_ref[...] = STATES * own / grand
             total_ref[...] = sum(got_ref[32 * k:32 * k + 32] for k in range(4))
             row_ref[...] = jnp.broadcast_to(visit_row_ref[...] / total_ref[w], (LANES, WIDTH)).T
-
-        col = visit_col_ref[pl.ds(g, 1), :] / total_ref[y * GROUPS + g]
-        for lo in range(0, WIDTH, LANES):
-            out_ref[:, lo:lo + LANES] = scale_ref[...] * sym_ref[:, lo:lo + LANES] / (
-                row_ref[...] + col[:, lo:lo + LANES])
-
+            for g in range(GROUPS):
+                col_ref[g:g + 1, :] = visit_col_ref[g:g + 1, :] / total_ref[y * GROUPS + g]
+
+        rows = pl.ds(pl.multiple_of(step * ROWS, ROWS), ROWS)
+        for k in range(COLS // LANES):
+            lo = k * LANES
+            g, at = divmod(lo, WIDTH)
+            out_ref[:, lo:lo + LANES] = scale_ref[rows, :] * sym_ref[:, lo:lo + LANES] / (
+                row_ref[rows, :] + col_ref[g:g + 1, at:at + LANES])
+
+    block = pl.BlockSpec((ROWS, COLS), lambda i: (i, 0))
     return pl.pallas_call(
         kernel,
-        grid=(GROUPS,),
-        in_specs=[SMEM, VMEM, VMEM, pl.BlockSpec((WIDTH, WIDTH), lambda g: (0, g)), VMEM, VMEM],
-        out_specs=[pl.BlockSpec((WIDTH, WIDTH), lambda g: (0, g)),
-                   pl.BlockSpec((1, WIDTH), lambda g: (0, 0))],
+        grid=(WIDTH // ROWS,),
+        in_specs=[SMEM, VMEM, VMEM, block, VMEM, VMEM],
+        out_specs=[block, pl.BlockSpec((1, WIDTH), lambda i: (0, 0))],
         out_shape=[f32(WIDTH, COLS), f32(1, WIDTH)],
-        scratch_shapes=[pltpu.VMEM((32, 1, WIDTH), jnp.float32)] + [pltpu.VMEM((WIDTH, LANES), jnp.float32)] * 2,
+        scratch_shapes=[pltpu.VMEM((32, 1, WIDTH), jnp.float32)]
+        + [pltpu.VMEM((WIDTH, LANES), jnp.float32)] * 2 + [pltpu.VMEM((GROUPS, WIDTH), jnp.float32)],
         compiler_params=pltpu.CompilerParams(vmem_limit_bytes=16 << 20),
     )(where, got, last, sym, visit_cols, visit_rows)
 
 
 def shards(member):
-    where = jnp.stack([lax.axis_index(a) for a in ("x", "y", "z", "c")])
-    x, y, z, c = (where[i] for i in range(4))
+    x, y, z, c = (lax.axis_index(a) for a in ("x", "y", "z", "c"))
+    where = jnp.stack([x, y, z, c])
     moved = lax.ppermute(member, ALL, across())
     part = jnp.sum(member, axis=1, dtype=jnp.float32)
-    part, where = lax.optimization_barrier((part, where))
+    w, first = (v.astype(jnp.uint32) for v in ((x * 4 + z) * 2 + c, y * GROUPS))
+    part, where, w, first = lax.optimization_barrier((part, where, w, first))
     frames = to_all(jnp.broadcast_to(part, (128, 1, BLOCK)))
     once_x = jnp.stack(ring(moved[:FIRST], "z"))
     once_z = jnp.stack(ring(moved[FIRST:], "x"))
@@ -269,12 +276,11 @@
     own = far(where, left, far_x, far_z, own)
     far_x, far_z = swapped(far_x), swapped(far_z)
     sym, visit_cols, send = far_and_first(where, left, far_x, far_z, sibling, own, ratio_rows)
-    w, first = (x * 4 + z) * 2 + c, y * GROUPS
     for _ in range(2):
         got = to_all(send)
         totals = jnp.sum(got.reshape(4, 32, WIDTH), axis=0)
-        total_rows = lax.dynamic_slice_in_dim(totals, w, 1).reshape(WIDTH)
-        total_cols = lax.dynamic_slice_in_dim(totals, first, GROUPS)
+        total_rows = lax.dynamic_slice(totals, (w, jnp.uint32(0)), (1, WIDTH)).reshape(WIDTH)
+        total_cols = lax.dynamic_slice(totals, (first, jnp.uint32(0)), (GROUPS, WIDTH))
         ratio_rows = visit_rows.reshape(WIDTH) / total_rows
         ratio = ratio_rows[:, None] + (visit_cols / total_cols).reshape(COLS)[None, :]
         send = jnp.broadcast_to(jnp.sum(sym / ratio, axis=1), (128, 1, WIDTH))

time: 157 us -> 155 us (0.987)
  blocking collectives: 28.2 us -> 41.9 us
  waiting for transfers between devices: 46.8 us -> 37 us
  starting transfers between devices: 62.5 us -> 58.6 us
  Pallas kernels: 15 us -> 13.2 us
    all_to_all x2 -> x3, blocking collectives: 28.2 us -> 41.9 us  [to_all(): return lax.all_to_all(sent, ('y',) + WIDE, 0, 0)]
    all_to_all x2 -> x1, waiting for transfers between devices: 14 us -> 4.22 us  [to_all(): return lax.all_to_all(sent, ('y',) + WIDE, 0, 0)]
    all_to_all x2 -> x1, starting transfers between devices: 14.6 us -> 10.8 us  [to_all(): return lax.all_to_all(sent, ('y',) + WIDE, 0, 0)]
  transfers between devices with their start and end apart: 30 -> 29, of which waited for: 10 -> 9; matrix products, arithmetic and copies ran while one was open for 1% -> 1% of each run, Pallas kernels for 5% -> 5%
where the time goes in v7:
time: 155 us
  starting transfers between devices  58.6 us (38%)
  blocking collectives  41.9 us (27%)
  waiting for transfers between devices  37 us (24%)
  Pallas kernels  13.2 us (9%)
  other arithmetic  2.26 us (1%)
    all_to_all x3, blocking collectives, to_all(): return lax.all_to_all(sent, ('y',) + WIDE, 0, 0)  41.9 us
    ppermute x6, starting transfers between devices, ring(): return [v] + [lax.ppermute(v, axis, along(k)) for k in (1, 2, 3)]  25.6 us
    ppermute x6, waiting for transfers between devices, ring(): return [v] + [lax.ppermute(v, axis, along(k)) for k in (1, 2, 3)]  12.7 us
    all_to_all x1, starting transfers between devices, to_all(): return lax.all_to_all(sent, ('y',) + WIDE, 0, 0)  10.8 us
    ppermute x3, waiting for transfers between devices, shards(): blocks = [member] + [lax.ppermute(kept, 'y', along(-k)) for k in (1, 2, 3)]  10.7 us
    pallas_call x6, Pallas kernels, call(): pl.pallas_call(kernel, in_specs=[SMEM] + [VMEM] * (len(operands) - 1), ou...  9.22 us
    ppermute x10, starting transfers between devices, swapped(): return [lax.ppermute(v, 'c', [(0, 1), (1, 0)]) for v in vs]  6.35 us
    ppermute x3, starting transfers between devices, shards(): blocks = [member] + [lax.ppermute(kept, 'y', along(-k)) for k in (1, 2, 3)]  5.75 us
  transfers between devices with their start and end apart: 29, of which 9 were waited for; matrix products, arithmetic and copies ran while one was open for 1% of the time, Pallas kernels for 5%

profile of v7, /device:TPU:1, one launch (start us, length us, event | category | flops | bytes accessed | tf_op | source)
XLA Modules:
  0.0 155.0 jit_solution(7895614881510618293)
XLA Ops:
  0.6 1.7 %collective-permute-start.3 = (bf16[512,256]{1,0:T(8,128)(2,1)}, bf16[512,256]{1,0:T(8,128)(2,1)S(1)}, u32[]{:S(2)}, u32[]{:S(2)}) collective-permute-start(bf16[512,256]{1,0:T(8,128)(2,1)} %refs_0_.1), channel_id=1, source_target_pairs={{0,0},{4,4},{8,8},{12,12},{16,16},{20,20},{24,24},{28,28},{1,32},{... | collective-permute-start | bytes 786440 | tf_op jit(solution)/shard_map/ppermute | solution.py:258
  2.4 18.8 %collective-permute-start.14 = (bf16[256,256]{1,0:T(8,128)(2,1)S(1)}, bf16[256,256]{1,0:T(8,128)(2,1)S(1)}, u32[]{:S(2)}, u32[]{:S(2)}) collective-permute-start(bf16[256,256]{1,0:T(8,128)(2,1)S(1)} %get-tuple-element.40), channel_id=1, source_target_pairs={{0,64},{32,96},{64,0},{96,32},{1,65},{33,97},{65,1},{97,33},{2,66}... | collective-permute-start | bytes 393224 | tf_op jit(solution)/shard_map/ppermute | solution.py:41
  25.0 10.8 %all-to-all-start = ((f32[128,1,512]{2,1,0:T(1,128)}), f32[128,1,512]{2,1,0:T(1,128)S(1)}, u32[]{:S(2)}, u32[]{:S(2)}) async-start(f32[128,1,512]{2,1,0:T(1,128)} %broadcast_in_dim.11), calls=%async_computation | async-start | bytes 524288 | tf_op jit(solution)/shard_map/all_to_all | solution.py:45
  36.0 1.6 %collective-permute-start.16 = (bf16[4,256,256]{2,1,0:T(8,128)(2,1)S(1)}, bf16[4,256,256]{2,1,0:T(8,128)(2,1)S(1)}, u32[]{:S(2)}, u32[]{:S(2)}) collective-permute-start(bf16[4,256,256]{2,1,0:T(8,128)(2,1)S(1)} %pad_maximum_fusion.1.refs_3_), channel_id=1, source_target_pairs={{0,8},{8,16},{16,24},{24,0},{1,9},{9,17},{17,25},{25,1},{2,10},{10... | collective-permute-start | bytes 1572872 | tf_op jit(solution)/shard_map/ppermute | solution.py:199
  37.5 1.5 collective-permute-start.4
  39.0 1.6 %collective-permute-start.5 = (bf16[256,256]{1,0:T(8,128)(2,1)S(1)}, bf16[256,256]{1,0:T(8,128)(2,1)S(1)}, u32[]{:S(2)}, u32[]{:S(2)}) collective-permute-start(bf16[256,256]{1,0:T(8,128)(2,1)S(1)} %get-tuple-element.41), channel_id=1, source_target_pairs={{0,16},{8,24},{16,0},{24,8},{1,17},{9,25},{17,1},{25,9},{2,18},{10... | collective-permute-start | bytes 393224 | tf_op jit(solution)/shard_map/ppermute | solution.py:41
  40.5 2.0 %collective-permute-start.6 = (bf16[256,256]{1,0:T(8,128)(2,1)S(1)}, bf16[256,256]{1,0:T(8,128)(2,1)S(1)}, u32[]{:S(2)}, u32[]{:S(2)}) collective-permute-start(bf16[256,256]{1,0:T(8,128)(2,1)S(1)} %get-tuple-element.41), channel_id=1, source_target_pairs={{0,24},{8,0},{16,8},{24,16},{1,25},{9,1},{17,9},{25,17},{2,26},{10... | collective-permute-start | bytes 393224 | tf_op jit(solution)/shard_map/ppermute | solution.py:41
  42.5 4.2 %all-to-all-done.refs_4_ = f32[128,1,512]{2,1,0:T(1,128)S(1)} async-done(((f32[128,1,512]{2,1,0:T(1,128)}), f32[128,1,512]{2,1,0:T(1,128)S(1)}, u32[]{:S(2)}, u32[]{:S(2)}) %all-to-all-start) | async-done | bytes 262176 | tf_op jit(solution)/shard_map/all_to_all | solution.py:45
  47.8 8.7 %collective-permute-done.4 = bf16[256,256]{1,0:T(8,128)(2,1)S(1)} collective-permute-done((bf16[256,256]{1,0:T(8,128)(2,1)S(1)}, bf16[256,256]{1,0:T(8,128)(2,1)S(1)}, u32[]{:S(2)}, u32[]{:S(2)}) %collective-permute-start.4) | collective-permute-done | bytes 131104 | tf_op jit(solution)/shard_map/ppermute | solution.py:41
  56.4 4.1 %collective-permute-done.5 = bf16[256,256]{1,0:T(8,128)(2,1)S(1)} collective-permute-done((bf16[256,256]{1,0:T(8,128)(2,1)S(1)}, bf16[256,256]{1,0:T(8,128)(2,1)S(1)}, u32[]{:S(2)}, u32[]{:S(2)}) %collective-permute-start.5) | collective-permute-done | bytes 131104 | tf_op jit(solution)/shard_map/ppermute | solution.py:41
  61.6 2.1 %collective-permute-start = (bf16[512,256]{1,0:T(8,128)(2,1)S(1)}, bf16[512,256]{1,0:T(8,128)(2,1)S(1)}, u32[]{:S(2)}, u32[]{:S(2)}) collective-permute-start(bf16[512,256]{1,0:T(8,128)(2,1)S(1)} %copy-done), channel_id=1, source_target_pairs={{0,3},{1,0},{2,1},{3,2},{4,7},{5,4},{6,5},{7,6},{8,11},{9,8},{10,9... | collective-permute-start | bytes 786440 | tf_op jit(solution)/shard_map/ppermute | solution.py:270
  63.7 2.0 %collective-permute-start.8 = (bf16[4,256,256]{2,1,0:T(8,128)(2,1)S(1)}, bf16[4,256,256]{2,1,0:T(8,128)(2,1)S(1)}, u32[]{:S(2)}, u32[]{:S(2)}) collective-permute-start(bf16[4,256,256]{2,1,0:T(8,128)(2,1)S(1)} %pad_maximum_fusion.refs_0_), channel_id=1, source_target_pairs={{0,96},{32,0},{64,32},{96,64},{1,97},{33,1},{65,33},{97,65},{2,98}... | collective-permute-start | bytes 1572872 | tf_op jit(solution)/shard_map/ppermute | solution.py:199
  65.7 2.9 %collective-permute-done.refs_1_ = bf16[512,256]{1,0:T(8,128)(2,1)S(1)} collective-permute-done((bf16[512,256]{1,0:T(8,128)(2,1)S(1)}, bf16[512,256]{1,0:T(8,128)(2,1)S(1)}, u32[]{:S(2)}, u32[]{:S(2)}) %collective-permute-start) | collective-permute-done | bytes 262176 | tf_op jit(solution)/shard_map/ppermute | solution.py:270
  68.6 1.7 %collective-permute-start.22 = (bf16[4,256,256]{2,1,0:T(8,128)(2,1)S(1)}, bf16[4,256,256]{2,1,0:T(8,128)(2,1)S(1)}, u32[]{:S(2)}, u32[]{:S(2)}) collective-permute-start(bf16[4,256,256]{2,1,0:T(8,128)(2,1)S(1)} %pad_maximum_fusion.refs_0_), channel_id=1, source_target_pairs={{0,4},{4,0},{1,5},{5,1},{2,6},{6,2},{3,7},{7,3},{8,12},{12,8},{9,1... | collective-permute-start | bytes 1572872 | tf_op jit(solution)/shard_map/ppermute | solution.py:213
  70.3 2.3 %collective-permute-start.1 = (bf16[512,256]{1,0:T(8,128)(2,1)S(1)}, bf16[512,256]{1,0:T(8,128)(2,1)S(1)}, u32[]{:S(2)}, u32[]{:S(2)}) collective-permute-start(bf16[512,256]{1,0:T(8,128)(2,1)S(1)} %copy-done), channel_id=1, source_target_pairs={{0,2},{1,3},{2,0},{3,1},{4,6},{5,7},{6,4},{7,5},{8,10},{9,11},{10,... | collective-permute-start | bytes 786440 | tf_op jit(solution)/shard_map/ppermute | solution.py:270
  72.6 1.8 %collective-permute-done.7.back_ref.refs_1_ = bf16[4,256,256]{2,1,0:T(8,128)(2,1)S(1)} collective-permute-done((bf16[4,256,256]{2,1,0:T(8,128)(2,1)S(1)}, bf16[4,256,256]{2,1,0:T(8,128)(2,1)S(1)}, u32[]{:S(2)}, u32[]{:S(2)}) %collective-permute-start.7) | collective-permute-done | bytes 524320 | tf_op jit(solution)/shard_map/ppermute | solution.py:199
  74.4 1.4 collective-permute-start.2
  77.1 2.3 %collective-permute-done.1.refs_2_ = bf16[512,256]{1,0:T(8,128)(2,1)S(1)} collective-permute-done((bf16[512,256]{1,0:T(8,128)(2,1)S(1)}, bf16[512,256]{1,0:T(8,128)(2,1)S(1)}, u32[]{:S(2)}, u32[]{:S(2)}) %collective-permute-start.1) | collective-permute-done | bytes 262176 | tf_op jit(solution)/shard_map/ppermute | solution.py:270
  79.8 5.5 %collective-permute-done.2.refs_3_ = bf16[512,256]{1,0:T(8,128)(2,1)S(1)} collective-permute-done((bf16[512,256]{1,0:T(8,128)(2,1)S(1)}, bf16[512,256]{1,0:T(8,128)(2,1)S(1)}, u32[]{:S(2)}, u32[]{:S(2)}) %collective-permute-start.2) | collective-permute-done | bytes 262176 | tf_op jit(solution)/shard_map/ppermute | solution.py:270
  85.3 2.2 %collective-permute-start.11 = (bf16[2,256,256]{2,1,0:T(8,128)(2,1)S(1)}, bf16[2,256,256]{2,1,0:T(8,128)(2,1)S(1)}, u32[]{:S(2)}, u32[]{:S(2)}) collective-permute-start(bf16[2,256,256]{2,1,0:T(8,128)(2,1)S(1)} %get-tuple-element.26), channel_id=1, source_target_pairs={{0,96},{32,0},{64,32},{96,64},{1,97},{33,1},{65,33},{97,65},{2,98}... | collective-permute-start | bytes 786440 | tf_op jit(solution)/shard_map/ppermute | solution.py:209
  89.0 3.7 %collective-permute-done.11.xb = bf16[2,256,256]{2,1,0:T(8,128)(2,1)S(1)} collective-permute-done((bf16[2,256,256]{2,1,0:T(8,128)(2,1)S(1)}, bf16[2,256,256]{2,1,0:T(8,128)(2,1)S(1)}, u32[]{:S(2)}, u32[]{:S(2)}) %collective-permute-start.11) | collective-permute-done | bytes 262176 | tf_op jit(solution)/shard_map/ppermute | solution.py:209
  92.7 1.5 collective-permute-start.27
  94.3 3.7 %collective-permute-done.9.xa = bf16[2,256,256]{2,1,0:T(8,128)(2,1)S(1)} collective-permute-done((bf16[2,256,256]{2,1,0:T(8,128)(2,1)S(1)}, bf16[2,256,256]{2,1,0:T(8,128)(2,1)S(1)}, u32[]{:S(2)}, u32[]{:S(2)}) %collective-permute-start.9) | collective-permute-done | bytes 262176 | tf_op jit(solution)/shard_map/ppermute | solution.py:209
  99.7 1.3 shard_map.30
  100.9 2.4 %shard_map.34.near_ref = f32[4,272,256]{2,1,0:T(8,128)S(1)} custom-call(s32[4]{0:T(128)S(1)} %pad_add_fusion.where_ref._, bf16[528,2048]{1,0:T(8,128)(2,1)S(1)} %get-tuple-element.24.left_ref, bf16[4,256,256]{2,1,0:T(8,128)(2,1)S(1)} %pad_maximum_fusion.refs_0_, bf16[4,256,256]{2,1,0:T(8,128)(2,1)S(1)} %collective-permute-done.7.back_ref.refs_1_, ...), custom_call_target="tpu_custom_call" | custom-call | tf_op jit(solution)/shard_map/pallas_call | solution.py:73
  103.4 1.3 shard_map.35.own_ref
  104.7 2.4 %shard_map.33.near_ref = f32[4,272,256]{2,1,0:T(8,128)S(1)} custom-call(s32[4]{0:T(128)S(1)} %pad_add_fusion.where_ref._, bf16[528,2048]{1,0:T(8,128)(2,1)S(1)} %get-tuple-element.24.left_ref, bf16[4,256,256]{2,1,0:T(8,128)(2,1)S(1)} %collective-permute-done.22.refs_0_, bf16[4,256,256]{2,1,0:T(8,128)(2,1)S(1)} %collective-permute-done.23.refs_1_, ...), custom_call_target="tpu_custom_call" | custom-call | tf_op jit(solution)/shard_map/pallas_call | solution.py:73
  107.1 2.0 %shard_map.36 = (f32[256,2048]{1,0:T(8,128)S(1)}, f32[8,256]{1,0:T(8,128)S(1)}, f32[128,1,256]{2,1,0:T(1,128)S(1)}, f32[8,256]{1,0:T(8,128)}) custom-call(s32[4]{0:T(128)S(1)} %pad_add_fusion.where_ref._, bf16[528,2048]{1,0:T(8,128)(2,1)S(1)} %get-tuple-element.24.left_ref, bf16[2,256,256]{2,1,0:T(8,128)(2,1)S(1)} %collective-permute-done.10.xa, ...), custom_call_target="tpu_custom_call" | custom-call | tf_op jit(solution)/shard_map/pallas_call | solution.py:73
  109.1 13.6 %all_to_all.20 = f32[128,1,256]{2,1,0:T(1,128)S(1)} all-to-all(f32[128,1,256]{2,1,0:T(1,128)S(1)} %get-tuple-element.32), channel_id=1, replica_groups=mesh['x'=4,'z'=4,'c'=2,'y'=4] {'y','x','z','c'}, dimensions={0} | all-to-all | bytes 262144 | tf_op jit(solution)/shard_map/all_to_all | solution.py:45
  123.3 14.2 %all_to_all.21.got_ref = f32[128,1,256]{2,1,0:T(1,128)S(1)} all-to-all(f32[128,1,256]{2,1,0:T(1,128)S(1)} %broadcast_in_dim.12), channel_id=1, replica_groups=mesh['x'=4,'z'=4,'c'=2,'y'=4] {'y','x','z','c'}, dimensions={0} | all-to-all | bytes 262144 | tf_op jit(solution)/shard_map/all_to_all | solution.py:45
  138.1 14.2 %all_to_all.22.last_ref = f32[128,1,256]{2,1,0:T(1,128)S(1)} all-to-all(f32[128,1,256]{2,1,0:T(1,128)S(1)} %broadcast_in_dim.13), channel_id=1, replica_groups=mesh['x'=4,'z'=4,'c'=2,'y'=4] {'y','x','z','c'}, dimensions={0} | all-to-all | bytes 262144 | tf_op jit(solution)/shard_map/all_to_all | solution.py:45
  152.2 2.7 %shard_map.37 = (f32[256,2048]{1,0:T(8,128)}, f32[1,256]{1,0:T(1,128)}) custom-call(s32[4]{0:T(128)S(1)} %pad_add_fusion.where_ref._, f32[128,1,256]{2,1,0:T(1,128)S(1)} %all_to_all.21.got_ref, f32[128,1,256]{2,1,0:T(1,128)S(1)} %all_to_all.22.last_ref, f32[256,2048]{1,0:T(8,128)S(1)} %get-tuple-element.30.sym_ref, ...), custom_call_target="tpu_custom_call" | custom-call | tf_op jit(solution)/shard_map/pallas_call | solution.py:243
  (59 shorter events, 11.9 us)
Async XLA Ops:
  0.6 61.0 %copy-start = (bf16[512,256]{1,0:T(8,128)(2,1)S(1)}, bf16[512,256]{1,0:T(8,128)(2,1)}, u32[]{:S(2)}) copy-start(bf16[512,256]{1,0:T(8,128)(2,1)} %refs_0_.1) | copy-start | bytes 786436
  0.6 1.7 %collective-permute-start.3 = (bf16[512,256]{1,0:T(8,128)(2,1)}, bf16[512,256]{1,0:T(8,128)(2,1)S(1)}, u32[]{:S(2)}, u32[]{:S(2)}) collective-permute-start(bf16[512,256]{1,0:T(8,128)(2,1)} %refs_0_.1), channel_id=1, source_target_pairs={{0,0},{4,4},{8,8},{12,12},{16,16},{20,20},{24,24},{28,28},{1,32},{... | collective-permute-start | bytes 786440 | tf_op jit(solution)/shard_map/ppermute | solution.py:258
  2.4 33.4 %collective-permute-start.14 = (bf16[256,256]{1,0:T(8,128)(2,1)S(1)}, bf16[256,256]{1,0:T(8,128)(2,1)S(1)}, u32[]{:S(2)}, u32[]{:S(2)}) collective-permute-start(bf16[256,256]{1,0:T(8,128)(2,1)S(1)} %get-tuple-element.40), channel_id=1, source_target_pairs={{0,64},{32,96},{64,0},{96,32},{1,65},{33,97},{65,1},{97,33},{2,66}... | collective-permute-start | bytes 393224 | tf_op jit(solution)/shard_map/ppermute | solution.py:41
  21.3 14.6 %collective-permute-start.15 = (bf16[256,256]{1,0:T(8,128)(2,1)S(1)}, bf16[256,256]{1,0:T(8,128)(2,1)S(1)}, u32[]{:S(2)}, u32[]{:S(2)}) collective-permute-start(bf16[256,256]{1,0:T(8,128)(2,1)S(1)} %get-tuple-element.40), channel_id=1, source_target_pairs={{0,96},{32,0},{64,32},{96,64},{1,97},{33,1},{65,33},{97,65},{2,98}... | collective-permute-start | bytes 393224 | tf_op jit(solution)/shard_map/ppermute | solution.py:41
  22.5 13.4 %collective-permute-start.13 = (bf16[256,256]{1,0:T(8,128)(2,1)S(1)}, bf16[256,256]{1,0:T(8,128)(2,1)S(1)}, u32[]{:S(2)}, u32[]{:S(2)}) collective-permute-start(bf16[256,256]{1,0:T(8,128)(2,1)S(1)} %get-tuple-element.40), channel_id=1, source_target_pairs={{0,32},{32,64},{64,96},{96,0},{1,33},{33,65},{65,97},{97,1},{2,34}... | collective-permute-start | bytes 393224 | tf_op jit(solution)/shard_map/ppermute | solution.py:41
  25.0 21.7 %all-to-all-start = ((f32[128,1,512]{2,1,0:T(1,128)}), f32[128,1,512]{2,1,0:T(1,128)S(1)}, u32[]{:S(2)}, u32[]{:S(2)}) async-start(f32[128,1,512]{2,1,0:T(1,128)} %broadcast_in_dim.11), calls=%async_computation | async-start | bytes 524288 | tf_op jit(solution)/shard_map/all_to_all | solution.py:45
  36.0 34.4 %collective-permute-start.16 = (bf16[4,256,256]{2,1,0:T(8,128)(2,1)S(1)}, bf16[4,256,256]{2,1,0:T(8,128)(2,1)S(1)}, u32[]{:S(2)}, u32[]{:S(2)}) collective-permute-start(bf16[4,256,256]{2,1,0:T(8,128)(2,1)S(1)} %pad_maximum_fusion.1.refs_3_), channel_id=1, source_target_pairs={{0,8},{8,16},{16,24},{24,0},{1,9},{9,17},{17,25},{25,1},{2,10},{10... | collective-permute-start | bytes 1572872 | tf_op jit(solution)/shard_map/ppermute | solution.py:199
  37.5 18.9 %collective-permute-start.4 = (bf16[256,256]{1,0:T(8,128)(2,1)S(1)}, bf16[256,256]{1,0:T(8,128)(2,1)S(1)}, u32[]{:S(2)}, u32[]{:S(2)}) collective-permute-start(bf16[256,256]{1,0:T(8,128)(2,1)S(1)} %get-tuple-element.41), channel_id=1, source_target_pairs={{0,8},{8,16},{16,24},{24,0},{1,9},{9,17},{17,25},{25,1},{2,10},{10... | collective-permute-start | bytes 393224 | tf_op jit(solution)/shard_map/ppermute | solution.py:41
  39.0 21.5 %collective-permute-start.5 = (bf16[256,256]{1,0:T(8,128)(2,1)S(1)}, bf16[256,256]{1,0:T(8,128)(2,1)S(1)}, u32[]{:S(2)}, u32[]{:S(2)}) collective-permute-start(bf16[256,256]{1,0:T(8,128)(2,1)S(1)} %get-tuple-element.41), channel_id=1, source_target_pairs={{0,16},{8,24},{16,0},{24,8},{1,17},{9,25},{17,1},{25,9},{2,18},{10... | collective-permute-start | bytes 393224 | tf_op jit(solution)/shard_map/ppermute | solution.py:41
  40.5 20.0 %collective-permute-start.6 = (bf16[256,256]{1,0:T(8,128)(2,1)S(1)}, bf16[256,256]{1,0:T(8,128)(2,1)S(1)}, u32[]{:S(2)}, u32[]{:S(2)}) collective-permute-start(bf16[256,256]{1,0:T(8,128)(2,1)S(1)} %get-tuple-element.41), channel_id=1, source_target_pairs={{0,24},{8,0},{16,8},{24,16},{1,25},{9,1},{17,9},{25,17},{2,26},{10... | collective-permute-start | bytes 393224 | tf_op jit(solution)/shard_map/ppermute | solution.py:41
  46.7 23.6 %collective-permute-start.17 = (bf16[4,256,256]{2,1,0:T(8,128)(2,1)S(1)}, bf16[4,256,256]{2,1,0:T(8,128)(2,1)S(1)}, u32[]{:S(2)}, u32[]{:S(2)}) collective-permute-start(bf16[4,256,256]{2,1,0:T(8,128)(2,1)S(1)} %pad_maximum_fusion.1.refs_3_), channel_id=1, source_target_pairs={{0,24},{8,0},{16,8},{24,16},{1,25},{9,1},{17,9},{25,17},{2,26},{10... | collective-permute-start | bytes 1572872 | tf_op jit(solution)/shard_map/ppermute | solution.py:199
  60.6 13.9 %collective-permute-start.7 = (bf16[4,256,256]{2,1,0:T(8,128)(2,1)S(1)}, bf16[4,256,256]{2,1,0:T(8,128)(2,1)S(1)}, u32[]{:S(2)}, u32[]{:S(2)}) collective-permute-start(bf16[4,256,256]{2,1,0:T(8,128)(2,1)S(1)} %pad_maximum_fusion.refs_0_), channel_id=1, source_target_pairs={{0,32},{32,64},{64,96},{96,0},{1,33},{33,65},{65,97},{97,1},{2,34}... | collective-permute-start | bytes 1572872 | tf_op jit(solution)/shard_map/ppermute | solution.py:199
  61.6 7.0 %collective-permute-start = (bf16[512,256]{1,0:T(8,128)(2,1)S(1)}, bf16[512,256]{1,0:T(8,128)(2,1)S(1)}, u32[]{:S(2)}, u32[]{:S(2)}) collective-permute-start(bf16[512,256]{1,0:T(8,128)(2,1)S(1)} %copy-done), channel_id=1, source_target_pairs={{0,3},{1,0},{2,1},{3,2},{4,7},{5,4},{6,5},{7,6},{8,11},{9,8},{10,9... | collective-permute-start | bytes 786440 | tf_op jit(solution)/shard_map/ppermute | solution.py:270
  63.7 12.7 %collective-permute-start.8 = (bf16[4,256,256]{2,1,0:T(8,128)(2,1)S(1)}, bf16[4,256,256]{2,1,0:T(8,128)(2,1)S(1)}, u32[]{:S(2)}, u32[]{:S(2)}) collective-permute-start(bf16[4,256,256]{2,1,0:T(8,128)(2,1)S(1)} %pad_maximum_fusion.refs_0_), channel_id=1, source_target_pairs={{0,96},{32,0},{64,32},{96,64},{1,97},{33,1},{65,33},{97,65},{2,98}... | collective-permute-start | bytes 1572872 | tf_op jit(solution)/shard_map/ppermute | solution.py:199
  68.6 19.0 %collective-permute-start.22 = (bf16[4,256,256]{2,1,0:T(8,128)(2,1)S(1)}, bf16[4,256,256]{2,1,0:T(8,128)(2,1)S(1)}, u32[]{:S(2)}, u32[]{:S(2)}) collective-permute-start(bf16[4,256,256]{2,1,0:T(8,128)(2,1)S(1)} %pad_maximum_fusion.refs_0_), channel_id=1, source_target_pairs={{0,4},{4,0},{1,5},{5,1},{2,6},{6,2},{3,7},{7,3},{8,12},{12,8},{9,1... | collective-permute-start | bytes 1572872 | tf_op jit(solution)/shard_map/ppermute | solution.py:213
  70.3 18.1 %collective-permute-start.25 = (bf16[4,256,256]{2,1,0:T(8,128)(2,1)S(1)}, bf16[4,256,256]{2,1,0:T(8,128)(2,1)S(1)}, u32[]{:S(2)}, u32[]{:S(2)}) collective-permute-start(bf16[4,256,256]{2,1,0:T(8,128)(2,1)S(1)} %pad_maximum_fusion.1.refs_3_), channel_id=1, source_target_pairs={{0,4},{4,0},{1,5},{5,1},{2,6},{6,2},{3,7},{7,3},{8,12},{12,8},{9,1... | collective-permute-start | bytes 1572872 | tf_op jit(solution)/shard_map/ppermute | solution.py:213
  70.3 9.0 %collective-permute-start.1 = (bf16[512,256]{1,0:T(8,128)(2,1)S(1)}, bf16[512,256]{1,0:T(8,128)(2,1)S(1)}, u32[]{:S(2)}, u32[]{:S(2)}) collective-permute-start(bf16[512,256]{1,0:T(8,128)(2,1)S(1)} %copy-done), channel_id=1, source_target_pairs={{0,2},{1,3},{2,0},{3,1},{4,6},{5,7},{6,4},{7,5},{8,10},{9,11},{10,... | collective-permute-start | bytes 786440 | tf_op jit(solution)/shard_map/ppermute | solution.py:270
  74.4 10.9 %collective-permute-start.2 = (bf16[512,256]{1,0:T(8,128)(2,1)S(1)}, bf16[512,256]{1,0:T(8,128)(2,1)S(1)}, u32[]{:S(2)}, u32[]{:S(2)}) collective-permute-start(bf16[512,256]{1,0:T(8,128)(2,1)S(1)} %copy-done), channel_id=1, source_target_pairs={{0,1},{1,2},{2,3},{3,0},{4,5},{5,6},{6,7},{7,4},{8,9},{9,10},{10,1... | collective-permute-start | bytes 786440 | tf_op jit(solution)/shard_map/ppermute | solution.py:270
  76.4 12.1 %collective-permute-start.18 = (bf16[2,256,256]{2,1,0:T(8,128)(2,1)S(1)}, bf16[2,256,256]{2,1,0:T(8,128)(2,1)S(1)}, u32[]{:S(2)}, u32[]{:S(2)}) collective-permute-start(bf16[2,256,256]{2,1,0:T(8,128)(2,1)S(1)} %get-tuple-element.27), channel_id=1, source_target_pairs={{0,8},{8,16},{16,24},{24,0},{1,9},{9,17},{17,25},{25,1},{2,10},{10... | collective-permute-start | bytes 786440 | tf_op jit(solution)/shard_map/ppermute | solution.py:209
  79.4 9.6 %collective-permute-start.20 = (bf16[2,256,256]{2,1,0:T(8,128)(2,1)S(1)}, bf16[2,256,256]{2,1,0:T(8,128)(2,1)S(1)}, u32[]{:S(2)}, u32[]{:S(2)}) collective-permute-start(bf16[2,256,256]{2,1,0:T(8,128)(2,1)S(1)} %get-tuple-element.28), channel_id=1, source_target_pairs={{0,24},{8,0},{16,8},{24,16},{1,25},{9,1},{17,9},{25,17},{2,26},{10... | collective-permute-start | bytes 786440 | tf_op jit(solution)/shard_map/ppermute | solution.py:209
  85.3 7.4 %collective-permute-start.11 = (bf16[2,256,256]{2,1,0:T(8,128)(2,1)S(1)}, bf16[2,256,256]{2,1,0:T(8,128)(2,1)S(1)}, u32[]{:S(2)}, u32[]{:S(2)}) collective-permute-start(bf16[2,256,256]{2,1,0:T(8,128)(2,1)S(1)} %get-tuple-element.26), channel_id=1, source_target_pairs={{0,96},{32,0},{64,32},{96,64},{1,97},{33,1},{65,33},{97,65},{2,98}... | collective-permute-start | bytes 786440 | tf_op jit(solution)/shard_map/ppermute | solution.py:209
  87.6 11.3 %collective-permute-start.23 = (bf16[4,256,256]{2,1,0:T(8,128)(2,1)S(1)}, bf16[4,256,256]{2,1,0:T(8,128)(2,1)S(1)}, u32[]{:S(2)}, u32[]{:S(2)}) collective-permute-start(bf16[4,256,256]{2,1,0:T(8,128)(2,1)S(1)} %collective-permute-done.7.back_ref.refs_1_), channel_id=1, source_target_pairs={{0,4},{4,0},{1,5},{5,1},{2,6},{6,2},{3,7},{7,3},{8,12},{12,8},{9,1... | collective-permute-start | bytes 1572872 | tf_op jit(solution)/shard_map/ppermute | solution.py:213
  88.4 10.5 %collective-permute-start.24 = (bf16[4,256,256]{2,1,0:T(8,128)(2,1)S(1)}, bf16[4,256,256]{2,1,0:T(8,128)(2,1)S(1)}, u32[]{:S(2)}, u32[]{:S(2)}) collective-permute-start(bf16[4,256,256]{2,1,0:T(8,128)(2,1)S(1)} %collective-permute-done.8.on_ref.refs_2_), channel_id=1, source_target_pairs={{0,4},{4,0},{1,5},{5,1},{2,6},{6,2},{3,7},{7,3},{8,12},{12,8},{9,1... | collective-permute-start | bytes 1572872 | tf_op jit(solution)/shard_map/ppermute | solution.py:213
  88.5 10.9 %collective-permute-start.26 = (bf16[4,256,256]{2,1,0:T(8,128)(2,1)S(1)}, bf16[4,256,256]{2,1,0:T(8,128)(2,1)S(1)}, u32[]{:S(2)}, u32[]{:S(2)}) collective-permute-start(bf16[4,256,256]{2,1,0:T(8,128)(2,1)S(1)} %collective-permute-done.16.back_ref.refs_4_), channel_id=1, source_target_pairs={{0,4},{4,0},{1,5},{5,1},{2,6},{6,2},{3,7},{7,3},{8,12},{12,8},{9,1... | collective-permute-start | bytes 1572872 | tf_op jit(solution)/shard_map/ppermute | solution.py:213
  89.0 9.0 %collective-permute-start.9 = (bf16[2,256,256]{2,1,0:T(8,128)(2,1)S(1)}, bf16[2,256,256]{2,1,0:T(8,128)(2,1)S(1)}, u32[]{:S(2)}, u32[]{:S(2)}) collective-permute-start(bf16[2,256,256]{2,1,0:T(8,128)(2,1)S(1)} %get-tuple-element.25), channel_id=1, source_target_pairs={{0,32},{32,64},{64,96},{96,0},{1,33},{33,65},{65,97},{97,1},{2,34}... | collective-permute-start | bytes 786440 | tf_op jit(solution)/shard_map/ppermute | solution.py:209
  92.7 12.0 %collective-permute-start.27 = (bf16[4,256,256]{2,1,0:T(8,128)(2,1)S(1)}, bf16[4,256,256]{2,1,0:T(8,128)(2,1)S(1)}, u32[]{:S(2)}, u32[]{:S(2)}) collective-permute-start(bf16[4,256,256]{2,1,0:T(8,128)(2,1)S(1)} %collective-permute-done.17.on_ref.refs_5_), channel_id=1, source_target_pairs={{0,4},{4,0},{1,5},{5,1},{2,6},{6,2},{3,7},{7,3},{8,12},{12,8},{9,1... | collective-permute-start | bytes 1572872 | tf_op jit(solution)/shard_map/ppermute | solution.py:213
  97.9 9.1 %collective-permute-start.19 = (bf16[2,256,256]{2,1,0:T(8,128)(2,1)S(1)}, bf16[2,256,256]{2,1,0:T(8,128)(2,1)S(1)}, u32[]{:S(2)}, u32[]{:S(2)}) collective-permute-start(bf16[2,256,256]{2,1,0:T(8,128)(2,1)S(1)} %collective-permute-done.18.za), channel_id=1, source_target_pairs={{0,4},{4,0},{1,5},{5,1},{2,6},{6,2},{3,7},{7,3},{8,12},{12,8},{9,1... | collective-permute-start | bytes 786440 | tf_op jit(solution)/shard_map/ppermute | solution.py:213
  98.9 8.2 %collective-permute-start.21 = (bf16[2,256,256]{2,1,0:T(8,128)(2,1)S(1)}, bf16[2,256,256]{2,1,0:T(8,128)(2,1)S(1)}, u32[]{:S(2)}, u32[]{:S(2)}) collective-permute-start(bf16[2,256,256]{2,1,0:T(8,128)(2,1)S(1)} %collective-permute-done.20.zb), channel_id=1, source_target_pairs={{0,4},{4,0},{1,5},{5,1},{2,6},{6,2},{3,7},{7,3},{8,12},{12,8},{9,1... | collective-permute-start | bytes 786440 | tf_op jit(solution)/shard_map/ppermute | solution.py:213
  98.9 8.2 %collective-permute-start.10 = (bf16[2,256,256]{2,1,0:T(8,128)(2,1)S(1)}, bf16[2,256,256]{2,1,0:T(8,128)(2,1)S(1)}, u32[]{:S(2)}, u32[]{:S(2)}) collective-permute-start(bf16[2,256,256]{2,1,0:T(8,128)(2,1)S(1)} %collective-permute-done.9.xa), channel_id=1, source_target_pairs={{0,4},{4,0},{1,5},{5,1},{2,6},{6,2},{3,7},{7,3},{8,12},{12,8},{9,1... | collective-permute-start | bytes 786440 | tf_op jit(solution)/shard_map/ppermute | solution.py:213
  99.4 7.7 %collective-permute-start.12 = (bf16[2,256,256]{2,1,0:T(8,128)(2,1)S(1)}, bf16[2,256,256]{2,1,0:T(8,128)(2,1)S(1)}, u32[]{:S(2)}, u32[]{:S(2)}) collective-permute-start(bf16[2,256,256]{2,1,0:T(8,128)(2,1)S(1)} %collective-permute-done.11.xb), channel_id=1, source_target_pairs={{0,4},{4,0},{1,5},{5,1},{2,6},{6,2},{3,7},{7,3},{8,12},{12,8},{9,1... | collective-permute-start | bytes 786440 | tf_op jit(solution)/shard_map/ppermute | solution.py:213

commit v8 on v7

--- a/solution.py
+++ b/solution.py
@@ -163,8 +163,8 @@
                 left_ref[:WIDTH, lo:lo + LANES] = turned
             if lo >= 2 * TAU:
                 left_ref[WIDTH:2 * WIDTH, lo - 2 * TAU:lo - 2 * TAU + LANES] = turned
-        total = jnp.concatenate(
-            [jnp.sum(frame_ref[32 * q:32 * q + 32], axis=0) for q in range(4)], axis=1)
+        total = [jnp.sum(frame_ref[32 * q:32 * q + 32].astype(jnp.float32), axis=0) for q in range(4)]
+        total = jnp.concatenate([v[i:i + 1] for v in total for i in range(2)], axis=1)
         total = jnp.broadcast_to(total, (16, FRAMES))
         at = lax.broadcasted_iota(jnp.int32, (16, FRAMES), 1)
         line = lax.broadcasted_iota(jnp.int32, (16, FRAMES), 0)
@@ -259,7 +259,7 @@
     part = jnp.sum(member, axis=1, dtype=jnp.float32)
     w, first = (v.astype(jnp.uint32) for v in ((x * 4 + z) * 2 + c, y * GROUPS))
     part, where, w, first = lax.optimization_barrier((part, where, w, first))
-    frames = to_all(jnp.broadcast_to(part, (128, 1, BLOCK)))
+    frames = to_all(jnp.broadcast_to(part.astype(jnp.bfloat16).reshape(2, WIDTH), (128, 2, WIDTH)))
     once_x = jnp.stack(ring(moved[:FIRST], "z"))
     once_z = jnp.stack(ring(moved[FIRST:], "x"))
     near_x = from_sides(once_x, "x")

time: 155 us -> 151 us (0.974)
  blocking collectives: 41.9 us -> 58.9 us
  waiting for transfers between devices: 37 us -> 21.1 us
  starting transfers between devices: 58.6 us -> 54.5 us
    all_to_all x3 -> x4, blocking collectives: 41.9 us -> 58.9 us  [to_all(): return lax.all_to_all(sent, ('y',) + WIDE, 0, 0)]
    all_to_all x1 -> x0, starting transfers between devices: 10.8 us -> none  [to_all(): return lax.all_to_all(sent, ('y',) + WIDE, 0, 0)]
    ppermute x6, waiting for transfers between devices: 12.7 us -> 3.96 us  [ring(): return [v] + [lax.ppermute(v, axis, along(k)) for k in (1, 2, 3)]]
    ppermute x2, starting transfers between devices: 2.71 us -> 7.11 us  [from_afar(): lax.ppermute(halves[1], axis, along(3))]
    all_to_all x1 -> x0, waiting for transfers between devices: 4.22 us -> none  [to_all(): return lax.all_to_all(sent, ('y',) + WIDE, 0, 0)]
    ppermute x3, waiting for transfers between devices: 10.7 us -> 7.62 us  [shards(): blocks = [member] + [lax.ppermute(kept, 'y', along(-k)) for k in (1, 2, 3)]]
    ppermute x3, starting transfers between devices: 5.75 us -> 7.97 us  [shards(): blocks = [member] + [lax.ppermute(kept, 'y', along(-k)) for k in (1, 2, 3)]]
  transfers between devices with their start and end apart: 29 -> 28, of which waited for: 9 -> 9; matrix products, arithmetic and copies ran while one was open for 1% -> 1% of each run, Pallas kernels for 5% -> 6%
where the time goes in v8:
time: 151 us
  blocking collectives  58.9 us (39%)
  starting transfers between devices  54.5 us (36%)
  waiting for transfers between devices  21.1 us (14%)
  Pallas kernels  13.2 us (9%)
  other arithmetic  2.25 us (1%)
    all_to_all x4, blocking collectives, to_all(): return lax.all_to_all(sent, ('y',) + WIDE, 0, 0)  58.9 us
    ppermute x6, starting transfers between devices, ring(): return [v] + [lax.ppermute(v, axis, along(k)) for k in (1, 2, 3)]  26 us
    pallas_call x6, Pallas kernels, call(): pl.pallas_call(kernel, in_specs=[SMEM] + [VMEM] * (len(operands) - 1), ou...  9.23 us
    ppermute x3, starting transfers between devices, shards(): blocks = [member] + [lax.ppermute(kept, 'y', along(-k)) for k in (1, 2, 3)]  7.97 us
    ppermute x3, waiting for transfers between devices, shards(): blocks = [member] + [lax.ppermute(kept, 'y', along(-k)) for k in (1, 2, 3)]  7.62 us
    ppermute x2, starting transfers between devices, from_afar(): lax.ppermute(halves[1], axis, along(3))  7.11 us
    ppermute x10, starting transfers between devices, swapped(): return [lax.ppermute(v, 'c', [(0, 1), (1, 0)]) for v in vs]  6.02 us
    ppermute x4, starting transfers between devices, from_sides(): return [lax.ppermute(v, axis, along(k)) for k in (1, 3)]  5.6 us
  transfers between devices with their start and end apart: 28, of which 9 were waited for; matrix products, arithmetic and copies ran while one was open for 1% of the time, Pallas kernels for 6%

profile of v8, /device:TPU:1, one launch (start us, length us, event | category | flops | bytes accessed | tf_op | source)
XLA Modules:
  0.0 151.1 jit_solution(10857425845272431324)
XLA Ops:
  0.6 1.7 %collective-permute-start.3 = (bf16[512,256]{1,0:T(8,128)(2,1)}, bf16[512,256]{1,0:T(8,128)(2,1)S(1)}, u32[]{:S(2)}, u32[]{:S(2)}) collective-permute-start(bf16[512,256]{1,0:T(8,128)(2,1)} %refs_0_.1), channel_id=1, source_target_pairs={{0,0},{4,4},{8,8},{12,12},{16,16},{20,20},{24,24},{28,28},{1,32},{... | collective-permute-start | bytes 786440 | tf_op jit(solution)/shard_map/ppermute | solution.py:258
  2.4 18.8 %collective-permute-start.14 = (bf16[256,256]{1,0:T(8,128)(2,1)S(1)}, bf16[256,256]{1,0:T(8,128)(2,1)S(1)}, u32[]{:S(2)}, u32[]{:S(2)}) collective-permute-start(bf16[256,256]{1,0:T(8,128)(2,1)S(1)} %get-tuple-element.40), channel_id=1, source_target_pairs={{0,64},{32,96},{64,0},{96,32},{1,65},{33,97},{65,1},{97,33},{2,66}... | collective-permute-start | bytes 393224 | tf_op jit(solution)/shard_map/ppermute | solution.py:41
  21.3 1.2 collective-permute-start.15
  23.0 1.1 convert_reduce_fusion
  24.1 3.8 %collective-permute-done.15 = bf16[256,256]{1,0:T(8,128)(2,1)S(1)} collective-permute-done((bf16[256,256]{1,0:T(8,128)(2,1)S(1)}, bf16[256,256]{1,0:T(8,128)(2,1)S(1)}, u32[]{:S(2)}, u32[]{:S(2)}) %collective-permute-start.15) | collective-permute-done | bytes 131104 | tf_op jit(solution)/shard_map/ppermute | solution.py:41
  28.1 1.7 %collective-permute-start.16 = (bf16[4,256,256]{2,1,0:T(8,128)(2,1)S(1)}, bf16[4,256,256]{2,1,0:T(8,128)(2,1)S(1)}, u32[]{:S(2)}, u32[]{:S(2)}) collective-permute-start(bf16[4,256,256]{2,1,0:T(8,128)(2,1)S(1)} %pad_maximum_fusion.1.refs_3_), channel_id=1, source_target_pairs={{0,8},{8,16},{16,24},{24,0},{1,9},{9,17},{17,25},{25,1},{2,10},{10... | collective-permute-start | bytes 1572872 | tf_op jit(solution)/shard_map/ppermute | solution.py:199
  29.9 1.6 %collective-permute-start.4 = (bf16[256,256]{1,0:T(8,128)(2,1)S(1)}, bf16[256,256]{1,0:T(8,128)(2,1)S(1)}, u32[]{:S(2)}, u32[]{:S(2)}) collective-permute-start(bf16[256,256]{1,0:T(8,128)(2,1)S(1)} %get-tuple-element.41), channel_id=1, source_target_pairs={{0,8},{8,16},{16,24},{24,0},{1,9},{9,17},{17,25},{25,1},{2,10},{10... | collective-permute-start | bytes 393224 | tf_op jit(solution)/shard_map/ppermute | solution.py:41
  31.6 1.8 %collective-permute-start.5 = (bf16[256,256]{1,0:T(8,128)(2,1)S(1)}, bf16[256,256]{1,0:T(8,128)(2,1)S(1)}, u32[]{:S(2)}, u32[]{:S(2)}) collective-permute-start(bf16[256,256]{1,0:T(8,128)(2,1)S(1)} %get-tuple-element.41), channel_id=1, source_target_pairs={{0,16},{8,24},{16,0},{24,8},{1,17},{9,25},{17,1},{25,9},{2,18},{10... | collective-permute-start | bytes 393224 | tf_op jit(solution)/shard_map/ppermute | solution.py:41
  33.3 2.0 %collective-permute-start.6 = (bf16[256,256]{1,0:T(8,128)(2,1)S(1)}, bf16[256,256]{1,0:T(8,128)(2,1)S(1)}, u32[]{:S(2)}, u32[]{:S(2)}) collective-permute-start(bf16[256,256]{1,0:T(8,128)(2,1)S(1)} %get-tuple-element.41), channel_id=1, source_target_pairs={{0,24},{8,0},{16,8},{24,16},{1,25},{9,1},{17,9},{25,17},{2,26},{10... | collective-permute-start | bytes 393224 | tf_op jit(solution)/shard_map/ppermute | solution.py:41
  35.4 17.5 %all_to_all.20.refs_4_ = bf16[128,2,256]{2,1,0:T(2,128)(2,1)S(1)} all-to-all(bf16[128,2,256]{2,1,0:T(2,128)(2,1)S(1)} %broadcast_in_dim.11), channel_id=1, replica_groups=mesh['x'=4,'z'=4,'c'=2,'y'=4] {'y','x','z','c'}, dimensions={0} | all-to-all | bytes 262144 | tf_op jit(solution)/shard_map/all_to_all | solution.py:45
  54.3 3.3 %collective-permute-start = (bf16[512,256]{1,0:T(8,128)(2,1)S(1)}, bf16[512,256]{1,0:T(8,128)(2,1)S(1)}, u32[]{:S(2)}, u32[]{:S(2)}) collective-permute-start(bf16[512,256]{1,0:T(8,128)(2,1)S(1)} %copy-done), channel_id=1, source_target_pairs={{0,3},{1,0},{2,1},{3,2},{4,7},{5,4},{6,5},{7,6},{8,11},{9,8},{10,9... | collective-permute-start | bytes 786440 | tf_op jit(solution)/shard_map/ppermute | solution.py:270
  57.6 2.6 %collective-permute-start.8 = (bf16[4,256,256]{2,1,0:T(8,128)(2,1)S(1)}, bf16[4,256,256]{2,1,0:T(8,128)(2,1)S(1)}, u32[]{:S(2)}, u32[]{:S(2)}) collective-permute-start(bf16[4,256,256]{2,1,0:T(8,128)(2,1)S(1)} %pad_maximum_fusion.refs_0_), channel_id=1, source_target_pairs={{0,96},{32,0},{64,32},{96,64},{1,97},{33,1},{65,33},{97,65},{2,98}... | collective-permute-start | bytes 1572872 | tf_op jit(solution)/shard_map/ppermute | solution.py:199
  60.2 2.4 %collective-permute-done.refs_1_ = bf16[512,256]{1,0:T(8,128)(2,1)S(1)} collective-permute-done((bf16[512,256]{1,0:T(8,128)(2,1)S(1)}, bf16[512,256]{1,0:T(8,128)(2,1)S(1)}, u32[]{:S(2)}, u32[]{:S(2)}) %collective-permute-start) | collective-permute-done | bytes 262176 | tf_op jit(solution)/shard_map/ppermute | solution.py:270
  62.6 1.5 %collective-permute-start.22 = (bf16[4,256,256]{2,1,0:T(8,128)(2,1)S(1)}, bf16[4,256,256]{2,1,0:T(8,128)(2,1)S(1)}, u32[]{:S(2)}, u32[]{:S(2)}) collective-permute-start(bf16[4,256,256]{2,1,0:T(8,128)(2,1)S(1)} %pad_maximum_fusion.refs_0_), channel_id=1, source_target_pairs={{0,4},{4,0},{1,5},{5,1},{2,6},{6,2},{3,7},{7,3},{8,12},{12,8},{9,1... | collective-permute-start | bytes 1572872 | tf_op jit(solution)/shard_map/ppermute | solution.py:213
  64.1 1.2 collective-permute-done.17.on_ref.refs_5_
  65.4 1.9 %collective-permute-start.1 = (bf16[512,256]{1,0:T(8,128)(2,1)S(1)}, bf16[512,256]{1,0:T(8,128)(2,1)S(1)}, u32[]{:S(2)}, u32[]{:S(2)}) collective-permute-start(bf16[512,256]{1,0:T(8,128)(2,1)S(1)} %copy-done), channel_id=1, source_target_pairs={{0,2},{1,3},{2,0},{3,1},{4,6},{5,7},{6,4},{7,5},{8,10},{9,11},{10,... | collective-permute-start | bytes 786440 | tf_op jit(solution)/shard_map/ppermute | solution.py:270
  68.0 2.7 %collective-permute-start.2 = (bf16[512,256]{1,0:T(8,128)(2,1)S(1)}, bf16[512,256]{1,0:T(8,128)(2,1)S(1)}, u32[]{:S(2)}, u32[]{:S(2)}) collective-permute-start(bf16[512,256]{1,0:T(8,128)(2,1)S(1)} %copy-done), channel_id=1, source_target_pairs={{0,1},{1,2},{2,3},{3,0},{4,5},{5,6},{6,7},{7,4},{8,9},{9,10},{10,1... | collective-permute-start | bytes 786440 | tf_op jit(solution)/shard_map/ppermute | solution.py:270
  72.9 3.4 %collective-permute-start.20 = (bf16[2,256,256]{2,1,0:T(8,128)(2,1)S(1)}, bf16[2,256,256]{2,1,0:T(8,128)(2,1)S(1)}, u32[]{:S(2)}, u32[]{:S(2)}) collective-permute-start(bf16[2,256,256]{2,1,0:T(8,128)(2,1)S(1)} %get-tuple-element.28), channel_id=1, source_target_pairs={{0,24},{8,0},{16,8},{24,16},{1,25},{9,1},{17,9},{25,17},{2,26},{10... | collective-permute-start | bytes 786440 | tf_op jit(solution)/shard_map/ppermute | solution.py:209
  76.3 4.3 %collective-permute-done.2.refs_3_ = bf16[512,256]{1,0:T(8,128)(2,1)S(1)} collective-permute-done((bf16[512,256]{1,0:T(8,128)(2,1)S(1)}, bf16[512,256]{1,0:T(8,128)(2,1)S(1)}, u32[]{:S(2)}, u32[]{:S(2)}) %collective-permute-start.2) | collective-permute-done | bytes 262176 | tf_op jit(solution)/shard_map/ppermute | solution.py:270
  80.5 3.7 %collective-permute-start.11 = (bf16[2,256,256]{2,1,0:T(8,128)(2,1)S(1)}, bf16[2,256,256]{2,1,0:T(8,128)(2,1)S(1)}, u32[]{:S(2)}, u32[]{:S(2)}) collective-permute-start(bf16[2,256,256]{2,1,0:T(8,128)(2,1)S(1)} %get-tuple-element.26), channel_id=1, source_target_pairs={{0,96},{32,0},{64,32},{96,64},{1,97},{33,1},{65,33},{97,65},{2,98}... | collective-permute-start | bytes 786440 | tf_op jit(solution)/shard_map/ppermute | solution.py:209
  85.6 3.7 %collective-permute-done.11.xb = bf16[2,256,256]{2,1,0:T(8,128)(2,1)S(1)} collective-permute-done((bf16[2,256,256]{2,1,0:T(8,128)(2,1)S(1)}, bf16[2,256,256]{2,1,0:T(8,128)(2,1)S(1)}, u32[]{:S(2)}, u32[]{:S(2)}) %collective-permute-start.11) | collective-permute-done | bytes 262176 | tf_op jit(solution)/shard_map/ppermute | solution.py:209
  89.4 1.4 collective-permute-start.27
  90.8 3.8 %collective-permute-done.9.xa = bf16[2,256,256]{2,1,0:T(8,128)(2,1)S(1)} collective-permute-done((bf16[2,256,256]{2,1,0:T(8,128)(2,1)S(1)}, bf16[2,256,256]{2,1,0:T(8,128)(2,1)S(1)}, u32[]{:S(2)}, u32[]{:S(2)}) %collective-permute-start.9) | collective-permute-done | bytes 262176 | tf_op jit(solution)/shard_map/ppermute | solution.py:209
  96.4 1.2 shard_map.30
  97.6 2.4 %shard_map.34.near_ref = f32[4,272,256]{2,1,0:T(8,128)S(1)} custom-call(s32[4]{0:T(128)S(1)} %pad_add_fusion.where_ref._, bf16[528,2048]{1,0:T(8,128)(2,1)S(1)} %get-tuple-element.24.left_ref, bf16[4,256,256]{2,1,0:T(8,128)(2,1)S(1)} %pad_maximum_fusion.refs_0_, bf16[4,256,256]{2,1,0:T(8,128)(2,1)S(1)} %collective-permute-done.7.back_ref.refs_1_, ...), custom_call_target="tpu_custom_call" | custom-call | tf_op jit(solution)/shard_map/pallas_call | solution.py:73
  100.0 1.3 shard_map.35.own_ref
  101.3 2.4 %shard_map.33.near_ref = f32[4,272,256]{2,1,0:T(8,128)S(1)} custom-call(s32[4]{0:T(128)S(1)} %pad_add_fusion.where_ref._, bf16[528,2048]{1,0:T(8,128)(2,1)S(1)} %get-tuple-element.24.left_ref, bf16[4,256,256]{2,1,0:T(8,128)(2,1)S(1)} %collective-permute-done.22.refs_0_, bf16[4,256,256]{2,1,0:T(8,128)(2,1)S(1)} %collective-permute-done.23.refs_1_, ...), custom_call_target="tpu_custom_call" | custom-call | tf_op jit(solution)/shard_map/pallas_call | solution.py:73
  103.8 2.0 %shard_map.36 = (f32[256,2048]{1,0:T(8,128)S(1)}, f32[8,256]{1,0:T(8,128)S(1)}, f32[128,1,256]{2,1,0:T(1,128)S(1)}, f32[8,256]{1,0:T(8,128)}) custom-call(s32[4]{0:T(128)S(1)} %pad_add_fusion.where_ref._, bf16[528,2048]{1,0:T(8,128)(2,1)S(1)} %get-tuple-element.24.left_ref, bf16[2,256,256]{2,1,0:T(8,128)(2,1)S(1)} %collective-permute-done.10.xa, ...), custom_call_target="tpu_custom_call" | custom-call | tf_op jit(solution)/shard_map/pallas_call | solution.py:73
  105.7 13.1 %all_to_all.21 = f32[128,1,256]{2,1,0:T(1,128)S(1)} all-to-all(f32[128,1,256]{2,1,0:T(1,128)S(1)} %get-tuple-element.32), channel_id=1, replica_groups=mesh['x'=4,'z'=4,'c'=2,'y'=4] {'y','x','z','c'}, dimensions={0} | all-to-all | bytes 262144 | tf_op jit(solution)/shard_map/all_to_all | solution.py:45
  119.4 14.2 %all_to_all.22.got_ref = f32[128,1,256]{2,1,0:T(1,128)S(1)} all-to-all(f32[128,1,256]{2,1,0:T(1,128)S(1)} %broadcast_in_dim.12), channel_id=1, replica_groups=mesh['x'=4,'z'=4,'c'=2,'y'=4] {'y','x','z','c'}, dimensions={0} | all-to-all | bytes 262144 | tf_op jit(solution)/shard_map/all_to_all | solution.py:45
  134.2 14.2 %all_to_all.23.last_ref = f32[128,1,256]{2,1,0:T(1,128)S(1)} all-to-all(f32[128,1,256]{2,1,0:T(1,128)S(1)} %broadcast_in_dim.13), channel_id=1, replica_groups=mesh['x'=4,'z'=4,'c'=2,'y'=4] {'y','x','z','c'}, dimensions={0} | all-to-all | bytes 262144 | tf_op jit(solution)/shard_map/all_to_all | solution.py:45
  148.4 2.7 %shard_map.37 = (f32[256,2048]{1,0:T(8,128)}, f32[1,256]{1,0:T(1,128)}) custom-call(s32[4]{0:T(128)S(1)} %pad_add_fusion.where_ref._, f32[128,1,256]{2,1,0:T(1,128)S(1)} %all_to_all.22.got_ref, f32[128,1,256]{2,1,0:T(1,128)S(1)} %all_to_all.23.last_ref, f32[256,2048]{1,0:T(8,128)S(1)} %get-tuple-element.30.sym_ref, ...), custom_call_target="tpu_custom_call" | custom-call | tf_op jit(solution)/shard_map/pallas_call | solution.py:243
  (59 shorter events, 9.4 us)
Async XLA Ops:
  0.6 53.6 %copy-start = (bf16[512,256]{1,0:T(8,128)(2,1)S(1)}, bf16[512,256]{1,0:T(8,128)(2,1)}, u32[]{:S(2)}) copy-start(bf16[512,256]{1,0:T(8,128)(2,1)} %refs_0_.1) | copy-start | bytes 786436
  0.6 1.7 %collective-permute-start.3 = (bf16[512,256]{1,0:T(8,128)(2,1)}, bf16[512,256]{1,0:T(8,128)(2,1)S(1)}, u32[]{:S(2)}, u32[]{:S(2)}) collective-permute-start(bf16[512,256]{1,0:T(8,128)(2,1)} %refs_0_.1), channel_id=1, source_target_pairs={{0,0},{4,4},{8,8},{12,12},{16,16},{20,20},{24,24},{28,28},{1,32},{... | collective-permute-start | bytes 786440 | tf_op jit(solution)/shard_map/ppermute | solution.py:258
  2.4 21.7 %collective-permute-start.14 = (bf16[256,256]{1,0:T(8,128)(2,1)S(1)}, bf16[256,256]{1,0:T(8,128)(2,1)S(1)}, u32[]{:S(2)}, u32[]{:S(2)}) collective-permute-start(bf16[256,256]{1,0:T(8,128)(2,1)S(1)} %get-tuple-element.40), channel_id=1, source_target_pairs={{0,64},{32,96},{64,0},{96,32},{1,65},{33,97},{65,1},{97,33},{2,66}... | collective-permute-start | bytes 393224 | tf_op jit(solution)/shard_map/ppermute | solution.py:41
  21.3 6.6 %collective-permute-start.15 = (bf16[256,256]{1,0:T(8,128)(2,1)S(1)}, bf16[256,256]{1,0:T(8,128)(2,1)S(1)}, u32[]{:S(2)}, u32[]{:S(2)}) collective-permute-start(bf16[256,256]{1,0:T(8,128)(2,1)S(1)} %get-tuple-element.40), channel_id=1, source_target_pairs={{0,96},{32,0},{64,32},{96,64},{1,97},{33,1},{65,33},{97,65},{2,98}... | collective-permute-start | bytes 393224 | tf_op jit(solution)/shard_map/ppermute | solution.py:41
  22.5 5.6 %collective-permute-start.13 = (bf16[256,256]{1,0:T(8,128)(2,1)S(1)}, bf16[256,256]{1,0:T(8,128)(2,1)S(1)}, u32[]{:S(2)}, u32[]{:S(2)}) collective-permute-start(bf16[256,256]{1,0:T(8,128)(2,1)S(1)} %get-tuple-element.40), channel_id=1, source_target_pairs={{0,32},{32,64},{64,96},{96,0},{1,33},{33,65},{65,97},{97,1},{2,34}... | collective-permute-start | bytes 393224 | tf_op jit(solution)/shard_map/ppermute | solution.py:41
  28.1 36.0 %collective-permute-start.16 = (bf16[4,256,256]{2,1,0:T(8,128)(2,1)S(1)}, bf16[4,256,256]{2,1,0:T(8,128)(2,1)S(1)}, u32[]{:S(2)}, u32[]{:S(2)}) collective-permute-start(bf16[4,256,256]{2,1,0:T(8,128)(2,1)S(1)} %pad_maximum_fusion.1.refs_3_), channel_id=1, source_target_pairs={{0,8},{8,16},{16,24},{24,0},{1,9},{9,17},{17,25},{25,1},{2,10},{10... | collective-permute-start | bytes 1572872 | tf_op jit(solution)/shard_map/ppermute | solution.py:199
  29.9 23.9 %collective-permute-start.4 = (bf16[256,256]{1,0:T(8,128)(2,1)S(1)}, bf16[256,256]{1,0:T(8,128)(2,1)S(1)}, u32[]{:S(2)}, u32[]{:S(2)}) collective-permute-start(bf16[256,256]{1,0:T(8,128)(2,1)S(1)} %get-tuple-element.41), channel_id=1, source_target_pairs={{0,8},{8,16},{16,24},{24,0},{1,9},{9,17},{17,25},{25,1},{2,10},{10... | collective-permute-start | bytes 393224 | tf_op jit(solution)/shard_map/ppermute | solution.py:41
  31.6 22.2 %collective-permute-start.5 = (bf16[256,256]{1,0:T(8,128)(2,1)S(1)}, bf16[256,256]{1,0:T(8,128)(2,1)S(1)}, u32[]{:S(2)}, u32[]{:S(2)}) collective-permute-start(bf16[256,256]{1,0:T(8,128)(2,1)S(1)} %get-tuple-element.41), channel_id=1, source_target_pairs={{0,16},{8,24},{16,0},{24,8},{1,17},{9,25},{17,1},{25,9},{2,18},{10... | collective-permute-start | bytes 393224 | tf_op jit(solution)/shard_map/ppermute | solution.py:41
  33.3 20.5 %collective-permute-start.6 = (bf16[256,256]{1,0:T(8,128)(2,1)S(1)}, bf16[256,256]{1,0:T(8,128)(2,1)S(1)}, u32[]{:S(2)}, u32[]{:S(2)}) collective-permute-start(bf16[256,256]{1,0:T(8,128)(2,1)S(1)} %get-tuple-element.41), channel_id=1, source_target_pairs={{0,24},{8,0},{16,8},{24,16},{1,25},{9,1},{17,9},{25,17},{2,26},{10... | collective-permute-start | bytes 393224 | tf_op jit(solution)/shard_map/ppermute | solution.py:41
  52.9 12.5 %collective-permute-start.17 = (bf16[4,256,256]{2,1,0:T(8,128)(2,1)S(1)}, bf16[4,256,256]{2,1,0:T(8,128)(2,1)S(1)}, u32[]{:S(2)}, u32[]{:S(2)}) collective-permute-start(bf16[4,256,256]{2,1,0:T(8,128)(2,1)S(1)} %pad_maximum_fusion.1.refs_3_), channel_id=1, source_target_pairs={{0,24},{8,0},{16,8},{24,16},{1,25},{9,1},{17,9},{25,17},{2,26},{10... | collective-permute-start | bytes 1572872 | tf_op jit(solution)/shard_map/ppermute | solution.py:199
  53.9 14.1 %collective-permute-start.7 = (bf16[4,256,256]{2,1,0:T(8,128)(2,1)S(1)}, bf16[4,256,256]{2,1,0:T(8,128)(2,1)S(1)}, u32[]{:S(2)}, u32[]{:S(2)}) collective-permute-start(bf16[4,256,256]{2,1,0:T(8,128)(2,1)S(1)} %pad_maximum_fusion.refs_0_), channel_id=1, source_target_pairs={{0,32},{32,64},{64,96},{96,0},{1,33},{33,65},{65,97},{97,1},{2,34}... | collective-permute-start | bytes 1572872 | tf_op jit(solution)/shard_map/ppermute | solution.py:199
  54.3 8.3 %collective-permute-start = (bf16[512,256]{1,0:T(8,128)(2,1)S(1)}, bf16[512,256]{1,0:T(8,128)(2,1)S(1)}, u32[]{:S(2)}, u32[]{:S(2)}) collective-permute-start(bf16[512,256]{1,0:T(8,128)(2,1)S(1)} %copy-done), channel_id=1, source_target_pairs={{0,3},{1,0},{2,1},{3,2},{4,7},{5,4},{6,5},{7,6},{8,11},{9,8},{10,9... | collective-permute-start | bytes 786440 | tf_op jit(solution)/shard_map/ppermute | solution.py:270
  57.6 13.7 %collective-permute-start.8 = (bf16[4,256,256]{2,1,0:T(8,128)(2,1)S(1)}, bf16[4,256,256]{2,1,0:T(8,128)(2,1)S(1)}, u32[]{:S(2)}, u32[]{:S(2)}) collective-permute-start(bf16[4,256,256]{2,1,0:T(8,128)(2,1)S(1)} %pad_maximum_fusion.refs_0_), channel_id=1, source_target_pairs={{0,96},{32,0},{64,32},{96,64},{1,97},{33,1},{65,33},{97,65},{2,98}... | collective-permute-start | bytes 1572872 | tf_op jit(solution)/shard_map/ppermute | solution.py:199
  62.6 21.7 %collective-permute-start.22 = (bf16[4,256,256]{2,1,0:T(8,128)(2,1)S(1)}, bf16[4,256,256]{2,1,0:T(8,128)(2,1)S(1)}, u32[]{:S(2)}, u32[]{:S(2)}) collective-permute-start(bf16[4,256,256]{2,1,0:T(8,128)(2,1)S(1)} %pad_maximum_fusion.refs_0_), channel_id=1, source_target_pairs={{0,4},{4,0},{1,5},{5,1},{2,6},{6,2},{3,7},{7,3},{8,12},{12,8},{9,1... | collective-permute-start | bytes 1572872 | tf_op jit(solution)/shard_map/ppermute | solution.py:213
  64.1 21.0 %collective-permute-start.25 = (bf16[4,256,256]{2,1,0:T(8,128)(2,1)S(1)}, bf16[4,256,256]{2,1,0:T(8,128)(2,1)S(1)}, u32[]{:S(2)}, u32[]{:S(2)}) collective-permute-start(bf16[4,256,256]{2,1,0:T(8,128)(2,1)S(1)} %pad_maximum_fusion.1.refs_3_), channel_id=1, source_target_pairs={{0,4},{4,0},{1,5},{5,1},{2,6},{6,2},{3,7},{7,3},{8,12},{12,8},{9,1... | collective-permute-start | bytes 1572872 | tf_op jit(solution)/shard_map/ppermute | solution.py:213
  65.4 7.5 %collective-permute-start.1 = (bf16[512,256]{1,0:T(8,128)(2,1)S(1)}, bf16[512,256]{1,0:T(8,128)(2,1)S(1)}, u32[]{:S(2)}, u32[]{:S(2)}) collective-permute-start(bf16[512,256]{1,0:T(8,128)(2,1)S(1)} %copy-done), channel_id=1, source_target_pairs={{0,2},{1,3},{2,0},{3,1},{4,6},{5,7},{6,4},{7,5},{8,10},{9,11},{10,... | collective-permute-start | bytes 786440 | tf_op jit(solution)/shard_map/ppermute | solution.py:270
  68.0 12.6 %collective-permute-start.2 = (bf16[512,256]{1,0:T(8,128)(2,1)S(1)}, bf16[512,256]{1,0:T(8,128)(2,1)S(1)}, u32[]{:S(2)}, u32[]{:S(2)}) collective-permute-start(bf16[512,256]{1,0:T(8,128)(2,1)S(1)} %copy-done), channel_id=1, source_target_pairs={{0,1},{1,2},{2,3},{3,0},{4,5},{5,6},{6,7},{7,4},{8,9},{9,10},{10,1... | collective-permute-start | bytes 786440 | tf_op jit(solution)/shard_map/ppermute | solution.py:270
  71.3 13.9 %collective-permute-start.18 = (bf16[2,256,256]{2,1,0:T(8,128)(2,1)S(1)}, bf16[2,256,256]{2,1,0:T(8,128)(2,1)S(1)}, u32[]{:S(2)}, u32[]{:S(2)}) collective-permute-start(bf16[2,256,256]{2,1,0:T(8,128)(2,1)S(1)} %get-tuple-element.27), channel_id=1, source_target_pairs={{0,8},{8,16},{16,24},{24,0},{1,9},{9,17},{17,25},{25,1},{2,10},{10... | collective-permute-start | bytes 786440 | tf_op jit(solution)/shard_map/ppermute | solution.py:209
  72.9 12.8 %collective-permute-start.20 = (bf16[2,256,256]{2,1,0:T(8,128)(2,1)S(1)}, bf16[2,256,256]{2,1,0:T(8,128)(2,1)S(1)}, u32[]{:S(2)}, u32[]{:S(2)}) collective-permute-start(bf16[2,256,256]{2,1,0:T(8,128)(2,1)S(1)} %get-tuple-element.28), channel_id=1, source_target_pairs={{0,24},{8,0},{16,8},{24,16},{1,25},{9,1},{17,9},{25,17},{2,26},{10... | collective-permute-start | bytes 786440 | tf_op jit(solution)/shard_map/ppermute | solution.py:209
  80.5 8.8 %collective-permute-start.11 = (bf16[2,256,256]{2,1,0:T(8,128)(2,1)S(1)}, bf16[2,256,256]{2,1,0:T(8,128)(2,1)S(1)}, u32[]{:S(2)}, u32[]{:S(2)}) collective-permute-start(bf16[2,256,256]{2,1,0:T(8,128)(2,1)S(1)} %get-tuple-element.26), channel_id=1, source_target_pairs={{0,96},{32,0},{64,32},{96,64},{1,97},{33,1},{65,33},{97,65},{2,98}... | collective-permute-start | bytes 786440 | tf_op jit(solution)/shard_map/ppermute | solution.py:209
  84.3 11.3 %collective-permute-start.23 = (bf16[4,256,256]{2,1,0:T(8,128)(2,1)S(1)}, bf16[4,256,256]{2,1,0:T(8,128)(2,1)S(1)}, u32[]{:S(2)}, u32[]{:S(2)}) collective-permute-start(bf16[4,256,256]{2,1,0:T(8,128)(2,1)S(1)} %collective-permute-done.7.back_ref.refs_1_), channel_id=1, source_target_pairs={{0,4},{4,0},{1,5},{5,1},{2,6},{6,2},{3,7},{7,3},{8,12},{12,8},{9,1... | collective-permute-start | bytes 1572872 | tf_op jit(solution)/shard_map/ppermute | solution.py:213
  85.1 10.5 %collective-permute-start.24 = (bf16[4,256,256]{2,1,0:T(8,128)(2,1)S(1)}, bf16[4,256,256]{2,1,0:T(8,128)(2,1)S(1)}, u32[]{:S(2)}, u32[]{:S(2)}) collective-permute-start(bf16[4,256,256]{2,1,0:T(8,128)(2,1)S(1)} %collective-permute-done.8.on_ref.refs_2_), channel_id=1, source_target_pairs={{0,4},{4,0},{1,5},{5,1},{2,6},{6,2},{3,7},{7,3},{8,12},{12,8},{9,1... | collective-permute-start | bytes 1572872 | tf_op jit(solution)/shard_map/ppermute | solution.py:213
  85.2 10.9 %collective-permute-start.26 = (bf16[4,256,256]{2,1,0:T(8,128)(2,1)S(1)}, bf16[4,256,256]{2,1,0:T(8,128)(2,1)S(1)}, u32[]{:S(2)}, u32[]{:S(2)}) collective-permute-start(bf16[4,256,256]{2,1,0:T(8,128)(2,1)S(1)} %collective-permute-done.16.back_ref.refs_4_), channel_id=1, source_target_pairs={{0,4},{4,0},{1,5},{5,1},{2,6},{6,2},{3,7},{7,3},{8,12},{12,8},{9,1... | collective-permute-start | bytes 1572872 | tf_op jit(solution)/shard_map/ppermute | solution.py:213
  85.6 9.0 %collective-permute-start.9 = (bf16[2,256,256]{2,1,0:T(8,128)(2,1)S(1)}, bf16[2,256,256]{2,1,0:T(8,128)(2,1)S(1)}, u32[]{:S(2)}, u32[]{:S(2)}) collective-permute-start(bf16[2,256,256]{2,1,0:T(8,128)(2,1)S(1)} %get-tuple-element.25), channel_id=1, source_target_pairs={{0,32},{32,64},{64,96},{96,0},{1,33},{33,65},{65,97},{97,1},{2,34}... | collective-permute-start | bytes 786440 | tf_op jit(solution)/shard_map/ppermute | solution.py:209
  89.4 11.9 %collective-permute-start.27 = (bf16[4,256,256]{2,1,0:T(8,128)(2,1)S(1)}, bf16[4,256,256]{2,1,0:T(8,128)(2,1)S(1)}, u32[]{:S(2)}, u32[]{:S(2)}) collective-permute-start(bf16[4,256,256]{2,1,0:T(8,128)(2,1)S(1)} %collective-permute-done.17.on_ref.refs_5_), channel_id=1, source_target_pairs={{0,4},{4,0},{1,5},{5,1},{2,6},{6,2},{3,7},{7,3},{8,12},{12,8},{9,1... | collective-permute-start | bytes 1572872 | tf_op jit(solution)/shard_map/ppermute | solution.py:213
  94.6 9.1 %collective-permute-start.19 = (bf16[2,256,256]{2,1,0:T(8,128)(2,1)S(1)}, bf16[2,256,256]{2,1,0:T(8,128)(2,1)S(1)}, u32[]{:S(2)}, u32[]{:S(2)}) collective-permute-start(bf16[2,256,256]{2,1,0:T(8,128)(2,1)S(1)} %collective-permute-done.18.za), channel_id=1, source_target_pairs={{0,4},{4,0},{1,5},{5,1},{2,6},{6,2},{3,7},{7,3},{8,12},{12,8},{9,1... | collective-permute-start | bytes 786440 | tf_op jit(solution)/shard_map/ppermute | solution.py:213
  95.6 8.2 %collective-permute-start.21 = (bf16[2,256,256]{2,1,0:T(8,128)(2,1)S(1)}, bf16[2,256,256]{2,1,0:T(8,128)(2,1)S(1)}, u32[]{:S(2)}, u32[]{:S(2)}) collective-permute-start(bf16[2,256,256]{2,1,0:T(8,128)(2,1)S(1)} %collective-permute-done.20.zb), channel_id=1, source_target_pairs={{0,4},{4,0},{1,5},{5,1},{2,6},{6,2},{3,7},{7,3},{8,12},{12,8},{9,1... | collective-permute-start | bytes 786440 | tf_op jit(solution)/shard_map/ppermute | solution.py:213
  95.6 8.2 %collective-permute-start.10 = (bf16[2,256,256]{2,1,0:T(8,128)(2,1)S(1)}, bf16[2,256,256]{2,1,0:T(8,128)(2,1)S(1)}, u32[]{:S(2)}, u32[]{:S(2)}) collective-permute-start(bf16[2,256,256]{2,1,0:T(8,128)(2,1)S(1)} %collective-permute-done.9.xa), channel_id=1, source_target_pairs={{0,4},{4,0},{1,5},{5,1},{2,6},{6,2},{3,7},{7,3},{8,12},{12,8},{9,1... | collective-permute-start | bytes 786440 | tf_op jit(solution)/shard_map/ppermute | solution.py:213
  96.1 7.7 %collective-permute-start.12 = (bf16[2,256,256]{2,1,0:T(8,128)(2,1)S(1)}, bf16[2,256,256]{2,1,0:T(8,128)(2,1)S(1)}, u32[]{:S(2)}, u32[]{:S(2)}) collective-permute-start(bf16[2,256,256]{2,1,0:T(8,128)(2,1)S(1)} %collective-permute-done.11.xb), channel_id=1, source_target_pairs={{0,4},{4,0},{1,5},{5,1},{2,6},{6,2},{3,7},{7,3},{8,12},{12,8},{9,1... | collective-permute-start | bytes 786440 | tf_op jit(solution)/shard_map/ppermute | solution.py:213

commit v9 on v8

--- a/solution.py
+++ b/solution.py
@@ -79,8 +79,8 @@
     )(operands[0], *[pltpu.with_memory_space_constraint(v, pltpu.VMEM) for v in operands[1:]])
 
 
-def left_of(where_ref, left_ref, dx, late):
-    lo = lax.rem(where_ref[0] + 4 - dx, 4) * BLOCK + late * FIRST
+def left_of(where_ref, left_ref, back, late):
+    lo = lax.rem(where_ref[late] + 4 - back, 4) * BLOCK + late * FIRST
     return left_ref[:, pl.ds(pl.multiple_of(lo, FIRST), FIRST)]
 
 
@@ -96,8 +96,8 @@
                 acc += jnp.dot(left_of(where_ref, left_ref, dx, 0), x_refs[i][dz],
                                preferred_element_type=jnp.float32)
             if dz in NEAR:
-                for dx in range(4):
-                    acc += jnp.dot(left_of(where_ref, left_ref, dx, 1), z_refs[NEAR.index(dz)][dx],
+                for dy in range(4):
+                    acc += jnp.dot(left_of(where_ref, left_ref, dy, 1), z_refs[NEAR.index(dz)][dy],
                                    preferred_element_type=jnp.float32)
             out_ref[dz] = grouped(acc)
 
@@ -108,8 +108,8 @@
     acc = jnp.dot(left_of(where_ref, left_ref, 2, 0), x_refs[dz // 2][dz % 2],
                   preferred_element_type=jnp.float32)
     if dz == 2:
-        for dx in range(4):
-            acc += jnp.dot(left_of(where_ref, left_ref, dx, 1), z_refs[dx // 2][dx % 2],
+        for dy in range(4):
+            acc += jnp.dot(left_of(where_ref, left_ref, dy, 1), z_refs[dy // 2][dy % 2],
                            preferred_element_type=jnp.float32)
     return grouped(acc)
 
@@ -255,13 +255,15 @@
 def shards(member):
     x, y, z, c = (lax.axis_index(a) for a in ("x", "y", "z", "c"))
     where = jnp.stack([x, y, z, c])
-    moved = lax.ppermute(member, ALL, across())
+    moved = lax.ppermute(member[:FIRST], ALL, across())
     part = jnp.sum(member, axis=1, dtype=jnp.float32)
     w, first = (v.astype(jnp.uint32) for v in ((x * 4 + z) * 2 + c, y * GROUPS))
     part, where, w, first = lax.optimization_barrier((part, where, w, first))
     frames = to_all(jnp.broadcast_to(part.astype(jnp.bfloat16).reshape(2, WIDTH), (128, 2, WIDTH)))
-    once_x = jnp.stack(ring(moved[:FIRST], "z"))
-    once_z = jnp.stack(ring(moved[FIRST:], "x"))
+    planes = jnp.stack(ring(member[FIRST:], "x"))
+    once_x = jnp.stack(ring(moved, "z"))
+    leave = [lax.dynamic_index_in_dim(planes, lax.rem(x + 8 - y - k, 4), 0, False) for k in range(4)]
+    once_z = jnp.stack([leave[0]] + [lax.ppermute(leave[k], "y", along(k)) for k in (1, 2, 3)])
     near_x = from_sides(once_x, "x")
     near_z = from_sides(once_z, "z")
     far_x = from_afar(where, near_x, "x")

time: 151 us -> 143 us (0.947)
  starting transfers between devices: 54.5 us -> 38.1 us
  blocking collectives: 58.9 us -> 63 us
  waiting for transfers between devices: 21.1 us -> 24.8 us
    ppermute x6, starting transfers between devices: 26 us -> 12.3 us  [ring(): return [v] + [lax.ppermute(v, axis, along(k)) for k in (1, 2, 3)]]
    ppermute x3, starting transfers between devices: 7.97 us -> 2.95 us  [shards(): blocks = [member] + [lax.ppermute(kept, 'y', along(-k)) for k in (1, 2, 3)]]
    all_to_all x4, blocking collectives: 58.9 us -> 63 us  [to_all(): return lax.all_to_all(sent, ('y',) + WIDE, 0, 0)]
    ppermute x1 -> x4, starting transfers between devices: 1.74 us -> 5.77 us  [the longest x3 5.12 us: shards(): lax.ppermute(leave[k], 'y', along(k))]
    ppermute x3, waiting for transfers between devices: 7.62 us -> 10.9 us  [shards(): blocks = [member] + [lax.ppermute(kept, 'y', along(-k)) for k in (1, 2, 3)]]
    ppermute x2, starting transfers between devices: 7.11 us -> 5.29 us  [from_afar(): lax.ppermute(halves[1], axis, along(3))]
  transfers between devices with their start and end apart: 28 -> 31, of which waited for: 9 -> 9; matrix products, arithmetic and copies ran while one was open for 1% -> 0% of each run, Pallas kernels for 6% -> 6%
where the time goes in v9:
time: 143 us
  blocking collectives  63 us (44%)
  starting transfers between devices  38.1 us (27%)
  waiting for transfers between devices  24.8 us (17%)
  Pallas kernels  13.2 us (9%)
    all_to_all x4, blocking collectives, to_all(): return lax.all_to_all(sent, ('y',) + WIDE, 0, 0)  63 us
    ppermute x6, starting transfers between devices, ring(): return [v] + [lax.ppermute(v, axis, along(k)) for k in (1, 2, 3)]  12.3 us
    ppermute x3, waiting for transfers between devices, shards(): blocks = [member] + [lax.ppermute(kept, 'y', along(-k)) for k in (1, 2, 3)]  10.9 us
    pallas_call x6, Pallas kernels, call(): pl.pallas_call(kernel, in_specs=[SMEM] + [VMEM] * (len(operands) - 1), ou...  9.23 us
    ppermute x10, starting transfers between devices, swapped(): return [lax.ppermute(v, 'c', [(0, 1), (1, 0)]) for v in vs]  7.11 us
    ppermute x2, starting transfers between devices, from_afar(): lax.ppermute(halves[1], axis, along(3))  5.29 us
    ppermute x3, starting transfers between devices, shards(): lax.ppermute(leave[k], 'y', along(k))  5.12 us
    ppermute x4, starting transfers between devices, from_sides(): return [lax.ppermute(v, axis, along(k)) for k in (1, 3)]  4.54 us
  transfers between devices with their start and end apart: 31, of which 9 were waited for; matrix products, arithmetic and copies ran while one was open for 0% of the time, Pallas kernels for 6%

profile of v9, /device:TPU:1, one launch (start us, length us, event | category | flops | bytes accessed | tf_op | source)
XLA Modules:
  0.0 142.7 jit_solution(13059795857177828437)
XLA Ops:
  0.6 1.0 slice_bitcast_fusion
  1.7 3.6 %collective-permute-start.14 = (bf16[256,256]{1,0:T(8,128)(2,1)S(1)}, bf16[256,256]{1,0:T(8,128)(2,1)S(1)}, u32[]{:S(2)}, u32[]{:S(2)}) collective-permute-start(bf16[256,256]{1,0:T(8,128)(2,1)S(1)} %get-tuple-element.43), channel_id=1, source_target_pairs={{0,64},{32,96},{64,0},{96,32},{1,65},{33,97},{65,1},{97,33},{2,66}... | collective-permute-start | bytes 393224 | tf_op jit(solution)/shard_map/ppermute | solution.py:41
  8.1 3.2 %collective-permute-done.15 = bf16[256,256]{1,0:T(8,128)(2,1)S(1)} collective-permute-done((bf16[256,256]{1,0:T(8,128)(2,1)S(1)}, bf16[256,256]{1,0:T(8,128)(2,1)S(1)}, u32[]{:S(2)}, u32[]{:S(2)}) %collective-permute-start.15) | collective-permute-done | bytes 131104 | tf_op jit(solution)/shard_map/ppermute | solution.py:41
  11.5 1.4 %collective-permute-start.16 = (bf16[256,256]{1,0:T(8,128)(2,1)S(1)}, bf16[256,256]{1,0:T(8,128)(2,1)S(1)}, u32[]{:S(2)}, u32[]{:S(2)}) collective-permute-start(bf16[256,256]{1,0:T(8,128)(2,1)S(1)} %get-tuple-element.41), channel_id=1, source_target_pairs={{0,1},{1,2},{2,3},{3,0},{4,5},{5,6},{6,7},{7,4},{8,9},{9,10},{10,1... | collective-permute-start | bytes 393224 | tf_op jit(solution)/shard_map/ppermute | solution.py:266
  12.9 2.6 %collective-permute-start.17 = (bf16[256,256]{1,0:T(8,128)(2,1)S(1)}, bf16[256,256]{1,0:T(8,128)(2,1)S(1)}, u32[]{:S(2)}, u32[]{:S(2)}) collective-permute-start(bf16[256,256]{1,0:T(8,128)(2,1)S(1)} %get-tuple-element.40), channel_id=1, source_target_pairs={{0,2},{1,3},{2,0},{3,1},{4,6},{5,7},{6,4},{7,5},{8,10},{9,11},{10,... | collective-permute-start | bytes 393224 | tf_op jit(solution)/shard_map/ppermute | solution.py:266
  15.5 1.1 collective-permute-start.18
  16.8 1.7 %collective-permute-start.4 = (bf16[256,256]{1,0:T(8,128)(2,1)S(1)}, bf16[256,256]{1,0:T(8,128)(2,1)S(1)}, u32[]{:S(2)}, u32[]{:S(2)}) collective-permute-start(bf16[256,256]{1,0:T(8,128)(2,1)S(1)} %collective-permute-done.3), channel_id=1, source_target_pairs={{0,8},{8,16},{16,24},{24,0},{1,9},{9,17},{17,25},{25,1},{2,10},{10... | collective-permute-start | bytes 393224 | tf_op jit(solution)/shard_map/ppermute | solution.py:41
  18.5 3.3 %collective-permute-start.5 = (bf16[256,256]{1,0:T(8,128)(2,1)S(1)}, bf16[256,256]{1,0:T(8,128)(2,1)S(1)}, u32[]{:S(2)}, u32[]{:S(2)}) collective-permute-start(bf16[256,256]{1,0:T(8,128)(2,1)S(1)} %collective-permute-done.3), channel_id=1, source_target_pairs={{0,16},{8,24},{16,0},{24,8},{1,17},{9,25},{17,1},{25,9},{2,18},{10... | collective-permute-start | bytes 393224 | tf_op jit(solution)/shard_map/ppermute | solution.py:41
  21.8 2.2 %collective-permute-start.6 = (bf16[256,256]{1,0:T(8,128)(2,1)S(1)}, bf16[256,256]{1,0:T(8,128)(2,1)S(1)}, u32[]{:S(2)}, u32[]{:S(2)}) collective-permute-start(bf16[256,256]{1,0:T(8,128)(2,1)S(1)} %collective-permute-done.3), channel_id=1, source_target_pairs={{0,24},{8,0},{16,8},{24,16},{1,25},{9,1},{17,9},{25,17},{2,26},{10... | collective-permute-start | bytes 393224 | tf_op jit(solution)/shard_map/ppermute | solution.py:41
  25.0 20.7 %all_to_all.20.refs_4_ = bf16[128,2,256]{2,1,0:T(2,128)(2,1)S(1)} all-to-all(bf16[128,2,256]{2,1,0:T(2,128)(2,1)S(1)} %broadcast_in_dim.11), channel_id=1, replica_groups=mesh['x'=4,'z'=4,'c'=2,'y'=4] {'y','x','z','c'}, dimensions={0} | all-to-all | bytes 262144 | tf_op jit(solution)/shard_map/all_to_all | solution.py:45
  47.9 2.5 %collective-permute-start.8 = (bf16[4,256,256]{2,1,0:T(8,128)(2,1)S(1)}, bf16[4,256,256]{2,1,0:T(8,128)(2,1)S(1)}, u32[]{:S(2)}, u32[]{:S(2)}) collective-permute-start(bf16[4,256,256]{2,1,0:T(8,128)(2,1)S(1)} %pad_maximum_fusion.refs_0_), channel_id=1, source_target_pairs={{0,96},{32,0},{64,32},{96,64},{1,97},{33,1},{65,33},{97,65},{2,98}... | collective-permute-start | bytes 1572872 | tf_op jit(solution)/shard_map/ppermute | solution.py:199
  50.4 3.6 %collective-permute-done.refs_1_ = bf16[512,256]{1,0:T(8,128)(2,1)S(1)} collective-permute-done((bf16[512,256]{1,0:T(8,128)(2,1)S(1)}, bf16[512,256]{1,0:T(8,128)(2,1)S(1)}, u32[]{:S(2)}, u32[]{:S(2)}) %collective-permute-start) | collective-permute-done | bytes 262176 | tf_op jit(solution)/shard_map/ppermute | solution.py:272
  54.0 1.8 %collective-permute-start.28 = (bf16[4,256,256]{2,1,0:T(8,128)(2,1)S(1)}, bf16[4,256,256]{2,1,0:T(8,128)(2,1)S(1)}, u32[]{:S(2)}, u32[]{:S(2)}) collective-permute-start(bf16[4,256,256]{2,1,0:T(8,128)(2,1)S(1)} %pad_maximum_fusion.2.refs_3_), channel_id=1, source_target_pairs={{0,4},{4,0},{1,5},{5,1},{2,6},{6,2},{3,7},{7,3},{8,12},{12,8},{9,1... | collective-permute-start | bytes 1572872 | tf_op jit(solution)/shard_map/ppermute | solution.py:213
  55.8 2.4 %collective-permute-done.20.on_ref.refs_5_ = bf16[4,256,256]{2,1,0:T(8,128)(2,1)S(1)} collective-permute-done((bf16[4,256,256]{2,1,0:T(8,128)(2,1)S(1)}, bf16[4,256,256]{2,1,0:T(8,128)(2,1)S(1)}, u32[]{:S(2)}, u32[]{:S(2)}) %collective-permute-start.20) | collective-permute-done | bytes 524320 | tf_op jit(solution)/shard_map/ppermute | solution.py:199
  58.2 1.8 %collective-permute-start.1 = (bf16[512,256]{1,0:T(8,128)(2,1)S(1)}, bf16[512,256]{1,0:T(8,128)(2,1)S(1)}, u32[]{:S(2)}, u32[]{:S(2)}) collective-permute-start(bf16[512,256]{1,0:T(8,128)(2,1)S(1)} %copy-done), channel_id=1, source_target_pairs={{0,2},{1,3},{2,0},{3,1},{4,6},{5,7},{6,4},{7,5},{8,10},{9,11},{10,... | collective-permute-start | bytes 786440 | tf_op jit(solution)/shard_map/ppermute | solution.py:272
  62.4 3.3 %collective-permute-done.1.refs_2_ = bf16[512,256]{1,0:T(8,128)(2,1)S(1)} collective-permute-done((bf16[512,256]{1,0:T(8,128)(2,1)S(1)}, bf16[512,256]{1,0:T(8,128)(2,1)S(1)}, u32[]{:S(2)}, u32[]{:S(2)}) %collective-permute-start.1) | collective-permute-done | bytes 262176 | tf_op jit(solution)/shard_map/ppermute | solution.py:272
  65.7 3.4 %collective-permute-start.23 = (bf16[2,256,256]{2,1,0:T(8,128)(2,1)S(1)}, bf16[2,256,256]{2,1,0:T(8,128)(2,1)S(1)}, u32[]{:S(2)}, u32[]{:S(2)}) collective-permute-start(bf16[2,256,256]{2,1,0:T(8,128)(2,1)S(1)} %get-tuple-element.28), channel_id=1, source_target_pairs={{0,24},{8,0},{16,8},{24,16},{1,25},{9,1},{17,9},{25,17},{2,26},{10... | collective-permute-start | bytes 786440 | tf_op jit(solution)/shard_map/ppermute | solution.py:209
  69.1 4.0 %collective-permute-done.2.refs_3_ = bf16[512,256]{1,0:T(8,128)(2,1)S(1)} collective-permute-done((bf16[512,256]{1,0:T(8,128)(2,1)S(1)}, bf16[512,256]{1,0:T(8,128)(2,1)S(1)}, u32[]{:S(2)}, u32[]{:S(2)}) %collective-permute-start.2) | collective-permute-done | bytes 262176 | tf_op jit(solution)/shard_map/ppermute | solution.py:272
  73.1 1.9 %collective-permute-start.11 = (bf16[2,256,256]{2,1,0:T(8,128)(2,1)S(1)}, bf16[2,256,256]{2,1,0:T(8,128)(2,1)S(1)}, u32[]{:S(2)}, u32[]{:S(2)}) collective-permute-start(bf16[2,256,256]{2,1,0:T(8,128)(2,1)S(1)} %get-tuple-element.26), channel_id=1, source_target_pairs={{0,96},{32,0},{64,32},{96,64},{1,97},{33,1},{65,33},{97,65},{2,98}... | collective-permute-start | bytes 786440 | tf_op jit(solution)/shard_map/ppermute | solution.py:209
  76.3 3.9 %collective-permute-done.11.xb = bf16[2,256,256]{2,1,0:T(8,128)(2,1)S(1)} collective-permute-done((bf16[2,256,256]{2,1,0:T(8,128)(2,1)S(1)}, bf16[2,256,256]{2,1,0:T(8,128)(2,1)S(1)}, u32[]{:S(2)}, u32[]{:S(2)}) %collective-permute-start.11) | collective-permute-done | bytes 262176 | tf_op jit(solution)/shard_map/ppermute | solution.py:209
  80.2 1.6 %collective-permute-start.27 = (bf16[4,256,256]{2,1,0:T(8,128)(2,1)S(1)}, bf16[4,256,256]{2,1,0:T(8,128)(2,1)S(1)}, u32[]{:S(2)}, u32[]{:S(2)}) collective-permute-start(bf16[4,256,256]{2,1,0:T(8,128)(2,1)S(1)} %collective-permute-done.8.on_ref.refs_2_), channel_id=1, source_target_pairs={{0,4},{4,0},{1,5},{5,1},{2,6},{6,2},{3,7},{7,3},{8,12},{12,8},{9,1... | collective-permute-start | bytes 1572872 | tf_op jit(solution)/shard_map/ppermute | solution.py:213
  81.8 2.8 %collective-permute-done.9.xa = bf16[2,256,256]{2,1,0:T(8,128)(2,1)S(1)} collective-permute-done((bf16[2,256,256]{2,1,0:T(8,128)(2,1)S(1)}, bf16[2,256,256]{2,1,0:T(8,128)(2,1)S(1)}, u32[]{:S(2)}, u32[]{:S(2)}) %collective-permute-start.9) | collective-permute-done | bytes 262176 | tf_op jit(solution)/shard_map/ppermute | solution.py:209
  84.7 1.6 %collective-permute-start.22 = (bf16[2,256,256]{2,1,0:T(8,128)(2,1)S(1)}, bf16[2,256,256]{2,1,0:T(8,128)(2,1)S(1)}, u32[]{:S(2)}, u32[]{:S(2)}) collective-permute-start(bf16[2,256,256]{2,1,0:T(8,128)(2,1)S(1)} %collective-permute-done.21.za), channel_id=1, source_target_pairs={{0,4},{4,0},{1,5},{5,1},{2,6},{6,2},{3,7},{7,3},{8,12},{12,8},{9,1... | collective-permute-start | bytes 786440 | tf_op jit(solution)/shard_map/ppermute | solution.py:213
  87.0 1.2 shard_map.30
  88.2 2.4 %shard_map.34.near_ref = f32[4,272,256]{2,1,0:T(8,128)S(1)} custom-call(s32[4]{0:T(128)S(1)} %pad_add_fusion.where_ref._, bf16[528,2048]{1,0:T(8,128)(2,1)S(1)} %get-tuple-element.24.left_ref, bf16[4,256,256]{2,1,0:T(8,128)(2,1)S(1)} %pad_maximum_fusion.refs_0_, bf16[4,256,256]{2,1,0:T(8,128)(2,1)S(1)} %collective-permute-done.7.back_ref.refs_1_, ...), custom_call_target="tpu_custom_call" | custom-call | tf_op jit(solution)/shard_map/pallas_call | solution.py:73
  90.7 1.3 shard_map.35.own_ref
  92.0 2.4 %shard_map.33.near_ref = f32[4,272,256]{2,1,0:T(8,128)S(1)} custom-call(s32[4]{0:T(128)S(1)} %pad_add_fusion.where_ref._, bf16[528,2048]{1,0:T(8,128)(2,1)S(1)} %get-tuple-element.24.left_ref, bf16[4,256,256]{2,1,0:T(8,128)(2,1)S(1)} %collective-permute-done.25.refs_0_, bf16[4,256,256]{2,1,0:T(8,128)(2,1)S(1)} %collective-permute-done.26.refs_1_, ...), custom_call_target="tpu_custom_call" | custom-call | tf_op jit(solution)/shard_map/pallas_call | solution.py:73
  94.4 2.0 %shard_map.36 = (f32[256,2048]{1,0:T(8,128)S(1)}, f32[8,256]{1,0:T(8,128)S(1)}, f32[128,1,256]{2,1,0:T(1,128)S(1)}, f32[8,256]{1,0:T(8,128)}) custom-call(s32[4]{0:T(128)S(1)} %pad_add_fusion.where_ref._, bf16[528,2048]{1,0:T(8,128)(2,1)S(1)} %get-tuple-element.24.left_ref, bf16[2,256,256]{2,1,0:T(8,128)(2,1)S(1)} %collective-permute-done.10.xa, ...), custom_call_target="tpu_custom_call" | custom-call | tf_op jit(solution)/shard_map/pallas_call | solution.py:73
  96.4 14.0 %all_to_all.21 = f32[128,1,256]{2,1,0:T(1,128)S(1)} all-to-all(f32[128,1,256]{2,1,0:T(1,128)S(1)} %get-tuple-element.32), channel_id=1, replica_groups=mesh['x'=4,'z'=4,'c'=2,'y'=4] {'y','x','z','c'}, dimensions={0} | all-to-all | bytes 262144 | tf_op jit(solution)/shard_map/all_to_all | solution.py:45
  111.0 14.2 %all_to_all.22.got_ref = f32[128,1,256]{2,1,0:T(1,128)S(1)} all-to-all(f32[128,1,256]{2,1,0:T(1,128)S(1)} %broadcast_in_dim.12), channel_id=1, replica_groups=mesh['x'=4,'z'=4,'c'=2,'y'=4] {'y','x','z','c'}, dimensions={0} | all-to-all | bytes 262144 | tf_op jit(solution)/shard_map/all_to_all | solution.py:45
  125.8 14.2 %all_to_all.23.last_ref = f32[128,1,256]{2,1,0:T(1,128)S(1)} all-to-all(f32[128,1,256]{2,1,0:T(1,128)S(1)} %broadcast_in_dim.13), channel_id=1, replica_groups=mesh['x'=4,'z'=4,'c'=2,'y'=4] {'y','x','z','c'}, dimensions={0} | all-to-all | bytes 262144 | tf_op jit(solution)/shard_map/all_to_all | solution.py:45
  140.0 2.7 %shard_map.37 = (f32[256,2048]{1,0:T(8,128)}, f32[1,256]{1,0:T(1,128)}) custom-call(s32[4]{0:T(128)S(1)} %pad_add_fusion.where_ref._, f32[128,1,256]{2,1,0:T(1,128)S(1)} %all_to_all.22.got_ref, f32[128,1,256]{2,1,0:T(1,128)S(1)} %all_to_all.23.last_ref, f32[256,2048]{1,0:T(8,128)S(1)} %get-tuple-element.30.sym_ref, ...), custom_call_target="tpu_custom_call" | custom-call | tf_op jit(solution)/shard_map/pallas_call | solution.py:243
  (67 shorter events, 11.9 us)
Async XLA Ops:
  0.6 16.0 %copy-start = (bf16[512,256]{1,0:T(8,128)(2,1)S(1)}, bf16[512,256]{1,0:T(8,128)(2,1)}, u32[]{:S(2)}) copy-start(bf16[512,256]{1,0:T(8,128)(2,1)} %refs_0_.1) | copy-start | bytes 786436
  1.7 6.5 %collective-permute-start.14 = (bf16[256,256]{1,0:T(8,128)(2,1)S(1)}, bf16[256,256]{1,0:T(8,128)(2,1)S(1)}, u32[]{:S(2)}, u32[]{:S(2)}) collective-permute-start(bf16[256,256]{1,0:T(8,128)(2,1)S(1)} %get-tuple-element.43), channel_id=1, source_target_pairs={{0,64},{32,96},{64,0},{96,32},{1,65},{33,97},{65,1},{97,33},{2,66}... | collective-permute-start | bytes 393224 | tf_op jit(solution)/shard_map/ppermute | solution.py:41
  5.3 6.0 %collective-permute-start.15 = (bf16[256,256]{1,0:T(8,128)(2,1)S(1)}, bf16[256,256]{1,0:T(8,128)(2,1)S(1)}, u32[]{:S(2)}, u32[]{:S(2)}) collective-permute-start(bf16[256,256]{1,0:T(8,128)(2,1)S(1)} %get-tuple-element.43), channel_id=1, source_target_pairs={{0,96},{32,0},{64,32},{96,64},{1,97},{33,1},{65,33},{97,65},{2,98}... | collective-permute-start | bytes 393224 | tf_op jit(solution)/shard_map/ppermute | solution.py:41
  6.2 5.2 %collective-permute-start.13 = (bf16[256,256]{1,0:T(8,128)(2,1)S(1)}, bf16[256,256]{1,0:T(8,128)(2,1)S(1)}, u32[]{:S(2)}, u32[]{:S(2)}) collective-permute-start(bf16[256,256]{1,0:T(8,128)(2,1)S(1)} %get-tuple-element.43), channel_id=1, source_target_pairs={{0,32},{32,64},{64,96},{96,0},{1,33},{33,65},{65,97},{97,1},{2,34}... | collective-permute-start | bytes 393224 | tf_op jit(solution)/shard_map/ppermute | solution.py:41
  6.8 10.0 %collective-permute-start.3 = (bf16[256,256]{1,0:T(8,128)(2,1)S(1)}, bf16[256,256]{1,0:T(8,128)(2,1)S(1)}, u32[]{:S(2)}, u32[]{:S(2)}) collective-permute-start(bf16[256,256]{1,0:T(8,128)(2,1)S(1)} %get-tuple-element.44), channel_id=1, source_target_pairs={{0,0},{4,4},{8,8},{12,12},{16,16},{20,20},{24,24},{28,28},{1,32},{... | collective-permute-start | bytes 393224 | tf_op jit(solution)/shard_map/ppermute | solution.py:258
  11.5 10.3 %collective-permute-start.16 = (bf16[256,256]{1,0:T(8,128)(2,1)S(1)}, bf16[256,256]{1,0:T(8,128)(2,1)S(1)}, u32[]{:S(2)}, u32[]{:S(2)}) collective-permute-start(bf16[256,256]{1,0:T(8,128)(2,1)S(1)} %get-tuple-element.41), channel_id=1, source_target_pairs={{0,1},{1,2},{2,3},{3,0},{4,5},{5,6},{6,7},{7,4},{8,9},{9,10},{10,1... | collective-permute-start | bytes 393224 | tf_op jit(solution)/shard_map/ppermute | solution.py:266
  12.9 11.1 %collective-permute-start.17 = (bf16[256,256]{1,0:T(8,128)(2,1)S(1)}, bf16[256,256]{1,0:T(8,128)(2,1)S(1)}, u32[]{:S(2)}, u32[]{:S(2)}) collective-permute-start(bf16[256,256]{1,0:T(8,128)(2,1)S(1)} %get-tuple-element.40), channel_id=1, source_target_pairs={{0,2},{1,3},{2,0},{3,1},{4,6},{5,7},{6,4},{7,5},{8,10},{9,11},{10,... | collective-permute-start | bytes 393224 | tf_op jit(solution)/shard_map/ppermute | solution.py:266
  15.5 8.5 %collective-permute-start.18 = (bf16[256,256]{1,0:T(8,128)(2,1)S(1)}, bf16[256,256]{1,0:T(8,128)(2,1)S(1)}, u32[]{:S(2)}, u32[]{:S(2)}) collective-permute-start(bf16[256,256]{1,0:T(8,128)(2,1)S(1)} %get-tuple-element.39), channel_id=1, source_target_pairs={{0,3},{1,0},{2,1},{3,2},{4,7},{5,4},{6,5},{7,6},{8,11},{9,8},{10,9... | collective-permute-start | bytes 393224 | tf_op jit(solution)/shard_map/ppermute | solution.py:266
  16.8 29.8 %collective-permute-start.4 = (bf16[256,256]{1,0:T(8,128)(2,1)S(1)}, bf16[256,256]{1,0:T(8,128)(2,1)S(1)}, u32[]{:S(2)}, u32[]{:S(2)}) collective-permute-start(bf16[256,256]{1,0:T(8,128)(2,1)S(1)} %collective-permute-done.3), channel_id=1, source_target_pairs={{0,8},{8,16},{16,24},{24,0},{1,9},{9,17},{17,25},{25,1},{2,10},{10... | collective-permute-start | bytes 393224 | tf_op jit(solution)/shard_map/ppermute | solution.py:41
  18.5 28.1 %collective-permute-start.5 = (bf16[256,256]{1,0:T(8,128)(2,1)S(1)}, bf16[256,256]{1,0:T(8,128)(2,1)S(1)}, u32[]{:S(2)}, u32[]{:S(2)}) collective-permute-start(bf16[256,256]{1,0:T(8,128)(2,1)S(1)} %collective-permute-done.3), channel_id=1, source_target_pairs={{0,16},{8,24},{16,0},{24,8},{1,17},{9,25},{17,1},{25,9},{2,18},{10... | collective-permute-start | bytes 393224 | tf_op jit(solution)/shard_map/ppermute | solution.py:41
  21.8 24.8 %collective-permute-start.6 = (bf16[256,256]{1,0:T(8,128)(2,1)S(1)}, bf16[256,256]{1,0:T(8,128)(2,1)S(1)}, u32[]{:S(2)}, u32[]{:S(2)}) collective-permute-start(bf16[256,256]{1,0:T(8,128)(2,1)S(1)} %collective-permute-done.3), channel_id=1, source_target_pairs={{0,24},{8,0},{16,8},{24,16},{1,25},{9,1},{17,9},{25,17},{2,26},{10... | collective-permute-start | bytes 393224 | tf_op jit(solution)/shard_map/ppermute | solution.py:41
  24.1 31.7 %collective-permute-start.19 = (bf16[4,256,256]{2,1,0:T(8,128)(2,1)S(1)}, bf16[4,256,256]{2,1,0:T(8,128)(2,1)S(1)}, u32[]{:S(2)}, u32[]{:S(2)}) collective-permute-start(bf16[4,256,256]{2,1,0:T(8,128)(2,1)S(1)} %pad_maximum_fusion.2.refs_3_), channel_id=1, source_target_pairs={{0,8},{8,16},{16,24},{24,0},{1,9},{9,17},{17,25},{25,1},{2,10},{10... | collective-permute-start | bytes 1572872 | tf_op jit(solution)/shard_map/ppermute | solution.py:199
  45.7 12.5 %collective-permute-start.20 = (bf16[4,256,256]{2,1,0:T(8,128)(2,1)S(1)}, bf16[4,256,256]{2,1,0:T(8,128)(2,1)S(1)}, u32[]{:S(2)}, u32[]{:S(2)}) collective-permute-start(bf16[4,256,256]{2,1,0:T(8,128)(2,1)S(1)} %pad_maximum_fusion.2.refs_3_), channel_id=1, source_target_pairs={{0,24},{8,0},{16,8},{24,16},{1,25},{9,1},{17,9},{25,17},{2,26},{10... | collective-permute-start | bytes 1572872 | tf_op jit(solution)/shard_map/ppermute | solution.py:199
  46.7 14.1 %collective-permute-start.7 = (bf16[4,256,256]{2,1,0:T(8,128)(2,1)S(1)}, bf16[4,256,256]{2,1,0:T(8,128)(2,1)S(1)}, u32[]{:S(2)}, u32[]{:S(2)}) collective-permute-start(bf16[4,256,256]{2,1,0:T(8,128)(2,1)S(1)} %pad_maximum_fusion.refs_0_), channel_id=1, source_target_pairs={{0,32},{32,64},{64,96},{96,0},{1,33},{33,65},{65,97},{97,1},{2,34}... | collective-permute-start | bytes 1572872 | tf_op jit(solution)/shard_map/ppermute | solution.py:199
  47.1 6.9 %collective-permute-start = (bf16[512,256]{1,0:T(8,128)(2,1)S(1)}, bf16[512,256]{1,0:T(8,128)(2,1)S(1)}, u32[]{:S(2)}, u32[]{:S(2)}) collective-permute-start(bf16[512,256]{1,0:T(8,128)(2,1)S(1)} %copy-done), channel_id=1, source_target_pairs={{0,3},{1,0},{2,1},{3,2},{4,7},{5,4},{6,5},{7,6},{8,11},{9,8},{10,9... | collective-permute-start | bytes 786440 | tf_op jit(solution)/shard_map/ppermute | solution.py:272
  47.9 13.8 %collective-permute-start.8 = (bf16[4,256,256]{2,1,0:T(8,128)(2,1)S(1)}, bf16[4,256,256]{2,1,0:T(8,128)(2,1)S(1)}, u32[]{:S(2)}, u32[]{:S(2)}) collective-permute-start(bf16[4,256,256]{2,1,0:T(8,128)(2,1)S(1)} %pad_maximum_fusion.refs_0_), channel_id=1, source_target_pairs={{0,96},{32,0},{64,32},{96,64},{1,97},{33,1},{65,33},{97,65},{2,98}... | collective-permute-start | bytes 1572872 | tf_op jit(solution)/shard_map/ppermute | solution.py:199
  54.0 21.1 %collective-permute-start.28 = (bf16[4,256,256]{2,1,0:T(8,128)(2,1)S(1)}, bf16[4,256,256]{2,1,0:T(8,128)(2,1)S(1)}, u32[]{:S(2)}, u32[]{:S(2)}) collective-permute-start(bf16[4,256,256]{2,1,0:T(8,128)(2,1)S(1)} %pad_maximum_fusion.2.refs_3_), channel_id=1, source_target_pairs={{0,4},{4,0},{1,5},{5,1},{2,6},{6,2},{3,7},{7,3},{8,12},{12,8},{9,1... | collective-permute-start | bytes 1572872 | tf_op jit(solution)/shard_map/ppermute | solution.py:213
  55.8 20.0 %collective-permute-start.25 = (bf16[4,256,256]{2,1,0:T(8,128)(2,1)S(1)}, bf16[4,256,256]{2,1,0:T(8,128)(2,1)S(1)}, u32[]{:S(2)}, u32[]{:S(2)}) collective-permute-start(bf16[4,256,256]{2,1,0:T(8,128)(2,1)S(1)} %pad_maximum_fusion.refs_0_), channel_id=1, source_target_pairs={{0,4},{4,0},{1,5},{5,1},{2,6},{6,2},{3,7},{7,3},{8,12},{12,8},{9,1... | collective-permute-start | bytes 1572872 | tf_op jit(solution)/shard_map/ppermute | solution.py:213
  58.2 7.5 %collective-permute-start.1 = (bf16[512,256]{1,0:T(8,128)(2,1)S(1)}, bf16[512,256]{1,0:T(8,128)(2,1)S(1)}, u32[]{:S(2)}, u32[]{:S(2)}) collective-permute-start(bf16[512,256]{1,0:T(8,128)(2,1)S(1)} %copy-done), channel_id=1, source_target_pairs={{0,2},{1,3},{2,0},{3,1},{4,6},{5,7},{6,4},{7,5},{8,10},{9,11},{10,... | collective-permute-start | bytes 786440 | tf_op jit(solution)/shard_map/ppermute | solution.py:272
  60.8 12.3 %collective-permute-start.2 = (bf16[512,256]{1,0:T(8,128)(2,1)S(1)}, bf16[512,256]{1,0:T(8,128)(2,1)S(1)}, u32[]{:S(2)}, u32[]{:S(2)}) collective-permute-start(bf16[512,256]{1,0:T(8,128)(2,1)S(1)} %copy-done), channel_id=1, source_target_pairs={{0,1},{1,2},{2,3},{3,0},{4,5},{5,6},{6,7},{7,4},{8,9},{9,10},{10,1... | collective-permute-start | bytes 786440 | tf_op jit(solution)/shard_map/ppermute | solution.py:272
  61.7 14.2 %collective-permute-start.21 = (bf16[2,256,256]{2,1,0:T(8,128)(2,1)S(1)}, bf16[2,256,256]{2,1,0:T(8,128)(2,1)S(1)}, u32[]{:S(2)}, u32[]{:S(2)}) collective-permute-start(bf16[2,256,256]{2,1,0:T(8,128)(2,1)S(1)} %get-tuple-element.27), channel_id=1, source_target_pairs={{0,8},{8,16},{16,24},{24,0},{1,9},{9,17},{17,25},{25,1},{2,10},{10... | collective-permute-start | bytes 786440 | tf_op jit(solution)/shard_map/ppermute | solution.py:209
  65.7 10.6 %collective-permute-start.23 = (bf16[2,256,256]{2,1,0:T(8,128)(2,1)S(1)}, bf16[2,256,256]{2,1,0:T(8,128)(2,1)S(1)}, u32[]{:S(2)}, u32[]{:S(2)}) collective-permute-start(bf16[2,256,256]{2,1,0:T(8,128)(2,1)S(1)} %get-tuple-element.28), channel_id=1, source_target_pairs={{0,24},{8,0},{16,8},{24,16},{1,25},{9,1},{17,9},{25,17},{2,26},{10... | collective-permute-start | bytes 786440 | tf_op jit(solution)/shard_map/ppermute | solution.py:209
  73.1 7.1 %collective-permute-start.11 = (bf16[2,256,256]{2,1,0:T(8,128)(2,1)S(1)}, bf16[2,256,256]{2,1,0:T(8,128)(2,1)S(1)}, u32[]{:S(2)}, u32[]{:S(2)}) collective-permute-start(bf16[2,256,256]{2,1,0:T(8,128)(2,1)S(1)} %get-tuple-element.26), channel_id=1, source_target_pairs={{0,96},{32,0},{64,32},{96,64},{1,97},{33,1},{65,33},{97,65},{2,98}... | collective-permute-start | bytes 786440 | tf_op jit(solution)/shard_map/ppermute | solution.py:209
  75.0 11.2 %collective-permute-start.29 = (bf16[4,256,256]{2,1,0:T(8,128)(2,1)S(1)}, bf16[4,256,256]{2,1,0:T(8,128)(2,1)S(1)}, u32[]{:S(2)}, u32[]{:S(2)}) collective-permute-start(bf16[4,256,256]{2,1,0:T(8,128)(2,1)S(1)} %collective-permute-done.19.back_ref.refs_4_), channel_id=1, source_target_pairs={{0,4},{4,0},{1,5},{5,1},{2,6},{6,2},{3,7},{7,3},{8,12},{12,8},{9,1... | collective-permute-start | bytes 1572872 | tf_op jit(solution)/shard_map/ppermute | solution.py:213
  75.8 10.5 %collective-permute-start.30 = (bf16[4,256,256]{2,1,0:T(8,128)(2,1)S(1)}, bf16[4,256,256]{2,1,0:T(8,128)(2,1)S(1)}, u32[]{:S(2)}, u32[]{:S(2)}) collective-permute-start(bf16[4,256,256]{2,1,0:T(8,128)(2,1)S(1)} %collective-permute-done.20.on_ref.refs_5_), channel_id=1, source_target_pairs={{0,4},{4,0},{1,5},{5,1},{2,6},{6,2},{3,7},{7,3},{8,12},{12,8},{9,1... | collective-permute-start | bytes 1572872 | tf_op jit(solution)/shard_map/ppermute | solution.py:213
  75.9 10.9 %collective-permute-start.26 = (bf16[4,256,256]{2,1,0:T(8,128)(2,1)S(1)}, bf16[4,256,256]{2,1,0:T(8,128)(2,1)S(1)}, u32[]{:S(2)}, u32[]{:S(2)}) collective-permute-start(bf16[4,256,256]{2,1,0:T(8,128)(2,1)S(1)} %collective-permute-done.7.back_ref.refs_1_), channel_id=1, source_target_pairs={{0,4},{4,0},{1,5},{5,1},{2,6},{6,2},{3,7},{7,3},{8,12},{12,8},{9,1... | collective-permute-start | bytes 1572872 | tf_op jit(solution)/shard_map/ppermute | solution.py:213
  76.3 8.3 %collective-permute-start.9 = (bf16[2,256,256]{2,1,0:T(8,128)(2,1)S(1)}, bf16[2,256,256]{2,1,0:T(8,128)(2,1)S(1)}, u32[]{:S(2)}, u32[]{:S(2)}) collective-permute-start(bf16[2,256,256]{2,1,0:T(8,128)(2,1)S(1)} %get-tuple-element.25), channel_id=1, source_target_pairs={{0,32},{32,64},{64,96},{96,0},{1,33},{33,65},{65,97},{97,1},{2,34}... | collective-permute-start | bytes 786440 | tf_op jit(solution)/shard_map/ppermute | solution.py:209
  80.2 11.8 %collective-permute-start.27 = (bf16[4,256,256]{2,1,0:T(8,128)(2,1)S(1)}, bf16[4,256,256]{2,1,0:T(8,128)(2,1)S(1)}, u32[]{:S(2)}, u32[]{:S(2)}) collective-permute-start(bf16[4,256,256]{2,1,0:T(8,128)(2,1)S(1)} %collective-permute-done.8.on_ref.refs_2_), channel_id=1, source_target_pairs={{0,4},{4,0},{1,5},{5,1},{2,6},{6,2},{3,7},{7,3},{8,12},{12,8},{9,1... | collective-permute-start | bytes 1572872 | tf_op jit(solution)/shard_map/ppermute | solution.py:213
  84.7 9.7 %collective-permute-start.22 = (bf16[2,256,256]{2,1,0:T(8,128)(2,1)S(1)}, bf16[2,256,256]{2,1,0:T(8,128)(2,1)S(1)}, u32[]{:S(2)}, u32[]{:S(2)}) collective-permute-start(bf16[2,256,256]{2,1,0:T(8,128)(2,1)S(1)} %collective-permute-done.21.za), channel_id=1, source_target_pairs={{0,4},{4,0},{1,5},{5,1},{2,6},{6,2},{3,7},{7,3},{8,12},{12,8},{9,1... | collective-permute-start | bytes 786440 | tf_op jit(solution)/shard_map/ppermute | solution.py:213
  86.3 8.2 %collective-permute-start.24 = (bf16[2,256,256]{2,1,0:T(8,128)(2,1)S(1)}, bf16[2,256,256]{2,1,0:T(8,128)(2,1)S(1)}, u32[]{:S(2)}, u32[]{:S(2)}) collective-permute-start(bf16[2,256,256]{2,1,0:T(8,128)(2,1)S(1)} %collective-permute-done.23.zb), channel_id=1, source_target_pairs={{0,4},{4,0},{1,5},{5,1},{2,6},{6,2},{3,7},{7,3},{8,12},{12,8},{9,1... | collective-permute-start | bytes 786440 | tf_op jit(solution)/shard_map/ppermute | solution.py:213
  86.3 8.2 %collective-permute-start.10 = (bf16[2,256,256]{2,1,0:T(8,128)(2,1)S(1)}, bf16[2,256,256]{2,1,0:T(8,128)(2,1)S(1)}, u32[]{:S(2)}, u32[]{:S(2)}) collective-permute-start(bf16[2,256,256]{2,1,0:T(8,128)(2,1)S(1)} %collective-permute-done.9.xa), channel_id=1, source_target_pairs={{0,4},{4,0},{1,5},{5,1},{2,6},{6,2},{3,7},{7,3},{8,12},{12,8},{9,1... | collective-permute-start | bytes 786440 | tf_op jit(solution)/shard_map/ppermute | solution.py:213
  86.8 7.7 %collective-permute-start.12 = (bf16[2,256,256]{2,1,0:T(8,128)(2,1)S(1)}, bf16[2,256,256]{2,1,0:T(8,128)(2,1)S(1)}, u32[]{:S(2)}, u32[]{:S(2)}) collective-permute-start(bf16[2,256,256]{2,1,0:T(8,128)(2,1)S(1)} %collective-permute-done.11.xb), channel_id=1, source_target_pairs={{0,4},{4,0},{1,5},{5,1},{2,6},{6,2},{3,7},{7,3},{8,12},{12,8},{9,1... | collective-permute-start | bytes 786440 | tf_op jit(solution)/shard_map/ppermute | solution.py:213

commit v10 on v8

--- a/solution.py
+++ b/solution.py
@@ -114,22 +114,13 @@
     return grouped(acc)
 
 
-def far(where, left, by_x, by_z, so_far):
-    def kernel(where_ref, left_ref, xa, xb, za, zb, near_ref, out_ref):
-        for dz in range(4):
-            out_ref[dz] = near_ref[dz] + far_sums(where_ref, left_ref, (xa, xb), (za, zb), dz)
-
-    return call(kernel, [f32(4, PART, WIDTH)], where, left, *by_x, *by_z, so_far)[0]
-
-
-def far_and_first(where, left, by_x, by_z, so_far, own, ratio_rows):
-    def kernel(where_ref, left_ref, xa, xb, za, zb, near_ref, own_ref, ratio_ref,
-               sym_ref, visit_ref, send_ref, total_ref):
+def far_and_first(where, left, own, sibling, ratio_rows):
+    def kernel(where_ref, left_ref, *refs):
+        ratio_ref, sym_ref, visit_ref, send_ref, total_ref = refs[10:]
         z, c = where_ref[2], where_ref[3]
-        for dz in range(4):
-            mine = own_ref[dz]
-            theirs = near_ref[dz] + far_sums(where_ref, left_ref, (xa, xb), (za, zb), dz)
-            for core, part in ((c, mine), (1 - c, theirs)):
+        for core, (near_ref, xa, xb, za, zb) in ((c, refs[:5]), (1 - c, refs[5:10])):
+            for dz in range(4):
+                part = near_ref[dz] + far_sums(where_ref, left_ref, (xa, xb), (za, zb), dz)
                 g = lax.rem(z + 4 - dz, 4) * 2 + core
                 sym_ref[:, pl.ds(pl.multiple_of(g * WIDTH, WIDTH), WIDTH)] = part[:WIDTH]
                 frame = part[WIDTH:]
@@ -139,7 +130,7 @@
         send_ref[...] = jnp.broadcast_to(sums[None], send_ref.shape)
 
     out = [f32(WIDTH, COLS), f32(GROUPS, WIDTH), f32(128, 1, WIDTH), f32(GROUPS, WIDTH)]
-    return call(kernel, out, where, left, *by_x, *by_z, so_far, own, ratio_rows)[:3]
+    return call(kernel, out, where, left, *own, *sibling, ratio_rows)[:3]
 
 
 def three_parts(v):
@@ -213,24 +204,20 @@
     return [lax.ppermute(v, "c", [(0, 1), (1, 0)]) for v in vs]
 
 
-def finish(where, got, last, sym, visit_cols, visit_rows):
-    def kernel(where_ref, got_ref, last_ref, sym_ref, visit_col_ref, visit_row_ref,
-               out_ref, share_ref, total_ref, row_ref, scale_ref, col_ref):
+def finish(where, last, sym, ratio_rows, ratio_cols):
+    def kernel(where_ref, last_ref, sym_ref, ratio_ref, col_ref,
+               out_ref, share_ref, total_ref, row_ref, scale_ref):
         step = pl.program_id(0)
-        x, y, z, c = (where_ref[i] for i in range(4))
+        x, _, z, c = (where_ref[i] for i in range(4))
 
         @pl.when(step == 0)
         def _():
-            w = (x * 4 + z) * 2 + c
             total_ref[...] = sum(last_ref[32 * k:32 * k + 32] for k in range(4))
-            own = total_ref[w]
+            own = total_ref[(x * 4 + z) * 2 + c]
             scale_ref[...] = jnp.broadcast_to(STATES / own, (LANES, WIDTH)).T
             grand = jnp.sum(jnp.sum(total_ref[...], axis=0), axis=1, keepdims=True)
             share_ref[...] = STATES * own / grand
-            total_ref[...] = sum(got_ref[32 * k:32 * k + 32] for k in range(4))
-            row_ref[...] = jnp.broadcast_to(visit_row_ref[...] / total_ref[w], (LANES, WIDTH)).T
-            for g in range(GROUPS):
-                col_ref[g:g + 1, :] = visit_col_ref[g:g + 1, :] / total_ref[y * GROUPS + g]
+            row_ref[...] = jnp.broadcast_to(ratio_ref[...], (LANES, WIDTH)).T
 
         rows = pl.ds(pl.multiple_of(step * ROWS, ROWS), ROWS)
         for k in range(COLS // LANES):
@@ -243,13 +230,13 @@
     return pl.pallas_call(
         kernel,
         grid=(WIDTH // ROWS,),
-        in_specs=[SMEM, VMEM, VMEM, block, VMEM, VMEM],
+        in_specs=[SMEM, VMEM, block, VMEM, VMEM],
         out_specs=[block, pl.BlockSpec((1, WIDTH), lambda i: (0, 0))],
         out_shape=[f32(WIDTH, COLS), f32(1, WIDTH)],
         scratch_shapes=[pltpu.VMEM((32, 1, WIDTH), jnp.float32)]
-        + [pltpu.VMEM((WIDTH, LANES), jnp.float32)] * 2 + [pltpu.VMEM((GROUPS, WIDTH), jnp.float32)],
+        + [pltpu.VMEM((WIDTH, LANES), jnp.float32)] * 2,
         compiler_params=pltpu.CompilerParams(vmem_limit_bytes=16 << 20),
-    )(where, got, last, sym, visit_cols, visit_rows)
+    )(where, last, sym, ratio_rows, ratio_cols)
 
 
 def shards(member):
@@ -273,18 +260,18 @@
     once_x, once_z = swapped([once_x, once_z])
     near_x, near_z = swapped(near_x), swapped(near_z)
     sibling = near(where, left, [once_x] + near_x, [once_z] + near_z)
-    own = far(where, left, far_x, far_z, own)
-    far_x, far_z = swapped(far_x), swapped(far_z)
-    sym, visit_cols, send = far_and_first(where, left, far_x, far_z, sibling, own, ratio_rows)
+    own, sibling = [own, *far_x, *far_z], [sibling, *swapped(far_x + far_z)]
+    sym, visit_cols, send = far_and_first(where, left, own, sibling, ratio_rows)
     for _ in range(2):
         got = to_all(send)
         totals = jnp.sum(got.reshape(4, 32, WIDTH), axis=0)
         total_rows = lax.dynamic_slice(totals, (w, jnp.uint32(0)), (1, WIDTH)).reshape(WIDTH)
         total_cols = lax.dynamic_slice(totals, (first, jnp.uint32(0)), (GROUPS, WIDTH))
         ratio_rows = visit_rows.reshape(WIDTH) / total_rows
-        ratio = ratio_rows[:, None] + (visit_cols / total_cols).reshape(COLS)[None, :]
+        ratio_cols = visit_cols / total_cols
+        ratio = ratio_rows[:, None] + ratio_cols.reshape(COLS)[None, :]
         send = jnp.broadcast_to(jnp.sum(sym / ratio, axis=1), (128, 1, WIDTH))
-    transition, stationary = finish(where, got, to_all(send), sym, visit_cols, visit_rows)
+    transition, stationary = finish(where, to_all(send), sym, ratio_rows.reshape(1, WIDTH), ratio_cols)
     return (transition, stationary.reshape(WIDTH))
 
 

time: 151 us -> 156 us (1.033)
  starting transfers between devices: 54.5 us -> 45 us
  waiting for transfers between devices: 21.1 us -> 29.4 us
  blocking collectives: 58.9 us -> 65.1 us
    ppermute x6, starting transfers between devices: 26 us -> 18.1 us  [ring(): return [v] + [lax.ppermute(v, axis, along(k)) for k in (1, 2, 3)]]
    ppermute x3, waiting for transfers between devices: 7.62 us -> 14.3 us  [shards(): blocks = [member] + [lax.ppermute(kept, 'y', along(-k)) for k in (1, 2, 3)]]
    all_to_all x4, blocking collectives: 58.9 us -> 65.1 us  [to_all(): return lax.all_to_all(sent, ('y',) + WIDE, 0, 0)]
    ppermute x3, starting transfers between devices: 7.97 us -> 2.09 us  [shards(): blocks = [member] + [lax.ppermute(kept, 'y', along(-k)) for k in (1, 2, 3)]]
    ppermute x4, starting transfers between devices: 5.6 us -> 11.1 us  [from_sides(): return [lax.ppermute(v, axis, along(k)) for k in (1, 3)]]
    ppermute x2, starting transfers between devices: 7.11 us -> 3.19 us  [from_afar(): lax.ppermute(halves[1], axis, along(3))]
    ppermute x2, waiting for transfers between devices: 3.74 us -> 0.06 us  [from_afar(): lax.ppermute(halves[1], axis, along(3))]
    ppermute x6, waiting for transfers between devices: 3.96 us -> 7.36 us  [ring(): return [v] + [lax.ppermute(v, axis, along(k)) for k in (1, 2, 3)]]
  transfers between devices with their start and end apart: 28 -> 28, of which waited for: 9 -> 10; matrix products, arithmetic and copies ran while one was open for 1% -> 1% of each run, Pallas kernels for 6% -> 5%
where the time goes in v10:
time: 156 us; the launch traced here: 155 us
  blocking collectives  65.1 us (42%)
  starting transfers between devices  45 us (29%)
  waiting for transfers between devices  29.4 us (19%)
  Pallas kernels  12.5 us (8%)
  other arithmetic  2.26 us (1%)
    all_to_all x4, blocking collectives, to_all(): return lax.all_to_all(sent, ('y',) + WIDE, 0, 0)  65.1 us
    ppermute x6, starting transfers between devices, ring(): return [v] + [lax.ppermute(v, axis, along(k)) for k in (1, 2, 3)]  18.1 us
    ppermute x3, waiting for transfers between devices, shards(): blocks = [member] + [lax.ppermute(kept, 'y', along(-k)) for k in (1, 2, 3)]  14.3 us
    ppermute x4, starting transfers between devices, from_sides(): return [lax.ppermute(v, axis, along(k)) for k in (1, 3)]  11.1 us
    pallas_call x5, Pallas kernels, call(): pl.pallas_call(kernel, in_specs=[SMEM] + [VMEM] * (len(operands) - 1), ou...  8.57 us
    ppermute x6, waiting for transfers between devices, ring(): return [v] + [lax.ppermute(v, axis, along(k)) for k in (1, 2, 3)]  7.36 us
    ppermute x10, starting transfers between devices, swapped(): return [lax.ppermute(v, 'c', [(0, 1), (1, 0)]) for v in vs]  6.24 us
    ppermute x2, waiting for transfers between devices, from_afar(): lax.ppermute(halves[0], axis, along(1))  4.61 us
  transfers between devices with their start and end apart: 28, of which 10 were waited for; matrix products, arithmetic and copies ran while one was open for 1% of the time, Pallas kernels for 5%

profile of v10, /device:TPU:1, one launch (start us, length us, event | category | flops | bytes accessed | tf_op | source)
XLA Modules:
  0.0 155.5 jit_solution(7496173775950075265)
XLA Ops:
  0.6 1.7 %collective-permute-start.3 = (bf16[512,256]{1,0:T(8,128)(2,1)}, bf16[512,256]{1,0:T(8,128)(2,1)S(1)}, u32[]{:S(2)}, u32[]{:S(2)}) collective-permute-start(bf16[512,256]{1,0:T(8,128)(2,1)} %refs_0_.1), channel_id=1, source_target_pairs={{0,0},{4,4},{8,8},{12,12},{16,16},{20,20},{24,24},{28,28},{1,32},{... | collective-permute-start | bytes 786440 | tf_op jit(solution)/shard_map/ppermute | solution.py:245
  2.4 4.6 %collective-permute-start.6 = (bf16[256,256]{1,0:T(8,128)(2,1)S(1)}, bf16[256,256]{1,0:T(8,128)(2,1)S(1)}, u32[]{:S(2)}, u32[]{:S(2)}) collective-permute-start(bf16[256,256]{1,0:T(8,128)(2,1)S(1)} %get-tuple-element.41), channel_id=1, source_target_pairs={{0,24},{8,0},{16,8},{24,16},{1,25},{9,1},{17,9},{25,17},{2,26},{10... | collective-permute-start | bytes 393224 | tf_op jit(solution)/shard_map/ppermute | solution.py:41
  7.8 1.1 convert_reduce_fusion
  8.9 3.8 %collective-permute-done.6 = bf16[256,256]{1,0:T(8,128)(2,1)S(1)} collective-permute-done((bf16[256,256]{1,0:T(8,128)(2,1)S(1)}, bf16[256,256]{1,0:T(8,128)(2,1)S(1)}, u32[]{:S(2)}, u32[]{:S(2)}) %collective-permute-start.6) | collective-permute-done | bytes 131104 | tf_op jit(solution)/shard_map/ppermute | solution.py:41
  12.8 3.5 %collective-permute-done.4 = bf16[256,256]{1,0:T(8,128)(2,1)S(1)} collective-permute-done((bf16[256,256]{1,0:T(8,128)(2,1)S(1)}, bf16[256,256]{1,0:T(8,128)(2,1)S(1)}, u32[]{:S(2)}, u32[]{:S(2)}) %collective-permute-start.4) | collective-permute-done | bytes 131104 | tf_op jit(solution)/shard_map/ppermute | solution.py:41
  16.3 8.0 %collective-permute-start.7 = (bf16[4,256,256]{2,1,0:T(8,128)(2,1)S(1)}, bf16[4,256,256]{2,1,0:T(8,128)(2,1)S(1)}, u32[]{:S(2)}, u32[]{:S(2)}) collective-permute-start(bf16[4,256,256]{2,1,0:T(8,128)(2,1)S(1)} %pad_maximum_fusion.refs_0_), channel_id=1, source_target_pairs={{0,32},{32,64},{64,96},{96,0},{1,33},{33,65},{65,97},{97,1},{2,34}... | collective-permute-start | bytes 1572872 | tf_op jit(solution)/shard_map/ppermute | solution.py:190
  24.3 10.8 %collective-permute-start.11 = (bf16[256,256]{1,0:T(8,128)(2,1)S(1)}, bf16[256,256]{1,0:T(8,128)(2,1)S(1)}, u32[]{:S(2)}, u32[]{:S(2)}) collective-permute-start(bf16[256,256]{1,0:T(8,128)(2,1)S(1)} %get-tuple-element.40), channel_id=1, source_target_pairs={{0,96},{32,0},{64,32},{96,64},{1,97},{33,1},{65,33},{97,65},{2,98}... | collective-permute-start | bytes 393224 | tf_op jit(solution)/shard_map/ppermute | solution.py:41
  35.1 1.3 collective-permute-start.10
  37.2 20.7 %all_to_all.20.refs_4_ = bf16[128,2,256]{2,1,0:T(2,128)(2,1)S(1)} all-to-all(bf16[128,2,256]{2,1,0:T(2,128)(2,1)S(1)} %broadcast_in_dim.11), channel_id=1, replica_groups=mesh['x'=4,'z'=4,'c'=2,'y'=4] {'y','x','z','c'}, dimensions={0} | all-to-all | bytes 262144 | tf_op jit(solution)/shard_map/all_to_all | solution.py:45
  58.0 1.3 collective-permute-start.12
  59.5 1.8 %collective-permute-start.13 = (bf16[4,256,256]{2,1,0:T(8,128)(2,1)S(1)}, bf16[4,256,256]{2,1,0:T(8,128)(2,1)S(1)}, u32[]{:S(2)}, u32[]{:S(2)}) collective-permute-start(bf16[4,256,256]{2,1,0:T(8,128)(2,1)S(1)} %pad_maximum_fusion.1.refs_3_), channel_id=1, source_target_pairs={{0,24},{8,0},{16,8},{24,16},{1,25},{9,1},{17,9},{25,17},{2,26},{10... | collective-permute-start | bytes 1572872 | tf_op jit(solution)/shard_map/ppermute | solution.py:190
  61.3 5.3 %collective-permute-done.refs_1_ = bf16[512,256]{1,0:T(8,128)(2,1)S(1)} collective-permute-done((bf16[512,256]{1,0:T(8,128)(2,1)S(1)}, bf16[512,256]{1,0:T(8,128)(2,1)S(1)}, u32[]{:S(2)}, u32[]{:S(2)}) %collective-permute-start) | collective-permute-done | bytes 262176 | tf_op jit(solution)/shard_map/ppermute | solution.py:257
  66.5 1.5 collective-permute-start.18
  68.1 2.9 %collective-permute-done.8.refs_2_.on_ref = bf16[4,256,256]{2,1,0:T(8,128)(2,1)S(1)} collective-permute-done((bf16[4,256,256]{2,1,0:T(8,128)(2,1)S(1)}, bf16[4,256,256]{2,1,0:T(8,128)(2,1)S(1)}, u32[]{:S(2)}, u32[]{:S(2)}) %collective-permute-start.8) | collective-permute-done | bytes 524320 | tf_op jit(solution)/shard_map/ppermute | solution.py:190
  71.0 1.2 collective-permute-start.1
  73.7 1.2 collective-permute-start.14
  75.6 3.6 %collective-permute-done.1.refs_2_ = bf16[512,256]{1,0:T(8,128)(2,1)S(1)} collective-permute-done((bf16[512,256]{1,0:T(8,128)(2,1)S(1)}, bf16[512,256]{1,0:T(8,128)(2,1)S(1)}, u32[]{:S(2)}, u32[]{:S(2)}) %collective-permute-start.1) | collective-permute-done | bytes 262176 | tf_op jit(solution)/shard_map/ppermute | solution.py:257
  79.2 1.8 %collective-permute-start.15 = (bf16[2,256,256]{2,1,0:T(8,128)(2,1)S(1)}, bf16[2,256,256]{2,1,0:T(8,128)(2,1)S(1)}, u32[]{:S(2)}, u32[]{:S(2)}) collective-permute-start(bf16[2,256,256]{2,1,0:T(8,128)(2,1)S(1)} %get-tuple-element.26), channel_id=1, source_target_pairs={{0,96},{32,0},{64,32},{96,64},{1,97},{33,1},{65,33},{97,65},{2,98}... | collective-permute-start | bytes 786440 | tf_op jit(solution)/shard_map/ppermute | solution.py:200
  80.9 5.4 %collective-permute-done.2.refs_3_ = bf16[512,256]{1,0:T(8,128)(2,1)S(1)} collective-permute-done((bf16[512,256]{1,0:T(8,128)(2,1)S(1)}, bf16[512,256]{1,0:T(8,128)(2,1)S(1)}, u32[]{:S(2)}, u32[]{:S(2)}) %collective-permute-start.2) | collective-permute-done | bytes 262176 | tf_op jit(solution)/shard_map/ppermute | solution.py:257
  86.4 1.3 collective-permute-start.16
  88.9 1.4 collective-permute-start.17
  90.3 4.6 %collective-permute-done.16.refs_3_ = bf16[2,256,256]{2,1,0:T(8,128)(2,1)S(1)} collective-permute-done((bf16[2,256,256]{2,1,0:T(8,128)(2,1)S(1)}, bf16[2,256,256]{2,1,0:T(8,128)(2,1)S(1)}, u32[]{:S(2)}, u32[]{:S(2)}) %collective-permute-start.16) | collective-permute-done | bytes 262176 | tf_op jit(solution)/shard_map/ppermute | solution.py:200
  94.9 1.3 collective-permute-start.23
  96.3 1.3 collective-permute-start.24
  98.4 1.2 shard_map.30
  99.6 2.4 %shard_map.31.refs_0_ = f32[4,272,256]{2,1,0:T(8,128)S(1)} custom-call(s32[4]{0:T(128)S(1)} %pad_add_fusion.where_ref._, bf16[528,2048]{1,0:T(8,128)(2,1)S(1)} %get-tuple-element.24.left_ref, bf16[4,256,256]{2,1,0:T(8,128)(2,1)S(1)} %pad_maximum_fusion.refs_0_, bf16[4,256,256]{2,1,0:T(8,128)(2,1)S(1)} %collective-permute-done.7.refs_1_.back_ref, ...), custom_call_target="tpu_custom_call" | custom-call | tf_op jit(solution)/shard_map/pallas_call | solution.py:73
  102.1 2.4 %shard_map.34.refs_5_ = f32[4,272,256]{2,1,0:T(8,128)S(1)} custom-call(s32[4]{0:T(128)S(1)} %pad_add_fusion.where_ref._, bf16[528,2048]{1,0:T(8,128)(2,1)S(1)} %get-tuple-element.24.left_ref, bf16[4,256,256]{2,1,0:T(8,128)(2,1)S(1)} %collective-permute-done.18.refs_0_, bf16[4,256,256]{2,1,0:T(8,128)(2,1)S(1)} %collective-permute-done.19.refs_1_, ...), custom_call_target="tpu_custom_call" | custom-call | tf_op jit(solution)/shard_map/pallas_call | solution.py:73
  104.5 2.6 %shard_map.35 = (f32[256,2048]{1,0:T(8,128)S(1)}, f32[8,256]{1,0:T(8,128)S(1)}, f32[128,1,256]{2,1,0:T(1,128)S(1)}, f32[8,256]{1,0:T(8,128)}) custom-call(s32[4]{0:T(128)S(1)} %pad_add_fusion.where_ref._, bf16[528,2048]{1,0:T(8,128)(2,1)S(1)} %get-tuple-element.24.left_ref, f32[4,272,256]{2,1,0:T(8,128)S(1)} %shard_map.31.refs_0_, ...), custom_call_target="tpu_custom_call" | custom-call | tf_op jit(solution)/shard_map/pallas_call | solution.py:73
  107.1 16.1 %all_to_all.21 = f32[128,1,256]{2,1,0:T(1,128)S(1)} all-to-all(f32[128,1,256]{2,1,0:T(1,128)S(1)} %get-tuple-element.32), channel_id=1, replica_groups=mesh['x'=4,'z'=4,'c'=2,'y'=4] {'y','x','z','c'}, dimensions={0} | all-to-all | bytes 262144 | tf_op jit(solution)/shard_map/all_to_all | solution.py:45
  123.8 14.2 %all_to_all.22 = f32[128,1,256]{2,1,0:T(1,128)S(1)} all-to-all(f32[128,1,256]{2,1,0:T(1,128)S(1)} %broadcast_in_dim.12), channel_id=1, replica_groups=mesh['x'=4,'z'=4,'c'=2,'y'=4] {'y','x','z','c'}, dimensions={0} | all-to-all | bytes 262144 | tf_op jit(solution)/shard_map/all_to_all | solution.py:45
  138.6 14.2 %all_to_all.23.last_ref = f32[128,1,256]{2,1,0:T(1,128)S(1)} all-to-all(f32[128,1,256]{2,1,0:T(1,128)S(1)} %broadcast_in_dim.13), channel_id=1, replica_groups=mesh['x'=4,'z'=4,'c'=2,'y'=4] {'y','x','z','c'}, dimensions={0} | all-to-all | bytes 262144 | tf_op jit(solution)/shard_map/all_to_all | solution.py:45
  152.8 2.7 %shard_map.36 = (f32[256,2048]{1,0:T(8,128)}, f32[1,256]{1,0:T(1,128)}) custom-call(s32[4]{0:T(128)S(1)} %pad_add_fusion.where_ref._, f32[128,1,256]{2,1,0:T(1,128)S(1)} %all_to_all.23.last_ref, f32[256,2048]{1,0:T(8,128)S(1)} %get-tuple-element.30.sym_ref, f32[1,256]{1,0:T(1,128)S(1)} %fusion.3.ratio_ref, f32[8,256]{1,0:T(8,128)S(1)} %dynamic-slice_divide_fusion.col_ref), custom_call_target="tpu_custom_call" | custom-call | tf_op jit(solution)/shard_map/pallas_call | solution.py:230
  (58 shorter events, 7.4 us)
Async XLA Ops:
  0.6 58.7 %copy-start = (bf16[512,256]{1,0:T(8,128)(2,1)S(1)}, bf16[512,256]{1,0:T(8,128)(2,1)}, u32[]{:S(2)}) copy-start(bf16[512,256]{1,0:T(8,128)(2,1)} %refs_0_.1) | copy-start | bytes 786436
  0.6 1.7 %collective-permute-start.3 = (bf16[512,256]{1,0:T(8,128)(2,1)}, bf16[512,256]{1,0:T(8,128)(2,1)S(1)}, u32[]{:S(2)}, u32[]{:S(2)}) collective-permute-start(bf16[512,256]{1,0:T(8,128)(2,1)} %refs_0_.1), channel_id=1, source_target_pairs={{0,0},{4,4},{8,8},{12,12},{16,16},{20,20},{24,24},{28,28},{1,32},{... | collective-permute-start | bytes 786440 | tf_op jit(solution)/shard_map/ppermute | solution.py:245
  2.4 10.2 %collective-permute-start.6 = (bf16[256,256]{1,0:T(8,128)(2,1)S(1)}, bf16[256,256]{1,0:T(8,128)(2,1)S(1)}, u32[]{:S(2)}, u32[]{:S(2)}) collective-permute-start(bf16[256,256]{1,0:T(8,128)(2,1)S(1)} %get-tuple-element.41), channel_id=1, source_target_pairs={{0,24},{8,0},{16,8},{24,16},{1,25},{9,1},{17,9},{25,17},{2,26},{10... | collective-permute-start | bytes 393224 | tf_op jit(solution)/shard_map/ppermute | solution.py:41
  7.1 5.7 %collective-permute-start.5 = (bf16[256,256]{1,0:T(8,128)(2,1)S(1)}, bf16[256,256]{1,0:T(8,128)(2,1)S(1)}, u32[]{:S(2)}, u32[]{:S(2)}) collective-permute-start(bf16[256,256]{1,0:T(8,128)(2,1)S(1)} %get-tuple-element.41), channel_id=1, source_target_pairs={{0,16},{8,24},{16,0},{24,8},{1,17},{9,25},{17,1},{25,9},{2,18},{10... | collective-permute-start | bytes 393224 | tf_op jit(solution)/shard_map/ppermute | solution.py:41
  7.1 9.1 %collective-permute-start.4 = (bf16[256,256]{1,0:T(8,128)(2,1)S(1)}, bf16[256,256]{1,0:T(8,128)(2,1)S(1)}, u32[]{:S(2)}, u32[]{:S(2)}) collective-permute-start(bf16[256,256]{1,0:T(8,128)(2,1)S(1)} %get-tuple-element.41), channel_id=1, source_target_pairs={{0,8},{8,16},{16,24},{24,0},{1,9},{9,17},{17,25},{25,1},{2,10},{10... | collective-permute-start | bytes 393224 | tf_op jit(solution)/shard_map/ppermute | solution.py:41
  16.3 51.8 %collective-permute-start.7 = (bf16[4,256,256]{2,1,0:T(8,128)(2,1)S(1)}, bf16[4,256,256]{2,1,0:T(8,128)(2,1)S(1)}, u32[]{:S(2)}, u32[]{:S(2)}) collective-permute-start(bf16[4,256,256]{2,1,0:T(8,128)(2,1)S(1)} %pad_maximum_fusion.refs_0_), channel_id=1, source_target_pairs={{0,32},{32,64},{64,96},{96,0},{1,33},{33,65},{65,97},{97,1},{2,34}... | collective-permute-start | bytes 1572872 | tf_op jit(solution)/shard_map/ppermute | solution.py:190
  24.3 33.6 %collective-permute-start.11 = (bf16[256,256]{1,0:T(8,128)(2,1)S(1)}, bf16[256,256]{1,0:T(8,128)(2,1)S(1)}, u32[]{:S(2)}, u32[]{:S(2)}) collective-permute-start(bf16[256,256]{1,0:T(8,128)(2,1)S(1)} %get-tuple-element.40), channel_id=1, source_target_pairs={{0,96},{32,0},{64,32},{96,64},{1,97},{33,1},{65,33},{97,65},{2,98}... | collective-permute-start | bytes 393224 | tf_op jit(solution)/shard_map/ppermute | solution.py:41
  35.1 22.8 %collective-permute-start.10 = (bf16[256,256]{1,0:T(8,128)(2,1)S(1)}, bf16[256,256]{1,0:T(8,128)(2,1)S(1)}, u32[]{:S(2)}, u32[]{:S(2)}) collective-permute-start(bf16[256,256]{1,0:T(8,128)(2,1)S(1)} %get-tuple-element.40), channel_id=1, source_target_pairs={{0,64},{32,96},{64,0},{96,32},{1,65},{33,97},{65,1},{97,33},{2,66}... | collective-permute-start | bytes 393224 | tf_op jit(solution)/shard_map/ppermute | solution.py:41
  36.3 21.6 %collective-permute-start.9 = (bf16[256,256]{1,0:T(8,128)(2,1)S(1)}, bf16[256,256]{1,0:T(8,128)(2,1)S(1)}, u32[]{:S(2)}, u32[]{:S(2)}) collective-permute-start(bf16[256,256]{1,0:T(8,128)(2,1)S(1)} %get-tuple-element.40), channel_id=1, source_target_pairs={{0,32},{32,64},{64,96},{96,0},{1,33},{33,65},{65,97},{97,1},{2,34}... | collective-permute-start | bytes 393224 | tf_op jit(solution)/shard_map/ppermute | solution.py:41
  57.9 13.1 %collective-permute-start.8 = (bf16[4,256,256]{2,1,0:T(8,128)(2,1)S(1)}, bf16[4,256,256]{2,1,0:T(8,128)(2,1)S(1)}, u32[]{:S(2)}, u32[]{:S(2)}) collective-permute-start(bf16[4,256,256]{2,1,0:T(8,128)(2,1)S(1)} %pad_maximum_fusion.refs_0_), channel_id=1, source_target_pairs={{0,96},{32,0},{64,32},{96,64},{1,97},{33,1},{65,33},{97,65},{2,98}... | collective-permute-start | bytes 1572872 | tf_op jit(solution)/shard_map/ppermute | solution.py:190
  58.0 14.4 %collective-permute-start.12 = (bf16[4,256,256]{2,1,0:T(8,128)(2,1)S(1)}, bf16[4,256,256]{2,1,0:T(8,128)(2,1)S(1)}, u32[]{:S(2)}, u32[]{:S(2)}) collective-permute-start(bf16[4,256,256]{2,1,0:T(8,128)(2,1)S(1)} %pad_maximum_fusion.1.refs_3_), channel_id=1, source_target_pairs={{0,8},{8,16},{16,24},{24,0},{1,9},{9,17},{17,25},{25,1},{2,10},{10... | collective-permute-start | bytes 1572872 | tf_op jit(solution)/shard_map/ppermute | solution.py:190
  59.3 7.2 %collective-permute-start = (bf16[512,256]{1,0:T(8,128)(2,1)S(1)}, bf16[512,256]{1,0:T(8,128)(2,1)S(1)}, u32[]{:S(2)}, u32[]{:S(2)}) collective-permute-start(bf16[512,256]{1,0:T(8,128)(2,1)S(1)} %copy-done), channel_id=1, source_target_pairs={{0,3},{1,0},{2,1},{3,2},{4,7},{5,4},{6,5},{7,6},{8,11},{9,8},{10,9... | collective-permute-start | bytes 786440 | tf_op jit(solution)/shard_map/ppermute | solution.py:257
  59.5 14.3 %collective-permute-start.13 = (bf16[4,256,256]{2,1,0:T(8,128)(2,1)S(1)}, bf16[4,256,256]{2,1,0:T(8,128)(2,1)S(1)}, u32[]{:S(2)}, u32[]{:S(2)}) collective-permute-start(bf16[4,256,256]{2,1,0:T(8,128)(2,1)S(1)} %pad_maximum_fusion.1.refs_3_), channel_id=1, source_target_pairs={{0,24},{8,0},{16,8},{24,16},{1,25},{9,1},{17,9},{25,17},{2,26},{10... | collective-permute-start | bytes 1572872 | tf_op jit(solution)/shard_map/ppermute | solution.py:190
  66.5 21.1 %collective-permute-start.18 = (bf16[4,256,256]{2,1,0:T(8,128)(2,1)S(1)}, bf16[4,256,256]{2,1,0:T(8,128)(2,1)S(1)}, u32[]{:S(2)}, u32[]{:S(2)}) collective-permute-start(bf16[4,256,256]{2,1,0:T(8,128)(2,1)S(1)} %pad_maximum_fusion.refs_0_), channel_id=1, source_target_pairs={{0,4},{4,0},{1,5},{5,1},{2,6},{6,2},{3,7},{7,3},{8,12},{12,8},{9,1... | collective-permute-start | bytes 1572872 | tf_op jit(solution)/shard_map/ppermute | solution.py:204
  68.1 20.3 %collective-permute-start.21 = (bf16[4,256,256]{2,1,0:T(8,128)(2,1)S(1)}, bf16[4,256,256]{2,1,0:T(8,128)(2,1)S(1)}, u32[]{:S(2)}, u32[]{:S(2)}) collective-permute-start(bf16[4,256,256]{2,1,0:T(8,128)(2,1)S(1)} %pad_maximum_fusion.1.refs_3_), channel_id=1, source_target_pairs={{0,4},{4,0},{1,5},{5,1},{2,6},{6,2},{3,7},{7,3},{8,12},{12,8},{9,1... | collective-permute-start | bytes 1572872 | tf_op jit(solution)/shard_map/ppermute | solution.py:204
  71.0 8.2 %collective-permute-start.1 = (bf16[512,256]{1,0:T(8,128)(2,1)S(1)}, bf16[512,256]{1,0:T(8,128)(2,1)S(1)}, u32[]{:S(2)}, u32[]{:S(2)}) collective-permute-start(bf16[512,256]{1,0:T(8,128)(2,1)S(1)} %copy-done), channel_id=1, source_target_pairs={{0,2},{1,3},{2,0},{3,1},{4,6},{5,7},{6,4},{7,5},{8,10},{9,11},{10,... | collective-permute-start | bytes 786440 | tf_op jit(solution)/shard_map/ppermute | solution.py:257
  72.4 14.0 %collective-permute-start.2 = (bf16[512,256]{1,0:T(8,128)(2,1)S(1)}, bf16[512,256]{1,0:T(8,128)(2,1)S(1)}, u32[]{:S(2)}, u32[]{:S(2)}) collective-permute-start(bf16[512,256]{1,0:T(8,128)(2,1)S(1)} %copy-done), channel_id=1, source_target_pairs={{0,1},{1,2},{2,3},{3,0},{4,5},{5,6},{6,7},{7,4},{8,9},{9,10},{10,1... | collective-permute-start | bytes 786440 | tf_op jit(solution)/shard_map/ppermute | solution.py:257
  73.7 14.7 %collective-permute-start.14 = (bf16[2,256,256]{2,1,0:T(8,128)(2,1)S(1)}, bf16[2,256,256]{2,1,0:T(8,128)(2,1)S(1)}, u32[]{:S(2)}, u32[]{:S(2)}) collective-permute-start(bf16[2,256,256]{2,1,0:T(8,128)(2,1)S(1)} %get-tuple-element.25), channel_id=1, source_target_pairs={{0,32},{32,64},{64,96},{96,0},{1,33},{33,65},{65,97},{97,1},{2,34}... | collective-permute-start | bytes 786440 | tf_op jit(solution)/shard_map/ppermute | solution.py:200
  79.2 9.7 %collective-permute-start.15 = (bf16[2,256,256]{2,1,0:T(8,128)(2,1)S(1)}, bf16[2,256,256]{2,1,0:T(8,128)(2,1)S(1)}, u32[]{:S(2)}, u32[]{:S(2)}) collective-permute-start(bf16[2,256,256]{2,1,0:T(8,128)(2,1)S(1)} %get-tuple-element.26), channel_id=1, source_target_pairs={{0,96},{32,0},{64,32},{96,64},{1,97},{33,1},{65,33},{97,65},{2,98}... | collective-permute-start | bytes 786440 | tf_op jit(solution)/shard_map/ppermute | solution.py:200
  86.4 8.6 %collective-permute-start.16 = (bf16[2,256,256]{2,1,0:T(8,128)(2,1)S(1)}, bf16[2,256,256]{2,1,0:T(8,128)(2,1)S(1)}, u32[]{:S(2)}, u32[]{:S(2)}) collective-permute-start(bf16[2,256,256]{2,1,0:T(8,128)(2,1)S(1)} %get-tuple-element.27), channel_id=1, source_target_pairs={{0,8},{8,16},{16,24},{24,0},{1,9},{9,17},{17,25},{25,1},{2,10},{10... | collective-permute-start | bytes 786440 | tf_op jit(solution)/shard_map/ppermute | solution.py:200
  87.6 10.0 %collective-permute-start.19 = (bf16[4,256,256]{2,1,0:T(8,128)(2,1)S(1)}, bf16[4,256,256]{2,1,0:T(8,128)(2,1)S(1)}, u32[]{:S(2)}, u32[]{:S(2)}) collective-permute-start(bf16[4,256,256]{2,1,0:T(8,128)(2,1)S(1)} %collective-permute-done.7.refs_1_.back_ref), channel_id=1, source_target_pairs={{0,4},{4,0},{1,5},{5,1},{2,6},{6,2},{3,7},{7,3},{8,12},{12,8},{9,1... | collective-permute-start | bytes 1572872 | tf_op jit(solution)/shard_map/ppermute | solution.py:204
  88.4 9.3 %collective-permute-start.20 = (bf16[4,256,256]{2,1,0:T(8,128)(2,1)S(1)}, bf16[4,256,256]{2,1,0:T(8,128)(2,1)S(1)}, u32[]{:S(2)}, u32[]{:S(2)}) collective-permute-start(bf16[4,256,256]{2,1,0:T(8,128)(2,1)S(1)} %collective-permute-done.8.refs_2_.on_ref), channel_id=1, source_target_pairs={{0,4},{4,0},{1,5},{5,1},{2,6},{6,2},{3,7},{7,3},{8,12},{12,8},{9,1... | collective-permute-start | bytes 1572872 | tf_op jit(solution)/shard_map/ppermute | solution.py:204
  88.5 9.7 %collective-permute-start.22 = (bf16[4,256,256]{2,1,0:T(8,128)(2,1)S(1)}, bf16[4,256,256]{2,1,0:T(8,128)(2,1)S(1)}, u32[]{:S(2)}, u32[]{:S(2)}) collective-permute-start(bf16[4,256,256]{2,1,0:T(8,128)(2,1)S(1)} %collective-permute-done.12.refs_4_.back_ref), channel_id=1, source_target_pairs={{0,4},{4,0},{1,5},{5,1},{2,6},{6,2},{3,7},{7,3},{8,12},{12,8},{9,1... | collective-permute-start | bytes 1572872 | tf_op jit(solution)/shard_map/ppermute | solution.py:204
  88.9 7.4 %collective-permute-start.17 = (bf16[2,256,256]{2,1,0:T(8,128)(2,1)S(1)}, bf16[2,256,256]{2,1,0:T(8,128)(2,1)S(1)}, u32[]{:S(2)}, u32[]{:S(2)}) collective-permute-start(bf16[2,256,256]{2,1,0:T(8,128)(2,1)S(1)} %get-tuple-element.28), channel_id=1, source_target_pairs={{0,24},{8,0},{16,8},{24,16},{1,25},{9,1},{17,9},{25,17},{2,26},{10... | collective-permute-start | bytes 786440 | tf_op jit(solution)/shard_map/ppermute | solution.py:200
  94.9 7.1 %collective-permute-start.23 = (bf16[4,256,256]{2,1,0:T(8,128)(2,1)S(1)}, bf16[4,256,256]{2,1,0:T(8,128)(2,1)S(1)}, u32[]{:S(2)}, u32[]{:S(2)}) collective-permute-start(bf16[4,256,256]{2,1,0:T(8,128)(2,1)S(1)} %collective-permute-done.13.refs_5_.on_ref), channel_id=1, source_target_pairs={{0,4},{4,0},{1,5},{5,1},{2,6},{6,2},{3,7},{7,3},{8,12},{12,8},{9,1... | collective-permute-start | bytes 1572872 | tf_op jit(solution)/shard_map/ppermute | solution.py:204
  96.3 8.1 %collective-permute-start.24 = (bf16[2,256,256]{2,1,0:T(8,128)(2,1)S(1)}, bf16[2,256,256]{2,1,0:T(8,128)(2,1)S(1)}, u32[]{:S(2)}, u32[]{:S(2)}) collective-permute-start(bf16[2,256,256]{2,1,0:T(8,128)(2,1)S(1)} %collective-permute-done.14.refs_1_), channel_id=1, source_target_pairs={{0,4},{4,0},{1,5},{5,1},{2,6},{6,2},{3,7},{7,3},{8,12},{12,8},{9,1... | collective-permute-start | bytes 786440 | tf_op jit(solution)/shard_map/ppermute | solution.py:204
  97.6 6.9 %collective-permute-start.25 = (bf16[2,256,256]{2,1,0:T(8,128)(2,1)S(1)}, bf16[2,256,256]{2,1,0:T(8,128)(2,1)S(1)}, u32[]{:S(2)}, u32[]{:S(2)}) collective-permute-start(bf16[2,256,256]{2,1,0:T(8,128)(2,1)S(1)} %collective-permute-done.15.refs_2_), channel_id=1, source_target_pairs={{0,4},{4,0},{1,5},{5,1},{2,6},{6,2},{3,7},{7,3},{8,12},{12,8},{9,1... | collective-permute-start | bytes 786440 | tf_op jit(solution)/shard_map/ppermute | solution.py:204
  97.6 6.9 %collective-permute-start.26 = (bf16[2,256,256]{2,1,0:T(8,128)(2,1)S(1)}, bf16[2,256,256]{2,1,0:T(8,128)(2,1)S(1)}, u32[]{:S(2)}, u32[]{:S(2)}) collective-permute-start(bf16[2,256,256]{2,1,0:T(8,128)(2,1)S(1)} %collective-permute-done.16.refs_3_), channel_id=1, source_target_pairs={{0,4},{4,0},{1,5},{5,1},{2,6},{6,2},{3,7},{7,3},{8,12},{12,8},{9,1... | collective-permute-start | bytes 786440 | tf_op jit(solution)/shard_map/ppermute | solution.py:204
  98.2 6.4 %collective-permute-start.27 = (bf16[2,256,256]{2,1,0:T(8,128)(2,1)S(1)}, bf16[2,256,256]{2,1,0:T(8,128)(2,1)S(1)}, u32[]{:S(2)}, u32[]{:S(2)}) collective-permute-start(bf16[2,256,256]{2,1,0:T(8,128)(2,1)S(1)} %collective-permute-done.17.refs_4_), channel_id=1, source_target_pairs={{0,4},{4,0},{1,5},{5,1},{2,6},{6,2},{3,7},{7,3},{8,12},{12,8},{9,1... | collective-permute-start | bytes 786440 | tf_op jit(solution)/shard_map/ppermute | solution.py:204
